TPU v7x, 32 devices: a whole 2x2x4 slice. The times are simulated.
32 devices in a mesh: rep: 8 (over z, x), shard: 4 (over y, core).
Axes of the slice: x: 2, y: 2, z: 4, core: 2. Of those that a mesh axis runs over, the one named last changes fastest.
Arguments:
- tokens: bfloat16 [16384, 1024], P(('rep', 'shard')), may hold values from -6 to 6
- seq_lengths: int32 [8, 8], P('rep'), may hold values from 128 to 384, as said below
- owner_order: int32 [8, 8], P('rep'), may hold values from 0 to 7, as said below
- gain_attn: bfloat16 [1024], P('shard'), may hold values from 0.5 to 1.5
- w_input: bfloat16 [1024, 4096], P('shard'), may hold values from -0.1875 to 0.1875
- w_step: bfloat16 [1024, 24], P('shard'), may hold values from -0.046875 to 0.046875
- step_bias: bfloat16 [24], P('shard'), may hold values from -4 to -1
- decay_log: bfloat16 [24], P('shard'), may hold values from 0 to 2.6875
- skip_scale: bfloat16 [24], P('shard'), may hold values from 0.5 to 1.5
- conv_weight: bfloat16 [4, 1792], P(None, 'shard'), may hold values from -3 to 3
- conv_bias: bfloat16 [1792], P('shard'), may hold values from -1.5 to 1.5
- gain_ssm: bfloat16 [1536], P('shard'), may hold values from 0.5 to 1.5
- w_output: bfloat16 [2048, 1024], P('shard'), may hold values from -0.1875 to 0.1875
- gain_ffn: bfloat16 [1024], P('shard'), may hold values from 0.5 to 1.5
- w_gate_up: bfloat16 [1024, 4096], P('shard'), may hold values from -0.1875 to 0.1875
- w_down: bfloat16 [2048, 1024], P('shard'), may hold values from -0.125 to 0.125
- cotangent: bfloat16 [16384, 1024], P(('rep', 'shard')), may hold values from -6 to 6
Outputs:
- block_out: bfloat16 [16384, 1024], P(('rep', 'shard'))
- grad_tokens: bfloat16 [16384, 1024], P(('rep', 'shard'))
- grad_gain_attn: float32 [1024], P('shard')
- grad_w_input: float32 [1024, 4096], P('shard')
- grad_w_step: float32 [1024, 24], P('shard')
- grad_step_bias: float32 [24], P('shard')
- grad_decay_log: float32 [24], P('shard')
- grad_skip_scale: float32 [24], P('shard')
- grad_conv_weight: float32 [4, 1792], P(None, 'shard')
- grad_conv_bias: float32 [1792], P('shard')
- grad_gain_ssm: float32 [1536], P('shard')
- grad_w_output: float32 [2048, 1024], P('shard')
- grad_gain_ffn: float32 [1024], P('shard')
- grad_w_gate_up: float32 [1024, 4096], P('shard')
- grad_w_down: float32 [2048, 1024], P('shard')
Inputs may be any that keep to these rules, and one draw needn't show every extreme that they name: `seq_lengths`: device d of a group (index along shard) owns the sequences at owner positions 2d and 2d+1, whose lengths sum to 512; in every group one sequence has exactly 128 tokens and its partner 512 - 128. `owner_order`: each row is a permutation of the group's 8 sequences.
All inputs are finite; a program needn't handle non-finite values.
Results may differ from a plain program's by a relative error of at most 0.012.
Values may be sent and summed in bfloat16 or wider, within the bound.
No kernel may reach another device: no remote copies, remote signals or barrier semaphores. Data moves between devices by JAX's collectives and lax.ppermute only.
A program may use at most 384 MiB of HBM per device.

v0:
```python
from functools import partial
import math

import jax
import jax.numpy as jnp
from jax import lax
from jax.sharding import PartitionSpec as P

QUERY_HEADS = 8
KEY_VALUE_HEADS = 2
HEAD_SIZE = 64
SSM_HEADS = 24
SSM_HD = 64
STATE = 128
INNER = 1536
QUERY_KEY_VALUE = 768


EPS = 1e-05
ROPE_BASE = 100000000000.0


def rms_scale(values):
    return lax.rsqrt(jnp.mean(values * values, axis=-1, keepdims=True) + EPS)


def rms_norm(values, gain):
    return values * rms_scale(values) * gain


def rope_angles(position, head_dim):
    half = head_dim // 2
    ladder = jnp.arange(half, dtype=jnp.float32) * (2.0 / head_dim)
    return position.astype(jnp.float32)[:, None] * jnp.exp(-math.log(ROPE_BASE) * ladder)


def apply_rotary(values, rotary_angles):
    half = values.shape[-1] // 2
    cosine = jnp.cos(rotary_angles)[:, None, :]
    sine = jnp.sin(rotary_angles)[:, None, :]
    first = values[..., :half]
    second = values[..., half:]
    return jnp.concatenate([first * cosine - second * sine, second * cosine + first * sine], -1)


def conv_silu(conv_in, conv_weight, conv_bias, segment):
    taps = conv_weight.shape[0]
    width = conv_in.shape[1]
    mixed = conv_bias + conv_in * conv_weight[taps - 1]
    for back in range(1, taps):
        shifted = jnp.concatenate([jnp.zeros((back, width), jnp.float32), conv_in[:-back]], 0)
        same = jnp.concatenate(
            [
                jnp.zeros((back,), jnp.float32),
                (segment[back:] == segment[:-back]).astype(jnp.float32),
            ],
            0,
        )
        mixed = mixed + shifted * same[:, None] * conv_weight[taps - 1 - back]
    return jax.nn.silu(mixed)


def gated_norm(ssm_y, gate_z, gain):
    gated = ssm_y * jax.nn.silu(gate_z)
    return gated * rms_scale(gated) * gain


def swiglu(gate_up):
    half = gate_up.shape[1] // 2
    return jax.nn.silu(gate_up[:, :half]) * gate_up[:, half:]


def group_tables(lengths, order, input_rows, device):
    count = lengths.shape[0]
    slots = jnp.arange(count, dtype=jnp.int32)
    starts = jnp.cumsum(lengths) - lengths
    pick = (order[:, None] == slots[None, :]).astype(jnp.int32)
    owner_len = jnp.sum(pick * lengths[None, :], 1)
    owner_start = jnp.cumsum(owner_len) - owner_len
    owner_src = jnp.sum(pick * starts[None, :], 1)
    first_len = jnp.sum(jnp.where(slots == 2 * device, owner_len, 0))
    first_src = jnp.sum(jnp.where(slots == 2 * device, owner_src, 0))
    second_src = jnp.sum(jnp.where(slots == 2 * device + 1, owner_src, 0))
    local = jnp.arange(input_rows, dtype=jnp.int32)
    segment = (local >= first_len).astype(jnp.int32)
    position = local - segment * first_len
    source = jnp.where(segment > 0, second_src, first_src) + position
    given = device * input_rows + local
    seq_id = jnp.sum((starts[None, :] <= given[:, None]).astype(jnp.int32), 1) - 1
    member = (seq_id[:, None] == slots[None, :]).astype(jnp.int32)
    seq_start = jnp.sum(member * starts[None, :], 1)
    seq_owner_start = jnp.sum(pick * owner_start[:, None], 0)
    target = jnp.sum(member * seq_owner_start[None, :], 1) + given - seq_start
    return (source, position, segment, target)


def pick_rows(carry, pieces, wanted):
    count = pieces[0].shape[0]
    inside = (wanted >= 0) & (wanted < count)
    index = jnp.clip(wanted, 0, count - 1)
    return tuple(
        (jnp.where(inside[:, None], piece[index], kept) for piece, kept in zip(pieces, carry))
    )


def block_mask(segment, count):
    places = jnp.arange(segment.shape[0])
    here = jnp.arange(count)
    return ((places[None, :] <= here[:, None]) & (segment[None, :] == segment[:, None])).astype(
        jnp.float32
    )


def attention_scores(grouped_heads, key_matrix, mask):
    score_matrix = jnp.einsum(
        "mytl,byl->ytmb", grouped_heads, key_matrix, preferred_element_type=jnp.float32
    ) * HEAD_SIZE ** (-0.5)
    return jnp.where(mask[None, None] > 0, score_matrix, -1e30)


def attention_forward(query_rows, key_matrix, value_matrix, segment):
    input_rows = query_rows.shape[0]
    hybrid_block = min(512, input_rows)
    head_group = QUERY_HEADS // KEY_VALUE_HEADS
    mask = block_mask(segment, hybrid_block)
    grouped_heads = query_rows.reshape(hybrid_block, KEY_VALUE_HEADS, head_group, HEAD_SIZE)
    score_matrix = attention_scores(grouped_heads, key_matrix, mask)
    largest = jnp.max(score_matrix, -1, keepdims=True)
    raised = jnp.exp(score_matrix - largest)
    total = jnp.sum(raised, -1, keepdims=True)
    attn_weights = (raised / total).astype(jnp.bfloat16)
    mixed = jnp.einsum(
        "kgij,jkd->ikgd", attn_weights, value_matrix, preferred_element_type=jnp.float32
    )
    outputs = mixed.reshape(hybrid_block, QUERY_HEADS * HEAD_SIZE).astype(jnp.bfloat16)
    totals = largest + jnp.log(total)
    return (outputs, totals)


def attention_backward(query_rows, key_matrix, value_matrix, segment, log_total, output_gradient):
    input_rows = query_rows.shape[0]
    hybrid_block = min(512, input_rows)
    head_group = QUERY_HEADS // KEY_VALUE_HEADS
    mask = block_mask(segment, hybrid_block)
    grouped_heads = query_rows.reshape(hybrid_block, KEY_VALUE_HEADS, head_group, HEAD_SIZE)
    score_matrix = attention_scores(grouped_heads, key_matrix, mask)
    attn_weights = jnp.exp(score_matrix - log_total)
    weights_low = attn_weights.astype(jnp.bfloat16)
    gradient_rows = output_gradient.reshape(hybrid_block, KEY_VALUE_HEADS, head_group, HEAD_SIZE)
    grad_weights = jnp.einsum(
        "mytl,byl->ytmb", gradient_rows, value_matrix, preferred_element_type=jnp.float32
    )
    value_gradient = jnp.einsum(
        "kgij,ikgd->jkd", weights_low, gradient_rows, preferred_element_type=jnp.float32
    )
    inner = jnp.sum(grad_weights * attn_weights, -1, keepdims=True)
    grad_scores = (attn_weights * (grad_weights - inner) * HEAD_SIZE ** (-0.5)).astype(jnp.bfloat16)
    grad_query_parts = jnp.einsum(
        "kgij,jkd->ikgd", grad_scores, key_matrix, preferred_element_type=jnp.float32
    ).reshape(hybrid_block, QUERY_HEADS, HEAD_SIZE)
    grad_keys = jnp.einsum(
        "kgij,ikgd->jkd", grad_scores, grouped_heads, preferred_element_type=jnp.float32
    )
    return (grad_query_parts, grad_keys, value_gradient)


def decay_weights(cumulative, step, mask, lower, count, first, each):
    cum_rows = cumulative[lower : lower + count, first : first + each]
    cum_all = cumulative[:, first : first + each]
    log_gap = cum_rows.T[:, :, None] - cum_all.T[:, None, :]
    decay = jnp.exp(jnp.where(mask[None] > 0, log_gap, 0.0)) * mask[None]
    return (decay, decay * step[:, first : first + each].T[:, None, :])


def ssd_forward(c_low, b_low, x_low, step, cumulative, segment):
    input_rows = c_low.shape[0]
    hybrid_block = min(512, input_rows)
    heads = x_low.shape[1]
    each = min(8, heads)
    mask = block_mask(segment, hybrid_block)
    intersection = jnp.einsum("is,js->ij", c_low, b_low, preferred_element_type=jnp.float32)
    parts = []
    for first in range(0, heads, each):
        decay, weighted = decay_weights(cumulative, step, mask, 0, hybrid_block, first, each)
        mixer = (intersection[None] * weighted).astype(jnp.bfloat16)
        parts.append(
            jnp.einsum(
                "hij,jhd->ihd",
                mixer,
                x_low[:, first : first + each],
                preferred_element_type=jnp.float32,
            )
        )
    outputs = jnp.concatenate(parts, 1)
    return outputs


def ssd_backward(c_low, b_low, x_low, step, cumulative, segment, grad_y):
    input_rows = c_low.shape[0]
    hybrid_block = min(512, input_rows)
    heads = x_low.shape[1]
    each = min(8, heads)
    grad_x = jnp.zeros(x_low.shape, jnp.float32)
    grad_cum = jnp.zeros((input_rows, heads), jnp.float32)
    grad_step = jnp.zeros((input_rows, heads), jnp.float32)
    mask = block_mask(segment, hybrid_block)
    intersection = jnp.einsum("is,js->ij", c_low, b_low, preferred_element_type=jnp.float32)
    grad_intersection = jnp.zeros((hybrid_block, input_rows), jnp.float32)
    for first in range(0, heads, each):
        decay, weighted = decay_weights(cumulative, step, mask, 0, hybrid_block, first, each)
        mixer = (intersection[None] * weighted).astype(jnp.bfloat16)
        gradient_rows = grad_y[0:hybrid_block, first : first + each]
        grad_mixer = jnp.einsum(
            "ihd,jhd->hij",
            gradient_rows,
            x_low[:, first : first + each],
            preferred_element_type=jnp.float32,
        )
        grad_x = grad_x.at[:, first : first + each].add(
            jnp.einsum("hij,ihd->jhd", mixer, gradient_rows, preferred_element_type=jnp.float32)
        )
        grad_intersection = grad_intersection + jnp.sum(grad_mixer * weighted, 0)
        grad_weighted = grad_mixer * intersection[None]
        grad_step = grad_step.at[:, first : first + each].add(jnp.sum(grad_weighted * decay, 1).T)
        grad_gap = grad_weighted * weighted
        grad_cum = grad_cum.at[0:hybrid_block, first : first + each].add(jnp.sum(grad_gap, 2).T)
        grad_cum = grad_cum.at[:, first : first + each].add(-jnp.sum(grad_gap, 1).T)
    intersection_low = grad_intersection.astype(jnp.bfloat16)
    grad_c_parts = jnp.dot(intersection_low, b_low, preferred_element_type=jnp.float32)
    grad_b = jnp.einsum("ij,is->js", intersection_low, c_low, preferred_element_type=jnp.float32)
    return (grad_x, grad_cum, grad_step, grad_b, grad_c_parts)


def layer_forward(weights, own_tokens, position, segment):
    (
        gain_attn,
        w_input,
        w_step,
        step_bias,
        decay_log,
        skip_scale,
        conv_weight,
        conv_bias,
        gain_ssm,
        w_output,
        gain_ffn,
        w_gate_up,
        w_down,
    ) = weights
    input_rows = own_tokens.shape[0]
    tokens_full = own_tokens.astype(jnp.float32)
    normed = rms_norm(tokens_full, gain_attn.astype(jnp.float32)).astype(jnp.bfloat16)
    projected_rows = jnp.dot(normed, w_input, preferred_element_type=jnp.float32)
    step_raw = jnp.dot(normed, w_step, preferred_element_type=jnp.float32)
    rotary_angles = rope_angles(position, HEAD_SIZE)
    query_rows = apply_rotary(
        projected_rows[:, : QUERY_HEADS * HEAD_SIZE].reshape(input_rows, QUERY_HEADS, HEAD_SIZE),
        rotary_angles,
    ).astype(jnp.bfloat16)
    key_matrix = apply_rotary(
        projected_rows[
            :, QUERY_HEADS * HEAD_SIZE : QUERY_KEY_VALUE - KEY_VALUE_HEADS * HEAD_SIZE
        ].reshape(input_rows, KEY_VALUE_HEADS, HEAD_SIZE),
        rotary_angles,
    ).astype(jnp.bfloat16)
    value_matrix = (
        projected_rows[:, QUERY_KEY_VALUE - KEY_VALUE_HEADS * HEAD_SIZE : QUERY_KEY_VALUE]
        .reshape(input_rows, KEY_VALUE_HEADS, HEAD_SIZE)
        .astype(jnp.bfloat16)
    )
    gate_z = projected_rows[:, QUERY_KEY_VALUE : QUERY_KEY_VALUE + INNER]
    conv_in = projected_rows[:, QUERY_KEY_VALUE + INNER :]
    conv_out = conv_silu(
        conv_in, conv_weight.astype(jnp.float32), conv_bias.astype(jnp.float32), segment
    )
    inner_x = conv_out[:, :INNER].reshape(input_rows, SSM_HEADS, SSM_HD)
    b_low = conv_out[:, INNER : INNER + STATE].astype(jnp.bfloat16)
    c_low = conv_out[:, INNER + STATE :].astype(jnp.bfloat16)
    step_pre = step_raw + step_bias.astype(jnp.float32)
    step = jax.nn.softplus(step_pre)
    rate = -jnp.exp(decay_log.astype(jnp.float32))
    cumulative = jnp.cumsum(step * rate, axis=0)
    x_low = inner_x.astype(jnp.bfloat16)
    ssd_out = ssd_forward(c_low, b_low, x_low, step, cumulative, segment)
    ssm_y = (ssd_out + skip_scale.astype(jnp.float32)[None, :, None] * inner_x).reshape(
        input_rows, INNER
    )
    ssm_out = gated_norm(ssm_y, gate_z, gain_ssm.astype(jnp.float32)).astype(jnp.bfloat16)
    attn_out, log_total = attention_forward(query_rows, key_matrix, value_matrix, segment)
    joined = jnp.concatenate([attn_out, ssm_out], 1)
    middle = tokens_full + jnp.dot(joined, w_output, preferred_element_type=jnp.float32)
    normed_ffn = rms_norm(middle, gain_ffn.astype(jnp.float32)).astype(jnp.bfloat16)
    gate_up = jnp.dot(normed_ffn, w_gate_up, preferred_element_type=jnp.float32)
    hidden = swiglu(gate_up).astype(jnp.bfloat16)
    block_out = middle + jnp.dot(hidden, w_down, preferred_element_type=jnp.float32)
    saved = {
        "tokens": tokens_full,
        "normed": normed,
        "projected": projected_rows,
        "angles": rotary_angles,
        "queries": query_rows,
        "key_rows": key_matrix,
        "value_rows": value_matrix,
        "gate_z": gate_z,
        "conv_in": conv_in,
        "inner_x": inner_x,
        "b_low": b_low,
        "c_low": c_low,
        "x_low": x_low,
        "step_pre": step_pre,
        "step": step,
        "rate": rate,
        "cumulative": cumulative,
        "ssm_y": ssm_y,
        "log_total": log_total,
        "joined": joined,
        "middle": middle,
        "normed_ffn": normed_ffn,
        "gate_up": gate_up,
        "hidden": hidden,
    }
    return (block_out.astype(jnp.bfloat16), saved)


def layer_backward(weights, saved, segment, cot_rows):
    (
        gain_attn,
        w_input,
        w_step,
        step_bias,
        decay_log,
        skip_scale,
        conv_weight,
        conv_bias,
        gain_ssm,
        w_output,
        gain_ffn,
        w_gate_up,
        w_down,
    ) = weights
    input_rows = cot_rows.shape[0]
    grad_w_down = jnp.einsum(
        "ti,td->id", saved["hidden"], cot_rows, preferred_element_type=jnp.float32
    )
    grad_hidden = jnp.einsum("td,id->ti", cot_rows, w_down, preferred_element_type=jnp.float32)
    swiglu_back = jax.vjp(swiglu, saved["gate_up"])[1]
    grad_gate_up = swiglu_back(grad_hidden)[0].astype(jnp.bfloat16)
    grad_w_gate_up = jnp.einsum(
        "ti,tj->ij", saved["normed_ffn"], grad_gate_up, preferred_element_type=jnp.float32
    )
    grad_normed_ffn = jnp.einsum(
        "tj,ij->ti", grad_gate_up, w_gate_up, preferred_element_type=jnp.float32
    )
    ffn_back = jax.vjp(rms_norm, saved["middle"], gain_ffn.astype(jnp.float32))[1]
    grad_middle_norm, grad_gain_ffn = ffn_back(grad_normed_ffn)
    grad_middle = cot_rows.astype(jnp.float32) + grad_middle_norm
    middle_low = grad_middle.astype(jnp.bfloat16)
    grad_w_output = jnp.einsum(
        "ti,td->id", saved["joined"], middle_low, preferred_element_type=jnp.float32
    )
    grad_joined = jnp.einsum("td,id->ti", middle_low, w_output, preferred_element_type=jnp.float32)
    grad_attn = grad_joined[:, : QUERY_HEADS * HEAD_SIZE].astype(jnp.bfloat16)
    grad_ssm_out = grad_joined[:, QUERY_HEADS * HEAD_SIZE :]
    gated_back = jax.vjp(gated_norm, saved["ssm_y"], saved["gate_z"], gain_ssm.astype(jnp.float32))[
        1
    ]
    grad_ssm_y, grad_gate_z, grad_gain_ssm = gated_back(grad_ssm_out)
    grad_ssm_y = grad_ssm_y.reshape(input_rows, SSM_HEADS, SSM_HD)
    grad_skip_scale = jnp.sum(grad_ssm_y * saved["inner_x"], (0, 2))
    grad_x, grad_cum, grad_step, grad_b, grad_c = ssd_backward(
        saved["c_low"],
        saved["b_low"],
        saved["x_low"],
        saved["step"],
        saved["cumulative"],
        segment,
        grad_ssm_y.astype(jnp.bfloat16),
    )
    grad_x = grad_x + skip_scale.astype(jnp.float32)[None, :, None] * grad_ssm_y
    grad_inc = lax.cumsum(grad_cum, axis=0, reverse=True)
    grad_step = grad_step + grad_inc * saved["rate"]
    grad_decay_log = jnp.sum(grad_inc * saved["step"], 0) * saved["rate"]
    grad_step_pre = grad_step * jax.nn.sigmoid(saved["step_pre"])
    grad_step_bias = jnp.sum(grad_step_pre, 0)
    step_low = grad_step_pre.astype(jnp.bfloat16)
    grad_w_step = jnp.einsum(
        "ti,th->ih", saved["normed"], step_low, preferred_element_type=jnp.float32
    )
    grad_conv_out = jnp.concatenate([grad_x.reshape(input_rows, INNER), grad_b, grad_c], 1)
    conv_back = jax.vjp(
        partial(conv_silu, segment=segment),
        saved["conv_in"],
        conv_weight.astype(jnp.float32),
        conv_bias.astype(jnp.float32),
    )[1]
    grad_conv_in, grad_conv_weight, grad_conv_bias = conv_back(grad_conv_out)
    grad_queries, grad_keys, value_gradient = attention_backward(
        saved["queries"],
        saved["key_rows"],
        saved["value_rows"],
        segment,
        saved["log_total"],
        grad_attn,
    )
    projected_rows = saved["projected"]
    query_back = jax.vjp(
        partial(apply_rotary, rotary_angles=saved["angles"]),
        projected_rows[:, : QUERY_HEADS * HEAD_SIZE].reshape(input_rows, QUERY_HEADS, HEAD_SIZE),
    )[1]
    key_back = jax.vjp(
        partial(apply_rotary, rotary_angles=saved["angles"]),
        projected_rows[
            :, QUERY_HEADS * HEAD_SIZE : QUERY_KEY_VALUE - KEY_VALUE_HEADS * HEAD_SIZE
        ].reshape(input_rows, KEY_VALUE_HEADS, HEAD_SIZE),
    )[1]
    grad_query_raw = query_back(grad_queries)[0]
    unrotated_key_gradient = key_back(grad_keys)[0]
    grad_projected = jnp.concatenate(
        [
            grad_query_raw.reshape(input_rows, QUERY_HEADS * HEAD_SIZE),
            unrotated_key_gradient.reshape(input_rows, KEY_VALUE_HEADS * HEAD_SIZE),
            value_gradient.reshape(input_rows, KEY_VALUE_HEADS * HEAD_SIZE),
            grad_gate_z,
            grad_conv_in,
        ],
        1,
    ).astype(jnp.bfloat16)
    grad_w_input = jnp.einsum(
        "ti,tj->ij", saved["normed"], grad_projected, preferred_element_type=jnp.float32
    )
    grad_normed = jnp.einsum(
        "tj,ij->ti", grad_projected, w_input, preferred_element_type=jnp.float32
    )
    grad_normed = grad_normed + jnp.einsum(
        "th,ih->ti", step_low, w_step, preferred_element_type=jnp.float32
    )
    attn_norm_back = jax.vjp(rms_norm, saved["tokens"], gain_attn.astype(jnp.float32))[1]
    grad_tokens_norm, grad_gain_attn = attn_norm_back(grad_normed)
    grad_tokens = grad_middle + grad_tokens_norm
    grads = (
        grad_gain_attn,
        grad_w_input,
        grad_w_step,
        grad_step_bias,
        grad_decay_log,
        grad_skip_scale,
        grad_conv_weight,
        grad_conv_bias,
        grad_gain_ssm,
        grad_w_output,
        grad_gain_ffn,
        grad_w_gate_up,
        grad_w_down,
    )
    return (grad_tokens.astype(jnp.bfloat16), grads)


def pack_grads(grads, split_dims, parts, multiple):
    blocks = []
    for grad, split_dim in zip(grads, split_dims):
        if split_dim == 0:
            blocks.append(grad.reshape(parts, -1))
        else:
            lead = grad.shape[0]
            blocks.append(grad.reshape(lead, parts, -1).transpose(1, 0, 2).reshape(parts, -1))
    packed = jnp.concatenate(blocks, 1)
    extra = -packed.shape[1] % multiple
    return jnp.pad(packed, ((0, 0), (0, extra)))


def unpack_grads(total, shapes):
    outputs = []
    offset = 0
    for shape in shapes:
        length = math.prod(shape)
        outputs.append(total[offset : offset + length].reshape(shape))
        offset += length
    return tuple(outputs)


def on_device(
    tokens,
    seq_lengths,
    owner_order,
    gain_attn,
    w_input,
    w_step,
    step_bias,
    decay_log,
    skip_scale,
    conv_weight,
    conv_bias,
    gain_ssm,
    w_output,
    gain_ffn,
    w_gate_up,
    w_down,
    cotangent,
):
    input_rows = tokens.shape[0]
    width = tokens.shape[1]
    device = lax.axis_index("shard")
    source, position, segment, target = group_tables(
        seq_lengths[0], owner_order[0], input_rows, device
    )
    empty = jnp.zeros((input_rows, width), jnp.bfloat16)
    own_tokens, own_cot = pick_rows(
        (empty, empty),
        (
            lax.all_gather(tokens, "shard", axis=0, tiled=True),
            lax.all_gather(cotangent, "shard", axis=0, tiled=True),
        ),
        source,
    )
    weights_full = (
        lax.all_gather(gain_attn, "shard", axis=0, tiled=True),
        lax.all_gather(w_input, "shard", axis=0, tiled=True),
        lax.all_gather(w_step, "shard", axis=0, tiled=True),
        lax.all_gather(step_bias, "shard", axis=0, tiled=True),
        lax.all_gather(decay_log, "shard", axis=0, tiled=True),
        lax.all_gather(skip_scale, "shard", axis=0, tiled=True),
        lax.all_gather(conv_weight, "shard", axis=1, tiled=True),
        lax.all_gather(conv_bias, "shard", axis=0, tiled=True),
        lax.all_gather(gain_ssm, "shard", axis=0, tiled=True),
        lax.all_gather(w_output, "shard", axis=0, tiled=True),
        lax.all_gather(gain_ffn, "shard", axis=0, tiled=True),
        lax.all_gather(w_gate_up, "shard", axis=0, tiled=True),
        lax.all_gather(w_down, "shard", axis=0, tiled=True),
    )
    out_low, saved = layer_forward(weights_full, own_tokens, position, segment)
    grad_low, grads = layer_backward(weights_full, saved, segment, own_cot)
    parts = lax.axis_size("shard")
    replicas = lax.axis_size("rep")
    split_dims = (0, 0, 0, 0, 0, 0, 1, 0, 0, 0, 0, 0, 0)
    packed = pack_grads(grads, split_dims, parts, replicas)
    length = packed.shape[1]
    spread = (
        packed.reshape(parts, replicas, length // replicas)
        .transpose(1, 0, 2)
        .reshape(replicas * parts, length // replicas)
    )
    piece = lax.psum_scatter(spread, ("rep", "shard"), scatter_dimension=0, tiled=True)
    total = (
        lax.all_gather(piece.astype(jnp.bfloat16), "rep", axis=0, tiled=True)
        .astype(piece.dtype)
        .reshape(length)
    )
    shapes = (
        gain_attn.shape,
        w_input.shape,
        w_step.shape,
        step_bias.shape,
        decay_log.shape,
        skip_scale.shape,
        conv_weight.shape,
        conv_bias.shape,
        gain_ssm.shape,
        w_output.shape,
        gain_ffn.shape,
        w_gate_up.shape,
        w_down.shape,
    )
    grad_shards = unpack_grads(total, shapes)
    block_out, grad_tokens = pick_rows(
        (empty, empty),
        (
            lax.all_gather(out_low, "shard", axis=0, tiled=True),
            lax.all_gather(grad_low, "shard", axis=0, tiled=True),
        ),
        target,
    )
    return (
        block_out,
        grad_tokens,
        grad_shards[0],
        grad_shards[1],
        grad_shards[2],
        grad_shards[3],
        grad_shards[4],
        grad_shards[5],
        grad_shards[6],
        grad_shards[7],
        grad_shards[8],
        grad_shards[9],
        grad_shards[10],
        grad_shards[11],
        grad_shards[12],
    )


def solution(mesh):
    placed = (
        P(("rep", "shard"), None),
        P("rep", None),
        P("rep", None),
        P("shard"),
        P("shard", None),
        P("shard", None),
        P("shard"),
        P("shard"),
        P("shard"),
        P(None, "shard"),
        P("shard"),
        P("shard"),
        P("shard", None),
        P("shard"),
        P("shard", None),
        P("shard", None),
        P(("rep", "shard"), None),
    )
    return jax.shard_map(
        on_device,
        mesh=mesh,
        in_specs=placed,
        out_specs=(
            P(("rep", "shard"), None),
            P(("rep", "shard"), None),
            P("shard"),
            P("shard", None),
            P("shard", None),
            P("shard"),
            P("shard"),
            P("shard"),
            P(None, "shard"),
            P("shard"),
            P("shard"),
            P("shard", None),
            P("shard"),
            P("shard", None),
            P("shard", None),
        ),
        check_vma=False,
    )
```

profile of v0, /device:TPU:0, one launch (start us, length us, event | category | flops | bytes accessed | tf_op | source)
XLA Modules:
  0.0 2321.4 jit_solution(15043472610452263475)
XLA Ops:
  89.4 53.7 %all-gather.17.cloned.1.call-done = bf16[1024,4096]{1,0:T(8,128)(2,1)} async-done(((bf16[256,4096]{1,0:T(8,128)(2,1)}), bf16[1024,4096]{1,0:T(8,128)(2,1)}) %all-gather.17.cloned.1.call-update) | async-done | bytes 8388624 | tf_op jit(solution)/shard_map/all_gather | solution.py:517
  205.9 32.9 %all-gather.21.cloned.1.call-done = bf16[1024,4096]{1,0:T(8,128)(2,1)} async-done(((bf16[256,4096]{1,0:T(8,128)(2,1)}), bf16[1024,4096]{1,0:T(8,128)(2,1)}) %all-gather.21.cloned.1.call-update) | async-done | bytes 8388624 | tf_op jit(solution)/shard_map/all_gather | solution.py:527
  251.0 23.7 %all-gather.23.cloned.1.call-done = bf16[2048,1024]{1,0:T(8,128)(2,1)} async-done(((bf16[512,1024]{1,0:T(8,128)(2,1)}), bf16[2048,1024]{1,0:T(8,128)(2,1)}) %all-gather.23.cloned.1.call-update) | async-done | bytes 4194320 | tf_op jit(solution)/shard_map/all_gather | solution.py:528
  274.7 12.9 fusion.89
  314.0 15.6 fusion.37
  329.6 15.3 fusion.68
  369.9 17.1 fusion.16
  491.5 25.3 %reshape.904 = f32[4,1048576]{1,0:T(4,128)} reshape(f32[1024,4096]{1,0:T(8,128)} %fusion.151) | data formatting | bytes 33554432 | tf_op jit(solution)/shard_map/reshape | solution.py:462
  530.4 25.6 %reshape.919 = f32[4,1048576]{1,0:T(4,128)} reshape(f32[1024,4096]{1,0:T(8,128)} %fusion.78) | data formatting | bytes 33554432 | tf_op jit(solution)/shard_map/reshape | solution.py:462
  561.7 12.5 reshape.920
  574.2 13.7 constant_dynamic-update-slice_fusion.4
  597.4 44.3 %dynamic-update-slice.49 = f32[4,3155026]{1,0:T(4,128)} dynamic-update-slice(f32[4,3155026]{1,0:T(4,128)} %dynamic-update-slice.48, f32[4,524288]{1,0:T(4,128)} %reshape.917, s32[]{} %constant.453, s32[]{} %constant.462) | dynamic-update-slice | bytes 16777220
  643.1 86.7 %dynamic-update-slice.51 = f32[4,3155026]{1,0:T(4,128)} dynamic-update-slice(f32[4,3155026]{1,0:T(4,128)} %dynamic-update-slice.50, f32[4,1048576]{1,0:T(4,128)} %reshape.919, s32[]{} %constant.453, s32[]{} %constant.464) | dynamic-update-slice | bytes 33554436
  729.9 44.0 %dynamic-update-slice.52 = f32[4,3155026]{1,0:T(4,128)} dynamic-update-slice(f32[4,3155026]{1,0:T(4,128)} %dynamic-update-slice.51, f32[4,524288]{1,0:T(4,128)} %reshape.920, s32[]{} %constant.453, s32[]{} %constant.465) | dynamic-update-slice | bytes 16777220 | tf_op jit(solution)/shard_map/concatenate | solution.py:466
  773.8 33.6 %pad.90 = f32[4,3155032]{1,0:T(4,128)} pad(f32[4,3155026]{1,0:T(4,128)} %dynamic-update-slice.52, f32[]{:T(128)} %constant.354.clone.1), padding=0_0x0_6 | pad | bytes 100960928 | tf_op jit(solution)/shard_map/jit(_pad)/pad | solution.py:468
  807.5 148.3 %reshape.1015 = f32[12620128]{0:T(1024)} reshape(f32[4,3155032]{1,0:T(4,128)} %pad.90) | data formatting | bytes 100961024
  955.8 63.1 %reshape.921 = f32[4,8,394379]{2,1,0:T(8,128)} reshape(f32[12620128]{0:T(1024)} %reshape.1015) | data formatting | bytes 100961024 | tf_op jit(solution)/shard_map/reshape | solution.py:538
  1018.9 36.3 %copy.177 = f32[8,4,394379]{2,1,0:T(4,128)} copy(f32[8,4,394379]{2,0,1:T(8,128)} %bitcast.252) | data formatting | bytes 100961024 | tf_op jit(solution)/shard_map/transpose | solution.py:539
  1055.3 54.2 %reshape.922 = f32[32,394379]{1,0:T(8,128)} reshape(f32[8,4,394379]{2,1,0:T(4,128)} %copy.177) | data formatting | bytes 100961024 | tf_op jit(solution)/shard_map/reshape | solution.py:540
  1109.4 798.7 %all-reduce.29 = bf16[32,394379]{1,0:T(8,128)(2,1)} all-reduce(f32[32,394379]{1,0:T(8,128)} %reshape.922), channel_id=2, replica_groups=mesh['rep'=8,'shard'=4] {'rep','shard'}, use_global_device_ids=true, to_apply=%region_50.51.clone | all-reduce | flops 12620128 | bytes 75720768
  1926.1 21.2 all-gather.25.cloned.1.call-done
  1954.3 172.7 %all-gather.31.cloned.1.call-done = bf16[8,1,394379]{2,1,0:T(2,128)(2,1)} async-done(((bf16[1,1,394379]{2,1,0:T(2,128)(2,1)}), bf16[8,1,394379]{2,1,0:T(2,128)(2,1)}) %all-gather.31.cloned.1.call-update) | async-done | bytes 6310080 | tf_op jit(solution)/shard_map/all_gather | solution.py:544
  2127.0 136.1 %convert_reduce_fusion = f32[8,394379]{1,0:T(8,128)} fusion(bf16[8,1,394379]{2,1,0:T(2,128)(2,1)} %all-gather.31.cloned.1.call-done), kind=kLoop, calls=%fused_computation.5 | loop fusion | flops 3155032 | bytes 18930192 | tf_op jit(solution)/shard_map/reshape | solution.py:546
  2263.1 16.2 reshape.932
  (531 shorter events, 399.9 us)
Async XLA Ops:
  7.2 56.7 %all-gather.15.cloned.1.call-start = ((), (), s32[]{:S(2)}) async-start(), calls=%async_computation | async-start | bytes 5242880 | tf_op jit(solution)/shard_map/all_gather | solution.py:510
  7.9 75.3 %all-gather.27.cloned.1.call-start = ((), (), s32[]{:S(2)}) async-start(), calls=%async_computation.6 | async-start | bytes 5242880 | tf_op jit(solution)/shard_map/all_gather | solution.py:511
  8.8 134.4 %all-gather.17.cloned.1.call-start = ((), (), s32[]{:S(2)}) async-start(), calls=%async_computation.1 | async-start | bytes 10485760 | tf_op jit(solution)/shard_map/all_gather | solution.py:517
  9.5 189.6 %all-gather.19.cloned.1.call-start = ((), (), s32[]{:S(2)}) async-start(), calls=%async_computation.2 | async-start | bytes 5242880 | tf_op jit(solution)/shard_map/all_gather | solution.py:525
  10.1 228.7 %all-gather.21.cloned.1.call-start = ((), (), s32[]{:S(2)}) async-start(), calls=%async_computation.3 | async-start | bytes 10485760 | tf_op jit(solution)/shard_map/all_gather | solution.py:527
  10.7 264.0 %all-gather.23.cloned.1.call-start = ((), (), s32[]{:S(2)}) async-start(), calls=%async_computation.4 | async-start | bytes 5242880 | tf_op jit(solution)/shard_map/all_gather | solution.py:528
  11.3 1908.7 %all-gather.29.cloned.1.call-start = ((), (), s32[]{:S(2)}) async-start(), calls=%async_computation.7 | async-start | bytes 5242880 | tf_op jit(solution)/shard_map/all_gather | solution.py:568
  21.0 122.1 %copy-start.61 = (f32[4,1,256]{2,1,0:T(1,128)}, f32[4,1,256]{2,1,0:T(1,128)S(1)}, u32[]{:S(2)}) copy-start(f32[4,1,256]{2,1,0:T(1,128)S(1)} %convert_element_type.218) | copy-start | bytes 12292
  24.0 274.2 %copy-start.106 = (pred[512]{0:T(512)(128)(4,1)}, pred[512]{0:T(512)(128)(4,1)S(1)}, u32[]{:S(2)}) copy-start(pred[512]{0:T(512)(128)(4,1)S(1)} %compare_and_fusion) | copy-start | bytes 1540
  32.3 119.1 %copy-start.45 = (f32[1792]{0:T(1024)}, f32[1792]{0:T(1024)S(1)}, u32[]{:S(2)}) copy-start(f32[1792]{0:T(1024)S(1)} %get-tuple-element.250) | copy-start | bytes 21508
  32.3 119.1 %copy-start.47 = (f32[1792]{0:T(1024)}, f32[1792]{0:T(1024)S(1)}, u32[]{:S(2)}) copy-start(f32[1792]{0:T(1024)S(1)} %get-tuple-element.251) | copy-start | bytes 21508
  32.3 119.1 %copy-start.49 = (f32[1792]{0:T(1024)}, f32[1792]{0:T(1024)S(1)}, u32[]{:S(2)}) copy-start(f32[1792]{0:T(1024)S(1)} %get-tuple-element.252) | copy-start | bytes 21508
  32.4 119.1 %copy-start.51 = (f32[1792]{0:T(1024)}, f32[1792]{0:T(1024)S(1)}, u32[]{:S(2)}) copy-start(f32[1792]{0:T(1024)S(1)} %get-tuple-element.253) | copy-start | bytes 21508
  32.4 119.0 %copy-start.65 = (f32[512]{0:T(512)}, f32[512]{0:T(512)S(1)}, u32[]{:S(2)}) copy-start(f32[512]{0:T(512)S(1)} %pad_convert_fusion.1) | copy-start | bytes 6148
  50.4 124.2 %copy-start.35 = (pred[512,512]{1,0:T(8,128)(4,1)}, pred[512,512]{1,0:T(8,128)(4,1)S(1)}, u32[]{:S(2)}) copy-start(pred[512,512]{1,0:T(8,128)(4,1)S(1)} %copy.156) | copy-start | bytes 786436
  61.5 236.7 %copy-start.82 = (f32[4,1,256]{2,1,0:T(1,128)}, f32[4,1,256]{2,1,0:T(1,128)S(1)}, u32[]{:S(2)}) copy-start(f32[4,1,256]{2,1,0:T(1,128)S(1)} %convert_element_type.221) | copy-start | bytes 12292
  70.5 97.0 %copy-start.88 = (f32[8,512]{1,0:T(8,128)}, f32[8,512]{1,0:T(8,128)S(1)}, u32[]{:S(2)}) copy-start(f32[8,512]{1,0:T(8,128)S(1)} %get-tuple-element.299) | copy-start | bytes 49156
  70.5 101.3 %copy-start.91 = (f32[8,512]{1,0:T(8,128)}, f32[8,512]{1,0:T(8,128)S(1)}, u32[]{:S(2)}) copy-start(f32[8,512]{1,0:T(8,128)S(1)} %get-tuple-element.300) | copy-start | bytes 49156
  70.5 104.0 %copy-start.100 = (f32[8,512]{1,0:T(8,128)}, f32[8,512]{1,0:T(8,128)S(1)}, u32[]{:S(2)}) copy-start(f32[8,512]{1,0:T(8,128)S(1)} %get-tuple-element.298) | copy-start | bytes 49156
  72.1 99.7 %copy-start.97 = (f32[8,512]{1,0:T(8,128)}, f32[8,512]{1,0:T(8,128)S(1)}, u32[]{:S(2)}) copy-start(f32[8,512]{1,0:T(8,128)S(1)} %get-tuple-element.297) | copy-start | bytes 49156
  72.1 102.5 %copy-start.102 = (f32[8,512]{1,0:T(8,128)}, f32[8,512]{1,0:T(8,128)S(1)}, u32[]{:S(2)}) copy-start(f32[8,512]{1,0:T(8,128)S(1)} %get-tuple-element.295) | copy-start | bytes 49156
  490.7 1456.6 %all-gather.25.cloned.1.call-start = ((), (), s32[]{:S(2)}) async-start(), calls=%async_computation.5 | async-start | bytes 5242880 | tf_op jit(solution)/shard_map/all_gather | solution.py:567
  1109.4 798.8 %copy-start.20 = (f32[512,1024]{1,0:T(8,128)S(1)}, f32[512,1024]{1,0:T(8,128)}, u32[]{:S(2)}) copy-start(f32[512,1024]{1,0:T(8,128)} %get-tuple-element.314) | copy-start | bytes 6291460
  1914.3 212.6 %all-gather.31.cloned.1.call-start = ((), (), s32[]{:S(2)}) async-start(), calls=%async_computation.8 | async-start | bytes 14201856 | tf_op jit(solution)/shard_map/all_gather | solution.py:544
  (127 other events, 1595.7 us)
Sparse Core Ops, SparseCore 0:
  9.6 37.5 all-gather.14
  48.7 34.4 all-gather.26
  84.8 58.2 all-gather.16
  144.5 34.4 all-gather.18
  180.5 58.2 all-gather.20
  240.2 34.4 all-gather.22
  490.8 34.4 all-gather.28
  1914.5 32.7 all-gather.24
  1950.1 176.8 all-gather.30
where the time goes:
time: 2330 us; the launch traced here: 2320 us
  blocking collectives  834 us (36%)
  local copies, waits for them, and re-layouts  741 us (32%)
  waiting for transfers between devices  319 us (14%)
  other arithmetic  221 us (9%)
  matrix products  188 us (8%)
    unnamed x2, blocking collectives  807 us
    unnamed x312, local copies, waits for them, and re-layouts  334 us
    all_gather x1, waiting for transfers between devices, on_device(): lax.all_gather(piece.astype(jnp.bfloat16), 'rep', axis=0, tiled=True)  173 us
    reshape x1, other arithmetic, on_device(): total = lax.all_gather(piece.astype(jnp.bfloat16), 'rep', axis=0, tiled=T...  136 us
    reshape x12, local copies, waits for them, and re-layouts, pack_grads(): blocks.append(grad.reshape(parts, -1))  76.5 us
    reshape x1, local copies, waits for them, and re-layouts, on_device(): packed.reshape(parts, replicas, length // replicas).transpose(1, 0, 2)  63.1 us
    reshape x1, local copies, waits for them, and re-layouts, on_device(): spread = packed.reshape(parts, replicas, length // replicas).transpose(1,...  54.2 us
    all_gather x1, waiting for transfers between devices, on_device(): lax.all_gather(w_input, 'shard', axis=0, tiled=True)  53.7 us
  transfers between devices with their start and end apart: 9, of which 6 were waited for; matrix products, arithmetic and copies ran while one was open for 32% of the time, Pallas kernels for 0%

commit v1 on v0

--- a/solution.py
+++ b/solution.py
@@ -92,15 +92,6 @@
     seq_owner_start = jnp.sum(pick * owner_start[:, None], 0)
     target = jnp.sum(member * seq_owner_start[None, :], 1) + given - seq_start
     return (source, position, segment, target)
-
-
-def pick_rows(carry, pieces, wanted):
-    count = pieces[0].shape[0]
-    inside = (wanted >= 0) & (wanted < count)
-    index = jnp.clip(wanted, 0, count - 1)
-    return tuple(
-        (jnp.where(inside[:, None], piece[index], kept) for piece, kept in zip(pieces, carry))
-    )
 
 
 def block_mask(segment, count):
@@ -455,27 +446,119 @@
     return (grad_tokens.astype(jnp.bfloat16), grads)
 
 
-def pack_grads(grads, split_dims, parts, multiple):
-    blocks = []
-    for grad, split_dim in zip(grads, split_dims):
-        if split_dim == 0:
-            blocks.append(grad.reshape(parts, -1))
-        else:
-            lead = grad.shape[0]
-            blocks.append(grad.reshape(lead, parts, -1).transpose(1, 0, 2).reshape(parts, -1))
-    packed = jnp.concatenate(blocks, 1)
-    extra = -packed.shape[1] % multiple
-    return jnp.pad(packed, ((0, 0), (0, extra)))
-
-
-def unpack_grads(total, shapes):
+def bit_of(axis, bit):
+    return (lax.axis_index(axis) >> bit) & 1
+
+
+def bit_count(axis):
+    return lax.axis_size(axis).bit_length() - 1
+
+
+def swap(values, axis, bit):
+    count = lax.axis_size(axis)
+    return lax.ppermute(values, axis, [(i, i ^ (1 << bit)) for i in range(count)])
+
+
+def join(values, other, axis, bit, dim):
+    flag = bit_of(axis, bit)
+    return jnp.stack([jnp.where(flag == 0, values, other), jnp.where(flag == 0, other, values)], dim)
+
+
+def gather_rows(piece):
+    rows, width = piece.shape
+    for bit in range(bit_count("shard")):
+        piece = join(piece, swap(piece, "shard", bit), "shard", bit, 0)
+    return piece.reshape(-1, width)
+
+
+def gather_weight(piece):
+    rows, width = piece.shape
+    near = bit_of("rep", 0)
+    held = piece
+    for bit in reversed(range(1, bit_count("shard"))):
+        lead = held.shape[:-2]
+        flat = held.reshape(-1, width)
+        halves = flat.reshape(2, -1, width)
+        mine = lax.dynamic_index_in_dim(halves, near, 0, keepdims=False)
+        direct = swap(mine, "shard", bit)
+        passed = swap(direct, "rep", 0)
+        other = join(direct, passed, "rep", 0, 0).reshape(lead + (rows, width))
+        held = join(held, other, "shard", bit, len(lead))
+    lead = held.shape[:-2]
+    held = join(held, swap(held, "shard", 0), "shard", 0, len(lead))
+    parts = len(lead)
+    order = tuple(range(parts)) [::-1]
+    return held.reshape(-1, width)
+
+
+def gather_small(pieces, dims):
+    flat = jnp.concatenate([piece.reshape(-1) for piece in pieces])
+    every = lax.all_gather(flat, "shard", axis=0, tiled=False)
+    parts = every.shape[0]
     outputs = []
     offset = 0
-    for shape in shapes:
-        length = math.prod(shape)
-        outputs.append(total[offset : offset + length].reshape(shape))
+    for piece, dim in zip(pieces, dims):
+        length = math.prod(piece.shape)
+        block = every[:, offset : offset + length].reshape((parts,) + piece.shape)
         offset += length
-    return tuple(outputs)
+        if dim == 0:
+            outputs.append(block.reshape((-1,) + piece.shape[1:]))
+        else:
+            outputs.append(jnp.swapaxes(block, 0, 1).reshape(piece.shape[0], -1))
+    return outputs
+
+
+def reduce_grad(grad, order):
+    rows_all, width = grad.shape
+    shard_bits, rep_bits = bit_count("shard"), bit_count("rep")
+    rows = rows_all >> (shard_bits + rep_bits)
+    left = [("shard", b) for b in reversed(range(shard_bits))]
+    left += [("rep", b) for b in reversed(range(rep_bits))]
+    total = grad.reshape((2,) * (shard_bits + rep_bits) + (rows, width))
+    for stage in order:
+        dim = left.index(stage)
+        left.pop(dim)
+        flag = bit_of(*stage)
+        away = lax.dynamic_index_in_dim(total, 1 - flag, dim, keepdims=False)
+        keep = lax.dynamic_index_in_dim(total, flag, dim, keepdims=False)
+        came = swap(away, *stage)
+        total = (keep.astype(jnp.float32) + came.astype(jnp.float32)).astype(jnp.bfloat16)
+    have = []
+    for stage in reversed(order):
+        if stage[0] == "shard":
+            continue
+        have.append(stage)
+        have.sort(key=lambda s: -s[1])
+        total = join(total, swap(total, *stage), *stage, have.index(stage))
+    return total.reshape(rows_all >> shard_bits, width).astype(jnp.float32)
+
+
+def reduce_small(grads):
+    flat = jnp.concatenate([grad.reshape(-1) for grad in grads])
+    extra = -flat.shape[0] % 1024
+    total = jnp.pad(flat, (0, extra)).reshape(-1, 128)
+    for axis in ("shard", "rep"):
+        for bit in range(bit_count(axis)):
+            total = total + swap(total, axis, bit)
+    total = total.reshape(-1)
+    outputs = []
+    offset = 0
+    for grad in grads:
+        length = math.prod(grad.shape)
+        outputs.append(total[offset : offset + length].reshape(grad.shape))
+        offset += length
+    return outputs
+
+
+def own_block(values, dim):
+    size = values.shape[dim] // lax.axis_size("shard")
+    return lax.dynamic_slice_in_dim(values, lax.axis_index("shard") * size, size, dim)
+
+
+def take_rows(values, wanted):
+    places = jnp.arange(values.shape[0], dtype=jnp.int32)
+    choice = (wanted[:, None] == places[None, :]).astype(jnp.bfloat16)
+    return jnp.dot(choice, values, preferred_element_type=jnp.float32).astype(jnp.bfloat16)
 
 
 def on_device(
@@ -498,94 +581,45 @@
     cotangent,
 ):
     input_rows = tokens.shape[0]
-    width = tokens.shape[1]
     device = lax.axis_index("shard")
     source, position, segment, target = group_tables(
         seq_lengths[0], owner_order[0], input_rows, device
     )
-    empty = jnp.zeros((input_rows, width), jnp.bfloat16)
-    own_tokens, own_cot = pick_rows(
-        (empty, empty),
-        (
-            lax.all_gather(tokens, "shard", axis=0, tiled=True),
-            lax.all_gather(cotangent, "shard", axis=0, tiled=True),
-        ),
-        source,
+    own_tokens = take_rows(gather_rows(tokens), source)
+    own_cot = take_rows(gather_rows(cotangent), source)
+    small = gather_small(
+        (gain_attn, w_step, step_bias, decay_log, skip_scale, conv_weight, conv_bias, gain_ssm, gain_ffn),
+        (0, 0, 0, 0, 0, 1, 0, 0, 0),
     )
     weights_full = (
-        lax.all_gather(gain_attn, "shard", axis=0, tiled=True),
-        lax.all_gather(w_input, "shard", axis=0, tiled=True),
-        lax.all_gather(w_step, "shard", axis=0, tiled=True),
-        lax.all_gather(step_bias, "shard", axis=0, tiled=True),
-        lax.all_gather(decay_log, "shard", axis=0, tiled=True),
-        lax.all_gather(skip_scale, "shard", axis=0, tiled=True),
-        lax.all_gather(conv_weight, "shard", axis=1, tiled=True),
-        lax.all_gather(conv_bias, "shard", axis=0, tiled=True),
-        lax.all_gather(gain_ssm, "shard", axis=0, tiled=True),
-        lax.all_gather(w_output, "shard", axis=0, tiled=True),
-        lax.all_gather(gain_ffn, "shard", axis=0, tiled=True),
-        lax.all_gather(w_gate_up, "shard", axis=0, tiled=True),
-        lax.all_gather(w_down, "shard", axis=0, tiled=True),
+        small[0],
+        gather_weight(w_input),
+        *small[1:8],
+        gather_weight(w_output),
+        small[8],
+        gather_weight(w_gate_up),
+        gather_weight(w_down),
     )
     out_low, saved = layer_forward(weights_full, own_tokens, position, segment)
     grad_low, grads = layer_backward(weights_full, saved, segment, own_cot)
-    parts = lax.axis_size("shard")
-    replicas = lax.axis_size("rep")
-    split_dims = (0, 0, 0, 0, 0, 0, 1, 0, 0, 0, 0, 0, 0)
-    packed = pack_grads(grads, split_dims, parts, replicas)
-    length = packed.shape[1]
-    spread = (
-        packed.reshape(parts, replicas, length // replicas)
-        .transpose(1, 0, 2)
-        .reshape(replicas * parts, length // replicas)
-    )
-    piece = lax.psum_scatter(spread, ("rep", "shard"), scatter_dimension=0, tiled=True)
-    total = (
-        lax.all_gather(piece.astype(jnp.bfloat16), "rep", axis=0, tiled=True)
-        .astype(piece.dtype)
-        .reshape(length)
-    )
-    shapes = (
-        gain_attn.shape,
-        w_input.shape,
-        w_step.shape,
-        step_bias.shape,
-        decay_log.shape,
-        skip_scale.shape,
-        conv_weight.shape,
-        conv_bias.shape,
-        gain_ssm.shape,
-        w_output.shape,
-        gain_ffn.shape,
-        w_gate_up.shape,
-        w_down.shape,
-    )
-    grad_shards = unpack_grads(total, shapes)
-    block_out, grad_tokens = pick_rows(
-        (empty, empty),
-        (
-            lax.all_gather(out_low, "shard", axis=0, tiled=True),
-            lax.all_gather(grad_low, "shard", axis=0, tiled=True),
-        ),
-        target,
-    )
-    return (
-        block_out,
-        grad_tokens,
-        grad_shards[0],
-        grad_shards[1],
-        grad_shards[2],
-        grad_shards[3],
-        grad_shards[4],
-        grad_shards[5],
-        grad_shards[6],
-        grad_shards[7],
-        grad_shards[8],
-        grad_shards[9],
-        grad_shards[10],
-        grad_shards[11],
-        grad_shards[12],
-    )
+    core = [("shard", 0)]
+    far = [("shard", b) for b in range(1, bit_count("shard"))]
+    near = [("rep", 0)]
+    rest = [("rep", b) for b in range(1, bit_count("rep"))]
+    first = core + far + near + rest
+    second = core + near + far + rest
+    places = (0, 2, 3, 4, 5, 6, 7, 8, 10)
+    summed = reduce_small([grads[i] for i in places])
+    outs = [None] * 13
+    for i, grad in zip(places, summed):
+        outs[i] = own_block(grad, 1 if i == 6 else 0)
+    outs[12] = reduce_grad(grads[12].astype(jnp.bfloat16), first)
+    outs[11] = reduce_grad(grads[11].astype(jnp.bfloat16), second)
+    outs[9] = reduce_grad(grads[9].astype(jnp.bfloat16), first)
+    outs[1] = reduce_grad(grads[1].astype(jnp.bfloat16), second)
+    block_out = take_rows(gather_rows(out_low), target)
+    grad_tokens = take_rows(gather_rows(grad_low), target)
+    return (block_out, grad_tokens, *outs)
 
 
 def solution(mesh):

time: 2330 us -> 1050 us (0.45)
  blocking collectives: 834 us -> 0 us
  local copies, waits for them, and re-layouts: 741 us -> 131 us
  waiting for transfers between devices: 319 us -> 485 us
  starting transfers between devices: 0.52 us -> 56.1 us
  other arithmetic: 221 us -> 172 us
    unnamed x2 -> x0, blocking collectives: 807 us -> none
    ppermute x0 -> x57, waiting for transfers between devices: none -> 475 us  [swap(): return lax.ppermute(values, axis, [(i, i ^ 1 << bit) for i in range(count)])]
    all_gather x9 -> x0, waiting for transfers between devices: 315 us -> none  [the longest x1 173 us: on_device(): lax.all_gather(piece.astype(jnp.bfloat16), 'rep', axis=0, tiled=True)]
    unnamed x312 -> x354, local copies, waits for them, and re-layouts: 334 us -> 29.6 us
    reshape x23 -> x7, local copies, waits for them, and re-layouts: 225 us -> 2.54 us  [the longest x2 1.15 us: reduce_small(): outputs.append(total[offset:offset + length].reshape(grad.shape))]
    reshape x1 -> x0, other arithmetic: 136 us -> none  [on_device(): total = lax.all_gather(piece.astype(jnp.bfloat16), 'rep', axis=0, tiled=T...]
    another operation x16 -> x71, other arithmetic: 15.7 us -> 88.8 us  [the longest x55 62.7 us: join(): jnp.stack([jnp.where(flag == 0, values, other), jnp.where(flag == 0, othe...]
    ppermute x0 -> x57, starting transfers between devices: none -> 56 us  [swap(): return lax.ppermute(values, axis, [(i, i ^ 1 << bit) for i in range(count)])]
  transfers between devices with their start and end apart: 9 -> 58, of which waited for: 6 -> 31; matrix products, arithmetic and copies ran while one was open for 32% -> 22% of each run, Pallas kernels for 0% -> 0%
where the time goes in v1:
time: 1050 us; the launch traced here: 1040 us
  waiting for transfers between devices  485 us (46%)
  matrix products  182 us (17%)
  other arithmetic  172 us (16%)
  local copies, waits for them, and re-layouts  131 us (12%)
  starting transfers between devices  56.1 us (5%)
  between operations  17.8 us (2%)
    ppermute x57, waiting for transfers between devices, swap(): return lax.ppermute(values, axis, [(i, i ^ 1 << bit) for i in range(count)])  475 us
    another operation x55, other arithmetic, join(): jnp.stack([jnp.where(flag == 0, values, other), jnp.where(flag == 0, othe...  62.7 us
    ppermute x57, starting transfers between devices, swap(): return lax.ppermute(values, axis, [(i, i ^ 1 << bit) for i in range(count)])  56 us
    unnamed x354, local copies, waits for them, and re-layouts  29.6 us
    another operation x16, other arithmetic  26.1 us
  transfers between devices with their start and end apart: 58, of which 31 were waited for; matrix products, arithmetic and copies ran while one was open for 22% of the time, Pallas kernels for 0%

profile of v1, /device:TPU:0, one launch (start us, length us, event | category | flops | bytes accessed | tf_op | source)
XLA Modules:
  0.0 1043.2 jit_solution(1215698992435429087)
XLA Ops:
  40.3 9.7 all-reduce.25.cloned.1.call-done
  73.2 10.1 collective-permute-done.6
  101.0 15.1 %collective-permute-done.9 = bf16[128,4096]{1,0:T(8,128)(2,1)S(1)} collective-permute-done((bf16[128,4096]{1,0:T(8,128)(2,1)}, bf16[128,4096]{1,0:T(8,128)(2,1)S(1)}, u32[]{:S(2)}, u32[]{:S(2)}) %collective-permute-start.9) | collective-permute-done | bytes 1048608 | tf_op jit(solution)/shard_map/ppermute | solution.py:459
  122.3 17.3 %collective-permute-done.3 = bf16[128,4096]{1,0:T(8,128)(2,1)S(1)} collective-permute-done((bf16[128,4096]{1,0:T(8,128)(2,1)}, bf16[128,4096]{1,0:T(8,128)(2,1)S(1)}, u32[]{:S(2)}, u32[]{:S(2)}) %collective-permute-start.3) | collective-permute-done | bytes 1048608 | tf_op jit(solution)/shard_map/ppermute | solution.py:459
  145.7 44.6 %collective-permute-done.17 = bf16[2,512,1024]{2,1,0:T(8,128)(2,1)S(1)} collective-permute-done((bf16[2,512,1024]{2,1,0:T(8,128)(2,1)S(1)}, bf16[2,512,1024]{2,1,0:T(8,128)(2,1)S(1)}, u32[]{:S(2)}, u32[]{:S(2)}) %collective-permute-start.17) | collective-permute-done | bytes 2097184 | tf_op jit(solution)/shard_map/ppermute | solution.py:459
  325.5 12.5 %multiply_reduce_fusion.14 = (f32[1024]{0:T(1024)}, f32[512]{0:T(512)S(1)}, f32[512,1024]{1,0:T(8,128)}) fusion(f32[512,1024]{1,0:T(8,128)S(1)} %get-tuple-element.346, f32[512]{0:T(512)S(1)} %fusion.150, f32[1024]{0:T(1024)S(1)} %bitcast.620, bf16[1024,4096]{1,0:T(8,128)(2,1)} %bitcast.558, f32[512,2048]{1,0:T(8,128)} %get-tuple-element.241, ...), kind=kOutput, calls=%fused_computation.176 | convolution fusion | flops 4302305792 | bytes 20983808 | tf_op jit(solution)/shard_map/tj,ij->ti/dot_general | solution.py:342
  338.0 10.7 %convolution_convert_fusion = bf16[1024,4096]{1,0:T(8,128)(2,1)} fusion(f32[512,2048]{1,0:T(8,128)} %get-tuple-element.241, f32[512,2048]{1,0:T(8,128)} %get-tuple-element.240, f32[512,1024]{1,0:T(8,128)S(1)} %get-tuple-element.346, f32[1024]{0:T(1024)S(1)} %bitcast.621, f32[512]{0:T(512)S(1)} %fusion.150), kind=kOutput, calls=%fused_computation.35 | convolution fusion | flops 4304928768 | bytes 18880512 | tf_op jit(solution)/shard_map/ti,tj->ij/dot_general | solution.py:339
  383.6 15.6 %fusion.88 = f32[512,2,64]{0,2,1:T(8,128)} fusion(f32[2,512,512,4]{2,1,3,0:T(8,128)} %fusion.188, f32[2,4,512,512]{2,3,1,0:T(8,128)} %copy-done.3, f32[2,4,512]{2,1,0:T(4,128)} %bitcast.611, bf16[512,2,4,32]{0,3,2,1:T(8,128)(2,1)} %bitcast.606, bf16[512,2,4,32]{0,3,2,1:T(8,128)(2,1)} %bitcast.604), kind=kOutput, calls=%fused_computation.215 | convolution fusion | flops 284168704 | bytes 17580032 | tf_op jit(solution)/shard_map/kgij,ikgd->jkd/dot_general | solution.py:152
  399.2 15.8 %fusion.47 = f32[2,64,4,512]{3,1,2,0:T(8,128)} fusion(f32[2,512,512,4]{2,1,3,0:T(8,128)} %fusion.188, f32[2,4,512,512]{2,3,1,0:T(8,128)} %copy-done.3, f32[2,4,512]{2,1,0:T(4,128)} %bitcast.612, bf16[512,2,32]{0,2,1:T(8,128)(2,1)} %copy-done.104, bf16[512,2,32]{0,2,1:T(8,128)(2,1)} %copy-done.103), kind=kOutput, calls=%fused_computation.132 | convolution fusion | flops 283382272 | bytes 17973248 | tf_op jit(solution)/shard_map/kgij,jkd->ikgd/dot_general | solution.py:149
  435.1 15.3 %fusion.18 = (f32[8,512]{1,0:T(8,128)S(1)}, f32[8,512]{1,0:T(8,128)S(1)}, f32[8,512]{1,0:T(8,128)}, f32[512,512]{1,0:T(8,128)S(1)}, f32[512,512]{1,0:T(8,128)S(1...) fusion(f32[8,512]{1,0:T(8,128)S(1)} %copy-done.125, ...), kind=kOutput, calls=%fused_computation.45 | convolution fusion | flops 343109632 | bytes 24674304 | tf_op jit(solution)/shard_map/ihd,jhd->hij/dot_general | solution.py:204
  530.8 10.7 %convolution_convert_fusion.1 = bf16[1024,4096]{1,0:T(8,128)(2,1)} fusion(bf16[512,4096]{1,0:T(8,128)(2,1)} %fusion.71, bf16[512,1024]{1,0:T(8,128)(2,1)} %copy-done.66, f32[1024]{0:T(1024)S(1)} %bitcast.616, f32[512]{0:T(512)S(1)} %copy-done.145), kind=kOutput, calls=%fused_computation.36 | convolution fusion | flops 4301258752 | bytes 13637632 | tf_op jit(solution)/shard_map/ti,tj->ij/dot_general | solution.py:419
  609.2 92.3 %collective-permute-done.34 = bf16[2,2,2,64,1024]{4,3,2,1,0:T(8,128)(2,1)} collective-permute-done((bf16[2,2,2,64,1024]{4,3,2,1,0:T(8,128)(2,1)}, bf16[2,2,2,64,1024]{4,3,2,1,0:T(8,128)(2,1)}, u32[]{:S(2)}, u32[]{:S(2)}) %collective-permute-start.34) | collective-permute-done | bytes 1048608 | tf_op jit(solution)/shard_map/ppermute | solution.py:459
  703.5 20.1 %collective-permute-done.50 = bf16[2,2,2,64,1024]{4,3,0,1,2:T(8,128)(2,1)} collective-permute-done((bf16[2,2,2,64,1024]{4,3,0,1,2:T(8,128)(2,1)}, bf16[2,2,2,64,1024]{4,3,0,1,2:T(8,128)(2,1)}, u32[]{:S(2)}, u32[]{:S(2)}) %collective-permute-start.50) | collective-permute-done | bytes 1048608 | tf_op jit(solution)/shard_map/ppermute | solution.py:459
  791.3 51.4 %collective-permute-done.40 = bf16[2,2,64,1024]{3,2,0,1:T(8,128)(2,1)S(1)} collective-permute-done((bf16[2,2,64,1024]{3,2,0,1:T(8,128)(2,1)S(1)}, bf16[2,2,64,1024]{3,2,0,1:T(8,128)(2,1)S(1)}, u32[]{:S(2)}, u32[]{:S(2)}) %collective-permute-start.40) | collective-permute-done | bytes 524320 | tf_op jit(solution)/shard_map/ppermute | solution.py:459
  844.4 9.6 collective-permute-done.56
  857.9 38.1 %collective-permute-done.26 = bf16[2,2,2,32,4096]{4,3,2,1,0:T(8,128)(2,1)S(1)} collective-permute-done((bf16[2,2,2,32,4096]{4,3,2,1,0:T(8,128)(2,1)S(1)}, bf16[2,2,2,32,4096]{4,3,2,1,0:T(8,128)(2,1)S(1)}, u32[]{:S(2)}, u32[]{:S(2)}) %collective-permute-start.26) | collective-permute-done | bytes 2097184 | tf_op jit(solution)/shard_map/ppermute | solution.py:459
  899.0 20.4 %collective-permute-done.27 = bf16[2,2,32,4096]{3,2,1,0:T(8,128)(2,1)S(1)} collective-permute-done((bf16[2,2,32,4096]{3,2,1,0:T(8,128)(2,1)S(1)}, bf16[2,2,32,4096]{3,2,1,0:T(8,128)(2,1)S(1)}, u32[]{:S(2)}, u32[]{:S(2)}) %collective-permute-start.27) | collective-permute-done | bytes 1048608 | tf_op jit(solution)/shard_map/ppermute | solution.py:459
  925.2 10.4 %collective-permute-done.28 = bf16[2,32,4096]{2,1,0:T(8,128)(2,1)S(1)} collective-permute-done((bf16[2,32,4096]{2,1,0:T(8,128)(2,1)S(1)}, bf16[2,32,4096]{2,1,0:T(8,128)(2,1)S(1)}, u32[]{:S(2)}, u32[]{:S(2)}) %collective-permute-start.28) | collective-permute-done | bytes 524320 | tf_op jit(solution)/shard_map/ppermute | solution.py:459
  940.1 17.6 %collective-permute-done.29 = bf16[32,4096]{1,0:T(8,128)(2,1)S(1)} collective-permute-done((bf16[32,4096]{1,0:T(8,128)(2,1)S(1)}, bf16[32,4096]{1,0:T(8,128)(2,1)S(1)}, u32[]{:S(2)}, u32[]{:S(2)}) %collective-permute-start.29) | collective-permute-done | bytes 262176 | tf_op jit(solution)/shard_map/ppermute | solution.py:459
  957.8 11.1 %collective-permute-done.46 = bf16[32,4096]{1,0:T(8,128)(2,1)S(1)} collective-permute-done((bf16[32,4096]{1,0:T(8,128)(2,1)S(1)}, bf16[32,4096]{1,0:T(8,128)(2,1)S(1)}, u32[]{:S(2)}, u32[]{:S(2)}) %collective-permute-start.46) | collective-permute-done | bytes 262176 | tf_op jit(solution)/shard_map/ppermute | solution.py:459
  974.7 11.0 %collective-permute-done.47 = bf16[2,32,4096]{2,1,0:T(8,128)(2,1)S(1)} collective-permute-done((bf16[2,32,4096]{2,1,0:T(8,128)(2,1)S(1)}, bf16[2,32,4096]{2,1,0:T(8,128)(2,1)S(1)}, u32[]{:S(2)}, u32[]{:S(2)}) %collective-permute-start.47) | collective-permute-done | bytes 524320 | tf_op jit(solution)/shard_map/ppermute | solution.py:459
  986.5 10.4 collective-permute-done.31
  997.7 14.4 %collective-permute-done.48 = bf16[2,2,32,4096]{3,2,0,1:T(8,128)(2,1)S(1)} collective-permute-done((bf16[2,2,32,4096]{3,2,0,1:T(8,128)(2,1)S(1)}, bf16[2,2,32,4096]{3,2,0,1:T(8,128)(2,1)S(1)}, u32[]{:S(2)}, u32[]{:S(2)}) %collective-permute-start.48) | collective-permute-done | bytes 1048608 | tf_op jit(solution)/shard_map/ppermute | solution.py:459
  1014.7 18.7 %collective-permute-done.32 = bf16[2,2,32,4096]{3,2,0,1:T(8,128)(2,1)S(1)} collective-permute-done((bf16[2,2,32,4096]{3,2,0,1:T(8,128)(2,1)S(1)}, bf16[2,2,32,4096]{3,2,0,1:T(8,128)(2,1)S(1)}, u32[]{:S(2)}, u32[]{:S(2)}) %collective-permute-start.32) | collective-permute-done | bytes 1048608 | tf_op jit(solution)/shard_map/ppermute | solution.py:459
  (771 shorter events, 522.7 us)
Async XLA Ops:
  7.2 42.7 %all-reduce.25.cloned.1.call-start = ((), (), s32[]{:S(2)}) async-start(), calls=%async_computation | async-start | bytes 151552
  18.9 41.7 %collective-permute-start.5 = (bf16[256,1024]{1,0:T(8,128)(2,1)}, bf16[256,1024]{1,0:T(8,128)(2,1)}, u32[]{:S(2)}, u32[]{:S(2)}) collective-permute-start(bf16[256,1024]{1,0:T(8,128)(2,1)} %dynamic-slice_bitcast_fusion.15), channel_id=1, source_target_pairs={{0,2},{1,3},{2,0},{3,1},{4,6},{5,7},{6,4},{7,5},{8,10},{9,11},{10,... | collective-permute-start | bytes 1572872 | tf_op jit(solution)/shard_map/ppermute | solution.py:459
  25.3 74.8 %collective-permute-start.2 = (bf16[128,4096]{1,0:T(8,128)(2,1)}, bf16[128,4096]{1,0:T(8,128)(2,1)}, u32[]{:S(2)}, u32[]{:S(2)}) collective-permute-start(bf16[128,4096]{1,0:T(8,128)(2,1)} %dynamic-slice_bitcast_fusion.9), channel_id=1, source_target_pairs={{0,2},{1,3},{2,0},{3,1},{4,6},{5,7},{6,4},{7,5},{8,10},{9,11},{10,... | collective-permute-start | bytes 3145736 | tf_op jit(solution)/shard_map/ppermute | solution.py:459
  28.3 63.3 %collective-permute-start.8 = (bf16[128,4096]{1,0:T(8,128)(2,1)}, bf16[128,4096]{1,0:T(8,128)(2,1)}, u32[]{:S(2)}, u32[]{:S(2)}) collective-permute-start(bf16[128,4096]{1,0:T(8,128)(2,1)} %dynamic-slice_bitcast_fusion.8), channel_id=1, source_target_pairs={{0,2},{1,3},{2,0},{3,1},{4,6},{5,7},{6,4},{7,5},{8,10},{9,11},{10,... | collective-permute-start | bytes 3145736 | tf_op jit(solution)/shard_map/ppermute | solution.py:459
  28.4 67.0 %collective-permute-start = (bf16[512,1024]{1,0:T(8,128)(2,1)}, bf16[512,1024]{1,0:T(8,128)(2,1)}, u32[]{:S(2)}, u32[]{:S(2)}) collective-permute-start(bf16[512,1024]{1,0:T(8,128)(2,1)} %param.41), channel_id=1, source_target_pairs={{0,1},{1,0},{2,3},{3,2},{4,5},{5,4},{6,7},{7,6},{8,9},{9,8},{10,11... | collective-permute-start | bytes 3145736 | tf_op jit(solution)/shard_map/ppermute | solution.py:459
  60.6 36.7 %collective-permute-start.16 = (bf16[512,1024]{1,0:T(8,128)(2,1)}, bf16[512,1024]{1,0:T(8,128)(2,1)S(1)}, u32[]{:S(2)}, u32[]{:S(2)}) collective-permute-start(bf16[512,1024]{1,0:T(8,128)(2,1)} %param.57), channel_id=1, source_target_pairs={{0,1},{1,0},{2,3},{3,2},{4,5},{5,4},{6,7},{7,6},{8,9},{9,8},{10,11... | collective-permute-start | bytes 3145736 | tf_op jit(solution)/shard_map/ppermute | solution.py:459
  83.4 121.3 %collective-permute-start.13 = (bf16[2,512,1024]{2,1,0:T(8,128)(2,1)}, bf16[2,512,1024]{2,1,0:T(8,128)(2,1)}, u32[]{:S(2)}, u32[]{:S(2)}) collective-permute-start(bf16[2,512,1024]{2,1,0:T(8,128)(2,1)} %pad_maximum_fusion.17), channel_id=1, source_target_pairs={{0,1},{1,0},{2,3},{3,2},{4,5},{5,4},{6,7},{7,6},{8,9},{9,8},{10,11... | collective-permute-start | bytes 6291464 | tf_op jit(solution)/shard_map/ppermute | solution.py:459
  95.3 111.9 %collective-permute-start.7 = (bf16[2,512,1024]{2,1,0:T(8,128)(2,1)}, bf16[2,512,1024]{2,1,0:T(8,128)(2,1)}, u32[]{:S(2)}, u32[]{:S(2)}) collective-permute-start(bf16[2,512,1024]{2,1,0:T(8,128)(2,1)} %pad_maximum_fusion.15), channel_id=1, source_target_pairs={{0,1},{1,0},{2,3},{3,2},{4,5},{5,4},{6,7},{7,6},{8,9},{9,8},{10,11... | collective-permute-start | bytes 6291464 | tf_op jit(solution)/shard_map/ppermute | solution.py:459
  97.2 48.5 %collective-permute-start.1 = (bf16[2,512,1024]{2,1,0:T(8,128)(2,1)S(1)}, bf16[2,512,1024]{2,1,0:T(8,128)(2,1)S(1)}, u32[]{:S(2)}, u32[]{:S(2)}) collective-permute-start(bf16[2,512,1024]{2,1,0:T(8,128)(2,1)S(1)} %pad_maximum_fusion.12), channel_id=1, source_target_pairs={{0,2},{1,3},{2,0},{3,1},{4,6},{5,7},{6,4},{7,5},{8,10},{9,11},{10,... | collective-permute-start | bytes 6291464 | tf_op jit(solution)/shard_map/ppermute | solution.py:459
  100.1 90.2 %collective-permute-start.17 = (bf16[2,512,1024]{2,1,0:T(8,128)(2,1)S(1)}, bf16[2,512,1024]{2,1,0:T(8,128)(2,1)S(1)}, u32[]{:S(2)}, u32[]{:S(2)}) collective-permute-start(bf16[2,512,1024]{2,1,0:T(8,128)(2,1)S(1)} %pad_maximum_fusion.19), channel_id=1, source_target_pairs={{0,2},{1,3},{2,0},{3,1},{4,6},{5,7},{6,4},{7,5},{8,10},{9,11},{10,... | collective-permute-start | bytes 6291464 | tf_op jit(solution)/shard_map/ppermute | solution.py:459
  139.7 108.8 %collective-permute-start.10 = (bf16[2,256,4096]{2,1,0:T(8,128)(2,1)}, bf16[2,256,4096]{2,1,0:T(8,128)(2,1)}, u32[]{:S(2)}, u32[]{:S(2)}) collective-permute-start(bf16[2,256,4096]{2,1,0:T(8,128)(2,1)} %pad_maximum_fusion.5), channel_id=1, source_target_pairs={{0,1},{1,0},{2,3},{3,2},{4,5},{5,4},{6,7},{7,6},{8,9},{9,8},{10,11... | collective-permute-start | bytes 12582920 | tf_op jit(solution)/shard_map/ppermute | solution.py:459
  145.7 75.1 %collective-permute-start.4 = (bf16[2,256,4096]{2,1,0:T(8,128)(2,1)}, bf16[2,256,4096]{2,1,0:T(8,128)(2,1)}, u32[]{:S(2)}, u32[]{:S(2)}) collective-permute-start(bf16[2,256,4096]{2,1,0:T(8,128)(2,1)} %pad_maximum_fusion.3), channel_id=1, source_target_pairs={{0,1},{1,0},{2,3},{3,2},{4,5},{5,4},{6,7},{7,6},{8,9},{9,8},{10,11... | collective-permute-start | bytes 12582920 | tf_op jit(solution)/shard_map/ppermute | solution.py:459
  479.5 102.9 %collective-permute-start.14 = (bf16[512,1024]{1,0:T(8,128)(2,1)}, bf16[512,1024]{1,0:T(8,128)(2,1)}, u32[]{:S(2)}, u32[]{:S(2)}) collective-permute-start(bf16[512,1024]{1,0:T(8,128)(2,1)} %add_convert_fusion.2), channel_id=1, source_target_pairs={{0,1},{1,0},{2,3},{3,2},{4,5},{5,4},{6,7},{7,6},{8,9},{9,8},{10,11... | collective-permute-start | bytes 3145736 | tf_op jit(solution)/shard_map/ppermute | solution.py:459
  582.1 196.6 %collective-permute-start.41 = (bf16[2,2,2,2,32,4096]{5,4,1,2,0,3:T(8,128)(2,1)}, bf16[2,2,2,2,32,4096]{5,4,1,2,0,3:T(8,128)(2,1)}, u32[]{:S(2)}, u32[]{:S(2)}) collective-permute-start(bf16[2,2,2,2,32,4096]{5,4,1,2,0,3:T(8,128)(2,1)} %bitcast.522), channel_id=1, source_target_pairs={{0,1},{1,0},{2,3},{3,2},{4,5},{5,4},{6,7},{7,6},{8,9},{9,8},{10,11... | collective-permute-start | bytes 12582920 | tf_op jit(solution)/shard_map/ppermute | solution.py:459
  585.3 140.5 %collective-permute-start.15 = (bf16[2,512,1024]{2,1,0:T(8,128)(2,1)}, bf16[2,512,1024]{2,1,0:T(8,128)(2,1)}, u32[]{:S(2)}, u32[]{:S(2)}) collective-permute-start(bf16[2,512,1024]{2,1,0:T(8,128)(2,1)} %pad_maximum_fusion.18), channel_id=1, source_target_pairs={{0,2},{1,3},{2,0},{3,1},{4,6},{5,7},{6,4},{7,5},{8,10},{9,11},{10,... | collective-permute-start | bytes 6291464 | tf_op jit(solution)/shard_map/ppermute | solution.py:459
  589.1 140.1 %collective-permute-start.19 = (bf16[2,512,1024]{2,1,0:T(8,128)(2,1)}, bf16[2,512,1024]{2,1,0:T(8,128)(2,1)}, u32[]{:S(2)}, u32[]{:S(2)}) collective-permute-start(bf16[2,512,1024]{2,1,0:T(8,128)(2,1)} %pad_maximum_fusion.20), channel_id=1, source_target_pairs={{0,2},{1,3},{2,0},{3,1},{4,6},{5,7},{6,4},{7,5},{8,10},{9,11},{10,... | collective-permute-start | bytes 6291464 | tf_op jit(solution)/shard_map/ppermute | solution.py:459
  593.7 107.7 %collective-permute-start.34 = (bf16[2,2,2,64,1024]{4,3,2,1,0:T(8,128)(2,1)}, bf16[2,2,2,64,1024]{4,3,2,1,0:T(8,128)(2,1)}, u32[]{:S(2)}, u32[]{:S(2)}) collective-permute-start(bf16[2,2,2,64,1024]{4,3,2,1,0:T(8,128)(2,1)} %dynamic-slice_bitcast_fusion.6), channel_id=1, source_target_pairs={{0,2},{1,3},{2,0},{3,1},{4,6},{5,7},{6,4},{7,5},{8,10},{9,11},{10,... | collective-permute-start | bytes 3145736 | tf_op jit(solution)/shard_map/ppermute | solution.py:459
  600.5 123.0 %collective-permute-start.50 = (bf16[2,2,2,64,1024]{4,3,0,1,2:T(8,128)(2,1)}, bf16[2,2,2,64,1024]{4,3,0,1,2:T(8,128)(2,1)}, u32[]{:S(2)}, u32[]{:S(2)}) collective-permute-start(bf16[2,2,2,64,1024]{4,3,0,1,2:T(8,128)(2,1)} %dynamic-slice_bitcast_fusion.4), channel_id=1, source_target_pairs={{0,2},{1,3},{2,0},{3,1},{4,6},{5,7},{6,4},{7,5},{8,10},{9,11},{10,... | collective-permute-start | bytes 3145736 | tf_op jit(solution)/shard_map/ppermute | solution.py:459
  701.5 82.0 %collective-permute-start.25 = (bf16[2,2,2,2,32,4096]{5,4,3,2,1,0:T(8,128)(2,1)}, bf16[2,2,2,2,32,4096]{5,4,3,2,1,0:T(8,128)(2,1)}, u32[]{:S(2)}, u32[]{:S(2)}) collective-permute-start(bf16[2,2,2,2,32,4096]{5,4,3,2,1,0:T(8,128)(2,1)} %dynamic-slice_bitcast_fusion), channel_id=1, source_target_pairs={{0,1},{1,0},{2,3},{3,2},{4,5},{5,4},{6,7},{7,6},{8,9},{9,8},{10,11... | collective-permute-start | bytes 12582920 | tf_op jit(solution)/shard_map/ppermute | solution.py:459
  782.8 72.8 %collective-permute-start.42 = (bf16[2,2,2,32,4096]{4,3,1,2,0:T(8,128)(2,1)S(1)}, bf16[2,2,2,32,4096]{4,3,1,2,0:T(8,128)(2,1)S(1)}, u32[]{:S(2)}, u32[]{:S(2)}) collective-permute-start(bf16[2,2,2,32,4096]{4,3,1,2,0:T(8,128)(2,1)S(1)} %dynamic-slice_bitcast_fusion.1), channel_id=1, source_target_pairs={{0,4},{4,0},{8,12},{12,8},{16,20},{20,16},{24,28},{28,24},{1,5},{5... | collective-permute-start | bytes 6291464 | tf_op jit(solution)/shard_map/ppermute | solution.py:459
  787.3 55.4 %collective-permute-start.40 = (bf16[2,2,64,1024]{3,2,0,1:T(8,128)(2,1)S(1)}, bf16[2,2,64,1024]{3,2,0,1:T(8,128)(2,1)S(1)}, u32[]{:S(2)}, u32[]{:S(2)}) collective-permute-start(bf16[2,2,64,1024]{3,2,0,1:T(8,128)(2,1)S(1)} %pad_maximum_fusion.29), channel_id=1, source_target_pairs={{0,4},{4,0},{8,12},{12,8},{16,20},{20,16},{24,28},{28,24},{1,5},{5... | collective-permute-start | bytes 1572872 | tf_op jit(solution)/shard_map/ppermute | solution.py:459
  789.0 65.0 %collective-permute-start.56 = (bf16[2,2,64,1024]{3,2,0,1:T(8,128)(2,1)S(1)}, bf16[2,2,64,1024]{3,2,0,1:T(8,128)(2,1)S(1)}, u32[]{:S(2)}, u32[]{:S(2)}) collective-permute-start(bf16[2,2,64,1024]{3,2,0,1:T(8,128)(2,1)S(1)} %pad_maximum_fusion.31), channel_id=1, source_target_pairs={{0,4},{4,0},{8,12},{12,8},{16,20},{20,16},{24,28},{28,24},{1,5},{5... | collective-permute-start | bytes 1572872 | tf_op jit(solution)/shard_map/ppermute | solution.py:459
  789.8 106.2 %collective-permute-start.26 = (bf16[2,2,2,32,4096]{4,3,2,1,0:T(8,128)(2,1)S(1)}, bf16[2,2,2,32,4096]{4,3,2,1,0:T(8,128)(2,1)S(1)}, u32[]{:S(2)}, u32[]{:S(2)}) collective-permute-start(bf16[2,2,2,32,4096]{4,3,2,1,0:T(8,128)(2,1)S(1)} %dynamic-slice_bitcast_fusion.3), channel_id=1, source_target_pairs={{0,4},{4,0},{8,12},{12,8},{16,20},{20,16},{24,28},{28,24},{1,5},{5... | collective-permute-start | bytes 6291464 | tf_op jit(solution)/shard_map/ppermute | solution.py:459
  856.7 41.7 %collective-permute-start.43 = (bf16[2,2,32,4096]{3,2,0,1:T(8,128)(2,1)S(1)}, bf16[2,2,32,4096]{3,2,0,1:T(8,128)(2,1)S(1)}, u32[]{:S(2)}, u32[]{:S(2)}) collective-permute-start(bf16[2,2,32,4096]{3,2,0,1:T(8,128)(2,1)S(1)} %dynamic-slice_bitcast_fusion.5), channel_id=1, source_target_pairs={{0,2},{1,3},{2,0},{3,1},{4,6},{5,7},{6,4},{7,5},{8,10},{9,11},{10,... | collective-permute-start | bytes 3145736 | tf_op jit(solution)/shard_map/ppermute | solution.py:459
  (208 other events, 2498.1 us)
Sparse Core Ops, SparseCore 0:
  17.1 32.7 all-reduce.24

commit v2 on v0

v2 whole, which is shorter than its diff:
```python
import math

import jax
import jax.numpy as jnp
from jax import lax
from jax.experimental import pallas as pl
from jax.experimental.pallas import tpu as pltpu
from jax.sharding import PartitionSpec as P

QUERY_HEADS = 8
KEY_VALUE_HEADS = 2
HEAD_SIZE = 64
SSM_HEADS = 24
SSM_HD = 64
STATE = 128
INNER = 1536
QUERY_KEY_VALUE = 768
TAPS = 4

EPS = 1e-05
ROPE_BASE = 100000000000.0
SIDE = 128
QUAD = 4
LOW = -1e30


def causal_bias(limit, rows, row0, cols):
    i = lax.broadcasted_iota(jnp.int32, (rows, cols), 0) + row0
    j = lax.broadcasted_iota(jnp.int32, (rows, cols), 1)
    seen = (j <= i) & ((j >= limit) | (i < limit))
    return jnp.where(seen, 0.0, LOW)


def contract_last(left, right):
    return lax.dot_general(left, right, (((1,), (1,)), ((), ())), preferred_element_type=jnp.float32)


def contract_first(left, right):
    return lax.dot_general(left, right, (((0,), (0,)), ((), ())), preferred_element_type=jnp.float32)


def halves(pair):
    lane = lax.broadcasted_iota(jnp.int32, pair.shape, 1)
    zero = jnp.zeros_like(pair)
    return (jnp.where(lane < HEAD_SIZE, pair, zero), jnp.where(lane >= HEAD_SIZE, pair, zero))


def ssd_forward_kernel(limit_ref, c_ref, b_ref, x_ref, cum_col_ref, cum_row_ref, out_ref, inter, bias):
    count = c_ref.shape[0]

    @pl.when(pl.program_id(0) == 0)
    def _():
        inter[...] = contract_last(c_ref[...], b_ref[...])
        bias[...] = causal_bias(limit_ref[0], count, 0, count)

    for pair in range(QUAD // 2):
        lanes = slice(pair * SIDE, (pair + 1) * SIDE)
        sides = halves(x_ref[:, lanes])
        for top in range(0, count, SIDE):
            rows = slice(top, top + SIDE)
            seen = top + SIDE
            total = None
            for half in range(2):
                h = pair * 2 + half
                gap = cum_col_ref[0, rows, h : h + 1] - cum_row_ref[0, h : h + 1, :seen]
                mixer = (inter[rows, :seen] * jnp.exp(gap + bias[rows, :seen])).astype(jnp.bfloat16)
                part = jnp.dot(mixer, sides[half][:seen], preferred_element_type=jnp.float32)
                total = part if total is None else total + part
            out_ref[rows, lanes] = total


def ssd_forward(limit, c_low, b_low, x_step, cum):
    count, heads = cum.shape
    steps = heads // QUAD
    whole = lambda width: pl.BlockSpec((count, width), lambda i: (0, 0))
    return pl.pallas_call(
        ssd_forward_kernel,
        grid=(steps,),
        out_shape=jax.ShapeDtypeStruct(x_step.shape, jnp.float32),
        in_specs=[
            pl.BlockSpec(memory_space=pltpu.SMEM),
            whole(c_low.shape[1]),
            whole(b_low.shape[1]),
            pl.BlockSpec((count, QUAD * HEAD_SIZE), lambda i: (0, i)),
            pl.BlockSpec((1, count, QUAD), lambda i: (i, 0, 0)),
            pl.BlockSpec((1, QUAD, count), lambda i: (i, 0, 0)),
        ],
        out_specs=pl.BlockSpec((count, QUAD * HEAD_SIZE), lambda i: (0, i)),
        scratch_shapes=[pltpu.VMEM((count, count), jnp.float32)] * 2,
        name="ssd_forward",
    )(
        limit,
        c_low,
        b_low,
        x_step,
        cum.reshape(count, steps, QUAD).transpose(1, 0, 2),
        cum.T.reshape(steps, QUAD, count),
    )


def ssd_backward_kernel(
    limit_ref, c_ref, b_ref, x_ref, dy_ref, cum_col_ref, cum_row_ref, z_ref, gc_ref, gb_ref, inter, bias, total
):
    count = c_ref.shape[0]

    @pl.when(pl.program_id(0) == 0)
    def _():
        inter[...] = contract_last(c_ref[...], b_ref[...])
        bias[...] = causal_bias(limit_ref[0], count, 0, count)
        total[...] = jnp.zeros_like(total)

    for pair in range(QUAD // 2):
        lanes = slice(pair * SIDE, (pair + 1) * SIDE)
        x_pair = x_ref[:, lanes]
        sides = halves(dy_ref[:, lanes])
        for top in reversed(range(0, count, SIDE)):
            rows = slice(top, top + SIDE)
            seen = top + SIDE
            grad = None
            back = None
            for half in range(2):
                h = pair * 2 + half
                gap = cum_col_ref[0, rows, h : h + 1] - cum_row_ref[0, h : h + 1, :seen]
                decay = jnp.exp(gap + bias[rows, :seen])
                mixer = (inter[rows, :seen] * decay).astype(jnp.bfloat16)
                grad_mixer = contract_last(sides[half][rows], x_pair[:seen])
                part = grad_mixer * decay
                grad = part if grad is None else grad + part
                part = contract_first(mixer, sides[half][rows])
                back = part if back is None else back + part
            total[rows, :seen] += grad
            if seen == count:
                z_ref[:, lanes] = back
            else:
                z_ref[:seen, lanes] += back

    @pl.when(pl.program_id(0) == pl.num_programs(0) - 1)
    def _():
        low = total[...].astype(jnp.bfloat16)
        gc_ref[...] = jnp.dot(low, b_ref[...], preferred_element_type=jnp.float32)
        gb_ref[...] = contract_first(low, c_ref[...])


def ssd_backward(limit, c_low, b_low, x_step, grad_y, cum):
    count, heads = cum.shape
    steps = heads // QUAD
    state = c_low.shape[1]
    whole = pl.BlockSpec((count, state), lambda i: (0, 0))
    quad = pl.BlockSpec((count, QUAD * HEAD_SIZE), lambda i: (0, i))
    return pl.pallas_call(
        ssd_backward_kernel,
        grid=(steps,),
        out_shape=(
            jax.ShapeDtypeStruct(x_step.shape, jnp.float32),
            jax.ShapeDtypeStruct((count, state), jnp.float32),
            jax.ShapeDtypeStruct((count, state), jnp.float32),
        ),
        in_specs=[
            pl.BlockSpec(memory_space=pltpu.SMEM),
            whole,
            whole,
            quad,
            quad,
            pl.BlockSpec((1, count, QUAD), lambda i: (i, 0, 0)),
            pl.BlockSpec((1, QUAD, count), lambda i: (i, 0, 0)),
        ],
        out_specs=(quad, whole, whole),
        scratch_shapes=[pltpu.VMEM((count, count), jnp.float32)] * 3,
        name="ssd_backward",
    )(
        limit,
        c_low,
        b_low,
        x_step,
        grad_y,
        cum.reshape(count, steps, QUAD).transpose(1, 0, 2),
        cum.T.reshape(steps, QUAD, count),
    )


def turn(values, cosine, sine):
    lane = lax.broadcasted_iota(jnp.int32, values.shape, 1) % HEAD_SIZE
    width = values.shape[1]
    ahead = pltpu.roll(values, width - HEAD_SIZE // 2, 1)
    behind = pltpu.roll(values, HEAD_SIZE // 2, 1)
    other = jnp.where(lane < HEAD_SIZE // 2, ahead, behind)
    return values * cosine + other * sine


def both_sides(pair, step):
    lane = lax.broadcasted_iota(jnp.int32, pair.shape, 1)
    mine = jnp.where((lane >= HEAD_SIZE) == (step > 0), pair, jnp.zeros_like(pair))
    return (mine + pltpu.roll(mine, HEAD_SIZE, 1)).astype(jnp.bfloat16)


def attention_forward_kernel(limit_ref, q_ref, k_ref, v_ref, cos_ref, sin_ref, out_ref, log_ref, bias):
    count = k_ref.shape[0]
    step = pl.program_id(0)

    @pl.when(step == 0)
    def _():
        bias[...] = causal_bias(limit_ref[0], count, 0, count)

    cosine, sine = cos_ref[...], sin_ref[...]
    key = both_sides(turn(k_ref[...], cosine, sine), step)
    value_sides = halves(both_sides(v_ref[...], step))
    for pair in range(2):
        lanes = slice(pair * SIDE, (pair + 1) * SIDE)
        sides = halves(turn(q_ref[:, lanes], cosine, sine).astype(jnp.bfloat16))
        for top in range(0, count, SIDE):
            rows = slice(top, top + SIDE)
            seen = top + SIDE
            total = None
            for half in range(2):
                score = contract_last(sides[half][rows], key[:seen]) * HEAD_SIZE ** (-0.5)
                score = score + bias[rows, :seen]
                largest = jnp.max(score, -1, keepdims=True)
                raised = jnp.exp(score - largest)
                mass = jnp.sum(raised, -1, keepdims=True)
                weights = (raised * (1.0 / mass)).astype(jnp.bfloat16)
                part = jnp.dot(weights, value_sides[half][:seen], preferred_element_type=jnp.float32)
                total = part if total is None else total + part
                h = pair * 2 + half
                log_ref[0, rows, h : h + 1] = largest + jnp.log(mass)
            out_ref[rows, lanes] = total.astype(jnp.bfloat16)


def attention_specs(count):
    wide = pl.BlockSpec((count, 2 * SIDE), lambda i: (0, i))
    whole = pl.BlockSpec((count, SIDE), lambda i: (0, 0))
    keys = pl.BlockSpec((count, SIDE), lambda i: (0, QUERY_HEADS * HEAD_SIZE // SIDE))
    values = pl.BlockSpec((count, SIDE), lambda i: (0, QUERY_HEADS * HEAD_SIZE // SIDE + 1))
    logs = pl.BlockSpec((1, count, QUAD), lambda i: (i, 0, 0))
    return wide, whole, keys, values, logs


def attention_forward(limit, projected, cosine, sine):
    count = projected.shape[0]
    wide, whole, keys, values, logs = attention_specs(count)
    return pl.pallas_call(
        attention_forward_kernel,
        grid=(KEY_VALUE_HEADS,),
        out_shape=(
            jax.ShapeDtypeStruct((count, QUERY_HEADS * HEAD_SIZE), jnp.bfloat16),
            jax.ShapeDtypeStruct((KEY_VALUE_HEADS, count, QUAD), jnp.float32),
        ),
        in_specs=[pl.BlockSpec(memory_space=pltpu.SMEM), wide, keys, values, whole, whole],
        out_specs=(wide, logs),
        scratch_shapes=[pltpu.VMEM((count, count), jnp.float32)],
        name="attention_forward",
    )(limit, projected, projected, projected, cosine, sine)


def attention_backward_kernel(
    limit_ref, q_ref, k_ref, v_ref, cos_ref, sin_ref, go_ref, log_ref, gq_ref, gkv_ref, bias, gk, gv
):
    count = k_ref.shape[0]
    step = pl.program_id(0)

    @pl.when(step == 0)
    def _():
        bias[...] = causal_bias(limit_ref[0], count, 0, count)

    cosine, sine = cos_ref[...], sin_ref[...]
    key = both_sides(turn(k_ref[...], cosine, sine), step)
    value = both_sides(v_ref[...], step)
    key_sides = halves(key)
    gk[...] = jnp.zeros_like(gk)
    gv[...] = jnp.zeros_like(gv)
    for pair in range(2):
        lanes = slice(pair * SIDE, (pair + 1) * SIDE)
        q_sides = halves(turn(q_ref[:, lanes], cosine, sine).astype(jnp.bfloat16))
        go_sides = halves(go_ref[:, lanes])
        for top in range(0, count, SIDE):
            rows = slice(top, top + SIDE)
            seen = top + SIDE
            total = None
            for half in range(2):
                h = pair * 2 + half
                score = contract_last(q_sides[half][rows], key[:seen]) * HEAD_SIZE ** (-0.5)
                weights = jnp.exp(score + bias[rows, :seen] - log_ref[0, rows, h : h + 1])
                grad = contract_last(go_sides[half][rows], value[:seen])
                inner = jnp.sum(grad * weights, -1, keepdims=True)
                low = (weights * (grad - inner) * HEAD_SIZE ** (-0.5)).astype(jnp.bfloat16)
                part = jnp.dot(low, key_sides[half][:seen], preferred_element_type=jnp.float32)
                total = part if total is None else total + part
                gk[:seen, :] += contract_first(low, q_sides[half][rows])
                gv[:seen, :] += contract_first(weights.astype(jnp.bfloat16), go_sides[half][rows])
            gq_ref[rows, lanes] = turn(total, cosine[rows], -sine[rows]).astype(jnp.bfloat16)
    lane = lax.broadcasted_iota(jnp.int32, (count, SIDE), 1)
    mine = (lane >= HEAD_SIZE) == (step > 0)
    for place, part in enumerate((gk, gv)):
        summed = part[...] + pltpu.roll(part[...], HEAD_SIZE, 1)
        if place == 0:
            summed = turn(summed, cosine, -sine)
        lanes = slice(place * SIDE, (place + 1) * SIDE)
        @pl.when(step == 0)
        def _():
            gkv_ref[:, lanes] = summed.astype(jnp.bfloat16)

        @pl.when(step > 0)
        def _():
            gkv_ref[:, lanes] = jnp.where(mine, summed, gkv_ref[:, lanes].astype(jnp.float32)).astype(jnp.bfloat16)


def attention_backward(limit, projected, cosine, sine, grad_out, logs_in):
    count = projected.shape[0]
    wide, whole, keys, values, logs = attention_specs(count)
    return pl.pallas_call(
        attention_backward_kernel,
        grid=(KEY_VALUE_HEADS,),
        out_shape=(
            jax.ShapeDtypeStruct((count, QUERY_HEADS * HEAD_SIZE), jnp.bfloat16),
            jax.ShapeDtypeStruct((count, 2 * SIDE), jnp.bfloat16),
        ),
        in_specs=[pl.BlockSpec(memory_space=pltpu.SMEM), wide, keys, values, whole, whole, wide, logs],
        out_specs=(wide, pl.BlockSpec((count, 2 * SIDE), lambda i: (0, 0))),
        scratch_shapes=[
            pltpu.VMEM((count, count), jnp.float32),
            pltpu.VMEM((count, SIDE), jnp.float32),
            pltpu.VMEM((count, SIDE), jnp.float32),
        ],
        name="attention_backward",
    )(limit, projected, projected, projected, cosine, sine, grad_out, logs_in)


def pick_kernel(shift_ref, wanted_ref, *refs):
    out_ref = refs[-1]
    pieces = refs[:-1]
    count = pieces[0].shape[0]
    place = lax.broadcasted_iota(jnp.int32, (out_ref.shape[0], count), 1)
    total = None
    for n, piece in enumerate(pieces):
        choice = (wanted_ref[...] - shift_ref[n] == place).astype(jnp.bfloat16)
        part = jnp.dot(choice, piece[...], preferred_element_type=jnp.float32)
        total = part if total is None else total + part
    out_ref[...] = total.astype(out_ref.dtype)


def pick_rows(pieces, shifts, wanted):
    vmem = pl.BlockSpec(memory_space=pltpu.VMEM)
    return pl.pallas_call(
        pick_kernel,
        out_shape=jax.ShapeDtypeStruct((wanted.shape[0], pieces[0].shape[1]), pieces[0].dtype),
        in_specs=[pl.BlockSpec(memory_space=pltpu.SMEM), vmem] + [vmem] * len(pieces),
        out_specs=vmem,
        name="pick_rows",
    )(shifts, wanted[:, None], *pieces)


def lay_rows_kernel(place_ref, *refs):
    sems = refs[-1]
    out_ref = refs[-2]
    pieces = refs[:-2]
    copies = []
    for n, piece in enumerate(pieces):
        rows = piece.shape[0]
        start = pl.multiple_of(place_ref[n] * 16, 16)
        copies.append(pltpu.make_async_copy(piece, out_ref.at[pl.ds(start, rows)], sems.at[n]))
    for copy in copies:
        copy.start()
    for copy in copies:
        copy.wait()


def lay_rows(pieces, places):
    rows = sum(piece.shape[0] for piece in pieces)
    hbm = pl.BlockSpec(memory_space=pl.ANY)
    return pl.pallas_call(
        lay_rows_kernel,
        out_shape=jax.ShapeDtypeStruct((rows, pieces[0].shape[1]), pieces[0].dtype),
        in_specs=[pl.BlockSpec(memory_space=pltpu.SMEM)] + [hbm] * len(pieces),
        out_specs=pl.BlockSpec(memory_space=pltpu.VMEM),
        scratch_shapes=[pltpu.SemaphoreType.DMA((len(pieces),))],
        name="lay_rows",
    )(places // 16, *pieces)


def sum_pieces_kernel(place_ref, *refs):
    out_ref = refs[-1]
    for n, piece in enumerate(refs[:-1]):
        rows = piece.shape[0]
        start = pl.multiple_of(place_ref[n] * 8, 8)
        out_ref[pl.ds(start, rows), :] = piece[...].astype(jnp.float32)


def widen_rows(pieces, places):
    rows = sum(piece.shape[0] for piece in pieces)
    vmem = pl.BlockSpec(memory_space=pltpu.VMEM)
    return pl.pallas_call(
        sum_pieces_kernel,
        out_shape=jax.ShapeDtypeStruct((rows, pieces[0].shape[1]), jnp.float32),
        in_specs=[pl.BlockSpec(memory_space=pltpu.SMEM)] + [vmem] * len(pieces),
        out_specs=vmem,
        name="widen_rows",
    )(places // 8, *pieces)


def swap(values, axis, mask):
    count = lax.axis_size(axis)
    return lax.ppermute(values, axis, [(i, i ^ mask) for i in range(count)])


def take(values, index, dim):
    return lax.dynamic_index_in_dim(values, index, dim, keepdims=False)


def add(first, *others):
    total = first.astype(jnp.float32)
    for other in others:
        total = total + other.astype(jnp.float32)
    return total.astype(jnp.bfloat16)


class Flow:
    def __init__(self):
        self.live = []

    def add(self, stream):
        slot = {"stream": stream, "sent": None, "result": None, "done": False}
        self.live.append(slot)
        self._advance(slot, None)
        return slot

    def _advance(self, slot, value):
        try:
            slot["sent"] = slot["stream"].send(value)
        except StopIteration as stop:
            slot["result"] = stop.value
            slot["sent"] = None
            slot["done"] = True
            self.live.remove(slot)

    def step(self, values=None, slots=None):
        slots = [slot for slot in (self.live if slots is None else slots) if not slot["done"]]
        values, sent = lax.optimization_barrier((values, [slot["sent"] for slot in slots]))
        for slot, came in zip(slots, sent):
            self._advance(slot, came)
        return values

    def until(self, slots, values=None):
        while any(not slot["done"] for slot in slots):
            values = self.step(values)
        return values


def rows_stream(piece):
    shard = lax.axis_index("shard")
    held = [(0, piece)]
    mask = lax.axis_size("shard") // 2
    first = True
    near = None
    while mask > 1:
        send = [swap(p, "shard", mask) for _, p in held]
        if first:
            send.append(swap(piece, "shard", 1))
        came = yield send
        if first:
            near = came[-1]
            first = False
        held = held + [(k ^ mask, p) for (k, _), p in zip(held, came)]
        mask //= 2
    came = yield [swap(p, "shard", 1) for k, p in held[1:]]
    held = held + [(1, near)] + [(k ^ 1, p) for (k, _), p in zip(held[1:], came)]
    keys = [k for k, _ in held]
    return [p for _, p in held], jnp.stack([shard ^ k for k in keys]).astype(jnp.int32)


def weight_stream(piece):
    rows, width = piece.shape
    shard, near = lax.axis_index("shard"), lax.axis_index("rep") & 1
    part = lax.dynamic_slice_in_dim(piece, near * (rows // 2), rows // 2, 0)
    held = [(0, part)]
    both = []
    mask = lax.axis_size("shard") // 2
    beside = None
    while mask > 1:
        send = [swap(p, "shard", mask) for _, p in held]
        if beside is None:
            send.append(swap(piece, "shard", 1))
        came = yield send
        if beside is None:
            beside = came[-1]
        fresh = [(k ^ mask, p) for (k, _), p in zip(held, came)]
        passed = yield [swap(p, "rep", 1) for _, p in fresh] + [swap(p, "shard", 1) for _, p in fresh]
        count = len(fresh)
        for n, (k, p) in enumerate(fresh):
            both.append((k, 0, p))
            both.append((k ^ 1, 0, passed[count + n]))
            both.append((k, 1, passed[n]))
        held = held + fresh
        mask //= 2
    late = [(k, p) for k, side, p in both if side == 1]
    came = yield [swap(p, "shard", 1) for _, p in late]
    both = both + [(k ^ 1, 1, p) for (k, _), p in zip(late, came)]
    pieces = [piece, beside] + [p for _, _, p in both]
    places = [shard * rows, (shard ^ 1) * rows]
    places += [(shard ^ k) * rows + (near ^ side) * (rows // 2) for k, side, _ in both]
    return lay_rows(pieces, jnp.stack(places).astype(jnp.int32))


def reduce_stream(grad, far_first):
    rows_all, width = grad.shape
    shards, replicas = lax.axis_size("shard"), lax.axis_size("rep")
    rows = rows_all // shards // replicas
    shard, replica = lax.axis_index("shard"), lax.axis_index("rep")
    core, far = shard & 1, shard >> 1
    near, rest = replica & 1, replica >> 1
    total = grad.reshape(shards // 2, 2, replicas // 2, 2, rows, width)
    away, keep = take(total, 1 - core, 1), take(total, core, 1)
    came = yield [swap(away, "shard", 1)]
    total = add(keep, came[0])

    def over_near(total):
        away, keep = take(total, 1 - near, total.ndim - 3), take(total, near, total.ndim - 3)
        came = yield [swap(away, "rep", 1)]
        return add(keep, came[0])

    def over_far(total):
        count = shards // 2
        while count > 1:
            count //= 2
            flag = (far // count) % 2
            total = total.reshape((2, count) + total.shape[1:])
            away, keep = take(total, 1 - flag, 0), take(total, flag, 0)
            came = yield [swap(away, "shard", 2 * count)]
            total = add(keep, came[0])
        return total[0]

    if far_first:
        total = yield from over_far(total)
        total = yield from over_near(total)
    else:
        total = yield from over_near(total)
        total = yield from over_far(total)
    others = range(1, replicas // 2)
    came = yield [swap(take(total, rest ^ k, 0), "rep", 2 * k) for k in others]
    total = add(take(total, rest, 0), *came)
    came = yield [swap(total, "rep", 2 * k) for k in others]
    mine = jnp.concatenate([total, *came], 0)
    came = yield [swap(mine, "rep", 1)]
    pieces = [mine[k * rows : (k + 1) * rows] for k in range(replicas // 2)]
    pieces += [came[0][k * rows : (k + 1) * rows] for k in range(replicas // 2)]
    places = [((rest ^ k) * 2 + (near ^ side)) * rows for side in range(2) for k in range(replicas // 2)]
    return pieces, jnp.stack(places).astype(jnp.int32)


def butterfly_stream(total):
    for axis in ("shard", "rep"):
        mask = 1
        while mask < lax.axis_size(axis):
            came = yield [swap(total, axis, mask)]
            total = total + came[0]
            mask *= 2
    return total


def small_stream(flat):
    held = flat[None]
    mask = 1
    shard = lax.axis_index("shard")
    while mask < lax.axis_size("shard"):
        came = yield [swap(held, "shard", mask)]
        flag = (shard & mask) == 0
        held = jnp.concatenate([jnp.where(flag, held, came[0]), jnp.where(flag, came[0], held)], 0)
        mask *= 2
    return held


def unpack_small(every, shapes, dims):
    parts = every.shape[0]
    outputs = []
    offset = 0
    for shape, dim in zip(shapes, dims):
        length = math.prod(shape)
        block = every[:, offset : offset + length].reshape((parts,) + shape)
        offset += length
        if dim == 0:
            outputs.append(block.reshape((-1,) + shape[1:]))
        else:
            outputs.append(jnp.swapaxes(block, 0, 1).reshape(shape[0], -1))
    return outputs


def own_block(values, dim):
    size = values.shape[dim] // lax.axis_size("shard")
    return lax.dynamic_slice_in_dim(values, lax.axis_index("shard") * size, size, dim)


def group_tables(lengths, order, input_rows, device):
    count = lengths.shape[0]
    slots = jnp.arange(count, dtype=jnp.int32)
    starts = jnp.cumsum(lengths) - lengths
    pick = (order[:, None] == slots[None, :]).astype(jnp.int32)
    owner_len = jnp.sum(pick * lengths[None, :], 1)
    owner_start = jnp.cumsum(owner_len) - owner_len
    owner_src = jnp.sum(pick * starts[None, :], 1)
    first_len = jnp.sum(jnp.where(slots == 2 * device, owner_len, 0))
    first_src = jnp.sum(jnp.where(slots == 2 * device, owner_src, 0))
    second_src = jnp.sum(jnp.where(slots == 2 * device + 1, owner_src, 0))
    local = jnp.arange(input_rows, dtype=jnp.int32)
    segment = (local >= first_len).astype(jnp.int32)
    position = local - segment * first_len
    source = jnp.where(segment > 0, second_src, first_src) + position
    given = device * input_rows + local
    seq_id = jnp.sum((starts[None, :] <= given[:, None]).astype(jnp.int32), 1) - 1
    member = (seq_id[:, None] == slots[None, :]).astype(jnp.int32)
    seq_start = jnp.sum(member * starts[None, :], 1)
    seq_owner_start = jnp.sum(pick * owner_start[:, None], 0)
    target = jnp.sum(member * seq_owner_start[None, :], 1) + given - seq_start
    return (source, position, first_len.reshape(1), target)


def rms_scale(values):
    return lax.rsqrt(jnp.mean(values * values, axis=-1, keepdims=True) + EPS)


def rms_norm(values, gain):
    return values * rms_scale(values) * gain


def rope_tables(position):
    half = HEAD_SIZE // 2
    lane = jnp.arange(SIDE, dtype=jnp.int32)
    ladder = (lane % half).astype(jnp.float32) * (2.0 / HEAD_SIZE)
    angles = position.astype(jnp.float32)[:, None] * jnp.exp(-math.log(ROPE_BASE) * ladder)
    sign = jnp.where(lane % HEAD_SIZE < half, -1.0, 1.0)
    return jnp.cos(angles), jnp.sin(angles) * sign


def conv_mixed(conv_in, conv_weight, conv_bias, position):
    width = conv_in.shape[1]
    mixed = conv_bias + conv_in * conv_weight[TAPS - 1]
    for back in range(1, TAPS):
        shifted = jnp.concatenate([jnp.zeros((back, width), jnp.float32), conv_in[:-back]], 0)
        same = (position >= back).astype(jnp.float32)[:, None]
        mixed = mixed + shifted * same * conv_weight[TAPS - 1 - back]
    return mixed


def gated_norm(ssm_y, gate_z, gain):
    gated = ssm_y * jax.nn.silu(gate_z)
    return gated * rms_scale(gated) * gain


def swiglu(gate_up):
    half = gate_up.shape[1] // 2
    return jax.nn.silu(gate_up[:, :half]) * gate_up[:, half:]


def dot(left, right):
    return jnp.dot(left, right, preferred_element_type=jnp.float32)


def head_lanes():
    head = lax.broadcasted_iota(jnp.int32, (SSM_HEADS, INNER), 0)
    lane = lax.broadcasted_iota(jnp.int32, (SSM_HEADS, INNER), 1)
    return (lane // SSM_HD == head).astype(jnp.float32)


def spread_heads(values):
    return jnp.dot(values, head_lanes(), precision=lax.Precision.HIGHEST)


def sum_heads(values):
    return lax.dot_general(
        values, head_lanes(), (((1,), (1,)), ((), ())), precision=lax.Precision.HIGHEST
    )


def on_device(
    tokens,
    seq_lengths,
    owner_order,
    gain_attn,
    w_input,
    w_step,
    step_bias,
    decay_log,
    skip_scale,
    conv_weight,
    conv_bias,
    gain_ssm,
    w_output,
    gain_ffn,
    w_gate_up,
    w_down,
    cotangent,
):
    input_rows = tokens.shape[0]
    shard = lax.axis_index("shard")
    flow = Flow()

    slot_tokens = flow.add(rows_stream(tokens))
    slot_input = flow.add(weight_stream(w_input))
    small_args = (gain_attn, w_step, step_bias, decay_log, skip_scale, conv_weight, conv_bias, gain_ssm, gain_ffn)
    small_dims = (0, 0, 0, 0, 0, 1, 0, 0, 0)
    slot_small = flow.add(small_stream(jnp.concatenate([a.reshape(-1) for a in small_args])))
    source, position, limit, target = group_tables(seq_lengths[0], owner_order[0], input_rows, shard)
    cosine, sine = rope_tables(position)
    source, position, limit, target, cosine, sine = flow.step((source, position, limit, target, cosine, sine))
    slot_output = flow.add(weight_stream(w_output))
    source, position = flow.step((source, position))
    slot_gate_up = flow.add(weight_stream(w_gate_up))
    source, position = flow.until([slot_tokens, slot_input, slot_small], (source, position))

    gain_attn_all, w_step_all, step_bias_all, decay_all, skip_all, conv_w_all, conv_b_all, gain_ssm_all, gain_ffn_all = (
        unpack_small(slot_small["result"], [a.shape for a in small_args], small_dims)
    )
    f32 = lambda v: v.astype(jnp.float32)
    gain_attn_f, gain_ssm_f, gain_ffn_f = f32(gain_attn_all), f32(gain_ssm_all), f32(gain_ffn_all)
    conv_w_f, conv_b_f = f32(conv_w_all), f32(conv_b_all)
    skip_lanes = jnp.repeat(f32(skip_all), SSM_HD)[None]
    pieces, owners = slot_tokens["result"]
    own_low = pick_rows(pieces, owners * input_rows, source)
    own = f32(own_low)
    w_input_all = slot_input["result"]

    normed = rms_norm(own, gain_attn_f).astype(jnp.bfloat16)
    projected = dot(normed, w_input_all)
    step_raw = dot(normed, w_step_all)
    projected, step_raw = flow.step((projected, step_raw))
    slot_down = flow.add(weight_stream(w_down))
    conv_in = projected[:, QUERY_KEY_VALUE + INNER :]
    gate_z = projected[:, QUERY_KEY_VALUE : QUERY_KEY_VALUE + INNER]
    conv_out = jax.nn.silu(conv_mixed(conv_in, conv_w_f, conv_b_f, position))
    inner_x = conv_out[:, :INNER]
    b_low = conv_out[:, INNER : INNER + STATE].astype(jnp.bfloat16)
    c_low = conv_out[:, INNER + STATE :].astype(jnp.bfloat16)
    step_pre = step_raw + f32(step_bias_all)
    step = jax.nn.softplus(step_pre)
    rate = -jnp.exp(f32(decay_all))
    cum = jnp.cumsum(step * rate, axis=0)
    step_lanes = spread_heads(step)
    x_step = (inner_x * step_lanes).astype(jnp.bfloat16)
    x_step, cum, b_low, c_low, inner_x, step_lanes = flow.step((x_step, cum, b_low, c_low, inner_x, step_lanes))
    ssd_out = ssd_forward(limit, c_low, b_low, x_step, cum)
    ssd_out, projected = flow.step((ssd_out, projected))
    attn_out, logs = attention_forward(limit, projected, cosine, sine)
    ssm_y = ssd_out + skip_lanes * inner_x
    gate_z = projected[:, QUERY_KEY_VALUE : QUERY_KEY_VALUE + INNER]
    ssm_out = gated_norm(ssm_y, gate_z, gain_ssm_f).astype(jnp.bfloat16)
    joined = jnp.concatenate([attn_out, ssm_out], 1)
    joined = flow.until([slot_output], joined)
    w_output_all = slot_output["result"]
    slot_cot = flow.add(rows_stream(cotangent))
    middle = own + dot(joined, w_output_all)
    normed_ffn = rms_norm(middle, gain_ffn_f).astype(jnp.bfloat16)
    normed_ffn, middle = flow.until([slot_gate_up], flow.step((normed_ffn, middle)))
    w_gate_up_all = slot_gate_up["result"]
    gate_up = dot(normed_ffn, w_gate_up_all)
    hidden = swiglu(gate_up).astype(jnp.bfloat16)
    gate_up, hidden = flow.until([slot_cot, slot_down], (gate_up, hidden))
    w_down_all = slot_down["result"]
    pieces, owners = slot_cot["result"]
    cot = pick_rows(pieces, owners * input_rows, source)

    def weight_grad(left, right):
        return lax.dot_general(
            left, right, (((0,), (0,)), ((), ())), preferred_element_type=jnp.float32
        ).astype(jnp.bfloat16)

    def back(left, weight):
        return lax.dot_general(left, weight, (((1,), (1,)), ((), ())), preferred_element_type=jnp.float32)

    grad_slots = {}
    grad_slots["down"] = [flow.add(reduce_stream(weight_grad(hidden, cot), True))]
    grad_hidden = back(cot, w_down_all)
    grad_gate_up = jax.vjp(swiglu, gate_up)[1](grad_hidden)[0].astype(jnp.bfloat16)
    grad_gate_up = flow.step(grad_gate_up)
    half = grad_gate_up.shape[1] // 2
    grad_slots["gate_up"] = [flow.add(reduce_stream(weight_grad(normed_ffn, grad_gate_up[:, :half]), True))]
    grad_normed_ffn = back(grad_gate_up, w_gate_up_all)
    grad_middle_norm, grad_gain_ffn = jax.vjp(rms_norm, middle, gain_ffn_f)[1](grad_normed_ffn)
    grad_middle = f32(cot) + grad_middle_norm
    grad_gate_up, grad_middle = flow.step((grad_gate_up, grad_middle))
    grad_slots["gate_up"].append(flow.add(reduce_stream(weight_grad(normed_ffn, grad_gate_up[:, half:]), False)))
    middle_low = grad_middle.astype(jnp.bfloat16)
    grad_joined = back(middle_low, w_output_all)
    grad_attn = grad_joined[:, : QUERY_HEADS * HEAD_SIZE].astype(jnp.bfloat16)
    grad_ssm_out = grad_joined[:, QUERY_HEADS * HEAD_SIZE :]
    grad_ssm_y, grad_z, grad_gain_ssm = jax.vjp(gated_norm, ssm_y, gate_z, gain_ssm_f)[1](grad_ssm_out)
    grad_z_low = grad_z.astype(jnp.bfloat16)
    grad_y_low = grad_ssm_y.astype(jnp.bfloat16)
    grad_ssm_y, grad_z_low, grad_attn, middle_low, grad_y_low = flow.step(
        (grad_ssm_y, grad_z_low, grad_attn, middle_low, grad_y_low)
    )
    grad_slots["output"] = [flow.add(reduce_stream(weight_grad(joined, middle_low), True))]
    grad_q, grad_kv = attention_backward(limit, projected, cosine, sine, grad_attn, logs)
    grad_q, grad_kv, grad_y_low = flow.step((grad_q, grad_kv, grad_y_low))
    grad_slots["input"] = [flow.add(reduce_stream(weight_grad(normed, grad_z_low), False))]
    back_x, grad_c, grad_b = ssd_backward(limit, c_low, b_low, x_step, grad_y_low, cum)
    back_x, grad_c, grad_b = flow.step((back_x, grad_c, grad_b))
    qkv = jnp.concatenate([grad_q, grad_kv], 1)
    grad_slots["input"].insert(0, flow.add(reduce_stream(weight_grad(normed, qkv), True)))
    grad_skip = jnp.sum(sum_heads(grad_ssm_y * inner_x), 0)
    grad_cum = sum_heads(f32(grad_y_low) * ssd_out - f32(x_step) * back_x)
    grad_step = sum_heads(back_x * inner_x)
    grad_x = back_x * step_lanes + skip_lanes * grad_ssm_y
    grad_inc = lax.cumsum(grad_cum, axis=0, reverse=True)
    grad_step = grad_step + grad_inc * rate
    grad_decay = jnp.sum(grad_inc * step, 0) * rate
    grad_step_pre = grad_step * jax.nn.sigmoid(step_pre)
    grad_step_bias = jnp.sum(grad_step_pre, 0)
    step_low = grad_step_pre.astype(jnp.bfloat16)
    grad_w_step = lax.dot_general(normed, step_low, (((0,), (0,)), ((), ())), preferred_element_type=jnp.float32)
    grad_conv = jnp.concatenate([grad_x, grad_b, grad_c], 1)
    mixed_back = jax.vjp(
        lambda u, w, b: jax.nn.silu(conv_mixed(u, w, b, position)), conv_in, conv_w_f, conv_b_f
    )[1]
    grad_u, grad_conv_w, grad_conv_b = mixed_back(grad_conv)
    grad_u_low = grad_u.astype(jnp.bfloat16)
    grad_u_low, step_low = flow.step((grad_u_low, step_low))
    grad_slots["input"].append(flow.add(reduce_stream(weight_grad(normed, grad_u_low), True)))
    grad_projected = jnp.concatenate([qkv, grad_z_low, grad_u_low], 1)
    grad_normed = back(grad_projected, w_input_all) + back(step_low, w_step_all)
    grad_tokens_norm, grad_gain_attn = jax.vjp(rms_norm, own, gain_attn_f)[1](grad_normed)
    grad_low = (grad_middle + grad_tokens_norm).astype(jnp.bfloat16)
    small_grads = (
        grad_gain_attn,
        grad_w_step,
        grad_step_bias,
        grad_decay,
        grad_skip,
        grad_conv_w,
        grad_conv_b,
        grad_gain_ssm,
        grad_gain_ffn,
    )
    flat = jnp.concatenate([g.reshape(-1) for g in small_grads])
    flat = jnp.pad(flat, (0, -flat.shape[0] % 1024)).reshape(-1, SIDE)
    grad_low, flat = flow.step((grad_low, flat))
    slot_grad = flow.add(rows_stream(grad_low))
    slot_flat = flow.add(butterfly_stream(flat))
    block_low = (middle + dot(hidden, w_down_all)).astype(jnp.bfloat16)
    slot_block = flow.add(rows_stream(block_low))
    target = flow.until(list(flow.live), target)

    pieces, owners = slot_block["result"]
    block_out = pick_rows(pieces, owners * input_rows, target)
    pieces, owners = slot_grad["result"]
    grad_tokens = pick_rows(pieces, owners * input_rows, target)
    outs = [None] * 13
    summed = slot_flat["result"].reshape(-1)
    offset = 0
    for i, grad in zip((0, 2, 3, 4, 5, 6, 7, 8, 10), small_grads):
        block = summed[offset : offset + grad.size].reshape(grad.shape)
        offset += grad.size
        outs[i] = own_block(block, 1 if i == 6 else 0)
    for i, name in ((1, "input"), (9, "output"), (11, "gate_up"), (12, "down")):
        parts = [widen_rows(*slot["result"]) for slot in grad_slots[name]]
        outs[i] = parts[0] if len(parts) == 1 else jnp.concatenate(parts, 1)
    return (block_out, grad_tokens, *outs)


def solution(mesh):
    placed = (
        P(("rep", "shard"), None),
        P("rep", None),
        P("rep", None),
        P("shard"),
        P("shard", None),
        P("shard", None),
        P("shard"),
        P("shard"),
        P("shard"),
        P(None, "shard"),
        P("shard"),
        P("shard"),
        P("shard", None),
        P("shard"),
        P("shard", None),
        P("shard", None),
        P(("rep", "shard"), None),
    )
    return jax.shard_map(
        on_device,
        mesh=mesh,
        in_specs=placed,
        out_specs=(
            P(("rep", "shard"), None),
            P(("rep", "shard"), None),
            P("shard"),
            P("shard", None),
            P("shard", None),
            P("shard"),
            P("shard"),
            P("shard"),
            P(None, "shard"),
            P("shard"),
            P("shard"),
            P("shard", None),
            P("shard"),
            P("shard", None),
            P("shard", None),
        ),
        check_vma=False,
    )
```

time: 2330 us -> 745 us (0.32)
  blocking collectives: 834 us -> 0 us
  local copies, waits for them, and re-layouts: 741 us -> 98.7 us
  waiting for transfers between devices: 319 us -> 171 us
  Pallas kernels: 0 us -> 117 us
  starting transfers between devices: 0.52 us -> 112 us
  matrix products: 188 us -> 89.3 us
  other arithmetic: 221 us -> 142 us
    unnamed x2 -> x0, blocking collectives: 807 us -> none
    unnamed x312 -> x390, local copies, waits for them, and re-layouts: 334 us -> 10.1 us
    all_gather x9 -> x0, waiting for transfers between devices: 315 us -> none  [the longest x1 173 us: on_device(): lax.all_gather(piece.astype(jnp.bfloat16), 'rep', axis=0, tiled=True)]
    reshape x31 -> x14, local copies, waits for them, and re-layouts: 231 us -> 6.42 us  [the longest x2 2.11 us: on_device(): flat = jnp.concatenate([g.reshape(-1) for g in small_grads])]
    ppermute x0 -> x109, waiting for transfers between devices: none -> 171 us  [swap(): return lax.ppermute(values, axis, [(i, i ^ mask) for i in range(count)])]
    reshape x1 -> x0, other arithmetic: 136 us -> none  [on_device(): total = lax.all_gather(piece.astype(jnp.bfloat16), 'rep', axis=0, tiled=T...]
    pallas_call x0 -> x19, Pallas kernels: none -> 117 us  [the longest x4 24.5 us: lay_rows(): pl.pallas_call(lay_rows_kernel, out_shape=jax.ShapeDtypeStruct((rows, pie...]
    ppermute x0 -> x109, starting transfers between devices: none -> 112 us  [swap(): return lax.ppermute(values, axis, [(i, i ^ mask) for i in range(count)])]
  transfers between devices with their start and end apart: 9 -> 109, of which waited for: 6 -> 28; matrix products, arithmetic and copies ran while one was open for 32% -> 40% of each run, Pallas kernels for 0% -> 13%
where the time goes in v2:
time: 745 us; the launch traced here: 733 us
  waiting for transfers between devices  171 us (23%)
  other arithmetic  142 us (19%)
  Pallas kernels  117 us (16%)
  starting transfers between devices  112 us (15%)
  local copies, waits for them, and re-layouts  98.7 us (13%)
  matrix products  89.3 us (12%)
    ppermute x109, waiting for transfers between devices, swap(): return lax.ppermute(values, axis, [(i, i ^ mask) for i in range(count)])  171 us
    ppermute x109, starting transfers between devices, swap(): return lax.ppermute(values, axis, [(i, i ^ mask) for i in range(count)])  112 us
    convert_element_type x28, other arithmetic, add(): return total.astype(jnp.bfloat16)  42.1 us
    dot_general x5, matrix products, back(): lax.dot_general(left, weight, (((1,), (1,)), ((), ())), preferred_element...  29 us
    dot_general x5, matrix products, dot(): return jnp.dot(left, right, preferred_element_type=jnp.float32)  26.2 us
    pallas_call x4, Pallas kernels, lay_rows(): pl.pallas_call(lay_rows_kernel, out_shape=jax.ShapeDtypeStruct((rows, pie...  24.5 us
    pallas_call x4, Pallas kernels, pick_rows(): pl.pallas_call(pick_kernel, out_shape=jax.ShapeDtypeStruct((wanted.shape[...  22.8 us
    dot_general x7, matrix products, weight_grad(): lax.dot_general(left, right, (((0,), (0,)), ((), ())), preferred_element_...  19.5 us
  transfers between devices with their start and end apart: 109, of which 28 were waited for; matrix products, arithmetic and copies ran while one was open for 40% of the time, Pallas kernels for 13%

profile of v2, /device:TPU:0, one launch (start us, length us, event | category | flops | bytes accessed | tf_op | source)
XLA Modules:
  0.0 732.9 jit_solution(16317725863078100998)
XLA Ops:
  32.2 18.2 %collective-permute-done.2.refs_2_ = bf16[128,4096]{1,0:T(8,128)(2,1)} collective-permute-done((bf16[128,4096]{1,0:T(8,128)(2,1)}, bf16[128,4096]{1,0:T(8,128)(2,1)}, u32[]{:S(2)}, u32[]{:S(2)}) %collective-permute-start.2) | collective-permute-done | bytes 1048608 | tf_op jit(solution)/shard_map/ppermute | solution.py:401
  53.2 7.7 %collective-permute-done.9.refs_2_ = bf16[256,1024]{1,0:T(8,128)(2,1)} collective-permute-done((bf16[256,1024]{1,0:T(8,128)(2,1)}, bf16[256,1024]{1,0:T(8,128)(2,1)}, u32[]{:S(2)}, u32[]{:S(2)}) %collective-permute-start.9) | collective-permute-done | bytes 524320 | tf_op jit(solution)/shard_map/ppermute | solution.py:401
  66.6 7.7 %collective-permute-done.6.refs_4_ = bf16[128,4096]{1,0:T(8,128)(2,1)} collective-permute-done((bf16[128,4096]{1,0:T(8,128)(2,1)}, bf16[128,4096]{1,0:T(8,128)(2,1)}, u32[]{:S(2)}, u32[]{:S(2)}) %collective-permute-start.6) | collective-permute-done | bytes 1048608 | tf_op jit(solution)/shard_map/ppermute | solution.py:401
  102.3 7.4 %lay_rows.4 = bf16[1024,4096]{1,0:T(8,128)(2,1)} custom-call(s32[6]{0:T(128)} %and_select_fusion.3.place_ref, bf16[256,4096]{1,0:T(8,128)(2,1)} %refs_0_.7, bf16[256,4096]{1,0:T(8,128)(2,1)} %collective-permute-done.3.refs_1_, bf16[128,4096]{1,0:T(8,128)(2,1)} %collective-permute-done.2.refs_2_, bf16[128,4096]{1,0:T(8,128)(2,1)} %collective-permute-done.7.refs_3_, ...), custom_call_target="tpu_custom_call" | custom-call | tf_op jit(solution)/shard_map/lay_rows/pallas_call | solution.py:369
  109.8 7.1 fusion.148.q_ref.k_ref.v_ref
  129.9 10.1 %fusion.155 = (bf16[512,1792]{1,0:T(8,128)(2,1)}, f32[512,1792]{1,0:T(8,128)S(1)}, f32[512,1792]{1,0:T(8,128)}) fusion(f32[1792]{0:T(1024)S(1)} %copy-done.131, f32[512]{0:T(512)S(1)} %copy-done.152, f32[509,1792]{1,0:T(8,128)} %slice.241, f32[1792]{0:T(1024)S(1)} %copy-done.133, f32[512]{0:T(512)S(1)} %copy-done.154, f32[510,1792]{1,0:T(8,128)} %slice.239, ...), kind=kLoop, calls=%fused_computation.391 | loop fusion | flops 14680064 | bytes 23854080 | tf_op jit(solution)/shard_map/convert.31
  155.1 7.4 %lay_rows.6 = bf16[1024,4096]{1,0:T(8,128)(2,1)} custom-call(s32[6]{0:T(128)} %and_select_fusion.3.place_ref, bf16[256,4096]{1,0:T(8,128)(2,1)} %refs_0_.9, bf16[256,4096]{1,0:T(8,128)(2,1)} %collective-permute-done.15.refs_1_, bf16[128,4096]{1,0:T(8,128)(2,1)} %copy-done.68, bf16[128,4096]{1,0:T(8,128)(2,1)} %copy-done.69, ...), custom_call_target="tpu_custom_call" | custom-call | tf_op jit(solution)/shard_map/lay_rows/pallas_call | solution.py:369
  162.5 9.1 %ssd_forward.1 = f32[512,1536]{1,0:T(8,128)} custom-call(s32[1]{0:T(128)} %bitcast.7.limit_ref, bf16[512,128]{1,0:T(8,128)(2,1)} %get-tuple-element.202.c_ref, bf16[512,128]{1,0:T(8,128)(2,1)} %get-tuple-element.203.b_ref, bf16[512,1536]{1,0:T(8,128)(2,1)} %get-tuple-element.204.x_ref, f32[6,512,4]{2,1,0:T(8,128)} %bitcast.285, ...), custom_call_target="tpu_custom_call" | custom-call | tf_op jit(solution)/shard_map/ssd_forward/pallas_call | solution.py:76
  177.5 11.9 %attention_forward.1 = (bf16[512,512]{1,0:T(8,128)(2,1)}, f32[2,512,4]{2,1,0:T(8,128)}) custom-call(s32[1]{0:T(128)} %bitcast.7.limit_ref, f32[512,4096]{1,0:T(8,128)} %copy-done, f32[512,4096]{1,0:T(8,128)} %copy-done, f32[512,4096]{1,0:T(8,128)} %copy-done, f32[512,128]{1,0:T(8,128)} %get-tuple-element.208.cos_ref, f32[512,128]{1,0:T(8,128)} %get-tuple-element.209.sin_ref), custom_call_target="tpu_custom_call" | custom-call | tf_op jit(solution)/shard_map/attention_forward/pallas_call | solution.py:240
  197.6 7.1 fusion.168
  229.6 7.4 %multiply_multiply_fusion = (f32[512,2048]{1,0:T(8,128)S(1)}, f32[512,2048]{1,0:T(8,128)}) fusion(f32[512,4096]{1,0:T(8,128)} %fusion.168, bf16[512,1024]{1,0:T(8,128)(2,1)S(1)} %copy-done.45, bf16[2048,1024]{1,0:T(8,128)(2,1)S(1)} %copy-done.38), kind=kOutput, calls=%fused_computation.27 | convolution fusion | flops 2160066560 | bytes 22020096 | tf_op jit(solution)/shard_map/dot_general | solution.py:764
  256.6 8.9 %multiply_reduce_fusion.7 = (f32[1024]{0:T(1024)}, f32[512]{0:T(512)S(1)}, f32[512,1024]{1,0:T(8,128)}) fusion(f32[512,1024]{1,0:T(8,128)S(1)} %copy-done.18, f32[512]{0:T(512)S(1)} %fusion.124, f32[1024]{0:T(1024)S(1)} %bitcast.309, bf16[512,4096]{1,0:T(8,128)(2,1)} %add_convert_fusion, bf16[1024,4096]{1,0:T(8,128)(2,1)S(1)} %bitcast.290), kind=kOutput, calls=%fused_computation.110 | convolution fusion | flops 4298111488 | bytes 16789504 | tf_op jit(solution)/shard_map/dot_general | solution.py:764
  267.9 9.1 %collective-permute-done.29 = bf16[1,4,2,64,1024]{4,3,1,2,0:T(8,128)(2,1)} collective-permute-done((bf16[1,4,2,64,1024]{4,3,1,2,0:T(8,128)(2,1)}, bf16[1,4,2,64,1024]{4,3,1,2,0:T(8,128)(2,1)}, u32[]{:S(2)}, u32[]{:S(2)}) %collective-permute-start.29) | collective-permute-done | bytes 1048608 | tf_op jit(solution)/shard_map/ppermute | solution.py:401
  299.3 17.1 %collective-permute-done.32 = bf16[1,4,2,32,2048]{4,3,1,2,0:T(8,128)(2,1)} collective-permute-done((bf16[1,4,2,32,2048]{4,3,1,2,0:T(8,128)(2,1)S(1)}, bf16[1,4,2,32,2048]{4,3,1,2,0:T(8,128)(2,1)}, u32[]{:S(2)}, u32[]{:S(2)}) %collective-permute-start.32) | collective-permute-done | bytes 1048608 | tf_op jit(solution)/shard_map/ppermute | solution.py:401
  342.1 16.7 %attention_backward.1 = (bf16[512,512]{1,0:T(8,128)(2,1)}, bf16[512,256]{1,0:T(8,128)(2,1)}) custom-call(s32[1]{0:T(128)} %bitcast.7.limit_ref, f32[512,4096]{1,0:T(8,128)} %copy-done, f32[512,4096]{1,0:T(8,128)} %copy-done, f32[512,4096]{1,0:T(8,128)} %copy-done, f32[512,128]{1,0:T(8,128)} %get-tuple-element.208.cos_ref, ...), custom_call_target="tpu_custom_call" | custom-call | tf_op jit(solution)/shard_map/attention_backward/pallas_call | solution.py:309
  358.9 9.0 %collective-permute-done.38 = bf16[2,4,32,2048]{3,2,1,0:T(8,128)(2,1)} collective-permute-done((bf16[2,4,32,2048]{3,2,1,0:T(8,128)(2,1)}, bf16[2,4,32,2048]{3,2,1,0:T(8,128)(2,1)}, u32[]{:S(2)}, u32[]{:S(2)}) %collective-permute-start.38) | collective-permute-done | bytes 1048608 | tf_op jit(solution)/shard_map/ppermute | solution.py:401
  384.1 13.3 %ssd_backward.1 = (f32[512,1536]{1,0:T(8,128)}, f32[512,128]{1,0:T(8,128)}, f32[512,128]{1,0:T(8,128)}) custom-call(s32[1]{0:T(128)} %bitcast.7.limit_ref, bf16[512,128]{1,0:T(8,128)(2,1)} %get-tuple-element.202.c_ref, bf16[512,128]{1,0:T(8,128)(2,1)} %get-tuple-element.203.b_ref, bf16[512,1536]{1,0:T(8,128)(2,1)} %get-tuple-element.204.x_ref, ...), custom_call_target="tpu_custom_call" | custom-call | tf_op jit(solution)/shard_map/ssd_backward/pallas_call | solution.py:150
  430.0 7.6 %fusion.150 = (f32[1792]{0:T(1024)}, f32[1792]{0:T(1024)}, f32[1792]{0:T(1024)}, f32[1792]{0:T(1024)}, f32[1792]{0:T(1024)}, /*index=5*/f32[512,1792]{1,0:T(8,128)S(1)}) fusion(f32[512,4096]{1,0:T(8,128)} %copy-done, f32[512]{0:T(512)S(1)} %copy-done.151, f32[511,1792]{1,0:T(8,128)S(1)} %copy-done.8, f32[512]{0:T(512)S(1)} %copy-done.155, ...), kind=kLoop, calls=%fused_computation.389 | loop fusion | flops 21093632 | bytes 25689088 | tf_op jit(solution)/shard_map/transpose(jvp())/reduce_sum | solution.py:633
  496.1 8.4 %collective-permute-done.56 = bf16[4,64,1024]{2,1,0:T(8,128)(2,1)} collective-permute-done((bf16[4,64,1024]{2,1,0:T(8,128)(2,1)}, bf16[4,64,1024]{2,1,0:T(8,128)(2,1)}, u32[]{:S(2)}, u32[]{:S(2)}) %collective-permute-start.56) | collective-permute-done | bytes 524320 | tf_op jit(solution)/shard_map/ppermute | solution.py:401
  515.5 8.7 %fusion.40 = (f32[1024]{0:T(1024)S(1)}, f32[512]{0:T(512)S(1)}, f32[512,1024]{1,0:T(8,128)S(1)}) fusion(bf16[512,1024]{1,0:T(8,128)(2,1)S(1)} %copy-done.26, f32[512]{0:T(512)S(1)} %copy-done.170, f32[1024]{0:T(1024)S(1)} %bitcast.317, f32[512,1024]{1,0:T(8,128)S(1)} %fusion.170, bf16[1024,4096]{1,0:T(8,128)(2,1)} %lay_rows.4, ...), kind=kOutput, calls=%fused_computation.92 | convolution fusion | flops 4315937280 | bytes 17838080 | tf_op jit(solution)/shard_map/dot_general | solution.py:764
  569.6 10.8 %collective-permute-done.81.refs_1_ = bf16[512,1024]{1,0:T(8,128)(2,1)S(1)} collective-permute-done((bf16[512,1024]{1,0:T(8,128)(2,1)}, bf16[512,1024]{1,0:T(8,128)(2,1)S(1)}, u32[]{:S(2)}, u32[]{:S(2)}) %collective-permute-start.81) | collective-permute-done | bytes 1048608 | tf_op jit(solution)/shard_map/ppermute | solution.py:401
  600.3 9.7 %collective-permute-done.76 = bf16[4,32,768]{2,1,0:T(8,128)(2,1)} collective-permute-done((bf16[4,32,768]{2,1,0:T(8,128)(2,1)}, bf16[4,32,768]{2,1,0:T(8,128)(2,1)}, u32[]{:S(2)}, u32[]{:S(2)}) %collective-permute-start.76) | collective-permute-done | bytes 196640 | tf_op jit(solution)/shard_map/ppermute | solution.py:401
  610.1 15.7 %collective-permute-done.77 = bf16[1,4,2,32,1792]{4,3,1,2,0:T(8,128)(2,1)} collective-permute-done((bf16[1,4,2,32,1792]{4,3,1,2,0:T(8,128)(2,1)}, bf16[1,4,2,32,1792]{4,3,1,2,0:T(8,128)(2,1)}, u32[]{:S(2)}, u32[]{:S(2)}) %collective-permute-start.77) | collective-permute-done | bytes 917536 | tf_op jit(solution)/shard_map/ppermute | solution.py:401
  651.9 11.8 %collective-permute-done.90 = bf16[4,32,1792]{2,1,0:T(8,128)(2,1)} collective-permute-done((bf16[4,32,1792]{2,1,0:T(8,128)(2,1)}, bf16[4,32,1792]{2,1,0:T(8,128)(2,1)}, u32[]{:S(2)}, u32[]{:S(2)}) %collective-permute-start.90) | collective-permute-done | bytes 458784 | tf_op jit(solution)/shard_map/ppermute | solution.py:401
  (850 shorter events, 481.5 us)
Async XLA Ops:
  3.7 46.8 %collective-permute-start.3 = (bf16[256,4096]{1,0:T(8,128)(2,1)}, bf16[256,4096]{1,0:T(8,128)(2,1)}, u32[]{:S(2)}, u32[]{:S(2)}) collective-permute-start(bf16[256,4096]{1,0:T(8,128)(2,1)} %refs_0_.7), channel_id=1, source_target_pairs={{0,1},{1,0},{2,3},{3,2},{4,5},{5,4},{6,7},{7,6},{8,9},{9,8},{10,11... | collective-permute-start | bytes 6291464 | tf_op jit(solution)/shard_map/ppermute | solution.py:401
  6.6 43.9 %collective-permute-start.2 = (bf16[128,4096]{1,0:T(8,128)(2,1)}, bf16[128,4096]{1,0:T(8,128)(2,1)}, u32[]{:S(2)}, u32[]{:S(2)}) collective-permute-start(bf16[128,4096]{1,0:T(8,128)(2,1)} %constant_dynamic-slice_fusion.26), channel_id=1, source_target_pairs={{0,2},{1,3},{2,0},{3,1},{4,6},{5,7},{6,4},{7,5},{8,10},{9,11},{10,... | collective-permute-start | bytes 3145736 | tf_op jit(solution)/shard_map/ppermute | solution.py:401
  29.8 35.3 %collective-permute-start.10 = (bf16[512,1024]{1,0:T(8,128)(2,1)S(1)}, bf16[512,1024]{1,0:T(8,128)(2,1)}, u32[]{:S(2)}, u32[]{:S(2)}) collective-permute-start(bf16[512,1024]{1,0:T(8,128)(2,1)S(1)} %copy-done.53), channel_id=1, source_target_pairs={{0,1},{1,0},{2,3},{3,2},{4,5},{5,4},{6,7},{7,6},{8,9},{9,8},{10,11... | collective-permute-start | bytes 3145736 | tf_op jit(solution)/shard_map/ppermute | solution.py:401
  90.8 52.9 %collective-permute-start.21 = (bf16[512,1024]{1,0:T(8,128)(2,1)}, bf16[512,1024]{1,0:T(8,128)(2,1)}, u32[]{:S(2)}, u32[]{:S(2)}) collective-permute-start(bf16[512,1024]{1,0:T(8,128)(2,1)} %refs_0_.11), channel_id=1, source_target_pairs={{0,1},{1,0},{2,3},{3,2},{4,5},{5,4},{6,7},{7,6},{8,9},{9,8},{10,11... | collective-permute-start | bytes 3145736 | tf_op jit(solution)/shard_map/ppermute | solution.py:401
  90.8 106.5 %collective-permute-start.25 = (bf16[512,1024]{1,0:T(8,128)(2,1)}, bf16[512,1024]{1,0:T(8,128)(2,1)}, u32[]{:S(2)}, u32[]{:S(2)}) collective-permute-start(bf16[512,1024]{1,0:T(8,128)(2,1)} %refs_0_.10), channel_id=1, source_target_pairs={{0,2},{1,3},{2,0},{3,1},{4,6},{5,7},{6,4},{7,5},{8,10},{9,11},{10,... | collective-permute-start | bytes 3145736 | tf_op jit(solution)/shard_map/ppermute | solution.py:401
  118.6 78.7 %collective-permute-start.26 = (bf16[512,1024]{1,0:T(8,128)(2,1)}, bf16[512,1024]{1,0:T(8,128)(2,1)}, u32[]{:S(2)}, u32[]{:S(2)}) collective-permute-start(bf16[512,1024]{1,0:T(8,128)(2,1)} %refs_0_.10), channel_id=1, source_target_pairs={{0,1},{1,0},{2,3},{3,2},{4,5},{5,4},{6,7},{7,6},{8,9},{9,8},{10,11... | collective-permute-start | bytes 3145736 | tf_op jit(solution)/shard_map/ppermute | solution.py:401
  319.9 38.8 %collective-permute-start.35 = (bf16[64,1024]{1,0:T(8,128)(2,1)}, bf16[64,1024]{1,0:T(8,128)(2,1)S(1)}, u32[]{:S(2)}, u32[]{:S(2)}) collective-permute-start(bf16[64,1024]{1,0:T(8,128)(2,1)} %get-tuple-element.447), channel_id=1, source_target_pairs={{0,16},{4,20},{8,24},{12,28},{16,0},{20,4},{24,8},{28,12},{1,17},{... | collective-permute-start | bytes 393224 | tf_op jit(solution)/shard_map/ppermute | solution.py:401
  329.9 38.0 %collective-permute-start.39 = (bf16[2,4,2,64,1024]{4,3,1,2,0:T(8,128)(2,1)}, bf16[2,4,2,64,1024]{4,3,1,2,0:T(8,128)(2,1)}, u32[]{:S(2)}, u32[]{:S(2)}) collective-permute-start(bf16[2,4,2,64,1024]{4,3,1,2,0:T(8,128)(2,1)} %bitcast.277), channel_id=1, source_target_pairs={{0,1},{1,0},{2,3},{3,2},{4,5},{5,4},{6,7},{7,6},{8,9},{9,8},{10,11... | collective-permute-start | bytes 6291464 | tf_op jit(solution)/shard_map/ppermute | solution.py:401
  333.4 34.5 %collective-permute-start.38 = (bf16[2,4,32,2048]{3,2,1,0:T(8,128)(2,1)}, bf16[2,4,32,2048]{3,2,1,0:T(8,128)(2,1)}, u32[]{:S(2)}, u32[]{:S(2)}) collective-permute-start(bf16[2,4,32,2048]{3,2,1,0:T(8,128)(2,1)} %dynamic-slice_bitcast_fusion), channel_id=1, source_target_pairs={{0,4},{4,0},{8,12},{12,8},{16,20},{20,16},{24,28},{28,24},{1,5},{5... | collective-permute-start | bytes 3145736 | tf_op jit(solution)/shard_map/ppermute | solution.py:401
  358.8 38.7 %collective-permute-start.48 = (bf16[2,4,2,32,1536]{4,3,1,0,2:T(8,128)(2,1)}, bf16[2,4,2,32,1536]{4,3,1,0,2:T(8,128)(2,1)}, u32[]{:S(2)}, u32[]{:S(2)}) collective-permute-start(bf16[2,4,2,32,1536]{4,3,1,0,2:T(8,128)(2,1)} %bitcast.298), channel_id=1, source_target_pairs={{0,1},{1,0},{2,3},{3,2},{4,5},{5,4},{6,7},{7,6},{8,9},{9,8},{10,11... | collective-permute-start | bytes 4718600 | tf_op jit(solution)/shard_map/ppermute | solution.py:401
  368.9 33.2 %collective-permute-start.40 = (bf16[64,1024]{1,0:T(8,128)(2,1)S(1)}, bf16[64,1024]{1,0:T(8,128)(2,1)S(1)}, u32[]{:S(2)}, u32[]{:S(2)}) collective-permute-start(bf16[64,1024]{1,0:T(8,128)(2,1)S(1)} %fusion.88.refs_0_), channel_id=1, source_target_pairs={{0,8},{4,12},{8,0},{12,4},{16,24},{20,28},{24,16},{28,20},{1,9},{5... | collective-permute-start | bytes 393224 | tf_op jit(solution)/shard_map/ppermute | solution.py:401
  369.4 32.8 %collective-permute-start.41 = (bf16[64,1024]{1,0:T(8,128)(2,1)S(1)}, bf16[64,1024]{1,0:T(8,128)(2,1)S(1)}, u32[]{:S(2)}, u32[]{:S(2)}) collective-permute-start(bf16[64,1024]{1,0:T(8,128)(2,1)S(1)} %fusion.88.refs_0_), channel_id=1, source_target_pairs={{0,16},{4,20},{8,24},{12,28},{16,0},{20,4},{24,8},{28,12},{1,17},{... | collective-permute-start | bytes 393224 | tf_op jit(solution)/shard_map/ppermute | solution.py:401
  372.6 41.9 %collective-permute-start.46 = (bf16[1,4,32,2048]{3,2,1,0:T(8,128)(2,1)}, bf16[1,4,32,2048]{3,2,1,0:T(8,128)(2,1)}, u32[]{:S(2)}, u32[]{:S(2)}) collective-permute-start(bf16[1,4,32,2048]{3,2,1,0:T(8,128)(2,1)} %constant_dynamic-slice_fusion.13), channel_id=1, source_target_pairs={{0,2},{1,3},{2,0},{3,1},{4,6},{5,7},{6,4},{7,5},{8,10},{9,11},{10,... | collective-permute-start | bytes 1572872 | tf_op jit(solution)/shard_map/ppermute | solution.py:401
  378.6 36.0 %collective-permute-start.47 = (bf16[1,4,2,64,1024]{4,3,1,2,0:T(8,128)(2,1)}, bf16[1,4,2,64,1024]{4,3,1,2,0:T(8,128)(2,1)}, u32[]{:S(2)}, u32[]{:S(2)}) collective-permute-start(bf16[1,4,2,64,1024]{4,3,1,2,0:T(8,128)(2,1)} %constant_dynamic-slice_fusion.11), channel_id=1, source_target_pairs={{0,2},{1,3},{2,0},{3,1},{4,6},{5,7},{6,4},{7,5},{8,10},{9,11},{10,... | collective-permute-start | bytes 3145736 | tf_op jit(solution)/shard_map/ppermute | solution.py:401
  412.8 56.6 %collective-permute-start.58 = (bf16[2,4,2,32,768]{4,3,1,2,0:T(8,128)(2,1)}, bf16[2,4,2,32,768]{4,3,1,2,0:T(8,128)(2,1)}, u32[]{:S(2)}, u32[]{:S(2)}) collective-permute-start(bf16[2,4,2,32,768]{4,3,1,2,0:T(8,128)(2,1)} %bitcast.283), channel_id=1, source_target_pairs={{0,1},{1,0},{2,3},{3,2},{4,5},{5,4},{6,7},{7,6},{8,9},{9,8},{10,11... | collective-permute-start | bytes 2359304 | tf_op jit(solution)/shard_map/ppermute | solution.py:401
  415.6 55.3 %collective-permute-start.50 = (bf16[32,2048]{1,0:T(8,128)(2,1)S(1)}, bf16[32,2048]{1,0:T(8,128)(2,1)}, u32[]{:S(2)}, u32[]{:S(2)}) collective-permute-start(bf16[32,2048]{1,0:T(8,128)(2,1)S(1)} %fusion.82.refs_0_), channel_id=1, source_target_pairs={{0,8},{4,12},{8,0},{12,4},{16,24},{20,28},{24,16},{28,20},{1,9},{5... | collective-permute-start | bytes 393224 | tf_op jit(solution)/shard_map/ppermute | solution.py:401
  418.2 53.2 %collective-permute-start.51 = (bf16[32,2048]{1,0:T(8,128)(2,1)S(1)}, bf16[32,2048]{1,0:T(8,128)(2,1)}, u32[]{:S(2)}, u32[]{:S(2)}) collective-permute-start(bf16[32,2048]{1,0:T(8,128)(2,1)S(1)} %fusion.82.refs_0_), channel_id=1, source_target_pairs={{0,16},{4,20},{8,24},{12,28},{16,0},{20,4},{24,8},{28,12},{1,17},{... | collective-permute-start | bytes 393224 | tf_op jit(solution)/shard_map/ppermute | solution.py:401
  419.9 58.5 %collective-permute-start.52 = (bf16[32,2048]{1,0:T(8,128)(2,1)S(1)}, bf16[32,2048]{1,0:T(8,128)(2,1)}, u32[]{:S(2)}, u32[]{:S(2)}) collective-permute-start(bf16[32,2048]{1,0:T(8,128)(2,1)S(1)} %fusion.82.refs_0_), channel_id=1, source_target_pairs={{0,24},{4,28},{8,16},{12,20},{16,8},{20,12},{24,0},{28,4},{1,25},{... | collective-permute-start | bytes 393224 | tf_op jit(solution)/shard_map/ppermute | solution.py:401
  464.0 40.5 %collective-permute-start.57 = (bf16[2,4,32,1536]{3,2,1,0:T(8,128)(2,1)}, bf16[2,4,32,1536]{3,2,1,0:T(8,128)(2,1)}, u32[]{:S(2)}, u32[]{:S(2)}) collective-permute-start(bf16[2,4,32,1536]{3,2,1,0:T(8,128)(2,1)} %dynamic-slice_bitcast_fusion.1), channel_id=1, source_target_pairs={{0,4},{4,0},{8,12},{12,8},{16,20},{20,16},{24,28},{28,24},{1,5},{5... | collective-permute-start | bytes 2359304 | tf_op jit(solution)/shard_map/ppermute | solution.py:401
  471.5 33.0 %collective-permute-start.56 = (bf16[4,64,1024]{2,1,0:T(8,128)(2,1)}, bf16[4,64,1024]{2,1,0:T(8,128)(2,1)}, u32[]{:S(2)}, u32[]{:S(2)}) collective-permute-start(bf16[4,64,1024]{2,1,0:T(8,128)(2,1)} %dynamic-slice_bitcast_fusion.2), channel_id=1, source_target_pairs={{0,4},{4,0},{8,12},{12,8},{16,20},{20,16},{24,28},{28,24},{1,5},{5... | collective-permute-start | bytes 1572872 | tf_op jit(solution)/shard_map/ppermute | solution.py:401
  582.4 43.4 %collective-permute-start.78 = (bf16[512,1024]{1,0:T(8,128)(2,1)S(1)}, bf16[512,1024]{1,0:T(8,128)(2,1)}, u32[]{:S(2)}, u32[]{:S(2)}) collective-permute-start(bf16[512,1024]{1,0:T(8,128)(2,1)S(1)} %fusion.43.refs_0_), channel_id=1, source_target_pairs={{0,2},{1,3},{2,0},{3,1},{4,6},{5,7},{6,4},{7,5},{8,10},{9,11},{10,... | collective-permute-start | bytes 3145736 | tf_op jit(solution)/shard_map/ppermute | solution.py:401
  583.2 42.5 %collective-permute-start.79 = (bf16[512,1024]{1,0:T(8,128)(2,1)S(1)}, bf16[512,1024]{1,0:T(8,128)(2,1)}, u32[]{:S(2)}, u32[]{:S(2)}) collective-permute-start(bf16[512,1024]{1,0:T(8,128)(2,1)S(1)} %fusion.43.refs_0_), channel_id=1, source_target_pairs={{0,1},{1,0},{2,3},{3,2},{4,5},{5,4},{6,7},{7,6},{8,9},{9,8},{10,11... | collective-permute-start | bytes 3145736 | tf_op jit(solution)/shard_map/ppermute | solution.py:401
  583.3 42.4 %collective-permute-start.77 = (bf16[1,4,2,32,1792]{4,3,1,2,0:T(8,128)(2,1)}, bf16[1,4,2,32,1792]{4,3,1,2,0:T(8,128)(2,1)}, u32[]{:S(2)}, u32[]{:S(2)}) collective-permute-start(bf16[1,4,2,32,1792]{4,3,1,2,0:T(8,128)(2,1)} %constant_dynamic-slice_fusion.2), channel_id=1, source_target_pairs={{0,2},{1,3},{2,0},{3,1},{4,6},{5,7},{6,4},{7,5},{8,10},{9,11},{10,... | collective-permute-start | bytes 2752520 | tf_op jit(solution)/shard_map/ppermute | solution.py:401
  631.4 32.3 %collective-permute-start.91 = (bf16[512,1024]{1,0:T(8,128)(2,1)}, bf16[512,1024]{1,0:T(8,128)(2,1)}, u32[]{:S(2)}, u32[]{:S(2)}) collective-permute-start(bf16[512,1024]{1,0:T(8,128)(2,1)} %collective-permute-done.78.refs_1_), channel_id=1, source_target_pairs={{0,1},{1,0},{2,3},{3,2},{4,5},{5,4},{6,7},{7,6},{8,9},{9,8},{10,11... | collective-permute-start | bytes 3145736 | tf_op jit(solution)/shard_map/ppermute | solution.py:401
  (278 other events, 3824.9 us)

commit v3 on v2

--- a/solution.py
+++ b/solution.py
@@ -1,3 +1,4 @@
+from functools import partial
 import math
 
 import jax
@@ -22,6 +23,7 @@
 SIDE = 128
 QUAD = 4
 LOW = -1e30
+SCALE = HEAD_SIZE ** (-0.5)
 
 
 def causal_bias(limit, rows, row0, cols):
@@ -45,6 +47,10 @@
     return (jnp.where(lane < HEAD_SIZE, pair, zero), jnp.where(lane >= HEAD_SIZE, pair, zero))
 
 
+def four_lanes(values, step):
+    return pltpu.roll(values, lax.rem(SIDE - QUAD * step, SIDE), 1)
+
+
 def ssd_forward_kernel(limit_ref, c_ref, b_ref, x_ref, cum_col_ref, cum_row_ref, out_ref, inter, bias):
     count = c_ref.shape[0]
 
@@ -53,6 +59,10 @@
         inter[...] = contract_last(c_ref[...], b_ref[...])
         bias[...] = causal_bias(limit_ref[0], count, 0, count)
 
+    step = pl.program_id(0)
+    cum_col = four_lanes(cum_col_ref[...], step)
+    cum_row = cum_row_ref[pl.ds(pl.multiple_of(step // 2 * 8, 8), 8), :]
+    cum_row = jnp.where(step % 2 == 0, cum_row[:QUAD], cum_row[QUAD:])
     for pair in range(QUAD // 2):
         lanes = slice(pair * SIDE, (pair + 1) * SIDE)
         sides = halves(x_ref[:, lanes])
@@ -62,44 +72,38 @@
             total = None
             for half in range(2):
                 h = pair * 2 + half
-                gap = cum_col_ref[0, rows, h : h + 1] - cum_row_ref[0, h : h + 1, :seen]
+                gap = cum_col[rows, h : h + 1] - cum_row[h : h + 1, :seen]
                 mixer = (inter[rows, :seen] * jnp.exp(gap + bias[rows, :seen])).astype(jnp.bfloat16)
                 part = jnp.dot(mixer, sides[half][:seen], preferred_element_type=jnp.float32)
                 total = part if total is None else total + part
             out_ref[rows, lanes] = total
 
 
-def ssd_forward(limit, c_low, b_low, x_step, cum):
-    count, heads = cum.shape
-    steps = heads // QUAD
-    whole = lambda width: pl.BlockSpec((count, width), lambda i: (0, 0))
+def ssd_forward(limit, low, tables):
+    count = low.shape[0]
+    steps = SSM_HEADS // QUAD
+    b_spec = pl.BlockSpec((count, STATE), lambda i: (0, INNER // STATE))
+    c_spec = pl.BlockSpec((count, STATE), lambda i: (0, INNER // STATE + 1))
     return pl.pallas_call(
         ssd_forward_kernel,
         grid=(steps,),
-        out_shape=jax.ShapeDtypeStruct(x_step.shape, jnp.float32),
+        out_shape=jax.ShapeDtypeStruct((count, INNER), jnp.float32),
         in_specs=[
             pl.BlockSpec(memory_space=pltpu.SMEM),
-            whole(c_low.shape[1]),
-            whole(b_low.shape[1]),
+            c_spec,
+            b_spec,
             pl.BlockSpec((count, QUAD * HEAD_SIZE), lambda i: (0, i)),
-            pl.BlockSpec((1, count, QUAD), lambda i: (i, 0, 0)),
-            pl.BlockSpec((1, QUAD, count), lambda i: (i, 0, 0)),
+            pl.BlockSpec((count, SIDE), lambda i: (0, 0)),
+            pl.BlockSpec((SIDE, count), lambda i: (0, 0)),
         ],
         out_specs=pl.BlockSpec((count, QUAD * HEAD_SIZE), lambda i: (0, i)),
         scratch_shapes=[pltpu.VMEM((count, count), jnp.float32)] * 2,
         name="ssd_forward",
-    )(
-        limit,
-        c_low,
-        b_low,
-        x_step,
-        cum.reshape(count, steps, QUAD).transpose(1, 0, 2),
-        cum.T.reshape(steps, QUAD, count),
-    )
+    )(limit, low, low, low, *tables)
 
 
 def ssd_backward_kernel(
-    limit_ref, c_ref, b_ref, x_ref, dy_ref, cum_col_ref, cum_row_ref, z_ref, gc_ref, gb_ref, inter, bias, total
+    limit_ref, c_ref, b_ref, x_ref, dy_ref, cum_col_ref, cum_row_ref, z_ref, gbc_ref, inter, bias, total
 ):
     count = c_ref.shape[0]
 
@@ -109,6 +113,10 @@
         bias[...] = causal_bias(limit_ref[0], count, 0, count)
         total[...] = jnp.zeros_like(total)
 
+    step = pl.program_id(0)
+    cum_col = four_lanes(cum_col_ref[...], step)
+    cum_row = cum_row_ref[pl.ds(pl.multiple_of(step // 2 * 8, 8), 8), :]
+    cum_row = jnp.where(step % 2 == 0, cum_row[:QUAD], cum_row[QUAD:])
     for pair in range(QUAD // 2):
         lanes = slice(pair * SIDE, (pair + 1) * SIDE)
         x_pair = x_ref[:, lanes]
@@ -120,7 +128,7 @@
             back = None
             for half in range(2):
                 h = pair * 2 + half
-                gap = cum_col_ref[0, rows, h : h + 1] - cum_row_ref[0, h : h + 1, :seen]
+                gap = cum_col[rows, h : h + 1] - cum_row[h : h + 1, :seen]
                 decay = jnp.exp(gap + bias[rows, :seen])
                 mixer = (inter[rows, :seen] * decay).astype(jnp.bfloat16)
                 grad_mixer = contract_last(sides[half][rows], x_pair[:seen])
@@ -137,45 +145,36 @@
     @pl.when(pl.program_id(0) == pl.num_programs(0) - 1)
     def _():
         low = total[...].astype(jnp.bfloat16)
-        gc_ref[...] = jnp.dot(low, b_ref[...], preferred_element_type=jnp.float32)
-        gb_ref[...] = contract_first(low, c_ref[...])
-
-
-def ssd_backward(limit, c_low, b_low, x_step, grad_y, cum):
-    count, heads = cum.shape
-    steps = heads // QUAD
-    state = c_low.shape[1]
-    whole = pl.BlockSpec((count, state), lambda i: (0, 0))
+        gbc_ref[:, :STATE] = contract_first(low, c_ref[...])
+        gbc_ref[:, STATE:] = jnp.dot(low, b_ref[...], preferred_element_type=jnp.float32)
+
+
+def ssd_backward(limit, low, grad_y, tables):
+    count = low.shape[0]
+    steps = SSM_HEADS // QUAD
+    b_spec = pl.BlockSpec((count, STATE), lambda i: (0, INNER // STATE))
+    c_spec = pl.BlockSpec((count, STATE), lambda i: (0, INNER // STATE + 1))
     quad = pl.BlockSpec((count, QUAD * HEAD_SIZE), lambda i: (0, i))
     return pl.pallas_call(
         ssd_backward_kernel,
         grid=(steps,),
         out_shape=(
-            jax.ShapeDtypeStruct(x_step.shape, jnp.float32),
-            jax.ShapeDtypeStruct((count, state), jnp.float32),
-            jax.ShapeDtypeStruct((count, state), jnp.float32),
+            jax.ShapeDtypeStruct((count, INNER), jnp.float32),
+            jax.ShapeDtypeStruct((count, 2 * STATE), jnp.float32),
         ),
         in_specs=[
             pl.BlockSpec(memory_space=pltpu.SMEM),
-            whole,
-            whole,
+            c_spec,
+            b_spec,
             quad,
             quad,
-            pl.BlockSpec((1, count, QUAD), lambda i: (i, 0, 0)),
-            pl.BlockSpec((1, QUAD, count), lambda i: (i, 0, 0)),
+            pl.BlockSpec((count, SIDE), lambda i: (0, 0)),
+            pl.BlockSpec((SIDE, count), lambda i: (0, 0)),
         ],
-        out_specs=(quad, whole, whole),
+        out_specs=(quad, pl.BlockSpec((count, 2 * STATE), lambda i: (0, 0))),
         scratch_shapes=[pltpu.VMEM((count, count), jnp.float32)] * 3,
         name="ssd_backward",
-    )(
-        limit,
-        c_low,
-        b_low,
-        x_step,
-        grad_y,
-        cum.reshape(count, steps, QUAD).transpose(1, 0, 2),
-        cum.T.reshape(steps, QUAD, count),
-    )
+    )(limit, low, low, low, grad_y, *tables)
 
 
 def turn(values, cosine, sine):
@@ -206,14 +205,13 @@
     value_sides = halves(both_sides(v_ref[...], step))
     for pair in range(2):
         lanes = slice(pair * SIDE, (pair + 1) * SIDE)
-        sides = halves(turn(q_ref[:, lanes], cosine, sine).astype(jnp.bfloat16))
+        sides = halves(turn(q_ref[:, lanes], cosine, sine).astype(jnp.bfloat16) * SCALE)
         for top in range(0, count, SIDE):
             rows = slice(top, top + SIDE)
             seen = top + SIDE
             total = None
             for half in range(2):
-                score = contract_last(sides[half][rows], key[:seen]) * HEAD_SIZE ** (-0.5)
-                score = score + bias[rows, :seen]
+                score = contract_last(sides[half][rows], key[:seen]) + bias[rows, :seen]
                 largest = jnp.max(score, -1, keepdims=True)
                 raised = jnp.exp(score - largest)
                 mass = jnp.sum(raised, -1, keepdims=True)
@@ -269,7 +267,7 @@
     gv[...] = jnp.zeros_like(gv)
     for pair in range(2):
         lanes = slice(pair * SIDE, (pair + 1) * SIDE)
-        q_sides = halves(turn(q_ref[:, lanes], cosine, sine).astype(jnp.bfloat16))
+        q_sides = halves(turn(q_ref[:, lanes], cosine, sine).astype(jnp.bfloat16) * SCALE)
         go_sides = halves(go_ref[:, lanes])
         for top in range(0, count, SIDE):
             rows = slice(top, top + SIDE)
@@ -277,16 +275,16 @@
             total = None
             for half in range(2):
                 h = pair * 2 + half
-                score = contract_last(q_sides[half][rows], key[:seen]) * HEAD_SIZE ** (-0.5)
+                score = contract_last(q_sides[half][rows], key[:seen])
                 weights = jnp.exp(score + bias[rows, :seen] - log_ref[0, rows, h : h + 1])
                 grad = contract_last(go_sides[half][rows], value[:seen])
                 inner = jnp.sum(grad * weights, -1, keepdims=True)
-                low = (weights * (grad - inner) * HEAD_SIZE ** (-0.5)).astype(jnp.bfloat16)
+                low = (weights * (grad - inner)).astype(jnp.bfloat16)
                 part = jnp.dot(low, key_sides[half][:seen], preferred_element_type=jnp.float32)
                 total = part if total is None else total + part
                 gk[:seen, :] += contract_first(low, q_sides[half][rows])
                 gv[:seen, :] += contract_first(weights.astype(jnp.bfloat16), go_sides[half][rows])
-            gq_ref[rows, lanes] = turn(total, cosine[rows], -sine[rows]).astype(jnp.bfloat16)
+            gq_ref[rows, lanes] = turn(total * SCALE, cosine[rows], -sine[rows]).astype(jnp.bfloat16)
     lane = lax.broadcasted_iota(jnp.int32, (count, SIDE), 1)
     mine = (lane >= HEAD_SIZE) == (step > 0)
     for place, part in enumerate((gk, gv)):
@@ -324,6 +322,161 @@
     )(limit, projected, projected, projected, cosine, sine, grad_out, logs_in)
 
 
+BLOCK = QUAD * HEAD_SIZE
+
+
+TILE = 128
+HALO = 8
+
+
+def conv_taps(u_ref, top, place, weight_ref, bias_ref, lanes):
+    mixed = bias_ref[:, lanes] + u_ref[HALO + top : HALO + top + TILE, lanes] * weight_ref[TAPS - 1 : TAPS, lanes]
+    for back in range(1, TAPS):
+        shifted = u_ref[HALO + top - back : HALO + top - back + TILE, lanes]
+        mixed = mixed + jnp.where(place >= back, shifted, 0.0) * weight_ref[TAPS - 1 - back : TAPS - back, lanes]
+    return mixed
+
+
+def conv_forward_kernel(u_ref, place_ref, weight_ref, bias_ref, step_ref, out_ref, low_ref, held):
+    count = u_ref.shape[0]
+    held[:HALO, :] = jnp.zeros((HALO, BLOCK), jnp.float32)
+    held[HALO:, :] = u_ref[...]
+    lane = lax.broadcasted_iota(jnp.int32, (TILE, SIDE), 1)
+    scale = four_lanes(step_ref[...], pl.program_id(0))
+    for side in range(BLOCK // SIDE):
+        lanes = slice(side * SIDE, (side + 1) * SIDE)
+        for top in range(0, count, TILE):
+            rows = slice(top, top + TILE)
+            mixed = conv_taps(held, top, place_ref[rows], weight_ref, bias_ref, lanes)
+            out = mixed / (1.0 + jnp.exp(-mixed))
+            out_ref[rows, lanes] = out
+            first, second = scale[rows, 2 * side : 2 * side + 1], scale[rows, 2 * side + 1 : 2 * side + 2]
+            low_ref[rows, lanes] = (out * jnp.where(lane < HEAD_SIZE, first, second)).astype(jnp.bfloat16)
+
+
+def conv_specs(count, width):
+    column = lambda i: (0, i)
+    first = (QUERY_KEY_VALUE + INNER) // BLOCK
+    return (
+        pl.BlockSpec((count, BLOCK), lambda i: (0, first + i)),
+        pl.BlockSpec((count, 1), lambda i: (0, 0)),
+        pl.BlockSpec((TAPS, BLOCK), column),
+        pl.BlockSpec((1, BLOCK), column),
+        pl.BlockSpec((count, SIDE), lambda i: (0, 0)),
+        pl.BlockSpec((count, BLOCK), column),
+    )
+
+
+def conv_forward(projected, position, weight, bias, step_quads):
+    count, width = projected.shape[0], weight.shape[1]
+    u, place, taps, row, quads, block = conv_specs(count, width)
+    return pl.pallas_call(
+        conv_forward_kernel,
+        grid=(width // BLOCK,),
+        out_shape=(
+            jax.ShapeDtypeStruct((count, width), jnp.float32),
+            jax.ShapeDtypeStruct((count, width), jnp.bfloat16),
+        ),
+        in_specs=[u, place, taps, row, quads],
+        out_specs=(block, block),
+        scratch_shapes=[pltpu.VMEM((HALO + count, BLOCK), jnp.float32)],
+        name="conv_forward",
+    )(projected, position[:, None], weight, bias[None], step_quads)
+
+
+def head_sums(values, chosen):
+    high = values.astype(jnp.bfloat16)
+    rest = values - high.astype(jnp.float32)
+    middle = rest.astype(jnp.bfloat16)
+    low = (rest - middle.astype(jnp.float32)).astype(jnp.bfloat16)
+    total = jnp.dot(high, chosen, preferred_element_type=jnp.float32)
+    total = total + jnp.dot(middle, chosen, preferred_element_type=jnp.float32)
+    return total + jnp.dot(low, chosen, preferred_element_type=jnp.float32)
+
+
+def conv_backward_kernel(
+    u_ref, place_ref, weight_ref, bias_ref, step_ref, skip_ref, z_ref, gy_ref, y_ref, low_ref, gbc_ref,
+    gu_ref, gw_ref, heads_ref, held, grads,
+):
+    count = u_ref.shape[0]
+    step = pl.program_id(0)
+    inner = step < pl.num_programs(0) - 1
+    scale = four_lanes(step_ref[...], step)
+    held[:HALO, :] = jnp.zeros((HALO, BLOCK), jnp.float32)
+    held[HALO:, :] = u_ref[...]
+    lane = lax.broadcasted_iota(jnp.int32, (TILE, SIDE), 1)
+
+    @pl.when(step == 0)
+    def _():
+        heads_ref[...] = jnp.zeros_like(heads_ref)
+
+    for side in range(BLOCK // SIDE):
+        lanes = slice(side * SIDE, (side + 1) * SIDE)
+        sums = [None] * (TAPS + 1)
+        head = lax.broadcasted_iota(jnp.int32, (SIDE, SIDE), 0) // HEAD_SIZE + 2 * side + QUAD * step
+        column = lax.broadcasted_iota(jnp.int32, (SIDE, SIDE), 1)
+        chosen = [(head + offset == column).astype(jnp.bfloat16) for offset in (0, 32, 64)]
+        for back in range(1, TAPS):
+            grads[back - 1, count:, lanes] = jnp.zeros((HALO, SIDE), jnp.float32)
+        for top in range(0, count, TILE):
+            rows = slice(top, top + TILE)
+            place = place_ref[rows]
+            mixed = conv_taps(held, top, place, weight_ref, bias_ref, lanes)
+            gate = 1.0 / (1.0 + jnp.exp(-mixed))
+            out = mixed * gate
+            z, gy = z_ref[rows, lanes], gy_ref[rows, lanes]
+            first, second = scale[rows, 2 * side : 2 * side + 1], scale[rows, 2 * side + 1 : 2 * side + 2]
+            grad = z * jnp.where(lane < HEAD_SIZE, first, second) + skip_ref[:, lanes] * gy
+            grad = jnp.where(inner, grad, gbc_ref[rows, lanes])
+            gy_low = gy.astype(jnp.bfloat16).astype(jnp.float32)
+            cum = gy_low * y_ref[rows, lanes] - low_ref[rows, lanes].astype(jnp.float32) * z
+            part = head_sums(z * out, chosen[0]) + head_sums(cum, chosen[1]) + head_sums(gy * out, chosen[2])
+            heads_ref[rows, :] += jnp.where(inner, part, 0.0)
+            grad = grad * (gate + out * (1.0 - gate))
+            parts = [jnp.sum(grad, 0, keepdims=True)]
+            parts.append(jnp.sum(grad * held[HALO + top : HALO + top + TILE, lanes], 0, keepdims=True))
+            grads[TAPS - 1, rows, lanes] = grad * weight_ref[TAPS - 1 : TAPS, lanes]
+            for back in range(1, TAPS):
+                seen = jnp.where(place >= back, grad, 0.0)
+                shifted = held[HALO + top - back : HALO + top - back + TILE, lanes]
+                parts.append(jnp.sum(seen * shifted, 0, keepdims=True))
+                grads[back - 1, rows, lanes] = seen * weight_ref[TAPS - 1 - back : TAPS - back, lanes]
+            sums = [p if s is None else s + p for s, p in zip(sums, parts)]
+        gw_ref[:, lanes] = jnp.zeros((8, SIDE), jnp.float32)
+        gw_ref[TAPS : TAPS + 1, lanes] = sums[0]
+        for back in range(TAPS):
+            gw_ref[TAPS - 1 - back : TAPS - back, lanes] = sums[1 + back]
+        for top in range(0, count, TILE):
+            total = grads[TAPS - 1, top : top + TILE, lanes]
+            for back in range(1, TAPS):
+                total = total + grads[back - 1, top + back : top + back + TILE, lanes]
+            gu_ref[top : top + TILE, lanes] = total.astype(jnp.bfloat16)
+
+
+def conv_backward(projected, position, weight, bias, step_quads, skip, z, grad_y, y, low, grad_bc):
+    count, width = projected.shape[0], weight.shape[1]
+    u, place, taps, row, quads, block = conv_specs(count, width)
+    last = INNER // BLOCK - 1
+    inner = pl.BlockSpec((count, BLOCK), lambda i: (0, jnp.minimum(i, last)))
+    skip_row = pl.BlockSpec((1, BLOCK), lambda i: (0, jnp.minimum(i, last)))
+    return pl.pallas_call(
+        conv_backward_kernel,
+        grid=(width // BLOCK,),
+        out_shape=(
+            jax.ShapeDtypeStruct((count, width), jnp.bfloat16),
+            jax.ShapeDtypeStruct((8, width), jnp.float32),
+            jax.ShapeDtypeStruct((count, SIDE), jnp.float32),
+        ),
+        in_specs=[u, place, taps, row, quads, skip_row, inner, inner, inner, block, pl.BlockSpec((count, BLOCK), lambda i: (0, 0))],
+        out_specs=(block, pl.BlockSpec((8, BLOCK), lambda i: (0, i)), pl.BlockSpec((count, SIDE), lambda i: (0, 0))),
+        scratch_shapes=[
+            pltpu.VMEM((HALO + count, BLOCK), jnp.float32),
+            pltpu.VMEM((TAPS, count + HALO, BLOCK), jnp.float32),
+        ],
+        name="conv_backward",
+    )(projected, position[:, None], weight, bias[None], step_quads, skip, z, grad_y, y, low, grad_bc)
+
+
 def pick_kernel(shift_ref, wanted_ref, *refs):
     out_ref = refs[-1]
     pieces = refs[:-1]
@@ -376,24 +529,32 @@
     )(places // 16, *pieces)
 
 
-def sum_pieces_kernel(place_ref, *refs):
+def widen_kernel(parts, columns, place_ref, *refs):
     out_ref = refs[-1]
-    for n, piece in enumerate(refs[:-1]):
-        rows = piece.shape[0]
-        start = pl.multiple_of(place_ref[n] * 8, 8)
-        out_ref[pl.ds(start, rows), :] = piece[...].astype(jnp.float32)
-
-
-def widen_rows(pieces, places):
-    rows = sum(piece.shape[0] for piece in pieces)
+    for n, block in enumerate(refs[:-1]):
+        rows = block.shape[0] // parts
+        left = columns[n // 2]
+        for k in range(parts):
+            start = pl.multiple_of(place_ref[(n % 2) * parts + k] * rows, rows)
+            piece = block[k * rows : (k + 1) * rows, :].astype(jnp.float32)
+            out_ref[pl.ds(start, rows), left : left + block.shape[1]] = piece
+
+
+def widen_rows(chunks, places):
+    flat = [block for chunk in chunks for block in chunk]
+    columns, left = [], 0
+    for chunk in chunks:
+        columns.append(left)
+        left += chunk[0].shape[1]
+    rows = 2 * chunks[0][0].shape[0]
     vmem = pl.BlockSpec(memory_space=pltpu.VMEM)
     return pl.pallas_call(
-        sum_pieces_kernel,
-        out_shape=jax.ShapeDtypeStruct((rows, pieces[0].shape[1]), jnp.float32),
-        in_specs=[pl.BlockSpec(memory_space=pltpu.SMEM)] + [vmem] * len(pieces),
+        partial(widen_kernel, places.shape[0] // 2, tuple(columns)),
+        out_shape=jax.ShapeDtypeStruct((rows, left), jnp.float32),
+        in_specs=[pl.BlockSpec(memory_space=pltpu.SMEM)] + [vmem] * len(flat),
         out_specs=vmem,
         name="widen_rows",
-    )(places // 8, *pieces)
+    )(places, *flat)
 
 
 def swap(values, axis, mask):
@@ -438,9 +599,9 @@
             self._advance(slot, came)
         return values
 
-    def until(self, slots, values=None):
+    def until(self, slots, values=None, alone=False):
         while any(not slot["done"] for slot in slots):
-            values = self.step(values)
+            values = self.step(values, slots if alone else None)
         return values
 
 
@@ -499,50 +660,80 @@
     return lay_rows(pieces, jnp.stack(places).astype(jnp.int32))
 
 
-def reduce_stream(grad, far_first):
-    rows_all, width = grad.shape
+def transposed_dot(left, right):
+    return lax.dot_general(left, right, (((0,), (0,)), ((), ())), preferred_element_type=jnp.float32)
+
+
+def reduce_stream(left, right, direct=False):
     shards, replicas = lax.axis_size("shard"), lax.axis_size("rep")
-    rows = rows_all // shards // replicas
+    block = left.shape[1] // shards
+    rows = block // replicas
+    width = right.shape[1]
     shard, replica = lax.axis_index("shard"), lax.axis_index("rep")
     core, far = shard & 1, shard >> 1
     near, rest = replica & 1, replica >> 1
-    total = grad.reshape(shards // 2, 2, replicas // 2, 2, rows, width)
-    away, keep = take(total, 1 - core, 1), take(total, core, 1)
-    came = yield [swap(away, "shard", 1)]
-    total = add(keep, came[0])
-
-    def over_near(total):
-        away, keep = take(total, 1 - near, total.ndim - 3), take(total, near, total.ndim - 3)
-        came = yield [swap(away, "rep", 1)]
-        return add(keep, came[0])
-
-    def over_far(total):
-        count = shards // 2
-        while count > 1:
-            count //= 2
-            flag = (far // count) % 2
-            total = total.reshape((2, count) + total.shape[1:])
-            away, keep = take(total, 1 - flag, 0), take(total, flag, 0)
-            came = yield [swap(away, "shard", 2 * count)]
-            total = add(keep, came[0])
-        return total[0]
-
-    if far_first:
-        total = yield from over_far(total)
-        total = yield from over_near(total)
-    else:
-        total = yield from over_near(total)
-        total = yield from over_far(total)
-    others = range(1, replicas // 2)
-    came = yield [swap(take(total, rest ^ k, 0), "rep", 2 * k) for k in others]
-    total = add(take(total, rest, 0), *came)
-    came = yield [swap(total, "rep", 2 * k) for k in others]
-    mine = jnp.concatenate([total, *came], 0)
+
+    def product(r, c, extras=(), half=None):
+        start, size = ((far ^ r) * 2 + c) * block, block
+        if half is not None:
+            size = block // 2
+            start = start + half * size
+            extras = [x if x.shape[0] == size else lax.dynamic_slice_in_dim(x, half * size, size, 0) for x in extras]
+        total = transposed_dot(lax.dynamic_slice_in_dim(left, start, size, 1), right)
+        for extra in extras:
+            total = total + extra.astype(jnp.float32)
+        return total.astype(jnp.bfloat16)
+
+    count = shards // 2
+    came = yield [swap(product(r, 1 - core), "shard", 1) for r in range(count)]
+    extras = [[c] for c in came]
+    while count > 1:
+        count //= 2
+        came = yield [swap(product(r, core, extras[r]), "shard", 2 * count) for r in range(count, 2 * count)]
+        for n, c in enumerate(came):
+            extras[n].append(c)
+    came = yield [swap(product(0, core, extras[0], 1 - near), "rep", 1)]
+    total = product(0, core, [*extras[0], came[0]], near)
+    if direct:
+        others = merge_order()[1:]
+        total = total.reshape(replicas // 2, rows, width)
+        came = yield [swap(take(total, rest ^ k, 0), "rep", 2 * k) for k in others]
+        total = add(take(total, rest, 0), *came)
+        came = yield [swap(total, "rep", 2 * k) for k in others]
+        mine = jnp.concatenate([total, *came], 0)
+        came = yield [swap(mine, "rep", 1)]
+        return mine, came[0]
+    mask = 1
+    while mask < replicas // 2:
+        flag = (rest // mask) % 2
+        total = total.reshape(-1, 2, rows, width)
+        came = yield [swap(take(total, 1 - flag, 1), "rep", 2 * mask)]
+        total = add(take(total, flag, 1), came[0])
+        mask *= 2
+    mine = total.reshape(rows, width)
+    while mask > 1:
+        mask //= 2
+        came = yield [swap(mine, "rep", 2 * mask)]
+        mine = jnp.concatenate([mine, came[0]], 0)
     came = yield [swap(mine, "rep", 1)]
-    pieces = [mine[k * rows : (k + 1) * rows] for k in range(replicas // 2)]
-    pieces += [came[0][k * rows : (k + 1) * rows] for k in range(replicas // 2)]
-    places = [((rest ^ k) * 2 + (near ^ side)) * rows for side in range(2) for k in range(replicas // 2)]
-    return pieces, jnp.stack(places).astype(jnp.int32)
+    return mine, came[0]
+
+
+def merge_order():
+    order = [0]
+    mask = lax.axis_size("rep") // 2
+    while mask > 1:
+        mask //= 2
+        order = order + [k ^ mask for k in order]
+    return order
+
+
+def piece_places():
+    replica = lax.axis_index("rep")
+    near, rest = replica & 1, replica >> 1
+    order = merge_order()
+    places = [(near ^ side) * len(order) + (rest ^ k) for side in range(2) for k in order]
+    return jnp.stack(places).astype(jnp.int32)
 
 
 def butterfly_stream(total):
@@ -628,16 +819,6 @@
     return jnp.cos(angles), jnp.sin(angles) * sign
 
 
-def conv_mixed(conv_in, conv_weight, conv_bias, position):
-    width = conv_in.shape[1]
-    mixed = conv_bias + conv_in * conv_weight[TAPS - 1]
-    for back in range(1, TAPS):
-        shifted = jnp.concatenate([jnp.zeros((back, width), jnp.float32), conv_in[:-back]], 0)
-        same = (position >= back).astype(jnp.float32)[:, None]
-        mixed = mixed + shifted * same * conv_weight[TAPS - 1 - back]
-    return mixed
-
-
 def gated_norm(ssm_y, gate_z, gain):
     gated = ssm_y * jax.nn.silu(gate_z)
     return gated * rms_scale(gated) * gain
@@ -652,20 +833,17 @@
     return jnp.dot(left, right, preferred_element_type=jnp.float32)
 
 
-def head_lanes():
-    head = lax.broadcasted_iota(jnp.int32, (SSM_HEADS, INNER), 0)
-    lane = lax.broadcasted_iota(jnp.int32, (SSM_HEADS, INNER), 1)
-    return (lane // SSM_HD == head).astype(jnp.float32)
-
-
-def spread_heads(values):
-    return jnp.dot(values, head_lanes(), precision=lax.Precision.HIGHEST)
-
-
-def sum_heads(values):
-    return lax.dot_general(
-        values, head_lanes(), (((1,), (1,)), ((), ())), precision=lax.Precision.HIGHEST
-    )
+def running_sum(values, reverse):
+    count = values.shape[0]
+    i = lax.broadcasted_iota(jnp.int32, (count, count), 0)
+    j = lax.broadcasted_iota(jnp.int32, (count, count), 1)
+    chosen = ((i <= j) if reverse else (j <= i)).astype(jnp.float32)
+    return jnp.dot(chosen, values, precision=lax.Precision.HIGHEST)
+
+
+def to_lanes(values, fill):
+    count, width = values.shape
+    return jnp.concatenate([values, jnp.full((count, SIDE - width), fill, values.dtype)], 1)
 
 
 def on_device(
@@ -690,91 +868,78 @@
     input_rows = tokens.shape[0]
     shard = lax.axis_index("shard")
     flow = Flow()
-
-    slot_tokens = flow.add(rows_stream(tokens))
+    f32 = lambda v: v.astype(jnp.float32)
+
     slot_input = flow.add(weight_stream(w_input))
     small_args = (gain_attn, w_step, step_bias, decay_log, skip_scale, conv_weight, conv_bias, gain_ssm, gain_ffn)
     small_dims = (0, 0, 0, 0, 0, 1, 0, 0, 0)
     slot_small = flow.add(small_stream(jnp.concatenate([a.reshape(-1) for a in small_args])))
     source, position, limit, target = group_tables(seq_lengths[0], owner_order[0], input_rows, shard)
     cosine, sine = rope_tables(position)
-    source, position, limit, target, cosine, sine = flow.step((source, position, limit, target, cosine, sine))
-    slot_output = flow.add(weight_stream(w_output))
-    source, position = flow.step((source, position))
-    slot_gate_up = flow.add(weight_stream(w_gate_up))
-    source, position = flow.until([slot_tokens, slot_input, slot_small], (source, position))
+    source, position, tokens, cosine, sine = flow.step((source, position, tokens, cosine, sine))
+    slot_tokens = flow.add(rows_stream(tokens))
+    source, position, w_output, w_gate_up, w_down, cotangent = flow.step(
+        (source, position, w_output, w_gate_up, w_down, cotangent)
+    )
+    w_output_all = lax.all_gather(w_output, "shard", axis=0, tiled=True)
+    w_gate_up_all = lax.all_gather(w_gate_up, "shard", axis=0, tiled=True)
+    source, position, w_down, cotangent = flow.until(
+        [slot_tokens, slot_input, slot_small], (source, position, w_down, cotangent)
+    )
+    w_down_all = lax.all_gather(w_down, "shard", axis=0, tiled=True)
+    slot_cot = flow.add(rows_stream(cotangent))
 
     gain_attn_all, w_step_all, step_bias_all, decay_all, skip_all, conv_w_all, conv_b_all, gain_ssm_all, gain_ffn_all = (
         unpack_small(slot_small["result"], [a.shape for a in small_args], small_dims)
     )
-    f32 = lambda v: v.astype(jnp.float32)
     gain_attn_f, gain_ssm_f, gain_ffn_f = f32(gain_attn_all), f32(gain_ssm_all), f32(gain_ffn_all)
     conv_w_f, conv_b_f = f32(conv_w_all), f32(conv_b_all)
     skip_lanes = jnp.repeat(f32(skip_all), SSM_HD)[None]
     pieces, owners = slot_tokens["result"]
-    own_low = pick_rows(pieces, owners * input_rows, source)
-    own = f32(own_low)
+    own = f32(pick_rows(pieces, owners * input_rows, source))
     w_input_all = slot_input["result"]
 
     normed = rms_norm(own, gain_attn_f).astype(jnp.bfloat16)
     projected = dot(normed, w_input_all)
-    step_raw = dot(normed, w_step_all)
-    projected, step_raw = flow.step((projected, step_raw))
-    slot_down = flow.add(weight_stream(w_down))
-    conv_in = projected[:, QUERY_KEY_VALUE + INNER :]
-    gate_z = projected[:, QUERY_KEY_VALUE : QUERY_KEY_VALUE + INNER]
-    conv_out = jax.nn.silu(conv_mixed(conv_in, conv_w_f, conv_b_f, position))
-    inner_x = conv_out[:, :INNER]
-    b_low = conv_out[:, INNER : INNER + STATE].astype(jnp.bfloat16)
-    c_low = conv_out[:, INNER + STATE :].astype(jnp.bfloat16)
-    step_pre = step_raw + f32(step_bias_all)
+    projected, normed = flow.step((projected, normed))
+    step_pre = dot(normed, w_step_all) + f32(step_bias_all)
     step = jax.nn.softplus(step_pre)
     rate = -jnp.exp(f32(decay_all))
-    cum = jnp.cumsum(step * rate, axis=0)
-    step_lanes = spread_heads(step)
-    x_step = (inner_x * step_lanes).astype(jnp.bfloat16)
-    x_step, cum, b_low, c_low, inner_x, step_lanes = flow.step((x_step, cum, b_low, c_low, inner_x, step_lanes))
-    ssd_out = ssd_forward(limit, c_low, b_low, x_step, cum)
-    ssd_out, projected = flow.step((ssd_out, projected))
+    cum = to_lanes(running_sum(step * rate, False), 0.0)
+    tables = (cum, cum.T)
+    step_lanes = to_lanes(step, 1.0)
+    conv_out, low = conv_forward(projected, position, conv_w_f, conv_b_f, step_lanes)
+    inner_x = conv_out[:, :INNER]
+    ssd_out = ssd_forward(limit, low, tables)
     attn_out, logs = attention_forward(limit, projected, cosine, sine)
+    gate_z = projected[:, QUERY_KEY_VALUE : QUERY_KEY_VALUE + INNER]
     ssm_y = ssd_out + skip_lanes * inner_x
-    gate_z = projected[:, QUERY_KEY_VALUE : QUERY_KEY_VALUE + INNER]
     ssm_out = gated_norm(ssm_y, gate_z, gain_ssm_f).astype(jnp.bfloat16)
     joined = jnp.concatenate([attn_out, ssm_out], 1)
-    joined = flow.until([slot_output], joined)
-    w_output_all = slot_output["result"]
-    slot_cot = flow.add(rows_stream(cotangent))
     middle = own + dot(joined, w_output_all)
     normed_ffn = rms_norm(middle, gain_ffn_f).astype(jnp.bfloat16)
-    normed_ffn, middle = flow.until([slot_gate_up], flow.step((normed_ffn, middle)))
-    w_gate_up_all = slot_gate_up["result"]
     gate_up = dot(normed_ffn, w_gate_up_all)
     hidden = swiglu(gate_up).astype(jnp.bfloat16)
-    gate_up, hidden = flow.until([slot_cot, slot_down], (gate_up, hidden))
-    w_down_all = slot_down["result"]
+    gate_up, hidden = flow.until([slot_cot], (gate_up, hidden))
     pieces, owners = slot_cot["result"]
     cot = pick_rows(pieces, owners * input_rows, source)
 
-    def weight_grad(left, right):
-        return lax.dot_general(
-            left, right, (((0,), (0,)), ((), ())), preferred_element_type=jnp.float32
-        ).astype(jnp.bfloat16)
-
     def back(left, weight):
         return lax.dot_general(left, weight, (((1,), (1,)), ((), ())), preferred_element_type=jnp.float32)
 
-    grad_slots = {}
-    grad_slots["down"] = [flow.add(reduce_stream(weight_grad(hidden, cot), True))]
+    slots = {}
+    block_low = (middle + dot(hidden, w_down_all)).astype(jnp.bfloat16)
+    slots["down"] = [flow.add(reduce_stream(hidden, cot))]
     grad_hidden = back(cot, w_down_all)
     grad_gate_up = jax.vjp(swiglu, gate_up)[1](grad_hidden)[0].astype(jnp.bfloat16)
     grad_gate_up = flow.step(grad_gate_up)
     half = grad_gate_up.shape[1] // 2
-    grad_slots["gate_up"] = [flow.add(reduce_stream(weight_grad(normed_ffn, grad_gate_up[:, :half]), True))]
+    slots["gate_up"] = [flow.add(reduce_stream(normed_ffn, grad_gate_up[:, :half]))]
     grad_normed_ffn = back(grad_gate_up, w_gate_up_all)
     grad_middle_norm, grad_gain_ffn = jax.vjp(rms_norm, middle, gain_ffn_f)[1](grad_normed_ffn)
     grad_middle = f32(cot) + grad_middle_norm
-    grad_gate_up, grad_middle = flow.step((grad_gate_up, grad_middle))
-    grad_slots["gate_up"].append(flow.add(reduce_stream(weight_grad(normed_ffn, grad_gate_up[:, half:]), False)))
+    grad_middle, grad_gate_up = flow.step((grad_middle, grad_gate_up))
+    slots["gate_up"].append(flow.add(reduce_stream(normed_ffn, grad_gate_up[:, half:])))
     middle_low = grad_middle.astype(jnp.bfloat16)
     grad_joined = back(middle_low, w_output_all)
     grad_attn = grad_joined[:, : QUERY_HEADS * HEAD_SIZE].astype(jnp.bfloat16)
@@ -785,71 +950,78 @@
     grad_ssm_y, grad_z_low, grad_attn, middle_low, grad_y_low = flow.step(
         (grad_ssm_y, grad_z_low, grad_attn, middle_low, grad_y_low)
     )
-    grad_slots["output"] = [flow.add(reduce_stream(weight_grad(joined, middle_low), True))]
+    block_all = lax.all_gather(block_low, "shard", axis=0, tiled=True)
+    slots["output"] = [flow.add(reduce_stream(joined, middle_low))]
     grad_q, grad_kv = attention_backward(limit, projected, cosine, sine, grad_attn, logs)
-    grad_q, grad_kv, grad_y_low = flow.step((grad_q, grad_kv, grad_y_low))
-    grad_slots["input"] = [flow.add(reduce_stream(weight_grad(normed, grad_z_low), False))]
-    back_x, grad_c, grad_b = ssd_backward(limit, c_low, b_low, x_step, grad_y_low, cum)
-    back_x, grad_c, grad_b = flow.step((back_x, grad_c, grad_b))
-    qkv = jnp.concatenate([grad_q, grad_kv], 1)
-    grad_slots["input"].insert(0, flow.add(reduce_stream(weight_grad(normed, qkv), True)))
-    grad_skip = jnp.sum(sum_heads(grad_ssm_y * inner_x), 0)
-    grad_cum = sum_heads(f32(grad_y_low) * ssd_out - f32(x_step) * back_x)
-    grad_step = sum_heads(back_x * inner_x)
-    grad_x = back_x * step_lanes + skip_lanes * grad_ssm_y
-    grad_inc = lax.cumsum(grad_cum, axis=0, reverse=True)
-    grad_step = grad_step + grad_inc * rate
+    grad_q, grad_kv, grad_y_low, grad_z_low = flow.step((grad_q, grad_kv, grad_y_low, grad_z_low))
+    qkvz = jnp.concatenate([grad_q, grad_kv, grad_z_low], 1)
+    slots["input"] = [flow.add(reduce_stream(normed, qkvz))]
+    back_x, grad_bc = ssd_backward(limit, low, grad_y_low, tables)
+    back_x, grad_bc = flow.step((back_x, grad_bc))
+    grad_u_low, grad_taps, head_parts = conv_backward(
+        projected, position, conv_w_f, conv_b_f, step_lanes, skip_lanes, back_x, grad_ssm_y, ssd_out, low, grad_bc
+    )
+    grad_u_low, head_parts = flow.step((grad_u_low, head_parts))
+    slots["input"].append(flow.add(reduce_stream(normed, grad_u_low, True)))
+    grad_projected = jnp.concatenate([qkvz, grad_u_low], 1)
+    heads_of = lambda offset: head_parts[:, offset : offset + SSM_HEADS]
+    grad_skip = jnp.sum(heads_of(64), 0)
+    grad_inc = running_sum(heads_of(32), True)
+    grad_step = heads_of(0) + grad_inc * rate
     grad_decay = jnp.sum(grad_inc * step, 0) * rate
     grad_step_pre = grad_step * jax.nn.sigmoid(step_pre)
     grad_step_bias = jnp.sum(grad_step_pre, 0)
     step_low = grad_step_pre.astype(jnp.bfloat16)
-    grad_w_step = lax.dot_general(normed, step_low, (((0,), (0,)), ((), ())), preferred_element_type=jnp.float32)
-    grad_conv = jnp.concatenate([grad_x, grad_b, grad_c], 1)
-    mixed_back = jax.vjp(
-        lambda u, w, b: jax.nn.silu(conv_mixed(u, w, b, position)), conv_in, conv_w_f, conv_b_f
-    )[1]
-    grad_u, grad_conv_w, grad_conv_b = mixed_back(grad_conv)
-    grad_u_low = grad_u.astype(jnp.bfloat16)
-    grad_u_low, step_low = flow.step((grad_u_low, step_low))
-    grad_slots["input"].append(flow.add(reduce_stream(weight_grad(normed, grad_u_low), True)))
-    grad_projected = jnp.concatenate([qkv, grad_z_low, grad_u_low], 1)
-    grad_normed = back(grad_projected, w_input_all) + back(step_low, w_step_all)
-    grad_tokens_norm, grad_gain_attn = jax.vjp(rms_norm, own, gain_attn_f)[1](grad_normed)
-    grad_low = (grad_middle + grad_tokens_norm).astype(jnp.bfloat16)
+    grad_w_step = transposed_dot(normed, step_low)
     small_grads = (
-        grad_gain_attn,
         grad_w_step,
         grad_step_bias,
         grad_decay,
         grad_skip,
-        grad_conv_w,
-        grad_conv_b,
+        grad_taps[:TAPS],
+        grad_taps[TAPS],
         grad_gain_ssm,
         grad_gain_ffn,
     )
+    grad_projected, step_low = flow.step((grad_projected, step_low))
     flat = jnp.concatenate([g.reshape(-1) for g in small_grads])
     flat = jnp.pad(flat, (0, -flat.shape[0] % 1024)).reshape(-1, SIDE)
-    grad_low, flat = flow.step((grad_low, flat))
+    slot_flat = flow.add(butterfly_stream(flat))
+    grad_normed = back(grad_projected, w_input_all) + back(step_low, w_step_all)
+    grad_tokens_norm, grad_gain_attn = jax.vjp(rms_norm, own, gain_attn_f)[1](grad_normed)
+    grad_low = (grad_middle + grad_tokens_norm).astype(jnp.bfloat16)
+    places = piece_places()
+    held = {}
+
+    def finish_ready():
+        for name in slots:
+            if name not in held and all(slot["done"] for slot in slots[name]):
+                held[name] = widen_rows([slot["result"] for slot in slots[name]], places)
+
+    grad_low, gain_late = flow.step((grad_low, grad_gain_attn.reshape(-1, SIDE)))
     slot_grad = flow.add(rows_stream(grad_low))
-    slot_flat = flow.add(butterfly_stream(flat))
-    block_low = (middle + dot(hidden, w_down_all)).astype(jnp.bfloat16)
-    slot_block = flow.add(rows_stream(block_low))
-    target = flow.until(list(flow.live), target)
-
-    pieces, owners = slot_block["result"]
-    block_out = pick_rows(pieces, owners * input_rows, target)
-    pieces, owners = slot_grad["result"]
-    grad_tokens = pick_rows(pieces, owners * input_rows, target)
+    slot_late = flow.add(butterfly_stream(gain_late))
+    finish_ready()
+    held["block"] = pick_rows([block_all], jnp.zeros((1,), jnp.int32), target)
+    held = flow.step(held, [slot for slot in flow.live if slot is not slot_grad])
+    while flow.live:
+        finish_ready()
+        if slot_grad["done"] and "tokens" not in held:
+            pieces, owners = slot_grad["result"]
+            held["tokens"] = pick_rows(pieces, owners * input_rows, target)
+        held = flow.step(held)
+    finish_ready()
+    block_out, grad_tokens, widened = held["block"], held["tokens"], held
     outs = [None] * 13
+    outs[0] = own_block(slot_late["result"].reshape(-1), 0)
     summed = slot_flat["result"].reshape(-1)
     offset = 0
-    for i, grad in zip((0, 2, 3, 4, 5, 6, 7, 8, 10), small_grads):
+    for i, grad in zip((2, 3, 4, 5, 6, 7, 8, 10), small_grads):
         block = summed[offset : offset + grad.size].reshape(grad.shape)
         offset += grad.size
         outs[i] = own_block(block, 1 if i == 6 else 0)
     for i, name in ((1, "input"), (9, "output"), (11, "gate_up"), (12, "down")):
-        parts = [widen_rows(*slot["result"]) for slot in grad_slots[name]]
-        outs[i] = parts[0] if len(parts) == 1 else jnp.concatenate(parts, 1)
+        outs[i] = widened[name]
     return (block_out, grad_tokens, *outs)
 
 

time: 745 us -> 646 us (0.87)
  other arithmetic: 142 us -> 56.4 us
  local copies, waits for them, and re-layouts: 98.7 us -> 51.4 us
  starting transfers between devices: 112 us -> 73.5 us
  matrix products: 89.3 us -> 119 us
  waiting for transfers between devices: 171 us -> 198 us
  between operations: 3.49 us -> 16 us
  Pallas kernels: 117 us -> 126 us
    ppermute x109 -> x82, starting transfers between devices: 112 us -> 72.9 us  [swap(): return lax.ppermute(values, axis, [(i, i ^ mask) for i in range(count)])]
    convert_element_type x28 -> x6, other arithmetic: 42.1 us -> 4.69 us  [add(): return total.astype(jnp.bfloat16)]
    dot_general x12 -> x33, matrix products: 34.2 us -> 63.2 us  [the longest x31 61.2 us: transposed_dot(): lax.dot_general(left, right, (((0,), (0,)), ((), ())), preferred_element_...]
    pallas_call x7 -> x6, Pallas kernels: 18.2 us -> 43.4 us  [the longest x1 20.6 us: conv_backward(): pl.pallas_call(conv_backward_kernel, grid=(width // BLOCK,), out_shape=(j...]
    all_gather x0 -> x4, waiting for transfers between devices: none -> 25.1 us  [the longest x1 13.2 us: on_device(): w_gate_up_all = lax.all_gather(w_gate_up, 'shard', axis=0, tiled=True)]
    another operation x9 -> x2, other arithmetic: 18.5 us -> 0.37 us
    dynamic_slice x14 -> x0, local copies, waits for them, and re-layouts: 17.2 us -> none  [take(): return lax.dynamic_index_in_dim(values, index, dim, keepdims=False)]
    pallas_call x4 -> x1, Pallas kernels: 24.5 us -> 7.5 us  [lay_rows(): pl.pallas_call(lay_rows_kernel, out_shape=jax.ShapeDtypeStruct((rows, pie...]
  transfers between devices with their start and end apart: 109 -> 86, of which waited for: 28 -> 25; matrix products, arithmetic and copies ran while one was open for 40% -> 30% of each run, Pallas kernels for 13% -> 20%
where the time goes in v3:
time: 646 us; the launch traced here: 640 us
  waiting for transfers between devices  198 us (31%)
  Pallas kernels  126 us (20%)
  matrix products  119 us (18%)
  starting transfers between devices  73.5 us (11%)
  other arithmetic  56.4 us (9%)
  local copies, waits for them, and re-layouts  51.4 us (8%)
  between operations  16 us (2%)
    ppermute x82, waiting for transfers between devices, swap(): return lax.ppermute(values, axis, [(i, i ^ mask) for i in range(count)])  172 us
    ppermute x82, starting transfers between devices, swap(): return lax.ppermute(values, axis, [(i, i ^ mask) for i in range(count)])  72.9 us
    dot_general x31, matrix products, transposed_dot(): lax.dot_general(left, right, (((0,), (0,)), ((), ())), preferred_element_...  61.2 us
    dot_general x5, matrix products, back(): lax.dot_general(left, weight, (((1,), (1,)), ((), ())), preferred_element...  29.5 us
    dot_general x5, matrix products, dot(): return jnp.dot(left, right, preferred_element_type=jnp.float32)  26.7 us
    pallas_call x4, Pallas kernels, pick_rows(): pl.pallas_call(pick_kernel, out_shape=jax.ShapeDtypeStruct((wanted.shape[...  22.9 us
    pallas_call x1, Pallas kernels, conv_backward(): pl.pallas_call(conv_backward_kernel, grid=(width // BLOCK,), out_shape=(j...  20.6 us
    unnamed x261, local copies, waits for them, and re-layouts  17.3 us
  transfers between devices with their start and end apart: 86, of which 25 were waited for; matrix products, arithmetic and copies ran while one was open for 30% of the time, Pallas kernels for 20%

profile of v3, /device:TPU:0, one launch (start us, length us, event | category | flops | bytes accessed | tf_op | source)
XLA Modules:
  0.0 639.9 jit_solution(9019283473757780118)
XLA Ops:
  26.2 17.1 %collective-permute-done.refs_2_ = bf16[128,4096]{1,0:T(8,128)(2,1)S(1)} collective-permute-done((bf16[128,4096]{1,0:T(8,128)(2,1)}, bf16[128,4096]{1,0:T(8,128)(2,1)S(1)}, u32[]{:S(2)}, u32[]{:S(2)}) %collective-permute-start) | collective-permute-done | bytes 1048608 | tf_op jit(solution)/shard_map/ppermute | solution.py:562
  47.6 24.2 %collective-permute-done.5 = bf16[2,9298]{1,0:T(2,128)(2,1)S(1)} collective-permute-done((bf16[2,9298]{1,0:T(2,128)(2,1)S(1)}, bf16[2,9298]{1,0:T(2,128)(2,1)S(1)}, u32[]{:S(2)}, u32[]{:S(2)}) %collective-permute-start.5) | collective-permute-done | bytes 37224 | tf_op jit(solution)/shard_map/ppermute | solution.py:562
  92.1 7.5 %lay_rows.1 = bf16[1024,4096]{1,0:T(8,128)(2,1)} custom-call(s32[6]{0:T(128)} %and_select_fusion.place_ref, bf16[256,4096]{1,0:T(8,128)(2,1)} %refs_0_.2, bf16[256,4096]{1,0:T(8,128)(2,1)} %copy-done.39, bf16[128,4096]{1,0:T(8,128)(2,1)} %copy-done.64, bf16[128,4096]{1,0:T(8,128)(2,1)} %copy-done.65, bf16[128,4096]{1,0:T(8,128)(2,1)} %copy-done.66, ...), custom_call_target="tpu_custom_call" | custom-call | tf_op jit(solution)/shard_map/lay_rows/pallas_call | solution.py:522
  99.6 10.1 %fusion.181.q_ref.k_ref.v_ref.u_ref = f32[512,4096]{1,0:T(8,128)} fusion(bf16[512,1024]{1,0:T(8,128)(2,1)S(1)} %fusion.33, bf16[1024,4096]{1,0:T(8,128)(2,1)} %lay_rows.1), kind=kOutput, calls=%fused_computation.356 | convolution fusion | flops 4294967296 | bytes 17825792 | tf_op jit(solution)/shard_map/dot_general | solution.py:833
  110.6 18.6 %collective-permute-done.10.refs_1_ = bf16[512,1024]{1,0:T(8,128)(2,1)} collective-permute-done((bf16[512,1024]{1,0:T(8,128)(2,1)}, bf16[512,1024]{1,0:T(8,128)(2,1)}, u32[]{:S(2)}, u32[]{:S(2)}) %collective-permute-start.10) | collective-permute-done | bytes 1048608 | tf_op jit(solution)/shard_map/ppermute | solution.py:562
  131.9 11.9 %attention_forward.1 = (bf16[512,512]{1,0:T(8,128)(2,1)}, f32[2,512,4]{2,1,0:T(8,128)}) custom-call(s32[1]{0:T(128)} %bitcast.12.limit_ref, f32[512,4096]{1,0:T(8,128)} %fusion.181.q_ref.k_ref.v_ref.u_ref, f32[512,4096]{1,0:T(8,128)} %fusion.181.q_ref.k_ref.v_ref.u_ref, f32[512,4096]{1,0:T(8,128)} %fusion.181.q_ref.k_ref.v_ref.u_ref, ...), custom_call_target="tpu_custom_call" | custom-call | tf_op jit(solution)/shard_map/attention_forward/pallas_call | solution.py:238
  143.8 9.9 %conv_forward.1 = (f32[512,1792]{1,0:T(8,128)}, bf16[512,1792]{1,0:T(8,128)(2,1)}) custom-call(f32[512,4096]{1,0:T(8,128)} %fusion.181.q_ref.k_ref.v_ref.u_ref, s32[512,1]{1,0:T(8,128)} %copy.85.place_ref, f32[4,1792]{1,0:T(4,128)} %reshape.385.weight_ref, f32[1,1792]{1,0:T(1,128)} %reshape.386.bias_ref, f32[512,128]{1,0:T(8,128)} %concatenate.69.step_ref), custom_call_target="tpu_custom_call" | custom-call | tf_op jit(solution)/shard_map/conv_forward/pallas_call | solution.py:373
  154.4 9.2 %ssd_forward.1.y_ref = f32[512,1536]{1,0:T(8,128)} custom-call(s32[1]{0:T(128)} %bitcast.12.limit_ref, bf16[512,1792]{1,0:T(8,128)(2,1)} %get-tuple-element.190.c_ref.b_ref.x_ref.low_ref, bf16[512,1792]{1,0:T(8,128)(2,1)} %get-tuple-element.190.c_ref.b_ref.x_ref.low_ref, bf16[512,1792]{1,0:T(8,128)(2,1)} %get-tuple-element.190.c_ref.b_ref.x_ref.low_ref, ...), custom_call_target="tpu_custom_call" | custom-call | tf_op jit(solution)/shard_map/ssd_forward/pallas_call | solution.py:87
  178.1 13.2 %all-gather.7.cloned.1.call-done = bf16[1024,4096]{1,0:T(8,128)(2,1)} async-done(((bf16[256,4096]{1,0:T(8,128)(2,1)}), bf16[1024,4096]{1,0:T(8,128)(2,1)}) %all-gather.7.cloned.1.call-update) | async-done | bytes 8388624 | tf_op jit(solution)/shard_map/all_gather | solution.py:885
  191.3 7.4 %fusion.182 = f32[512,4096]{1,0:T(8,128)S(1)} fusion(bf16[512,1024]{1,0:T(8,128)(2,1)} %multiply_convert_fusion.1, bf16[1024,4096]{1,0:T(8,128)(2,1)} %all-gather.7.cloned.1.call-done), kind=kOutput, calls=%fused_computation.357 | convolution fusion | flops 4294967296 | bytes 17825792 | tf_op jit(solution)/shard_map/dot_general | solution.py:833
  215.4 11.9 %all-gather.9.cloned.1.call-done = bf16[2048,1024]{1,0:T(8,128)(2,1)} async-done(((bf16[512,1024]{1,0:T(8,128)(2,1)}), bf16[2048,1024]{1,0:T(8,128)(2,1)}) %all-gather.9.cloned.1.call-update) | async-done | bytes 4194320 | tf_op jit(solution)/shard_map/all_gather | solution.py:889
  227.4 10.4 %multiply_multiply_fusion = (f32[512,2048]{1,0:T(8,128)S(1)}, f32[512,2048]{1,0:T(8,128)}) fusion(f32[512,4096]{1,0:T(8,128)} %copy-done.28, bf16[512,1024]{1,0:T(8,128)(2,1)} %pick_rows.6, bf16[2048,1024]{1,0:T(8,128)(2,1)} %all-gather.9.cloned.1.call-done), kind=kOutput, calls=%fused_computation.16 | convolution fusion | flops 2160066560 | bytes 22020096 | tf_op jit(solution)/shard_map/dot_general | solution.py:928
  247.3 8.0 %multiply_reduce_fusion.3 = (f32[1024]{0:T(1024)}, f32[512]{0:T(512)S(1)}, f32[512,1024]{1,0:T(8,128)S(1)}) fusion(f32[512,1024]{1,0:T(8,128)S(1)} %copy-done.30, f32[512]{0:T(512)S(1)} %fusion.156, f32[1024]{0:T(1024)S(1)} %bitcast.174, bf16[512,4096]{1,0:T(8,128)(2,1)S(1)} %add_convert_fusion, bf16[1024,4096]{1,0:T(8,128)(2,1)} %all-gather.7.cloned.1.call-done), kind=kOutput, calls=%fused_computation.94 | convolution fusion | flops 4298111488 | bytes 16789504 | tf_op jit(solution)/shard_map/dot_general | solution.py:928
  255.9 16.6 %collective-permute-done.15 = bf16[512,1024]{1,0:T(8,128)(2,1)S(1)} collective-permute-done((bf16[512,1024]{1,0:T(8,128)(2,1)}, bf16[512,1024]{1,0:T(8,128)(2,1)S(1)}, u32[]{:S(2)}, u32[]{:S(2)}) %collective-permute-start.15) | collective-permute-done | bytes 1048608 | tf_op jit(solution)/shard_map/ppermute | solution.py:562
  283.2 6.1 fusion.177
  290.2 17.3 %collective-permute-done.19 = bf16[256,2048]{1,0:T(8,128)(2,1)S(1)} collective-permute-done((bf16[256,2048]{1,0:T(8,128)(2,1)S(1)}, bf16[256,2048]{1,0:T(8,128)(2,1)S(1)}, u32[]{:S(2)}, u32[]{:S(2)}) %collective-permute-start.19) | collective-permute-done | bytes 1048608 | tf_op jit(solution)/shard_map/ppermute | solution.py:562
  320.8 16.7 %attention_backward.1 = (bf16[512,512]{1,0:T(8,128)(2,1)}, bf16[512,256]{1,0:T(8,128)(2,1)}) custom-call(s32[1]{0:T(128)} %bitcast.12.limit_ref, f32[512,4096]{1,0:T(8,128)} %fusion.181.q_ref.k_ref.v_ref.u_ref, f32[512,4096]{1,0:T(8,128)} %fusion.181.q_ref.k_ref.v_ref.u_ref, f32[512,4096]{1,0:T(8,128)} %fusion.181.q_ref.k_ref.v_ref.u_ref, ...), custom_call_target="tpu_custom_call" | custom-call | tf_op jit(solution)/shard_map/attention_backward/pallas_call | solution.py:307
  363.5 14.1 %ssd_backward.1 = (f32[512,1536]{1,0:T(8,128)}, f32[512,256]{1,0:T(8,128)}) custom-call(s32[1]{0:T(128)} %bitcast.12.limit_ref, bf16[512,1792]{1,0:T(8,128)(2,1)} %get-tuple-element.190.c_ref.b_ref.x_ref.low_ref, bf16[512,1792]{1,0:T(8,128)(2,1)} %get-tuple-element.190.c_ref.b_ref.x_ref.low_ref, ...), custom_call_target="tpu_custom_call" | custom-call | tf_op jit(solution)/shard_map/ssd_backward/pallas_call | solution.py:158
  398.7 20.6 %conv_backward.1 = (bf16[512,1792]{1,0:T(8,128)(2,1)}, f32[8,1792]{1,0:T(8,128)}, f32[512,128]{1,0:T(8,128)}) custom-call(f32[512,4096]{1,0:T(8,128)} %fusion.181.q_ref.k_ref.v_ref.u_ref, s32[512,1]{1,0:T(8,128)} %copy.85.place_ref, f32[4,1792]{1,0:T(4,128)} %reshape.385.weight_ref, f32[1,1792]{1,0:T(1,128)} %reshape.386.bias_ref, ...), custom_call_target="tpu_custom_call" | custom-call | tf_op jit(solution)/shard_map/conv_backward/pallas_call | solution.py:462
  477.6 8.3 %fusion.34 = (f32[1024]{0:T(1024)S(1)}, f32[512]{0:T(512)S(1)}, f32[512,1024]{1,0:T(8,128)S(1)}) fusion(bf16[512,1024]{1,0:T(8,128)(2,1)S(1)} %copy-done.20, f32[512]{0:T(512)S(1)} %fusion.154, f32[1024]{0:T(1024)S(1)} %bitcast.171, f32[512,1024]{1,0:T(8,128)S(1)} %fusion.184, bf16[512,4096]{1,0:T(8,128)(2,1)S(1)} %copy-done.36, bf16[1024,4096]{1,0:T(8,128)(2,1)} %lay_rows.1), kind=kOutput, calls=%fused_computation.87 | convolution fusion | flops 4299160064 | bytes 17838080 | tf_op jit(solution)/shard_map/dot_general | solution.py:928
  534.4 12.0 %collective-permute-done.68 = f32[8,128]{1,0:T(8,128)S(1)} collective-permute-done((f32[8,128]{1,0:T(8,128)S(1)}, f32[8,128]{1,0:T(8,128)S(1)}, u32[]{:S(2)}, u32[]{:S(2)}) %collective-permute-start.68) | collective-permute-done | bytes 4128 | tf_op jit(solution)/shard_map/ppermute | solution.py:562
  552.7 7.2 %collective-permute-done.62 = bf16[32,1792]{1,0:T(8,128)(2,1)} collective-permute-done((bf16[32,1792]{1,0:T(8,128)(2,1)S(1)}, bf16[32,1792]{1,0:T(8,128)(2,1)}, u32[]{:S(2)}, u32[]{:S(2)}) %collective-permute-start.62) | collective-permute-done | bytes 114720 | tf_op jit(solution)/shard_map/ppermute | solution.py:562
  575.3 9.5 %collective-permute-done.76 = f32[8,128]{1,0:T(8,128)S(1)} collective-permute-done((f32[8,128]{1,0:T(8,128)S(1)}, f32[8,128]{1,0:T(8,128)S(1)}, u32[]{:S(2)}, u32[]{:S(2)}) %collective-permute-start.76) | collective-permute-done | bytes 4128 | tf_op jit(solution)/shard_map/ppermute | solution.py:562
  613.3 6.6 %collective-permute-done.78.refs_3_ = bf16[128,1792]{1,0:T(8,128)(2,1)} collective-permute-done((bf16[128,1792]{1,0:T(8,128)(2,1)S(1)}, bf16[128,1792]{1,0:T(8,128)(2,1)}, u32[]{:S(2)}, u32[]{:S(2)}) %collective-permute-start.78) | collective-permute-done | bytes 458784 | tf_op jit(solution)/shard_map/ppermute | solution.py:562
  (613 shorter events, 329.6 us)
Async XLA Ops:
  7.2 162.9 %all-gather.5.cloned.1.call-start = ((), (), s32[]{:S(2)}) async-start(), calls=%async_computation | async-start | bytes 5242880 | tf_op jit(solution)/shard_map/all_gather | solution.py:884
  7.2 36.0 %collective-permute-start.1 = (bf16[256,4096]{1,0:T(8,128)(2,1)}, bf16[256,4096]{1,0:T(8,128)(2,1)S(1)}, u32[]{:S(2)}, u32[]{:S(2)}) collective-permute-start(bf16[256,4096]{1,0:T(8,128)(2,1)} %refs_0_.2), channel_id=1, source_target_pairs={{0,1},{1,0},{2,3},{3,2},{4,5},{5,4},{6,7},{7,6},{8,9},{9,8},{10,11... | collective-permute-start | bytes 6291464 | tf_op jit(solution)/shard_map/ppermute | solution.py:562
  43.3 28.4 %collective-permute-start.4 = (bf16[128,4096]{1,0:T(8,128)(2,1)S(1)}, bf16[128,4096]{1,0:T(8,128)(2,1)S(1)}, u32[]{:S(2)}, u32[]{:S(2)}) collective-permute-start(bf16[128,4096]{1,0:T(8,128)(2,1)S(1)} %collective-permute-done.refs_2_), channel_id=1, source_target_pairs={{0,1},{1,0},{2,3},{3,2},{4,5},{5,4},{6,7},{7,6},{8,9},{9,8},{10,11... | collective-permute-start | bytes 3145736 | tf_op jit(solution)/shard_map/ppermute | solution.py:562
  45.3 29.3 %collective-permute-start.6 = (bf16[512,1024]{1,0:T(8,128)(2,1)}, bf16[512,1024]{1,0:T(8,128)(2,1)}, u32[]{:S(2)}, u32[]{:S(2)}) collective-permute-start(bf16[512,1024]{1,0:T(8,128)(2,1)} %refs_0_.1), channel_id=1, source_target_pairs={{0,2},{1,3},{2,0},{3,1},{4,6},{5,7},{6,4},{7,5},{8,10},{9,11},{10,... | collective-permute-start | bytes 3145736 | tf_op jit(solution)/shard_map/ppermute | solution.py:562
  74.7 116.6 %all-gather.7.cloned.1.call-start = ((), (), s32[]{:S(2)}) async-start(), calls=%async_computation.1 | async-start | bytes 10485760 | tf_op jit(solution)/shard_map/all_gather | solution.py:885
  75.4 152.0 %all-gather.9.cloned.1.call-start = ((), (), s32[]{:S(2)}) async-start(), calls=%async_computation.2 | async-start | bytes 5242880 | tf_op jit(solution)/shard_map/all_gather | solution.py:889
  81.2 29.3 %collective-permute-start.11 = (bf16[512,1024]{1,0:T(8,128)(2,1)}, bf16[512,1024]{1,0:T(8,128)(2,1)S(1)}, u32[]{:S(2)}, u32[]{:S(2)}) collective-permute-start(bf16[512,1024]{1,0:T(8,128)(2,1)} %refs_0_.3), channel_id=1, source_target_pairs={{0,1},{1,0},{2,3},{3,2},{4,5},{5,4},{6,7},{7,6},{8,9},{9,8},{10,11... | collective-permute-start | bytes 3145736 | tf_op jit(solution)/shard_map/ppermute | solution.py:562
  81.4 47.8 %collective-permute-start.10 = (bf16[512,1024]{1,0:T(8,128)(2,1)}, bf16[512,1024]{1,0:T(8,128)(2,1)}, u32[]{:S(2)}, u32[]{:S(2)}) collective-permute-start(bf16[512,1024]{1,0:T(8,128)(2,1)} %refs_0_.3), channel_id=1, source_target_pairs={{0,2},{1,3},{2,0},{3,1},{4,6},{5,7},{6,4},{7,5},{8,10},{9,11},{10,... | collective-permute-start | bytes 3145736 | tf_op jit(solution)/shard_map/ppermute | solution.py:562
  91.3 420.8 %all-gather.11.cloned.1.call-start = ((), (), s32[]{:S(2)}) async-start(), calls=%async_computation.3 | async-start | bytes 5242880 | tf_op jit(solution)/shard_map/all_gather | solution.py:953
  130.4 72.9 %collective-permute-start.12 = (bf16[512,1024]{1,0:T(8,128)(2,1)}, bf16[512,1024]{1,0:T(8,128)(2,1)}, u32[]{:S(2)}, u32[]{:S(2)}) collective-permute-start(bf16[512,1024]{1,0:T(8,128)(2,1)} %collective-permute-done.10.refs_1_), channel_id=1, source_target_pairs={{0,1},{1,0},{2,3},{3,2},{4,5},{5,4},{6,7},{7,6},{8,9},{9,8},{10,11... | collective-permute-start | bytes 3145736 | tf_op jit(solution)/shard_map/ppermute | solution.py:562
  212.1 28.6 %collective-permute-start.13 = (bf16[512,1024]{1,0:T(8,128)(2,1)}, bf16[512,1024]{1,0:T(8,128)(2,1)}, u32[]{:S(2)}, u32[]{:S(2)}) collective-permute-start(bf16[512,1024]{1,0:T(8,128)(2,1)} %convolution_convert_fusion.11), channel_id=1, source_target_pairs={{0,1},{1,0},{2,3},{3,2},{4,5},{5,4},{6,7},{7,6},{8,9},{9,8},{10,11... | collective-permute-start | bytes 3145736 | tf_op jit(solution)/shard_map/ppermute | solution.py:562
  347.9 29.8 %collective-permute-start.31 = (bf16[256,2304]{1,0:T(8,128)(2,1)}, bf16[256,2304]{1,0:T(8,128)(2,1)}, u32[]{:S(2)}, u32[]{:S(2)}) collective-permute-start(bf16[256,2304]{1,0:T(8,128)(2,1)} %convolution_convert_fusion.1), channel_id=1, source_target_pairs={{0,1},{1,0},{2,3},{3,2},{4,5},{5,4},{6,7},{7,6},{8,9},{9,8},{10,11... | collective-permute-start | bytes 3538952 | tf_op jit(solution)/shard_map/ppermute | solution.py:562
  347.9 29.8 %collective-permute-start.32 = (bf16[256,2304]{1,0:T(8,128)(2,1)}, bf16[256,2304]{1,0:T(8,128)(2,1)}, u32[]{:S(2)}, u32[]{:S(2)}) collective-permute-start(bf16[256,2304]{1,0:T(8,128)(2,1)} %convolution_convert_fusion), channel_id=1, source_target_pairs={{0,1},{1,0},{2,3},{3,2},{4,5},{5,4},{6,7},{7,6},{8,9},{9,8},{10,11... | collective-permute-start | bytes 3538952 | tf_op jit(solution)/shard_map/ppermute | solution.py:562
  382.5 41.2 %collective-permute-start.34 = (bf16[1,32,2048]{2,1,0:T(8,128)(2,1)}, bf16[1,32,2048]{2,1,0:T(8,128)(2,1)}, u32[]{:S(2)}, u32[]{:S(2)}) collective-permute-start(bf16[1,32,2048]{2,1,0:T(8,128)(2,1)} %constant_dynamic-slice_fusion.4), channel_id=1, source_target_pairs={{0,16},{4,20},{8,24},{12,28},{16,0},{20,4},{24,8},{28,12},{1,17},{... | collective-permute-start | bytes 393224 | tf_op jit(solution)/shard_map/ppermute | solution.py:562
  384.5 39.2 %collective-permute-start.33 = (bf16[64,1024]{1,0:T(8,128)(2,1)S(1)}, bf16[64,1024]{1,0:T(8,128)(2,1)}, u32[]{:S(2)}, u32[]{:S(2)}) collective-permute-start(bf16[64,1024]{1,0:T(8,128)(2,1)S(1)} %fusion.104), channel_id=1, source_target_pairs={{0,16},{4,20},{8,24},{12,28},{16,0},{20,4},{24,8},{28,12},{1,17},{... | collective-permute-start | bytes 393224 | tf_op jit(solution)/shard_map/ppermute | solution.py:562
  389.6 38.0 %collective-permute-start.37 = (bf16[256,2304]{1,0:T(8,128)(2,1)}, bf16[256,2304]{1,0:T(8,128)(2,1)}, u32[]{:S(2)}, u32[]{:S(2)}) collective-permute-start(bf16[256,2304]{1,0:T(8,128)(2,1)} %fusion.3), channel_id=1, source_target_pairs={{0,2},{1,3},{2,0},{3,1},{4,6},{5,7},{6,4},{7,5},{8,10},{9,11},{10,... | collective-permute-start | bytes 3538952 | tf_op jit(solution)/shard_map/ppermute | solution.py:562
  391.1 32.6 %collective-permute-start.35 = (bf16[2,32,2048]{2,1,0:T(8,128)(2,1)}, bf16[2,32,2048]{2,1,0:T(8,128)(2,1)}, u32[]{:S(2)}, u32[]{:S(2)}) collective-permute-start(bf16[2,32,2048]{2,1,0:T(8,128)(2,1)} %dynamic-slice_bitcast_fusion.2), channel_id=1, source_target_pairs={{0,8},{4,12},{8,0},{12,4},{16,24},{20,28},{24,16},{28,20},{1,9},{5... | collective-permute-start | bytes 786440 | tf_op jit(solution)/shard_map/ppermute | solution.py:562
  394.3 29.4 %collective-permute-start.36 = (bf16[256,1024]{1,0:T(8,128)(2,1)S(1)}, bf16[256,1024]{1,0:T(8,128)(2,1)}, u32[]{:S(2)}, u32[]{:S(2)}) collective-permute-start(bf16[256,1024]{1,0:T(8,128)(2,1)S(1)} %fusion.50), channel_id=1, source_target_pairs={{0,4},{4,0},{8,12},{12,8},{16,20},{20,16},{24,28},{28,24},{1,5},{5... | collective-permute-start | bytes 1572872 | tf_op jit(solution)/shard_map/ppermute | solution.py:562
  469.9 28.6 %collective-permute-start.45 = (bf16[256,1024]{1,0:T(8,128)(2,1)S(1)}, bf16[256,1024]{1,0:T(8,128)(2,1)S(1)}, u32[]{:S(2)}, u32[]{:S(2)}) collective-permute-start(bf16[256,1024]{1,0:T(8,128)(2,1)S(1)} %pad_maximum_fusion.6.refs_0_), channel_id=1, source_target_pairs={{0,4},{4,0},{8,12},{12,8},{16,20},{20,16},{24,28},{28,24},{1,5},{5... | collective-permute-start | bytes 1572872 | tf_op jit(solution)/shard_map/ppermute | solution.py:562
  520.4 47.0 %collective-permute-start.67 = (bf16[512,1024]{1,0:T(8,128)(2,1)}, bf16[512,1024]{1,0:T(8,128)(2,1)}, u32[]{:S(2)}, u32[]{:S(2)}) collective-permute-start(bf16[512,1024]{1,0:T(8,128)(2,1)} %fusion.37.refs_0_), channel_id=1, source_target_pairs={{0,1},{1,0},{2,3},{3,2},{4,5},{5,4},{6,7},{7,6},{8,9},{9,8},{10,11... | collective-permute-start | bytes 3145736 | tf_op jit(solution)/shard_map/ppermute | solution.py:562
  520.5 47.6 %collective-permute-start.66 = (bf16[512,1024]{1,0:T(8,128)(2,1)}, bf16[512,1024]{1,0:T(8,128)(2,1)}, u32[]{:S(2)}, u32[]{:S(2)}) collective-permute-start(bf16[512,1024]{1,0:T(8,128)(2,1)} %fusion.37.refs_0_), channel_id=1, source_target_pairs={{0,2},{1,3},{2,0},{3,1},{4,6},{5,7},{6,4},{7,5},{8,10},{9,11},{10,... | collective-permute-start | bytes 3145736 | tf_op jit(solution)/shard_map/ppermute | solution.py:562
  532.5 34.9 %collective-permute-start.59 = (bf16[128,2048]{1,0:T(8,128)(2,1)S(1)}, bf16[128,2048]{1,0:T(8,128)(2,1)S(1)}, u32[]{:S(2)}, u32[]{:S(2)}) collective-permute-start(bf16[128,2048]{1,0:T(8,128)(2,1)S(1)} %pad_maximum_fusion.8.refs_2_), channel_id=1, source_target_pairs={{0,4},{4,0},{8,12},{12,8},{16,20},{20,16},{24,28},{28,24},{1,5},{5... | collective-permute-start | bytes 1572872 | tf_op jit(solution)/shard_map/ppermute | solution.py:562
  568.1 29.7 %collective-permute-start.75 = (bf16[512,1024]{1,0:T(8,128)(2,1)}, bf16[512,1024]{1,0:T(8,128)(2,1)S(1)}, u32[]{:S(2)}, u32[]{:S(2)}) collective-permute-start(bf16[512,1024]{1,0:T(8,128)(2,1)} %collective-permute-done.66.refs_1_), channel_id=1, source_target_pairs={{0,1},{1,0},{2,3},{3,2},{4,5},{5,4},{6,7},{7,6},{8,9},{9,8},{10,11... | collective-permute-start | bytes 3145736 | tf_op jit(solution)/shard_map/ppermute | solution.py:562
  568.8 29.0 %collective-permute-start.70 = (bf16[64,2304]{1,0:T(8,128)(2,1)}, bf16[64,2304]{1,0:T(8,128)(2,1)}, u32[]{:S(2)}, u32[]{:S(2)}) collective-permute-start(bf16[64,2304]{1,0:T(8,128)(2,1)} %pad_maximum_fusion.11), channel_id=1, source_target_pairs={{0,8},{4,12},{8,0},{12,4},{16,24},{20,28},{24,16},{28,20},{1,9},{5... | collective-permute-start | bytes 884744 | tf_op jit(solution)/shard_map/ppermute | solution.py:562
  (189 other events, 2337.1 us)
Sparse Core Ops, SparseCore 0:
  74.8 56.2 all-gather.4
  132.6 58.5 all-gather.6
  192.8 34.5 all-gather.8
  398.8 41.5 all-gather.10

commit v4 on v3

--- a/solution.py
+++ b/solution.py
@@ -102,18 +102,20 @@
     )(limit, low, low, low, *tables)
 
 
-def ssd_backward_kernel(
-    limit_ref, c_ref, b_ref, x_ref, dy_ref, cum_col_ref, cum_row_ref, z_ref, gbc_ref, inter, bias, total
-):
+def ssd_backward_kernel(part, limit_ref, c_ref, b_ref, x_ref, dy_ref, cum_col_ref, cum_row_ref, *refs):
+    if part == 0:
+        z_ref, total, inter, bias = refs
+    else:
+        held_ref, z_ref, total, gbc_ref, inter, bias = refs
     count = c_ref.shape[0]
 
     @pl.when(pl.program_id(0) == 0)
     def _():
         inter[...] = contract_last(c_ref[...], b_ref[...])
         bias[...] = causal_bias(limit_ref[0], count, 0, count)
-        total[...] = jnp.zeros_like(total)
-
-    step = pl.program_id(0)
+        total[...] = jnp.zeros_like(total) if part == 0 else held_ref[...]
+
+    step = pl.program_id(0) + part * (SSM_HEADS // QUAD // 2)
     cum_col = four_lanes(cum_col_ref[...], step)
     cum_row = cum_row_ref[pl.ds(pl.multiple_of(step // 2 * 8, 8), 8), :]
     cum_row = jnp.where(step % 2 == 0, cum_row[:QUAD], cum_row[QUAD:])
@@ -132,36 +134,45 @@
                 decay = jnp.exp(gap + bias[rows, :seen])
                 mixer = (inter[rows, :seen] * decay).astype(jnp.bfloat16)
                 grad_mixer = contract_last(sides[half][rows], x_pair[:seen])
-                part = grad_mixer * decay
-                grad = part if grad is None else grad + part
-                part = contract_first(mixer, sides[half][rows])
-                back = part if back is None else back + part
+                piece = grad_mixer * decay
+                grad = piece if grad is None else grad + piece
+                piece = contract_first(mixer, sides[half][rows])
+                back = piece if back is None else back + piece
             total[rows, :seen] += grad
             if seen == count:
                 z_ref[:, lanes] = back
             else:
                 z_ref[:seen, lanes] += back
 
-    @pl.when(pl.program_id(0) == pl.num_programs(0) - 1)
-    def _():
-        low = total[...].astype(jnp.bfloat16)
-        gbc_ref[:, :STATE] = contract_first(low, c_ref[...])
-        gbc_ref[:, STATE:] = jnp.dot(low, b_ref[...], preferred_element_type=jnp.float32)
-
-
-def ssd_backward(limit, low, grad_y, tables):
+    if part == 1:
+
+        @pl.when(pl.program_id(0) == pl.num_programs(0) - 1)
+        def _():
+            low = total[...].astype(jnp.bfloat16)
+            gbc_ref[:, :STATE] = contract_first(low, c_ref[...])
+            gbc_ref[:, STATE:] = jnp.dot(low, b_ref[...], preferred_element_type=jnp.float32)
+
+
+def ssd_backward(part, limit, low, grad_y, tables, held=None):
     count = low.shape[0]
-    steps = SSM_HEADS // QUAD
+    steps = SSM_HEADS // QUAD // 2
     b_spec = pl.BlockSpec((count, STATE), lambda i: (0, INNER // STATE))
     c_spec = pl.BlockSpec((count, STATE), lambda i: (0, INNER // STATE + 1))
-    quad = pl.BlockSpec((count, QUAD * HEAD_SIZE), lambda i: (0, i))
+    quad = pl.BlockSpec((count, QUAD * HEAD_SIZE), lambda i: (0, i + part * steps))
+    square = pl.BlockSpec((count, count), lambda i: (0, 0))
+    out_shape = [
+        jax.ShapeDtypeStruct((count, INNER // 2), jnp.float32),
+        jax.ShapeDtypeStruct((count, count), jnp.float32),
+    ]
+    out_specs = [pl.BlockSpec((count, QUAD * HEAD_SIZE), lambda i: (0, i)), square]
+    if part == 1:
+        out_shape.append(jax.ShapeDtypeStruct((count, 2 * STATE), jnp.float32))
+        out_specs.append(pl.BlockSpec((count, 2 * STATE), lambda i: (0, 0)))
+    more = [] if held is None else [held]
     return pl.pallas_call(
-        ssd_backward_kernel,
+        partial(ssd_backward_kernel, part),
         grid=(steps,),
-        out_shape=(
-            jax.ShapeDtypeStruct((count, INNER), jnp.float32),
-            jax.ShapeDtypeStruct((count, 2 * STATE), jnp.float32),
-        ),
+        out_shape=tuple(out_shape),
         in_specs=[
             pl.BlockSpec(memory_space=pltpu.SMEM),
             c_spec,
@@ -170,11 +181,12 @@
             quad,
             pl.BlockSpec((count, SIDE), lambda i: (0, 0)),
             pl.BlockSpec((SIDE, count), lambda i: (0, 0)),
-        ],
-        out_specs=(quad, pl.BlockSpec((count, 2 * STATE), lambda i: (0, 0))),
-        scratch_shapes=[pltpu.VMEM((count, count), jnp.float32)] * 3,
+        ]
+        + [square] * len(more),
+        out_specs=tuple(out_specs),
+        scratch_shapes=[pltpu.VMEM((count, count), jnp.float32)] * 2,
         name="ssd_backward",
-    )(limit, low, low, low, grad_y, *tables)
+    )(limit, low, low, low, grad_y, *tables, *more)
 
 
 def turn(values, cosine, sine):
@@ -249,16 +261,10 @@
     )(limit, projected, projected, projected, cosine, sine)
 
 
-def attention_backward_kernel(
-    limit_ref, q_ref, k_ref, v_ref, cos_ref, sin_ref, go_ref, log_ref, gq_ref, gkv_ref, bias, gk, gv
-):
+def attention_backward_kernel(step, limit_ref, q_ref, k_ref, v_ref, cos_ref, sin_ref, go_ref, log_ref, *refs):
+    (gq_ref, gkv_ref), (bias, gk, gv) = refs[-5:-3], refs[-3:]
     count = k_ref.shape[0]
-    step = pl.program_id(0)
-
-    @pl.when(step == 0)
-    def _():
-        bias[...] = causal_bias(limit_ref[0], count, 0, count)
-
+    bias[...] = causal_bias(limit_ref[0], count, 0, count)
     cosine, sine = cos_ref[...], sin_ref[...]
     key = both_sides(turn(k_ref[...], cosine, sine), step)
     value = both_sides(v_ref[...], step)
@@ -292,34 +298,35 @@
         if place == 0:
             summed = turn(summed, cosine, -sine)
         lanes = slice(place * SIDE, (place + 1) * SIDE)
-        @pl.when(step == 0)
-        def _():
-            gkv_ref[:, lanes] = summed.astype(jnp.bfloat16)
-
-        @pl.when(step > 0)
-        def _():
-            gkv_ref[:, lanes] = jnp.where(mine, summed, gkv_ref[:, lanes].astype(jnp.float32)).astype(jnp.bfloat16)
-
-
-def attention_backward(limit, projected, cosine, sine, grad_out, logs_in):
+        if step > 0:
+            summed = jnp.where(mine, summed, refs[0][:, lanes].astype(jnp.float32))
+        gkv_ref[:, lanes] = summed.astype(jnp.bfloat16)
+
+
+def attention_backward(step, limit, projected, cosine, sine, grad_out, logs_in, other=None):
     count = projected.shape[0]
-    wide, whole, keys, values, logs = attention_specs(count)
+    _, whole, keys, values, _ = attention_specs(count)
+    at = lambda spec: pl.BlockSpec(spec.block_shape, lambda i: spec.index_map(step))
+    wide, _, _, _, logs = attention_specs(count)
+    both = pl.BlockSpec((count, 2 * SIDE), lambda i: (0, 0))
+    more = [] if other is None else [other]
     return pl.pallas_call(
-        attention_backward_kernel,
-        grid=(KEY_VALUE_HEADS,),
+        partial(attention_backward_kernel, step),
+        grid=(1,),
         out_shape=(
-            jax.ShapeDtypeStruct((count, QUERY_HEADS * HEAD_SIZE), jnp.bfloat16),
+            jax.ShapeDtypeStruct((count, 2 * SIDE), jnp.bfloat16),
             jax.ShapeDtypeStruct((count, 2 * SIDE), jnp.bfloat16),
         ),
-        in_specs=[pl.BlockSpec(memory_space=pltpu.SMEM), wide, keys, values, whole, whole, wide, logs],
-        out_specs=(wide, pl.BlockSpec((count, 2 * SIDE), lambda i: (0, 0))),
+        in_specs=[pl.BlockSpec(memory_space=pltpu.SMEM), at(wide), keys, values, whole, whole, at(wide), at(logs)]
+        + [both] * len(more),
+        out_specs=(both, both),
         scratch_shapes=[
             pltpu.VMEM((count, count), jnp.float32),
             pltpu.VMEM((count, SIDE), jnp.float32),
             pltpu.VMEM((count, SIDE), jnp.float32),
         ],
         name="attention_backward",
-    )(limit, projected, projected, projected, cosine, sine, grad_out, logs_in)
+    )(limit, projected, projected, projected, cosine, sine, grad_out, logs_in, *more)
 
 
 BLOCK = QUAD * HEAD_SIZE
@@ -354,9 +361,9 @@
             low_ref[rows, lanes] = (out * jnp.where(lane < HEAD_SIZE, first, second)).astype(jnp.bfloat16)
 
 
-def conv_specs(count, width):
-    column = lambda i: (0, i)
-    first = (QUERY_KEY_VALUE + INNER) // BLOCK
+def conv_specs(count, begin=0):
+    column = lambda i: (0, i + begin)
+    first = (QUERY_KEY_VALUE + INNER) // BLOCK + begin
     return (
         pl.BlockSpec((count, BLOCK), lambda i: (0, first + i)),
         pl.BlockSpec((count, 1), lambda i: (0, 0)),
@@ -369,7 +376,7 @@
 
 def conv_forward(projected, position, weight, bias, step_quads):
     count, width = projected.shape[0], weight.shape[1]
-    u, place, taps, row, quads, block = conv_specs(count, width)
+    u, place, taps, row, quads, block = conv_specs(count)
     return pl.pallas_call(
         conv_forward_kernel,
         grid=(width // BLOCK,),
@@ -395,18 +402,18 @@
 
 
 def conv_backward_kernel(
-    u_ref, place_ref, weight_ref, bias_ref, step_ref, skip_ref, z_ref, gy_ref, y_ref, low_ref, gbc_ref,
+    first, u_ref, place_ref, weight_ref, bias_ref, step_ref, skip_ref, z_ref, gy_ref, y_ref, low_ref, gbc_ref,
     gu_ref, gw_ref, heads_ref, held, grads,
 ):
     count = u_ref.shape[0]
-    step = pl.program_id(0)
-    inner = step < pl.num_programs(0) - 1
+    step = pl.program_id(0) + first
+    inner = step < INNER // BLOCK
     scale = four_lanes(step_ref[...], step)
     held[:HALO, :] = jnp.zeros((HALO, BLOCK), jnp.float32)
     held[HALO:, :] = u_ref[...]
     lane = lax.broadcasted_iota(jnp.int32, (TILE, SIDE), 1)
 
-    @pl.when(step == 0)
+    @pl.when(pl.program_id(0) == 0)
     def _():
         heads_ref[...] = jnp.zeros_like(heads_ref)
 
@@ -453,28 +460,35 @@
             gu_ref[top : top + TILE, lanes] = total.astype(jnp.bfloat16)
 
 
-def conv_backward(projected, position, weight, bias, step_quads, skip, z, grad_y, y, low, grad_bc):
-    count, width = projected.shape[0], weight.shape[1]
-    u, place, taps, row, quads, block = conv_specs(count, width)
+def conv_backward(part, projected, position, weight, bias, step_lanes, skip, z, grad_y, y, low, grad_bc):
+    count = projected.shape[0]
+    cut = INNER // BLOCK // 2
+    begin, blocks = (0, cut) if part == 0 else (cut, weight.shape[1] // BLOCK - cut)
+    u, place, taps, row, lanes, block = conv_specs(count, begin)
     last = INNER // BLOCK - 1
-    inner = pl.BlockSpec((count, BLOCK), lambda i: (0, jnp.minimum(i, last)))
-    skip_row = pl.BlockSpec((1, BLOCK), lambda i: (0, jnp.minimum(i, last)))
+    inner = pl.BlockSpec((count, BLOCK), lambda i: (0, jnp.minimum(i + begin, last)))
+    half = pl.BlockSpec((count, BLOCK), lambda i: (0, jnp.minimum(i, cut - 1)))
+    skip_row = pl.BlockSpec((1, BLOCK), lambda i: (0, jnp.minimum(i + begin, last)))
     return pl.pallas_call(
-        conv_backward_kernel,
-        grid=(width // BLOCK,),
+        partial(conv_backward_kernel, begin),
+        grid=(blocks,),
         out_shape=(
-            jax.ShapeDtypeStruct((count, width), jnp.bfloat16),
-            jax.ShapeDtypeStruct((8, width), jnp.float32),
+            jax.ShapeDtypeStruct((count, blocks * BLOCK), jnp.bfloat16),
+            jax.ShapeDtypeStruct((8, blocks * BLOCK), jnp.float32),
             jax.ShapeDtypeStruct((count, SIDE), jnp.float32),
         ),
-        in_specs=[u, place, taps, row, quads, skip_row, inner, inner, inner, block, pl.BlockSpec((count, BLOCK), lambda i: (0, 0))],
-        out_specs=(block, pl.BlockSpec((8, BLOCK), lambda i: (0, i)), pl.BlockSpec((count, SIDE), lambda i: (0, 0))),
+        in_specs=[u, place, taps, row, lanes, skip_row, half, inner, inner, block, pl.BlockSpec((count, BLOCK), lambda i: (0, 0))],
+        out_specs=(
+            pl.BlockSpec((count, BLOCK), lambda i: (0, i)),
+            pl.BlockSpec((8, BLOCK), lambda i: (0, i)),
+            pl.BlockSpec((count, SIDE), lambda i: (0, 0)),
+        ),
         scratch_shapes=[
             pltpu.VMEM((HALO + count, BLOCK), jnp.float32),
             pltpu.VMEM((TAPS, count + HALO, BLOCK), jnp.float32),
         ],
         name="conv_backward",
-    )(projected, position[:, None], weight, bias[None], step_quads, skip, z, grad_y, y, low, grad_bc)
+    )(projected, position[:, None], weight, bias[None], step_lanes, skip, z, grad_y, y, low, grad_bc)
 
 
 def pick_kernel(shift_ref, wanted_ref, *refs):
@@ -529,18 +543,15 @@
     )(places // 16, *pieces)
 
 
-def widen_kernel(parts, columns, place_ref, *refs):
+def widen_kernel(columns, near_ref, *refs):
     out_ref = refs[-1]
     for n, block in enumerate(refs[:-1]):
-        rows = block.shape[0] // parts
-        left = columns[n // 2]
-        for k in range(parts):
-            start = pl.multiple_of(place_ref[(n % 2) * parts + k] * rows, rows)
-            piece = block[k * rows : (k + 1) * rows, :].astype(jnp.float32)
-            out_ref[pl.ds(start, rows), left : left + block.shape[1]] = piece
-
-
-def widen_rows(chunks, places):
+        rows, left = block.shape[0], columns[n // 2]
+        start = pl.multiple_of((near_ref[0] ^ (n % 2)) * rows, rows)
+        out_ref[pl.ds(start, rows), left : left + block.shape[1]] = block[...].astype(jnp.float32)
+
+
+def widen_rows(chunks, near):
     flat = [block for chunk in chunks for block in chunk]
     columns, left = [], 0
     for chunk in chunks:
@@ -549,12 +560,12 @@
     rows = 2 * chunks[0][0].shape[0]
     vmem = pl.BlockSpec(memory_space=pltpu.VMEM)
     return pl.pallas_call(
-        partial(widen_kernel, places.shape[0] // 2, tuple(columns)),
+        partial(widen_kernel, tuple(columns)),
         out_shape=jax.ShapeDtypeStruct((rows, left), jnp.float32),
         in_specs=[pl.BlockSpec(memory_space=pltpu.SMEM)] + [vmem] * len(flat),
         out_specs=vmem,
         name="widen_rows",
-    )(places, *flat)
+    )(near, *flat)
 
 
 def swap(values, axis, mask):
@@ -578,22 +589,26 @@
         self.live = []
 
     def add(self, stream):
-        slot = {"stream": stream, "sent": None, "result": None, "done": False}
+        slot = {"stream": stream, "sent": None, "left": 0, "result": None, "done": False}
         self.live.append(slot)
         self._advance(slot, None)
         return slot
 
     def _advance(self, slot, value):
         try:
-            slot["sent"] = slot["stream"].send(value)
+            sent = slot["stream"].send(value)
+            slot["sent"], slot["left"] = sent if isinstance(sent, tuple) else (sent, 1)
         except StopIteration as stop:
             slot["result"] = stop.value
             slot["sent"] = None
             slot["done"] = True
             self.live.remove(slot)
 
-    def step(self, values=None, slots=None):
+    def step(self, values=None, slots=None, force=False):
         slots = [slot for slot in (self.live if slots is None else slots) if not slot["done"]]
+        for slot in slots:
+            slot["left"] -= 1
+        slots = [slot for slot in slots if slot["left"] <= 0 or force]
         values, sent = lax.optimization_barrier((values, [slot["sent"] for slot in slots]))
         for slot, came in zip(slots, sent):
             self._advance(slot, came)
@@ -605,7 +620,7 @@
         return values
 
 
-def rows_stream(piece):
+def rows_stream(piece, wait=1):
     shard = lax.axis_index("shard")
     held = [(0, piece)]
     mask = lax.axis_size("shard") // 2
@@ -615,7 +630,7 @@
         send = [swap(p, "shard", mask) for _, p in held]
         if first:
             send.append(swap(piece, "shard", 1))
-        came = yield send
+        came = yield send, wait
         if first:
             near = came[-1]
             first = False
@@ -664,14 +679,11 @@
     return lax.dot_general(left, right, (((0,), (0,)), ((), ())), preferred_element_type=jnp.float32)
 
 
-def reduce_stream(left, right, direct=False):
+def reduce_stream(left, right, waits=(1, 1, 1, 1)):
     shards, replicas = lax.axis_size("shard"), lax.axis_size("rep")
     block = left.shape[1] // shards
-    rows = block // replicas
-    width = right.shape[1]
-    shard, replica = lax.axis_index("shard"), lax.axis_index("rep")
+    shard, near = lax.axis_index("shard"), lax.axis_index("rep") & 1
     core, far = shard & 1, shard >> 1
-    near, rest = replica & 1, replica >> 1
 
     def product(r, c, extras=(), half=None):
         start, size = ((far ^ r) * 2 + c) * block, block
@@ -685,55 +697,22 @@
         return total.astype(jnp.bfloat16)
 
     count = shards // 2
-    came = yield [swap(product(r, 1 - core), "shard", 1) for r in range(count)]
+    came = yield [swap(product(r, 1 - core), "shard", 1) for r in range(count)], waits[0]
     extras = [[c] for c in came]
     while count > 1:
         count //= 2
-        came = yield [swap(product(r, core, extras[r]), "shard", 2 * count) for r in range(count, 2 * count)]
+        came = yield [swap(product(r, core, extras[r]), "shard", 2 * count) for r in range(count, 2 * count)], waits[1]
         for n, c in enumerate(came):
             extras[n].append(c)
-    came = yield [swap(product(0, core, extras[0], 1 - near), "rep", 1)]
+    came = yield [swap(product(0, core, extras[0], 1 - near), "rep", 1)], waits[2]
     total = product(0, core, [*extras[0], came[0]], near)
-    if direct:
-        others = merge_order()[1:]
-        total = total.reshape(replicas // 2, rows, width)
-        came = yield [swap(take(total, rest ^ k, 0), "rep", 2 * k) for k in others]
-        total = add(take(total, rest, 0), *came)
-        came = yield [swap(total, "rep", 2 * k) for k in others]
-        mine = jnp.concatenate([total, *came], 0)
-        came = yield [swap(mine, "rep", 1)]
-        return mine, came[0]
-    mask = 1
-    while mask < replicas // 2:
-        flag = (rest // mask) % 2
-        total = total.reshape(-1, 2, rows, width)
-        came = yield [swap(take(total, 1 - flag, 1), "rep", 2 * mask)]
-        total = add(take(total, flag, 1), came[0])
+    mask = 2
+    while mask < replicas:
+        came = yield [swap(total, "rep", mask)], waits[3]
+        total = add(total, came[0])
         mask *= 2
-    mine = total.reshape(rows, width)
-    while mask > 1:
-        mask //= 2
-        came = yield [swap(mine, "rep", 2 * mask)]
-        mine = jnp.concatenate([mine, came[0]], 0)
-    came = yield [swap(mine, "rep", 1)]
-    return mine, came[0]
-
-
-def merge_order():
-    order = [0]
-    mask = lax.axis_size("rep") // 2
-    while mask > 1:
-        mask //= 2
-        order = order + [k ^ mask for k in order]
-    return order
-
-
-def piece_places():
-    replica = lax.axis_index("rep")
-    near, rest = replica & 1, replica >> 1
-    order = merge_order()
-    places = [(near ^ side) * len(order) + (rest ^ k) for side in range(2) for k in order]
-    return jnp.stack(places).astype(jnp.int32)
+    came = yield [swap(total, "rep", 1)]
+    return total, came[0]
 
 
 def butterfly_stream(total):
@@ -844,6 +823,15 @@
 def to_lanes(values, fill):
     count, width = values.shape
     return jnp.concatenate([values, jnp.full((count, SIDE - width), fill, values.dtype)], 1)
+
+
+WAITS = {
+    "down": (1, 2, 1, 1),
+    "gate": (1, 2, 1, 1),
+    "up": (1, 2, 1, 1),
+    "output": (1, 3, 1, 1),
+    "qkvz": (1, 3, 1, 1),
+}
 
 
 def on_device(
@@ -876,18 +864,15 @@
     slot_small = flow.add(small_stream(jnp.concatenate([a.reshape(-1) for a in small_args])))
     source, position, limit, target = group_tables(seq_lengths[0], owner_order[0], input_rows, shard)
     cosine, sine = rope_tables(position)
-    source, position, tokens, cosine, sine = flow.step((source, position, tokens, cosine, sine))
+    source, position, tokens, cosine, sine, w_output = flow.step((source, position, tokens, cosine, sine, w_output))
     slot_tokens = flow.add(rows_stream(tokens))
     source, position, w_output, w_gate_up, w_down, cotangent = flow.step(
         (source, position, w_output, w_gate_up, w_down, cotangent)
     )
     w_output_all = lax.all_gather(w_output, "shard", axis=0, tiled=True)
     w_gate_up_all = lax.all_gather(w_gate_up, "shard", axis=0, tiled=True)
-    source, position, w_down, cotangent = flow.until(
-        [slot_tokens, slot_input, slot_small], (source, position, w_down, cotangent)
-    )
     w_down_all = lax.all_gather(w_down, "shard", axis=0, tiled=True)
-    slot_cot = flow.add(rows_stream(cotangent))
+    source, position, cotangent = flow.until([slot_tokens, slot_input, slot_small], (source, position, cotangent))
 
     gain_attn_all, w_step_all, step_bias_all, decay_all, skip_all, conv_w_all, conv_b_all, gain_ssm_all, gain_ffn_all = (
         unpack_small(slot_small["result"], [a.shape for a in small_args], small_dims)
@@ -901,7 +886,8 @@
 
     normed = rms_norm(own, gain_attn_f).astype(jnp.bfloat16)
     projected = dot(normed, w_input_all)
-    projected, normed = flow.step((projected, normed))
+    projected, normed, cotangent = lax.optimization_barrier((projected, normed, cotangent))
+    slot_cot = flow.add(rows_stream(cotangent))
     step_pre = dot(normed, w_step_all) + f32(step_bias_all)
     step = jax.nn.softplus(step_pre)
     rate = -jnp.exp(f32(decay_all))
@@ -929,17 +915,17 @@
 
     slots = {}
     block_low = (middle + dot(hidden, w_down_all)).astype(jnp.bfloat16)
-    slots["down"] = [flow.add(reduce_stream(hidden, cot))]
+    slots["down"] = [flow.add(reduce_stream(hidden, cot, WAITS["down"]))]
     grad_hidden = back(cot, w_down_all)
     grad_gate_up = jax.vjp(swiglu, gate_up)[1](grad_hidden)[0].astype(jnp.bfloat16)
     grad_gate_up = flow.step(grad_gate_up)
     half = grad_gate_up.shape[1] // 2
-    slots["gate_up"] = [flow.add(reduce_stream(normed_ffn, grad_gate_up[:, :half]))]
+    slots["gate_up"] = [flow.add(reduce_stream(normed_ffn, grad_gate_up[:, :half], WAITS["gate"]))]
     grad_normed_ffn = back(grad_gate_up, w_gate_up_all)
     grad_middle_norm, grad_gain_ffn = jax.vjp(rms_norm, middle, gain_ffn_f)[1](grad_normed_ffn)
     grad_middle = f32(cot) + grad_middle_norm
     grad_middle, grad_gate_up = flow.step((grad_middle, grad_gate_up))
-    slots["gate_up"].append(flow.add(reduce_stream(normed_ffn, grad_gate_up[:, half:])))
+    slots["gate_up"].append(flow.add(reduce_stream(normed_ffn, grad_gate_up[:, half:], WAITS["up"])))
     middle_low = grad_middle.astype(jnp.bfloat16)
     grad_joined = back(middle_low, w_output_all)
     grad_attn = grad_joined[:, : QUERY_HEADS * HEAD_SIZE].astype(jnp.bfloat16)
@@ -947,22 +933,30 @@
     grad_ssm_y, grad_z, grad_gain_ssm = jax.vjp(gated_norm, ssm_y, gate_z, gain_ssm_f)[1](grad_ssm_out)
     grad_z_low = grad_z.astype(jnp.bfloat16)
     grad_y_low = grad_ssm_y.astype(jnp.bfloat16)
-    grad_ssm_y, grad_z_low, grad_attn, middle_low, grad_y_low = flow.step(
-        (grad_ssm_y, grad_z_low, grad_attn, middle_low, grad_y_low)
+    grad_ssm_y, grad_z_low, grad_attn, middle_low, grad_y_low, block_low = flow.step(
+        (grad_ssm_y, grad_z_low, grad_attn, middle_low, grad_y_low, block_low)
     )
+    slots["output"] = [flow.add(reduce_stream(joined, middle_low, WAITS["output"]))]
     block_all = lax.all_gather(block_low, "shard", axis=0, tiled=True)
-    slots["output"] = [flow.add(reduce_stream(joined, middle_low))]
-    grad_q, grad_kv = attention_backward(limit, projected, cosine, sine, grad_attn, logs)
-    grad_q, grad_kv, grad_y_low, grad_z_low = flow.step((grad_q, grad_kv, grad_y_low, grad_z_low))
-    qkvz = jnp.concatenate([grad_q, grad_kv, grad_z_low], 1)
-    slots["input"] = [flow.add(reduce_stream(normed, qkvz))]
-    back_x, grad_bc = ssd_backward(limit, low, grad_y_low, tables)
-    back_x, grad_bc = flow.step((back_x, grad_bc))
-    grad_u_low, grad_taps, head_parts = conv_backward(
-        projected, position, conv_w_f, conv_b_f, step_lanes, skip_lanes, back_x, grad_ssm_y, ssd_out, low, grad_bc
-    )
-    grad_u_low, head_parts = flow.step((grad_u_low, head_parts))
-    slots["input"].append(flow.add(reduce_stream(normed, grad_u_low, True)))
+    first = attention_backward(0, limit, projected, cosine, sine, grad_attn, logs)
+    first, grad_attn = flow.step((first, grad_attn))
+    second = attention_backward(1, limit, projected, cosine, sine, grad_attn, logs, first[1])
+    second, grad_y_low, grad_z_low = flow.step((second, grad_y_low, grad_z_low))
+    qkvz = jnp.concatenate([first[0], second[0], second[1], grad_z_low], 1)
+    slots["input"] = [flow.add(reduce_stream(normed, qkvz, WAITS["qkvz"]))]
+    upper = ssd_backward(0, limit, low, grad_y_low, tables)
+    upper, grad_y_low = flow.step((upper, grad_y_low))
+    lower = ssd_backward(1, limit, low, grad_y_low, tables, upper[1])
+    lower, upper = flow.step((lower, upper))
+    conv_args = (projected, position, conv_w_f, conv_b_f, step_lanes, skip_lanes)
+    conv_upper = conv_backward(0, *conv_args, upper[0], grad_ssm_y, ssd_out, low, lower[2])
+    conv_upper, lower = flow.step((conv_upper, lower))
+    conv_lower = conv_backward(1, *conv_args, lower[0], grad_ssm_y, ssd_out, low, lower[2])
+    conv_upper, conv_lower = flow.step((conv_upper, conv_lower))
+    grad_u_low = jnp.concatenate([conv_upper[0], conv_lower[0]], 1)
+    grad_taps = jnp.concatenate([conv_upper[1], conv_lower[1]], 1)
+    head_parts = conv_upper[2] + conv_lower[2]
+    slots["input"].append(flow.add(reduce_stream(normed, grad_u_low)))
     grad_projected = jnp.concatenate([qkvz, grad_u_low], 1)
     heads_of = lambda offset: head_parts[:, offset : offset + SSM_HEADS]
     grad_skip = jnp.sum(heads_of(64), 0)
@@ -990,13 +984,13 @@
     grad_normed = back(grad_projected, w_input_all) + back(step_low, w_step_all)
     grad_tokens_norm, grad_gain_attn = jax.vjp(rms_norm, own, gain_attn_f)[1](grad_normed)
     grad_low = (grad_middle + grad_tokens_norm).astype(jnp.bfloat16)
-    places = piece_places()
+    near_flag = (lax.axis_index("rep") & 1).reshape(1).astype(jnp.int32)
     held = {}
 
     def finish_ready():
         for name in slots:
             if name not in held and all(slot["done"] for slot in slots[name]):
-                held[name] = widen_rows([slot["result"] for slot in slots[name]], places)
+                held[name] = widen_rows([slot["result"] for slot in slots[name]], near_flag)
 
     grad_low, gain_late = flow.step((grad_low, grad_gain_attn.reshape(-1, SIDE)))
     slot_grad = flow.add(rows_stream(grad_low))

time: 646 us -> 598 us (0.926)
  waiting for transfers between devices: 198 us -> 159 us
  starting transfers between devices: 73.5 us -> 55.4 us
  local copies, waits for them, and re-layouts: 51.4 us -> 39.1 us
  matrix products: 119 us -> 131 us
  Pallas kernels: 126 us -> 136 us
    ppermute x82 -> x68, waiting for transfers between devices: 172 us -> 126 us  [swap(): return lax.ppermute(values, axis, [(i, i ^ mask) for i in range(count)])]
    ppermute x82 -> x68, starting transfers between devices: 72.9 us -> 55.3 us  [swap(): return lax.ppermute(values, axis, [(i, i ^ mask) for i in range(count)])]
    convert_element_type x6 -> x12, other arithmetic: 4.69 us -> 18.1 us  [add(): return total.astype(jnp.bfloat16)]
    concatenate x12 -> x0, other arithmetic: 10.8 us -> none  [the longest x10 7.48 us: reduce_stream(): mine = jnp.concatenate([mine, came[0]], 0)]
    dot_general x31, matrix products: 61.2 us -> 71.7 us  [transposed_dot(): lax.dot_general(left, right, (((0,), (0,)), ((), ())), preferred_element_...]
    all_gather x1, waiting for transfers between devices: 13.2 us -> 22.8 us  [on_device(): w_gate_up_all = lax.all_gather(w_gate_up, 'shard', axis=0, tiled=True)]
    pallas_call x7 -> x10, Pallas kernels: 64.4 us -> 73.9 us  [the longest x2 23.5 us: conv_backward(): pl.pallas_call(partial(conv_backward_kernel, begin), grid=(blocks,), out_...]
    unnamed x261 -> x209, local copies, waits for them, and re-layouts: 17.3 us -> 15.8 us
  transfers between devices with their start and end apart: 86 -> 72, of which waited for: 25 -> 22; matrix products, arithmetic and copies ran while one was open for 30% -> 35% of each run, Pallas kernels for 20% -> 23%
where the time goes in v4:
time: 598 us; the launch traced here: 592 us
  waiting for transfers between devices  159 us (27%)
  Pallas kernels  136 us (23%)
  matrix products  131 us (22%)
  other arithmetic  56.1 us (9%)
  starting transfers between devices  55.4 us (9%)
  local copies, waits for them, and re-layouts  39.1 us (7%)
  between operations  15.8 us (3%)
    ppermute x68, waiting for transfers between devices, swap(): return lax.ppermute(values, axis, [(i, i ^ mask) for i in range(count)])  126 us
    dot_general x31, matrix products, transposed_dot(): lax.dot_general(left, right, (((0,), (0,)), ((), ())), preferred_element_...  71.7 us
    ppermute x68, starting transfers between devices, swap(): return lax.ppermute(values, axis, [(i, i ^ mask) for i in range(count)])  55.3 us
    dot_general x5, matrix products, dot(): return jnp.dot(left, right, preferred_element_type=jnp.float32)  30.2 us
    dot_general x5, matrix products, back(): lax.dot_general(left, weight, (((1,), (1,)), ((), ())), preferred_element...  27.6 us
    pallas_call x2, Pallas kernels, conv_backward(): pl.pallas_call(partial(conv_backward_kernel, begin), grid=(blocks,), out_...  23.5 us
    pallas_call x4, Pallas kernels, pick_rows(): pl.pallas_call(pick_kernel, out_shape=jax.ShapeDtypeStruct((wanted.shape[...  23.4 us
    all_gather x1, waiting for transfers between devices, on_device(): w_gate_up_all = lax.all_gather(w_gate_up, 'shard', axis=0, tiled=True)  22.8 us
  transfers between devices with their start and end apart: 72, of which 22 were waited for; matrix products, arithmetic and copies ran while one was open for 35% of the time, Pallas kernels for 23%

profile of v4, /device:TPU:0, one launch (start us, length us, event | category | flops | bytes accessed | tf_op | source)
XLA Modules:
  0.0 592.2 jit_solution(5854113441556717655)
XLA Ops:
  19.9 16.8 %collective-permute-done.refs_2_ = bf16[128,4096]{1,0:T(8,128)(2,1)S(1)} collective-permute-done((bf16[128,4096]{1,0:T(8,128)(2,1)}, bf16[128,4096]{1,0:T(8,128)(2,1)S(1)}, u32[]{:S(2)}, u32[]{:S(2)}) %collective-permute-start) | collective-permute-done | bytes 1048608 | tf_op jit(solution)/shard_map/ppermute | solution.py:573
  41.0 24.1 %collective-permute-done.5 = bf16[2,9298]{1,0:T(2,128)(2,1)S(1)} collective-permute-done((bf16[2,9298]{1,0:T(2,128)(2,1)S(1)}, bf16[2,9298]{1,0:T(2,128)(2,1)S(1)}, u32[]{:S(2)}, u32[]{:S(2)}) %collective-permute-start.5) | collective-permute-done | bytes 37224 | tf_op jit(solution)/shard_map/ppermute | solution.py:573
  84.9 7.5 %lay_rows.1 = bf16[1024,4096]{1,0:T(8,128)(2,1)} custom-call(s32[6]{0:T(128)} %and_select_fusion.place_ref, bf16[256,4096]{1,0:T(8,128)(2,1)} %refs_0_.2, bf16[256,4096]{1,0:T(8,128)(2,1)} %copy-done.38, bf16[128,4096]{1,0:T(8,128)(2,1)} %copy-done.41, bf16[128,4096]{1,0:T(8,128)(2,1)} %copy-done.43, bf16[128,4096]{1,0:T(8,128)(2,1)} %copy-done.42, ...), custom_call_target="tpu_custom_call" | custom-call | tf_op jit(solution)/shard_map/lay_rows/pallas_call | solution.py:536
  92.4 10.6 %fusion.170.q_ref.k_ref.v_ref.u_ref = f32[512,4096]{1,0:T(8,128)} fusion(bf16[512,1024]{1,0:T(8,128)(2,1)S(1)} %fusion.33, bf16[1024,4096]{1,0:T(8,128)(2,1)} %lay_rows.1), kind=kOutput, calls=%fused_computation.331 | convolution fusion | flops 4294967296 | bytes 17825792 | tf_op jit(solution)/shard_map/dot_general | solution.py:812
  108.7 12.1 %attention_forward.1 = (bf16[512,512]{1,0:T(8,128)(2,1)}, f32[2,512,4]{2,1,0:T(8,128)}) custom-call(s32[1]{0:T(128)} %bitcast.18.limit_ref, f32[512,4096]{1,0:T(8,128)} %fusion.170.q_ref.k_ref.v_ref.u_ref, f32[512,4096]{1,0:T(8,128)} %fusion.170.q_ref.k_ref.v_ref.u_ref, f32[512,4096]{1,0:T(8,128)} %fusion.170.q_ref.k_ref.v_ref.u_ref, ...), custom_call_target="tpu_custom_call" | custom-call | tf_op jit(solution)/shard_map/attention_forward/pallas_call | solution.py:250
  120.8 9.7 %conv_forward.1 = (f32[512,1792]{1,0:T(8,128)}, bf16[512,1792]{1,0:T(8,128)(2,1)}) custom-call(f32[512,4096]{1,0:T(8,128)} %fusion.170.q_ref.k_ref.v_ref.u_ref, s32[512,1]{1,0:T(8,128)} %copy.80.place_ref, f32[4,1792]{1,0:T(4,128)} %reshape.298.weight_ref, f32[1,1792]{1,0:T(1,128)} %reshape.299.bias_ref, f32[512,128]{1,0:T(8,128)} %concatenate.37.step_ref), custom_call_target="tpu_custom_call" | custom-call | tf_op jit(solution)/shard_map/conv_forward/pallas_call | solution.py:380
  130.4 9.2 %ssd_forward.1.y_ref = f32[512,1536]{1,0:T(8,128)} custom-call(s32[1]{0:T(128)} %bitcast.18.limit_ref, bf16[512,1792]{1,0:T(8,128)(2,1)} %get-tuple-element.209.c_ref.b_ref.x_ref.low_ref, bf16[512,1792]{1,0:T(8,128)(2,1)} %get-tuple-element.209.c_ref.b_ref.x_ref.low_ref, bf16[512,1792]{1,0:T(8,128)(2,1)} %get-tuple-element.209.c_ref.b_ref.x_ref.low_ref, ...), custom_call_target="tpu_custom_call" | custom-call | tf_op jit(solution)/shard_map/ssd_forward/pallas_call | solution.py:87
  154.4 22.8 %all-gather.7.cloned.1.call-done = bf16[1024,4096]{1,0:T(8,128)(2,1)} async-done(((bf16[256,4096]{1,0:T(8,128)(2,1)}), bf16[1024,4096]{1,0:T(8,128)(2,1)}) %all-gather.7.cloned.1.call-update) | async-done | bytes 8388624 | tf_op jit(solution)/shard_map/all_gather | solution.py:873
  177.1 7.4 %fusion.171 = f32[512,4096]{1,0:T(8,128)S(1)} fusion(bf16[512,1024]{1,0:T(8,128)(2,1)} %multiply_convert_fusion.1, bf16[1024,4096]{1,0:T(8,128)(2,1)} %all-gather.7.cloned.1.call-done), kind=kOutput, calls=%fused_computation.332 | convolution fusion | flops 4294967296 | bytes 17825792 | tf_op jit(solution)/shard_map/dot_general | solution.py:812
  204.4 9.2 %all-gather.9.cloned.1.call-done = bf16[2048,1024]{1,0:T(8,128)(2,1)} async-done(((bf16[512,1024]{1,0:T(8,128)(2,1)}), bf16[2048,1024]{1,0:T(8,128)(2,1)}) %all-gather.9.cloned.1.call-update) | async-done | bytes 4194320 | tf_op jit(solution)/shard_map/all_gather | solution.py:874
  213.6 8.4 %multiply_multiply_fusion = (f32[512,2048]{1,0:T(8,128)S(1)}, f32[512,2048]{1,0:T(8,128)S(1)}) fusion(f32[512,4096]{1,0:T(8,128)} %copy-done.25, bf16[512,1024]{1,0:T(8,128)(2,1)} %pick_rows.5, bf16[2048,1024]{1,0:T(8,128)(2,1)} %all-gather.9.cloned.1.call-done), kind=kOutput, calls=%fused_computation.15 | convolution fusion | flops 2160066560 | bytes 22020096 | tf_op jit(solution)/shard_map/dot_general | solution.py:914
  240.9 8.0 %multiply_reduce_fusion.3 = (f32[1024]{0:T(1024)}, f32[512]{0:T(512)S(1)}, f32[512,1024]{1,0:T(8,128)S(1)}) fusion(f32[512,1024]{1,0:T(8,128)S(1)} %copy-done.28, f32[512]{0:T(512)S(1)} %fusion.144, f32[1024]{0:T(1024)S(1)} %bitcast.95, bf16[512,4096]{1,0:T(8,128)(2,1)S(1)} %copy-done, bf16[1024,4096]{1,0:T(8,128)(2,1)} %all-gather.7.cloned.1.call-done), kind=kOutput, calls=%fused_computation.93 | convolution fusion | flops 4298111488 | bytes 16789504 | tf_op jit(solution)/shard_map/dot_general | solution.py:914
  280.5 9.6 %attention_backward.2 = (bf16[512,256]{1,0:T(8,128)(2,1)}, bf16[512,256]{1,0:T(8,128)(2,1)}) custom-call(s32[1]{0:T(128)} %bitcast.18.limit_ref, f32[512,4096]{1,0:T(8,128)} %fusion.170.q_ref.k_ref.v_ref.u_ref, f32[512,4096]{1,0:T(8,128)} %fusion.170.q_ref.k_ref.v_ref.u_ref, f32[512,4096]{1,0:T(8,128)} %fusion.170.q_ref.k_ref.v_ref.u_ref, ...), custom_call_target="tpu_custom_call" | custom-call | tf_op jit(solution)/shard_map/attention_backward/pallas_call | solution.py:313
  298.1 9.6 %attention_backward.3 = (bf16[512,256]{1,0:T(8,128)(2,1)}, bf16[512,256]{1,0:T(8,128)(2,1)}) custom-call(s32[1]{0:T(128)} %bitcast.18.limit_ref, f32[512,4096]{1,0:T(8,128)} %fusion.170.q_ref.k_ref.v_ref.u_ref, f32[512,4096]{1,0:T(8,128)} %fusion.170.q_ref.k_ref.v_ref.u_ref, f32[512,4096]{1,0:T(8,128)} %fusion.170.q_ref.k_ref.v_ref.u_ref, ...), custom_call_target="tpu_custom_call" | custom-call | tf_op jit(solution)/shard_map/attention_backward/pallas_call | solution.py:313
  334.3 8.4 %ssd_backward.2 = (f32[512,768]{1,0:T(8,128)}, f32[512,512]{1,0:T(8,128)}) custom-call(s32[1]{0:T(128)} %bitcast.18.limit_ref, bf16[512,1792]{1,0:T(8,128)(2,1)} %get-tuple-element.209.c_ref.b_ref.x_ref.low_ref, bf16[512,1792]{1,0:T(8,128)(2,1)} %get-tuple-element.209.c_ref.b_ref.x_ref.low_ref, ...), custom_call_target="tpu_custom_call" | custom-call | tf_op jit(solution)/shard_map/ssd_backward/pallas_call | solution.py:172
  362.1 9.8 %ssd_backward.3 = (f32[512,768]{1,0:T(8,128)}, f32[512,512]{1,0:T(8,128)}, f32[512,256]{1,0:T(8,128)}) custom-call(s32[1]{0:T(128)} %bitcast.18.limit_ref, bf16[512,1792]{1,0:T(8,128)(2,1)} %get-tuple-element.209.c_ref.b_ref.x_ref.low_ref, bf16[512,1792]{1,0:T(8,128)(2,1)} %get-tuple-element.209.c_ref.b_ref.x_ref.low_ref, ...), custom_call_target="tpu_custom_call" | custom-call | tf_op jit(solution)/shard_map/ssd_backward/pallas_call | solution.py:172
  371.9 8.6 %collective-permute-done.33 = bf16[128,2048]{1,0:T(8,128)(2,1)} collective-permute-done((bf16[128,2048]{1,0:T(8,128)(2,1)}, bf16[128,2048]{1,0:T(8,128)(2,1)}, u32[]{:S(2)}, u32[]{:S(2)}) %collective-permute-start.33) | collective-permute-done | bytes 524320 | tf_op jit(solution)/shard_map/ppermute | solution.py:573
  397.3 10.3 %conv_backward.2 = (bf16[512,768]{1,0:T(8,128)(2,1)}, f32[8,768]{1,0:T(8,128)}, f32[512,128]{1,0:T(8,128)}) custom-call(f32[512,4096]{1,0:T(8,128)} %fusion.170.q_ref.k_ref.v_ref.u_ref, s32[512,1]{1,0:T(8,128)} %copy.80.place_ref, f32[4,1792]{1,0:T(4,128)} %reshape.298.weight_ref, f32[1,1792]{1,0:T(1,128)} %reshape.299.bias_ref, ...), custom_call_target="tpu_custom_call" | custom-call | tf_op jit(solution)/shard_map/conv_backward/pallas_call | solution.py:472
  420.1 13.2 %conv_backward.3 = (bf16[512,1024]{1,0:T(8,128)(2,1)}, f32[8,1024]{1,0:T(8,128)}, f32[512,128]{1,0:T(8,128)}) custom-call(f32[512,4096]{1,0:T(8,128)} %fusion.170.q_ref.k_ref.v_ref.u_ref, s32[512,1]{1,0:T(8,128)} %copy.80.place_ref, f32[4,1792]{1,0:T(4,128)} %reshape.298.weight_ref, f32[1,1792]{1,0:T(1,128)} %reshape.299.bias_ref, ...), custom_call_target="tpu_custom_call" | custom-call | tf_op jit(solution)/shard_map/conv_backward/pallas_call | solution.py:472
  469.9 8.3 %fusion.34 = (f32[1024]{0:T(1024)S(1)}, f32[512]{0:T(512)S(1)}, f32[512,1024]{1,0:T(8,128)S(1)}) fusion(bf16[512,1024]{1,0:T(8,128)(2,1)S(1)} %copy-done.19, f32[512]{0:T(512)S(1)} %copy-done.80, f32[1024]{0:T(1024)S(1)} %bitcast.92, f32[512,1024]{1,0:T(8,128)S(1)} %fusion.173, bf16[512,4096]{1,0:T(8,128)(2,1)S(1)} %copy-done.84, ...), kind=kOutput, calls=%fused_computation.86 | convolution fusion | flops 4299160064 | bytes 17838080 | tf_op jit(solution)/shard_map/dot_general | solution.py:914
  479.8 9.2 %collective-permute-done.48 = bf16[256,1792]{1,0:T(8,128)(2,1)S(1)} collective-permute-done((bf16[256,1792]{1,0:T(8,128)(2,1)S(1)}, bf16[256,1792]{1,0:T(8,128)(2,1)S(1)}, u32[]{:S(2)}, u32[]{:S(2)}) %collective-permute-start.48) | collective-permute-done | bytes 917536 | tf_op jit(solution)/shard_map/ppermute | solution.py:573
  522.7 10.2 %collective-permute-done.59 = f32[8,128]{1,0:T(8,128)S(1)} collective-permute-done((f32[8,128]{1,0:T(8,128)S(1)}, f32[8,128]{1,0:T(8,128)S(1)}, u32[]{:S(2)}, u32[]{:S(2)}) %collective-permute-start.59) | collective-permute-done | bytes 4128 | tf_op jit(solution)/shard_map/ppermute | solution.py:573
  544.7 8.2 %collective-permute-done.61 = f32[288,128]{1,0:T(8,128)S(1)} collective-permute-done((f32[288,128]{1,0:T(8,128)S(1)}, f32[288,128]{1,0:T(8,128)S(1)}, u32[]{:S(2)}, u32[]{:S(2)}) %collective-permute-start.61) | collective-permute-done | bytes 147488 | tf_op jit(solution)/shard_map/ppermute | solution.py:573
  552.9 9.2 %collective-permute-done.60 = bf16[128,1792]{1,0:T(8,128)(2,1)S(1)} collective-permute-done((bf16[128,1792]{1,0:T(8,128)(2,1)S(1)}, bf16[128,1792]{1,0:T(8,128)(2,1)S(1)}, u32[]{:S(2)}, u32[]{:S(2)}) %collective-permute-start.60) | collective-permute-done | bytes 458784 | tf_op jit(solution)/shard_map/ppermute | solution.py:573
  (515 shorter events, 316.1 us)
Async XLA Ops:
  7.3 139.0 %all-gather.5.cloned.1.call-start = ((), (), s32[]{:S(2)}) async-start(), calls=%async_computation | async-start | bytes 5242880 | tf_op jit(solution)/shard_map/all_gather | solution.py:872
  7.3 29.4 %collective-permute-start.1 = (bf16[256,4096]{1,0:T(8,128)(2,1)}, bf16[256,4096]{1,0:T(8,128)(2,1)S(1)}, u32[]{:S(2)}, u32[]{:S(2)}) collective-permute-start(bf16[256,4096]{1,0:T(8,128)(2,1)} %refs_0_.2), channel_id=1, source_target_pairs={{0,1},{1,0},{2,3},{3,2},{4,5},{5,4},{6,7},{7,6},{8,9},{9,8},{10,11... | collective-permute-start | bytes 6291464 | tf_op jit(solution)/shard_map/ppermute | solution.py:573
  10.1 26.6 %collective-permute-start = (bf16[128,4096]{1,0:T(8,128)(2,1)}, bf16[128,4096]{1,0:T(8,128)(2,1)S(1)}, u32[]{:S(2)}, u32[]{:S(2)}) collective-permute-start(bf16[128,4096]{1,0:T(8,128)(2,1)} %constant_dynamic-slice_fusion.2), channel_id=1, source_target_pairs={{0,2},{1,3},{2,0},{3,1},{4,6},{5,7},{6,4},{7,5},{8,10},{9,11},{10,... | collective-permute-start | bytes 3145736 | tf_op jit(solution)/shard_map/ppermute | solution.py:573
  36.7 28.4 %collective-permute-start.3 = (bf16[128,4096]{1,0:T(8,128)(2,1)S(1)}, bf16[128,4096]{1,0:T(8,128)(2,1)S(1)}, u32[]{:S(2)}, u32[]{:S(2)}) collective-permute-start(bf16[128,4096]{1,0:T(8,128)(2,1)S(1)} %collective-permute-done.refs_2_), channel_id=1, source_target_pairs={{0,4},{4,0},{8,12},{12,8},{16,20},{20,16},{24,28},{28,24},{1,5},{5... | collective-permute-start | bytes 3145736 | tf_op jit(solution)/shard_map/ppermute | solution.py:573
  38.5 26.6 %collective-permute-start.4 = (bf16[128,4096]{1,0:T(8,128)(2,1)S(1)}, bf16[128,4096]{1,0:T(8,128)(2,1)S(1)}, u32[]{:S(2)}, u32[]{:S(2)}) collective-permute-start(bf16[128,4096]{1,0:T(8,128)(2,1)S(1)} %collective-permute-done.refs_2_), channel_id=1, source_target_pairs={{0,1},{1,0},{2,3},{3,2},{4,5},{5,4},{6,7},{7,6},{8,9},{9,8},{10,11... | collective-permute-start | bytes 3145736 | tf_op jit(solution)/shard_map/ppermute | solution.py:573
  38.5 27.6 %collective-permute-start.6 = (bf16[512,1024]{1,0:T(8,128)(2,1)}, bf16[512,1024]{1,0:T(8,128)(2,1)S(1)}, u32[]{:S(2)}, u32[]{:S(2)}) collective-permute-start(bf16[512,1024]{1,0:T(8,128)(2,1)} %refs_0_.1), channel_id=1, source_target_pairs={{0,2},{1,3},{2,0},{3,1},{4,6},{5,7},{6,4},{7,5},{8,10},{9,11},{10,... | collective-permute-start | bytes 3145736 | tf_op jit(solution)/shard_map/ppermute | solution.py:573
  40.0 28.0 %collective-permute-start.7 = (bf16[512,1024]{1,0:T(8,128)(2,1)}, bf16[512,1024]{1,0:T(8,128)(2,1)}, u32[]{:S(2)}, u32[]{:S(2)}) collective-permute-start(bf16[512,1024]{1,0:T(8,128)(2,1)} %refs_0_.1), channel_id=1, source_target_pairs={{0,1},{1,0},{2,3},{3,2},{4,5},{5,4},{6,7},{7,6},{8,9},{9,8},{10,11... | collective-permute-start | bytes 3145736 | tf_op jit(solution)/shard_map/ppermute | solution.py:573
  68.0 109.1 %all-gather.7.cloned.1.call-start = ((), (), s32[]{:S(2)}) async-start(), calls=%async_computation.1 | async-start | bytes 10485760 | tf_op jit(solution)/shard_map/all_gather | solution.py:873
  68.8 144.8 %all-gather.9.cloned.1.call-start = ((), (), s32[]{:S(2)}) async-start(), calls=%async_computation.2 | async-start | bytes 5242880 | tf_op jit(solution)/shard_map/all_gather | solution.py:874
  73.6 434.0 %all-gather.11.cloned.1.call-start = ((), (), s32[]{:S(2)}) async-start(), calls=%async_computation.3 | async-start | bytes 5242880 | tf_op jit(solution)/shard_map/all_gather | solution.py:940
  105.0 84.2 %collective-permute-start.10 = (bf16[512,1024]{1,0:T(8,128)(2,1)}, bf16[512,1024]{1,0:T(8,128)(2,1)}, u32[]{:S(2)}, u32[]{:S(2)}) collective-permute-start(bf16[512,1024]{1,0:T(8,128)(2,1)} %refs_0_.3), channel_id=1, source_target_pairs={{0,2},{1,3},{2,0},{3,1},{4,6},{5,7},{6,4},{7,5},{8,10},{9,11},{10,... | collective-permute-start | bytes 3145736 | tf_op jit(solution)/shard_map/ppermute | solution.py:573
  106.4 82.8 %collective-permute-start.11 = (bf16[512,1024]{1,0:T(8,128)(2,1)}, bf16[512,1024]{1,0:T(8,128)(2,1)}, u32[]{:S(2)}, u32[]{:S(2)}) collective-permute-start(bf16[512,1024]{1,0:T(8,128)(2,1)} %refs_0_.3), channel_id=1, source_target_pairs={{0,1},{1,0},{2,3},{3,2},{4,5},{5,4},{6,7},{7,6},{8,9},{9,8},{10,11... | collective-permute-start | bytes 3145736 | tf_op jit(solution)/shard_map/ppermute | solution.py:573
  201.2 29.6 %collective-permute-start.13 = (bf16[512,1024]{1,0:T(8,128)(2,1)}, bf16[512,1024]{1,0:T(8,128)(2,1)}, u32[]{:S(2)}, u32[]{:S(2)}) collective-permute-start(bf16[512,1024]{1,0:T(8,128)(2,1)} %convolution_convert_fusion.11), channel_id=1, source_target_pairs={{0,1},{1,0},{2,3},{3,2},{4,5},{5,4},{6,7},{7,6},{8,9},{9,8},{10,11... | collective-permute-start | bytes 3145736 | tf_op jit(solution)/shard_map/ppermute | solution.py:573
  204.2 26.6 %collective-permute-start.14 = (bf16[512,1024]{1,0:T(8,128)(2,1)}, bf16[512,1024]{1,0:T(8,128)(2,1)}, u32[]{:S(2)}, u32[]{:S(2)}) collective-permute-start(bf16[512,1024]{1,0:T(8,128)(2,1)} %convolution_convert_fusion.10), channel_id=1, source_target_pairs={{0,1},{1,0},{2,3},{3,2},{4,5},{5,4},{6,7},{7,6},{8,9},{9,8},{10,11... | collective-permute-start | bytes 3145736 | tf_op jit(solution)/shard_map/ppermute | solution.py:573
  240.6 27.3 %collective-permute-start.17 = (bf16[512,1024]{1,0:T(8,128)(2,1)}, bf16[512,1024]{1,0:T(8,128)(2,1)S(1)}, u32[]{:S(2)}, u32[]{:S(2)}) collective-permute-start(bf16[512,1024]{1,0:T(8,128)(2,1)} %add_convert_fusion.2), channel_id=1, source_target_pairs={{0,2},{1,3},{2,0},{3,1},{4,6},{5,7},{6,4},{7,5},{8,10},{9,11},{10,... | collective-permute-start | bytes 3145736 | tf_op jit(solution)/shard_map/ppermute | solution.py:573
  259.9 30.1 %collective-permute-start.21 = (bf16[256,2048]{1,0:T(8,128)(2,1)S(1)}, bf16[256,2048]{1,0:T(8,128)(2,1)}, u32[]{:S(2)}, u32[]{:S(2)}) collective-permute-start(bf16[256,2048]{1,0:T(8,128)(2,1)S(1)} %fusion.13), channel_id=1, source_target_pairs={{0,2},{1,3},{2,0},{3,1},{4,6},{5,7},{6,4},{7,5},{8,10},{9,11},{10,... | collective-permute-start | bytes 3145736 | tf_op jit(solution)/shard_map/ppermute | solution.py:573
  279.4 31.8 %collective-permute-start.26 = (bf16[256,2048]{1,0:T(8,128)(2,1)}, bf16[256,2048]{1,0:T(8,128)(2,1)}, u32[]{:S(2)}, u32[]{:S(2)}) collective-permute-start(bf16[256,2048]{1,0:T(8,128)(2,1)} %fusion.14), channel_id=1, source_target_pairs={{0,2},{1,3},{2,0},{3,1},{4,6},{5,7},{6,4},{7,5},{8,10},{9,11},{10,... | collective-permute-start | bytes 3145736 | tf_op jit(solution)/shard_map/ppermute | solution.py:573
  318.4 31.6 %collective-permute-start.30 = (bf16[256,2304]{1,0:T(8,128)(2,1)}, bf16[256,2304]{1,0:T(8,128)(2,1)}, u32[]{:S(2)}, u32[]{:S(2)}) collective-permute-start(bf16[256,2304]{1,0:T(8,128)(2,1)} %convolution_convert_fusion.1), channel_id=1, source_target_pairs={{0,1},{1,0},{2,3},{3,2},{4,5},{5,4},{6,7},{7,6},{8,9},{9,8},{10,11... | collective-permute-start | bytes 3538952 | tf_op jit(solution)/shard_map/ppermute | solution.py:573
  318.4 31.6 %collective-permute-start.31 = (bf16[256,2304]{1,0:T(8,128)(2,1)}, bf16[256,2304]{1,0:T(8,128)(2,1)}, u32[]{:S(2)}, u32[]{:S(2)}) collective-permute-start(bf16[256,2304]{1,0:T(8,128)(2,1)} %convolution_convert_fusion), channel_id=1, source_target_pairs={{0,1},{1,0},{2,3},{3,2},{4,5},{5,4},{6,7},{7,6},{8,9},{9,8},{10,11... | collective-permute-start | bytes 3538952 | tf_op jit(solution)/shard_map/ppermute | solution.py:573
  320.9 26.4 %collective-permute-start.27 = (bf16[256,1024]{1,0:T(8,128)(2,1)}, bf16[256,1024]{1,0:T(8,128)(2,1)}, u32[]{:S(2)}, u32[]{:S(2)}) collective-permute-start(bf16[256,1024]{1,0:T(8,128)(2,1)} %add_convert_fusion.13), channel_id=1, source_target_pairs={{0,16},{4,20},{8,24},{12,28},{16,0},{20,4},{24,8},{28,12},{1,17},{... | collective-permute-start | bytes 1572872 | tf_op jit(solution)/shard_map/ppermute | solution.py:573
  396.6 36.7 %collective-permute-start.41 = (bf16[256,2304]{1,0:T(8,128)(2,1)}, bf16[256,2304]{1,0:T(8,128)(2,1)}, u32[]{:S(2)}, u32[]{:S(2)}) collective-permute-start(bf16[256,2304]{1,0:T(8,128)(2,1)} %fusion.3), channel_id=1, source_target_pairs={{0,2},{1,3},{2,0},{3,1},{4,6},{5,7},{6,4},{7,5},{8,10},{9,11},{10,... | collective-permute-start | bytes 3538952 | tf_op jit(solution)/shard_map/ppermute | solution.py:573
  435.6 25.9 %collective-permute-start.42 = (bf16[256,1024]{1,0:T(8,128)(2,1)}, bf16[256,1024]{1,0:T(8,128)(2,1)}, u32[]{:S(2)}, u32[]{:S(2)}) collective-permute-start(bf16[256,1024]{1,0:T(8,128)(2,1)} %add_convert_fusion.7), channel_id=1, source_target_pairs={{0,16},{4,20},{8,24},{12,28},{16,0},{20,4},{24,8},{28,12},{1,17},{... | collective-permute-start | bytes 1572872 | tf_op jit(solution)/shard_map/ppermute | solution.py:573
  489.2 26.8 %collective-permute-start.50 = (bf16[128,2304]{1,0:T(8,128)(2,1)S(1)}, bf16[128,2304]{1,0:T(8,128)(2,1)}, u32[]{:S(2)}, u32[]{:S(2)}) collective-permute-start(bf16[128,2304]{1,0:T(8,128)(2,1)S(1)} %add_convert_fusion.5), channel_id=1, source_target_pairs={{0,16},{4,20},{8,24},{12,28},{16,0},{20,4},{24,8},{28,12},{1,17},{... | collective-permute-start | bytes 1769480 | tf_op jit(solution)/shard_map/ppermute | solution.py:573
  506.9 31.4 %collective-permute-start.57 = (bf16[512,1024]{1,0:T(8,128)(2,1)}, bf16[512,1024]{1,0:T(8,128)(2,1)}, u32[]{:S(2)}, u32[]{:S(2)}) collective-permute-start(bf16[512,1024]{1,0:T(8,128)(2,1)} %fusion.37.refs_0_), channel_id=1, source_target_pairs={{0,2},{1,3},{2,0},{3,1},{4,6},{5,7},{6,4},{7,5},{8,10},{9,11},{10,... | collective-permute-start | bytes 3145736 | tf_op jit(solution)/shard_map/ppermute | solution.py:573
  (147 other events, 1598.6 us)
Sparse Core Ops, SparseCore 0:
  68.1 34.8 all-gather.4
  104.6 72.5 all-gather.6
  178.7 34.8 all-gather.8
  420.2 33.6 all-gather.10

commit v5 on v4

--- a/solution.py
+++ b/solution.py
@@ -393,12 +393,10 @@
 
 def head_sums(values, chosen):
     high = values.astype(jnp.bfloat16)
-    rest = values - high.astype(jnp.float32)
-    middle = rest.astype(jnp.bfloat16)
-    low = (rest - middle.astype(jnp.float32)).astype(jnp.bfloat16)
-    total = jnp.dot(high, chosen, preferred_element_type=jnp.float32)
-    total = total + jnp.dot(middle, chosen, preferred_element_type=jnp.float32)
-    return total + jnp.dot(low, chosen, preferred_element_type=jnp.float32)
+    low = (values - high.astype(jnp.float32)).astype(jnp.bfloat16)
+    return jnp.dot(high, chosen, preferred_element_type=jnp.float32) + jnp.dot(
+        low, chosen, preferred_element_type=jnp.float32
+    )
 
 
 def conv_backward_kernel(
@@ -543,15 +541,22 @@
     )(places // 16, *pieces)
 
 
-def widen_kernel(columns, near_ref, *refs):
+def widen_kernel(columns, parts, replica_ref, *refs):
     out_ref = refs[-1]
+    near, rest = replica_ref[0] & 1, replica_ref[0] >> 1
     for n, block in enumerate(refs[:-1]):
-        rows, left = block.shape[0], columns[n // 2]
-        start = pl.multiple_of((near_ref[0] ^ (n % 2)) * rows, rows)
-        out_ref[pl.ds(start, rows), left : left + block.shape[1]] = block[...].astype(jnp.float32)
-
-
-def widen_rows(chunks, near):
+        left, count = columns[n // 2], parts[n // 2]
+        rows = block.shape[0] // count
+        for k in range(count):
+            place = near ^ (n % 2)
+            if count > 1:
+                place = place * count + (rest ^ k)
+            start = pl.multiple_of(place * rows, rows)
+            piece = block[k * rows : (k + 1) * rows, :]
+            out_ref[pl.ds(start, rows), left : left + block.shape[1]] = piece.astype(jnp.float32)
+
+
+def widen_rows(chunks, parts, replica):
     flat = [block for chunk in chunks for block in chunk]
     columns, left = [], 0
     for chunk in chunks:
@@ -560,12 +565,12 @@
     rows = 2 * chunks[0][0].shape[0]
     vmem = pl.BlockSpec(memory_space=pltpu.VMEM)
     return pl.pallas_call(
-        partial(widen_kernel, tuple(columns)),
+        partial(widen_kernel, tuple(columns), tuple(parts)),
         out_shape=jax.ShapeDtypeStruct((rows, left), jnp.float32),
         in_specs=[pl.BlockSpec(memory_space=pltpu.SMEM)] + [vmem] * len(flat),
         out_specs=vmem,
         name="widen_rows",
-    )(near, *flat)
+    )(replica, *flat)
 
 
 def swap(values, axis, mask):
@@ -642,7 +647,7 @@
     return [p for _, p in held], jnp.stack([shard ^ k for k in keys]).astype(jnp.int32)
 
 
-def weight_stream(piece):
+def weight_stream(piece, wait=1):
     rows, width = piece.shape
     shard, near = lax.axis_index("shard"), lax.axis_index("rep") & 1
     part = lax.dynamic_slice_in_dim(piece, near * (rows // 2), rows // 2, 0)
@@ -654,7 +659,7 @@
         send = [swap(p, "shard", mask) for _, p in held]
         if beside is None:
             send.append(swap(piece, "shard", 1))
-        came = yield send
+        came = yield send, wait
         if beside is None:
             beside = came[-1]
         fresh = [(k ^ mask, p) for (k, _), p in zip(held, came)]
@@ -679,7 +684,7 @@
     return lax.dot_general(left, right, (((0,), (0,)), ((), ())), preferred_element_type=jnp.float32)
 
 
-def reduce_stream(left, right, waits=(1, 1, 1, 1)):
+def reduce_stream(left, right, waits=(1, 1, 1, 1, 1), direct=False):
     shards, replicas = lax.axis_size("shard"), lax.axis_size("rep")
     block = left.shape[1] // shards
     shard, near = lax.axis_index("shard"), lax.axis_index("rep") & 1
@@ -706,9 +711,20 @@
             extras[n].append(c)
     came = yield [swap(product(0, core, extras[0], 1 - near), "rep", 1)], waits[2]
     total = product(0, core, [*extras[0], came[0]], near)
+    if direct:
+        parts = lax.axis_size("rep") // 2
+        rest = lax.axis_index("rep") >> 1
+        split = total.reshape(parts, -1, right.shape[1])
+        others = range(1, parts)
+        came = yield [swap(take(split, rest ^ k, 0), "rep", 2 * k) for k in others]
+        mine = add(take(split, rest, 0), *came)
+        came = yield [swap(mine, "rep", 2 * k) for k in others]
+        total = jnp.concatenate([mine, *came], 0)
+        came = yield [swap(total, "rep", 1)]
+        return total, came[0]
     mask = 2
     while mask < replicas:
-        came = yield [swap(total, "rep", mask)], waits[3]
+        came = yield [swap(total, "rep", mask)], waits[3 if mask == 2 else 4]
         total = add(total, came[0])
         mask *= 2
     came = yield [swap(total, "rep", 1)]
@@ -825,12 +841,15 @@
     return jnp.concatenate([values, jnp.full((count, SIDE - width), fill, values.dtype)], 1)
 
 
+SMALL = (2, 3, 4, 5, 6, 7, 8, 10)
+PLAN = (0, 2, 2)
 WAITS = {
-    "down": (1, 2, 1, 1),
-    "gate": (1, 2, 1, 1),
-    "up": (1, 2, 1, 1),
-    "output": (1, 3, 1, 1),
-    "qkvz": (1, 3, 1, 1),
+    "down": (1, 2, 1, 1, 1),
+    "gate": (1, 2, 1, 1, 1),
+    "up": (1, 2, 1, 1, 1),
+    "output": (1, 3, 1, 1, 1),
+    "qkvz": (1, 3, 1, 1, 1),
+    "u": (1, 1, 1, 1, 1),
 }
 
 
@@ -869,10 +888,10 @@
     source, position, w_output, w_gate_up, w_down, cotangent = flow.step(
         (source, position, w_output, w_gate_up, w_down, cotangent)
     )
-    w_output_all = lax.all_gather(w_output, "shard", axis=0, tiled=True)
+    slot_output = flow.add(weight_stream(w_output, 2))
     w_gate_up_all = lax.all_gather(w_gate_up, "shard", axis=0, tiled=True)
     w_down_all = lax.all_gather(w_down, "shard", axis=0, tiled=True)
-    source, position, cotangent = flow.until([slot_tokens, slot_input, slot_small], (source, position, cotangent))
+    source, position, cotangent = flow.until([slot_tokens, slot_input, slot_small], (source, position, cotangent), True)
 
     gain_attn_all, w_step_all, step_bias_all, decay_all, skip_all, conv_w_all, conv_b_all, gain_ssm_all, gain_ffn_all = (
         unpack_small(slot_small["result"], [a.shape for a in small_args], small_dims)
@@ -886,18 +905,22 @@
 
     normed = rms_norm(own, gain_attn_f).astype(jnp.bfloat16)
     projected = dot(normed, w_input_all)
-    projected, normed, cotangent = lax.optimization_barrier((projected, normed, cotangent))
-    slot_cot = flow.add(rows_stream(cotangent))
     step_pre = dot(normed, w_step_all) + f32(step_bias_all)
     step = jax.nn.softplus(step_pre)
     rate = -jnp.exp(f32(decay_all))
     cum = to_lanes(running_sum(step * rate, False), 0.0)
     tables = (cum, cum.T)
     step_lanes = to_lanes(step, 1.0)
+    projected, normed = flow.step((projected, normed))
     conv_out, low = conv_forward(projected, position, conv_w_f, conv_b_f, step_lanes)
     inner_x = conv_out[:, :INNER]
+    low, cotangent, projected = flow.step((low, cotangent, projected))
+    slot_cot = flow.add(rows_stream(cotangent, 2))
+    attn_out, logs = attention_forward(limit, projected, cosine, sine)
+    attn_out, low = flow.step((attn_out, low))
     ssd_out = ssd_forward(limit, low, tables)
-    attn_out, logs = attention_forward(limit, projected, cosine, sine)
+    ssd_out, projected = flow.until([slot_output], (ssd_out, projected), True)
+    w_output_all = slot_output["result"]
     gate_z = projected[:, QUERY_KEY_VALUE : QUERY_KEY_VALUE + INNER]
     ssm_y = ssd_out + skip_lanes * inner_x
     ssm_out = gated_norm(ssm_y, gate_z, gain_ssm_f).astype(jnp.bfloat16)
@@ -914,7 +937,6 @@
         return lax.dot_general(left, weight, (((1,), (1,)), ((), ())), preferred_element_type=jnp.float32)
 
     slots = {}
-    block_low = (middle + dot(hidden, w_down_all)).astype(jnp.bfloat16)
     slots["down"] = [flow.add(reduce_stream(hidden, cot, WAITS["down"]))]
     grad_hidden = back(cot, w_down_all)
     grad_gate_up = jax.vjp(swiglu, gate_up)[1](grad_hidden)[0].astype(jnp.bfloat16)
@@ -933,11 +955,10 @@
     grad_ssm_y, grad_z, grad_gain_ssm = jax.vjp(gated_norm, ssm_y, gate_z, gain_ssm_f)[1](grad_ssm_out)
     grad_z_low = grad_z.astype(jnp.bfloat16)
     grad_y_low = grad_ssm_y.astype(jnp.bfloat16)
-    grad_ssm_y, grad_z_low, grad_attn, middle_low, grad_y_low, block_low = flow.step(
-        (grad_ssm_y, grad_z_low, grad_attn, middle_low, grad_y_low, block_low)
+    grad_ssm_y, grad_z_low, grad_attn, middle_low, grad_y_low = flow.step(
+        (grad_ssm_y, grad_z_low, grad_attn, middle_low, grad_y_low)
     )
     slots["output"] = [flow.add(reduce_stream(joined, middle_low, WAITS["output"]))]
-    block_all = lax.all_gather(block_low, "shard", axis=0, tiled=True)
     first = attention_backward(0, limit, projected, cosine, sine, grad_attn, logs)
     first, grad_attn = flow.step((first, grad_attn))
     second = attention_backward(1, limit, projected, cosine, sine, grad_attn, logs, first[1])
@@ -945,9 +966,11 @@
     qkvz = jnp.concatenate([first[0], second[0], second[1], grad_z_low], 1)
     slots["input"] = [flow.add(reduce_stream(normed, qkvz, WAITS["qkvz"]))]
     upper = ssd_backward(0, limit, low, grad_y_low, tables)
-    upper, grad_y_low = flow.step((upper, grad_y_low))
+    upper, grad_y_low, hidden = flow.step((upper, grad_y_low, hidden))
+    block_low = (middle + dot(hidden, w_down_all)).astype(jnp.bfloat16)
     lower = ssd_backward(1, limit, low, grad_y_low, tables, upper[1])
-    lower, upper = flow.step((lower, upper))
+    lower, upper, block_low = flow.step((lower, upper, block_low))
+    block_all = lax.all_gather(block_low, "shard", axis=0, tiled=True)
     conv_args = (projected, position, conv_w_f, conv_b_f, step_lanes, skip_lanes)
     conv_upper = conv_backward(0, *conv_args, upper[0], grad_ssm_y, ssd_out, low, lower[2])
     conv_upper, lower = flow.step((conv_upper, lower))
@@ -956,7 +979,8 @@
     grad_u_low = jnp.concatenate([conv_upper[0], conv_lower[0]], 1)
     grad_taps = jnp.concatenate([conv_upper[1], conv_lower[1]], 1)
     head_parts = conv_upper[2] + conv_lower[2]
-    slots["input"].append(flow.add(reduce_stream(normed, grad_u_low)))
+    slots["input"].append(flow.add(reduce_stream(normed, grad_u_low, WAITS["u"], True)))
+    last = slots["input"][-1:]
     grad_projected = jnp.concatenate([qkvz, grad_u_low], 1)
     heads_of = lambda offset: head_parts[:, offset : offset + SSM_HEADS]
     grad_skip = jnp.sum(heads_of(64), 0)
@@ -984,36 +1008,63 @@
     grad_normed = back(grad_projected, w_input_all) + back(step_low, w_step_all)
     grad_tokens_norm, grad_gain_attn = jax.vjp(rms_norm, own, gain_attn_f)[1](grad_normed)
     grad_low = (grad_middle + grad_tokens_norm).astype(jnp.bfloat16)
-    near_flag = (lax.axis_index("rep") & 1).reshape(1).astype(jnp.int32)
+    replica = lax.axis_index("rep").reshape(1).astype(jnp.int32)
+    line = lax.axis_size("rep") // 2
     held = {}
 
-    def finish_ready():
-        for name in slots:
-            if name not in held and all(slot["done"] for slot in slots[name]):
-                held[name] = widen_rows([slot["result"] for slot in slots[name]], near_flag)
-
-    grad_low, gain_late = flow.step((grad_low, grad_gain_attn.reshape(-1, SIDE)))
+    def widen(name):
+        parts = [line if slot in last else 1 for slot in slots[name]]
+        held[name] = widen_rows([slot["result"] for slot in slots[name]], parts, replica)
+
+    grad_low, gain_late, block_all = flow.step((grad_low, grad_gain_attn.reshape(-1, SIDE), block_all))
     slot_grad = flow.add(rows_stream(grad_low))
     slot_late = flow.add(butterfly_stream(gain_late))
-    finish_ready()
-    held["block"] = pick_rows([block_all], jnp.zeros((1,), jnp.int32), target)
-    held = flow.step(held, [slot for slot in flow.live if slot is not slot_grad])
+    queue = ["late", "small", "down", "gate_up", "block", "output", "tokens", "input"]
+
+    def small_outputs():
+        summed = slot_flat["result"].reshape(-1)
+        offset = 0
+        blocks = []
+        for i, grad in zip(SMALL, small_grads):
+            block = summed[offset : offset + grad.size].reshape(grad.shape)
+            offset += grad.size
+            blocks.append(own_block(block, 1 if i == 6 else 0))
+        return blocks
+
+    def work(limit):
+        for name in list(queue):
+            if limit == 0:
+                return
+            if name in ("late", "small"):
+                if not (slot_late if name == "late" else slot_flat)["done"]:
+                    continue
+                held[name] = small_outputs() if name == "small" else own_block(slot_late["result"].reshape(-1), 0)
+                limit += 1
+            elif name == "block":
+                held["block"] = pick_rows([block_all], jnp.zeros((1,), jnp.int32), target)
+            elif name == "tokens":
+                if not slot_grad["done"]:
+                    continue
+                pieces, owners = slot_grad["result"]
+                held["tokens"] = pick_rows(pieces, owners * input_rows, target)
+            else:
+                if not all(slot["done"] for slot in slots[name]):
+                    continue
+                widen(name)
+            queue.remove(name)
+            limit -= 1
+
+    boundary = 0
     while flow.live:
-        finish_ready()
-        if slot_grad["done"] and "tokens" not in held:
-            pieces, owners = slot_grad["result"]
-            held["tokens"] = pick_rows(pieces, owners * input_rows, target)
-        held = flow.step(held)
-    finish_ready()
+        work(PLAN[boundary] if boundary < len(PLAN) else 2)
+        held = flow.step(held, [slot for slot in flow.live if slot is not slot_grad] if boundary == 0 else None)
+        boundary += 1
+    work(len(queue))
     block_out, grad_tokens, widened = held["block"], held["tokens"], held
     outs = [None] * 13
-    outs[0] = own_block(slot_late["result"].reshape(-1), 0)
-    summed = slot_flat["result"].reshape(-1)
-    offset = 0
-    for i, grad in zip((2, 3, 4, 5, 6, 7, 8, 10), small_grads):
-        block = summed[offset : offset + grad.size].reshape(grad.shape)
-        offset += grad.size
-        outs[i] = own_block(block, 1 if i == 6 else 0)
+    outs[0] = held["late"]
+    for i, name in enumerate(SMALL):
+        outs[name] = held["small"][i]
     for i, name in ((1, "input"), (9, "output"), (11, "gate_up"), (12, "down")):
         outs[i] = widened[name]
     return (block_out, grad_tokens, *outs)

time: 598 us -> 557 us (0.931)
  waiting for transfers between devices: 159 us -> 111 us
    all_gather x1, waiting for transfers between devices: 22.8 us -> 0.01 us  [on_device(): w_gate_up_all = lax.all_gather(w_gate_up, 'shard', axis=0, tiled=True)]
    ppermute x68 -> x77, waiting for transfers between devices: 126 us -> 111 us  [swap(): return lax.ppermute(values, axis, [(i, i ^ mask) for i in range(count)])]
    all_gather x1, waiting for transfers between devices: 9.15 us -> 0.01 us  [on_device(): w_down_all = lax.all_gather(w_down, 'shard', axis=0, tiled=True)]
    pallas_call x1 -> x2, Pallas kernels: 7.49 us -> 12.8 us  [lay_rows(): pl.pallas_call(lay_rows_kernel, out_shape=jax.ShapeDtypeStruct((rows, pie...]
    ppermute x68 -> x77, starting transfers between devices: 55.3 us -> 57.6 us  [swap(): return lax.ppermute(values, axis, [(i, i ^ mask) for i in range(count)])]
    convert_element_type x12 -> x11, other arithmetic: 18.1 us -> 20.1 us  [add(): return total.astype(jnp.bfloat16)]
    unnamed x209 -> x224, local copies, waits for them, and re-layouts: 15.8 us -> 14.1 us
  transfers between devices with their start and end apart: 72 -> 80, of which waited for: 22 -> 23; matrix products, arithmetic and copies ran while one was open for 35% -> 37% of each run, Pallas kernels for 23% -> 25%
where the time goes in v5:
time: 557 us; the launch traced here: 553 us
  Pallas kernels  140 us (25%)
  matrix products  133 us (24%)
  waiting for transfers between devices  111 us (20%)
  starting transfers between devices  58.1 us (10%)
  other arithmetic  57.7 us (10%)
  local copies, waits for them, and re-layouts  37.7 us (7%)
  between operations  15.7 us (3%)
    ppermute x77, waiting for transfers between devices, swap(): return lax.ppermute(values, axis, [(i, i ^ mask) for i in range(count)])  111 us
    dot_general x31, matrix products, transposed_dot(): lax.dot_general(left, right, (((0,), (0,)), ((), ())), preferred_element_...  71.8 us
    ppermute x77, starting transfers between devices, swap(): return lax.ppermute(values, axis, [(i, i ^ mask) for i in range(count)])  57.6 us
    dot_general x5, matrix products, back(): lax.dot_general(left, weight, (((1,), (1,)), ((), ())), preferred_element...  31.3 us
    dot_general x5, matrix products, dot(): return jnp.dot(left, right, preferred_element_type=jnp.float32)  27.7 us
    pallas_call x4, Pallas kernels, pick_rows(): pl.pallas_call(pick_kernel, out_shape=jax.ShapeDtypeStruct((wanted.shape[...  23.2 us
    pallas_call x2, Pallas kernels, conv_backward(): pl.pallas_call(partial(conv_backward_kernel, begin), grid=(blocks,), out_...  22.4 us
    convert_element_type x11, other arithmetic, add(): return total.astype(jnp.bfloat16)  20.1 us
  transfers between devices with their start and end apart: 80, of which 23 were waited for; matrix products, arithmetic and copies ran while one was open for 37% of the time, Pallas kernels for 25%

profile of v5, /device:TPU:0, one launch (start us, length us, event | category | flops | bytes accessed | tf_op | source)
XLA Modules:
  0.0 552.5 jit_solution(16809974276918947065)
XLA Ops:
  20.3 16.5 %collective-permute-done.refs_2_ = bf16[128,4096]{1,0:T(8,128)(2,1)} collective-permute-done((bf16[128,4096]{1,0:T(8,128)(2,1)}, bf16[128,4096]{1,0:T(8,128)(2,1)}, u32[]{:S(2)}, u32[]{:S(2)}) %collective-permute-start) | collective-permute-done | bytes 1048608 | tf_op jit(solution)/shard_map/ppermute | solution.py:578
  41.0 24.1 %collective-permute-done.5 = bf16[2,9298]{1,0:T(2,128)(2,1)S(1)} collective-permute-done((bf16[2,9298]{1,0:T(2,128)(2,1)S(1)}, bf16[2,9298]{1,0:T(2,128)(2,1)S(1)}, u32[]{:S(2)}, u32[]{:S(2)}) %collective-permute-start.5) | collective-permute-done | bytes 37224 | tf_op jit(solution)/shard_map/ppermute | solution.py:578
  74.0 6.3 %pick_rows.4 = bf16[512,1024]{1,0:T(8,128)(2,1)} custom-call(s32[4]{0:T(128)} %add_multiply_fusion.shift_ref, s32[512,1]{1,0:T(8,128)} %copy.82.wanted_ref, bf16[512,1024]{1,0:T(8,128)(2,1)} %refs_0_.1, bf16[512,1024]{1,0:T(8,128)(2,1)} %collective-permute-done.6.refs_1_, bf16[512,1024]{1,0:T(8,128)(2,1)} %collective-permute-done.7.refs_2_, ...), custom_call_target="tpu_custom_call" | custom-call | tf_op jit(solution)/shard_map/pick_rows/pallas_call | solution.py:507
  80.3 7.6 %lay_rows.2 = bf16[1024,4096]{1,0:T(8,128)(2,1)} custom-call(s32[6]{0:T(128)} %and_select_fusion.1.place_ref, bf16[256,4096]{1,0:T(8,128)(2,1)} %refs_0_.2, bf16[256,4096]{1,0:T(8,128)(2,1)} %copy-done.45, bf16[128,4096]{1,0:T(8,128)(2,1)} %collective-permute-done.refs_2_, bf16[128,4096]{1,0:T(8,128)(2,1)} %collective-permute-done.4.refs_3_, ...), custom_call_target="tpu_custom_call" | custom-call | tf_op jit(solution)/shard_map/lay_rows/pallas_call | solution.py:534
  88.6 10.5 %fusion.173.u_ref.q_ref.k_ref.v_ref = f32[512,4096]{1,0:T(8,128)} fusion(bf16[512,1024]{1,0:T(8,128)(2,1)S(1)} %fusion.33, bf16[1024,4096]{1,0:T(8,128)(2,1)} %lay_rows.2), kind=kOutput, calls=%fused_computation.342 | convolution fusion | flops 4294967296 | bytes 17825792 | tf_op jit(solution)/shard_map/dot_general | solution.py:828
  101.2 9.7 %conv_forward.1 = (f32[512,1792]{1,0:T(8,128)}, bf16[512,1792]{1,0:T(8,128)(2,1)}) custom-call(f32[512,4096]{1,0:T(8,128)} %fusion.173.u_ref.q_ref.k_ref.v_ref, s32[512,1]{1,0:T(8,128)} %copy.80.place_ref, f32[4,1792]{1,0:T(4,128)} %reshape.304.weight_ref, f32[1,1792]{1,0:T(1,128)} %reshape.305.bias_ref, f32[512,128]{1,0:T(8,128)} %concatenate.40.step_ref), custom_call_target="tpu_custom_call" | custom-call | tf_op jit(solution)/shard_map/conv_forward/pallas_call | solution.py:380
  112.2 11.9 %attention_forward.1 = (bf16[512,512]{1,0:T(8,128)(2,1)}, f32[2,512,4]{2,1,0:T(8,128)}) custom-call(s32[1]{0:T(128)} %bitcast.20.limit_ref, f32[512,4096]{1,0:T(8,128)} %fusion.173.u_ref.q_ref.k_ref.v_ref, f32[512,4096]{1,0:T(8,128)} %fusion.173.u_ref.q_ref.k_ref.v_ref, f32[512,4096]{1,0:T(8,128)} %fusion.173.u_ref.q_ref.k_ref.v_ref, ...), custom_call_target="tpu_custom_call" | custom-call | tf_op jit(solution)/shard_map/attention_forward/pallas_call | solution.py:250
  129.1 9.2 %ssd_forward.1.y_ref = f32[512,1536]{1,0:T(8,128)} custom-call(s32[1]{0:T(128)} %bitcast.20.limit_ref, bf16[512,1792]{1,0:T(8,128)(2,1)} %get-tuple-element.233.c_ref.b_ref.x_ref.low_ref, bf16[512,1792]{1,0:T(8,128)(2,1)} %get-tuple-element.233.c_ref.b_ref.x_ref.low_ref, bf16[512,1792]{1,0:T(8,128)(2,1)} %get-tuple-element.233.c_ref.b_ref.x_ref.low_ref, ...), custom_call_target="tpu_custom_call" | custom-call | tf_op jit(solution)/shard_map/ssd_forward/pallas_call | solution.py:87
  156.0 7.6 %fusion.174 = f32[512,4096]{1,0:T(8,128)S(1)} fusion(bf16[512,1024]{1,0:T(8,128)(2,1)} %multiply_convert_fusion.1, bf16[1024,4096]{1,0:T(8,128)(2,1)} %all-gather.4.cloned.1.call-done), kind=kOutput, calls=%fused_computation.343 | convolution fusion | flops 4294967296 | bytes 17825792 | tf_op jit(solution)/shard_map/dot_general | solution.py:828
  170.7 5.7 %pick_rows.5 = bf16[512,1024]{1,0:T(8,128)(2,1)} custom-call(s32[4]{0:T(128)} %add_multiply_fusion.shift_ref, s32[512,1]{1,0:T(8,128)} %copy.82.wanted_ref, bf16[512,1024]{1,0:T(8,128)(2,1)} %refs_0_.4, bf16[512,1024]{1,0:T(8,128)(2,1)} %collective-permute-done.15.refs_1_, bf16[512,1024]{1,0:T(8,128)(2,1)} %collective-permute-done.16.refs_2_, ...), custom_call_target="tpu_custom_call" | custom-call | tf_op jit(solution)/shard_map/pick_rows/pallas_call | solution.py:507
  182.9 10.4 %multiply_multiply_fusion = (f32[512,2048]{1,0:T(8,128)S(1)}, f32[512,2048]{1,0:T(8,128)}) fusion(f32[512,4096]{1,0:T(8,128)} %copy-done.28, bf16[512,1024]{1,0:T(8,128)(2,1)} %pick_rows.5, bf16[2048,1024]{1,0:T(8,128)(2,1)} %all-gather.6.cloned.1.call-done), kind=kOutput, calls=%fused_computation.15 | convolution fusion | flops 2160066560 | bytes 22020096 | tf_op jit(solution)/shard_map/dot_general | solution.py:937
  205.1 10.2 %multiply_reduce_fusion.3 = (f32[1024]{0:T(1024)}, f32[512]{0:T(512)S(1)}, f32[512,1024]{1,0:T(8,128)}) fusion(f32[512,1024]{1,0:T(8,128)S(1)} %copy-done.30, f32[512]{0:T(512)S(1)} %fusion.147, f32[1024]{0:T(1024)S(1)} %bitcast.113, bf16[512,4096]{1,0:T(8,128)(2,1)S(1)} %add_convert_fusion, bf16[1024,4096]{1,0:T(8,128)(2,1)} %all-gather.4.cloned.1.call-done), kind=kOutput, calls=%fused_computation.93 | convolution fusion | flops 4298111488 | bytes 16789504 | tf_op jit(solution)/shard_map/dot_general | solution.py:937
  229.1 5.9 %fusion.169 = (bf16[512,1536]{1,0:T(8,128)(2,1)}, f32[512,1536]{1,0:T(8,128)}, bf16[512,1536]{1,0:T(8,128)(2,1)}) fusion(f32[512,4096]{1,0:T(8,128)} %fusion.173.u_ref.q_ref.k_ref.v_ref, f32[512,1536]{1,0:T(8,128)S(1)} %copy-done.7, f32[512]{0:T(512)S(1)} %multiply_multiply_fusion.2, f32[512]{0:T(512)S(1)} %fusion.146, f32[1536]{0:T(1024)S(1)} %reshape.308, ...), kind=kLoop, calls=%fused_computation.340 | loop fusion | flops 16515072 | bytes 22036480 | tf_op jit(solution)/shard_map/convert_element_type | solution.py:957
  247.2 9.5 %attention_backward.2 = (bf16[512,256]{1,0:T(8,128)(2,1)}, bf16[512,256]{1,0:T(8,128)(2,1)}) custom-call(s32[1]{0:T(128)} %bitcast.20.limit_ref, f32[512,4096]{1,0:T(8,128)} %fusion.173.u_ref.q_ref.k_ref.v_ref, f32[512,4096]{1,0:T(8,128)} %fusion.173.u_ref.q_ref.k_ref.v_ref, f32[512,4096]{1,0:T(8,128)} %fusion.173.u_ref.q_ref.k_ref.v_ref, ...), custom_call_target="tpu_custom_call" | custom-call | tf_op jit(solution)/shard_map/attention_backward/pallas_call | solution.py:313
  265.6 9.9 %attention_backward.3 = (bf16[512,256]{1,0:T(8,128)(2,1)}, bf16[512,256]{1,0:T(8,128)(2,1)}) custom-call(s32[1]{0:T(128)} %bitcast.20.limit_ref, f32[512,4096]{1,0:T(8,128)} %fusion.173.u_ref.q_ref.k_ref.v_ref, f32[512,4096]{1,0:T(8,128)} %fusion.173.u_ref.q_ref.k_ref.v_ref, f32[512,4096]{1,0:T(8,128)} %fusion.173.u_ref.q_ref.k_ref.v_ref, ...), custom_call_target="tpu_custom_call" | custom-call | tf_op jit(solution)/shard_map/attention_backward/pallas_call | solution.py:313
  299.9 8.5 %ssd_backward.2 = (f32[512,768]{1,0:T(8,128)}, f32[512,512]{1,0:T(8,128)}) custom-call(s32[1]{0:T(128)} %bitcast.20.limit_ref, bf16[512,1792]{1,0:T(8,128)(2,1)} %get-tuple-element.233.c_ref.b_ref.x_ref.low_ref, bf16[512,1792]{1,0:T(8,128)(2,1)} %get-tuple-element.233.c_ref.b_ref.x_ref.low_ref, ...), custom_call_target="tpu_custom_call" | custom-call | tf_op jit(solution)/shard_map/ssd_backward/pallas_call | solution.py:172
  326.7 9.7 %ssd_backward.3 = (f32[512,768]{1,0:T(8,128)}, f32[512,512]{1,0:T(8,128)}, f32[512,256]{1,0:T(8,128)}) custom-call(s32[1]{0:T(128)} %bitcast.20.limit_ref, bf16[512,1792]{1,0:T(8,128)(2,1)} %get-tuple-element.233.c_ref.b_ref.x_ref.low_ref, bf16[512,1792]{1,0:T(8,128)(2,1)} %get-tuple-element.233.c_ref.b_ref.x_ref.low_ref, ...), custom_call_target="tpu_custom_call" | custom-call | tf_op jit(solution)/shard_map/ssd_backward/pallas_call | solution.py:172
  336.4 6.8 %add_convert_fusion.2 = bf16[512,1024]{1,0:T(8,128)(2,1)} fusion(f32[512,1024]{1,0:T(8,128)} %copy-done.29, bf16[512,2048]{1,0:T(8,128)(2,1)} %fusion.2, bf16[2048,1024]{1,0:T(8,128)(2,1)} %all-gather.6.cloned.1.call-done), kind=kOutput, calls=%fused_computation.95 | convolution fusion | flops 2148532224 | bytes 9437184 | tf_op jit(solution)/shard_map/dot_general | solution.py:828
  363.7 9.9 %conv_backward.2 = (bf16[512,768]{1,0:T(8,128)(2,1)}, f32[8,768]{1,0:T(8,128)}, f32[512,128]{1,0:T(8,128)}) custom-call(f32[512,4096]{1,0:T(8,128)} %fusion.173.u_ref.q_ref.k_ref.v_ref, s32[512,1]{1,0:T(8,128)} %copy.80.place_ref, f32[4,1792]{1,0:T(4,128)} %reshape.304.weight_ref, f32[1,1792]{1,0:T(1,128)} %reshape.305.bias_ref, ...), custom_call_target="tpu_custom_call" | custom-call | tf_op jit(solution)/shard_map/conv_backward/pallas_call | solution.py:470
  384.6 12.5 %conv_backward.3 = (bf16[512,1024]{1,0:T(8,128)(2,1)}, f32[8,1024]{1,0:T(8,128)}, f32[512,128]{1,0:T(8,128)}) custom-call(f32[512,4096]{1,0:T(8,128)} %fusion.173.u_ref.q_ref.k_ref.v_ref, s32[512,1]{1,0:T(8,128)} %copy.80.place_ref, f32[4,1792]{1,0:T(4,128)} %reshape.304.weight_ref, f32[1,1792]{1,0:T(1,128)} %reshape.305.bias_ref, ...), custom_call_target="tpu_custom_call" | custom-call | tf_op jit(solution)/shard_map/conv_backward/pallas_call | solution.py:470
  418.9 6.8 %collective-permute-done.47 = bf16[256,1024]{1,0:T(8,128)(2,1)} collective-permute-done((bf16[256,1024]{1,0:T(8,128)(2,1)}, bf16[256,1024]{1,0:T(8,128)(2,1)}, u32[]{:S(2)}, u32[]{:S(2)}) %collective-permute-start.47) | collective-permute-done | bytes 524320 | tf_op jit(solution)/shard_map/ppermute | solution.py:578
  433.5 7.8 %fusion.34 = (f32[1024]{0:T(1024)S(1)}, f32[512]{0:T(512)S(1)}, f32[512,1024]{1,0:T(8,128)S(1)}) fusion(bf16[512,1024]{1,0:T(8,128)(2,1)S(1)} %copy-done.22, f32[512]{0:T(512)S(1)} %copy-done.84, f32[1024]{0:T(1024)S(1)} %bitcast.110, f32[512,1024]{1,0:T(8,128)S(1)} %fusion.176, bf16[512,4096]{1,0:T(8,128)(2,1)S(1)} %copy-done.88, ...), kind=kOutput, calls=%fused_computation.86 | convolution fusion | flops 4299160064 | bytes 17838080 | tf_op jit(solution)/shard_map/dot_general | solution.py:937
  445.1 8.6 %collective-permute-done.53 = bf16[256,1792]{1,0:T(8,128)(2,1)} collective-permute-done((bf16[256,1792]{1,0:T(8,128)(2,1)S(1)}, bf16[256,1792]{1,0:T(8,128)(2,1)}, u32[]{:S(2)}, u32[]{:S(2)}) %collective-permute-start.53) | collective-permute-done | bytes 917536 | tf_op jit(solution)/shard_map/ppermute | solution.py:578
  469.5 12.8 %collective-permute-done.55 = bf16[128,2304]{1,0:T(8,128)(2,1)} collective-permute-done((bf16[128,2304]{1,0:T(8,128)(2,1)S(1)}, bf16[128,2304]{1,0:T(8,128)(2,1)}, u32[]{:S(2)}, u32[]{:S(2)}) %collective-permute-start.55) | collective-permute-done | bytes 589856 | tf_op jit(solution)/shard_map/ppermute | solution.py:578
  (551 shorter events, 298.7 us)
Async XLA Ops:
  7.3 148.7 %all-gather.4.cloned.1.call-start = ((), (), s32[]{:S(2)}) async-start(), calls=%async_computation | async-start | bytes 10485760 | tf_op jit(solution)/shard_map/all_gather | solution.py:892
  7.3 29.5 %collective-permute-start.1 = (bf16[256,4096]{1,0:T(8,128)(2,1)}, bf16[256,4096]{1,0:T(8,128)(2,1)S(1)}, u32[]{:S(2)}, u32[]{:S(2)}) collective-permute-start(bf16[256,4096]{1,0:T(8,128)(2,1)} %refs_0_.2), channel_id=1, source_target_pairs={{0,1},{1,0},{2,3},{3,2},{4,5},{5,4},{6,7},{7,6},{8,9},{9,8},{10,11... | collective-permute-start | bytes 6291464 | tf_op jit(solution)/shard_map/ppermute | solution.py:578
  10.1 26.7 %collective-permute-start = (bf16[128,4096]{1,0:T(8,128)(2,1)}, bf16[128,4096]{1,0:T(8,128)(2,1)}, u32[]{:S(2)}, u32[]{:S(2)}) collective-permute-start(bf16[128,4096]{1,0:T(8,128)(2,1)} %constant_dynamic-slice_fusion.3), channel_id=1, source_target_pairs={{0,2},{1,3},{2,0},{3,1},{4,6},{5,7},{6,4},{7,5},{8,10},{9,11},{10,... | collective-permute-start | bytes 3145736 | tf_op jit(solution)/shard_map/ppermute | solution.py:578
  36.8 28.3 %collective-permute-start.3 = (bf16[128,4096]{1,0:T(8,128)(2,1)}, bf16[128,4096]{1,0:T(8,128)(2,1)}, u32[]{:S(2)}, u32[]{:S(2)}) collective-permute-start(bf16[128,4096]{1,0:T(8,128)(2,1)} %collective-permute-done.refs_2_), channel_id=1, source_target_pairs={{0,4},{4,0},{8,12},{12,8},{16,20},{20,16},{24,28},{28,24},{1,5},{5... | collective-permute-start | bytes 3145736 | tf_op jit(solution)/shard_map/ppermute | solution.py:578
  38.5 26.6 %collective-permute-start.4 = (bf16[128,4096]{1,0:T(8,128)(2,1)}, bf16[128,4096]{1,0:T(8,128)(2,1)}, u32[]{:S(2)}, u32[]{:S(2)}) collective-permute-start(bf16[128,4096]{1,0:T(8,128)(2,1)} %collective-permute-done.refs_2_), channel_id=1, source_target_pairs={{0,1},{1,0},{2,3},{3,2},{4,5},{5,4},{6,7},{7,6},{8,9},{9,8},{10,11... | collective-permute-start | bytes 3145736 | tf_op jit(solution)/shard_map/ppermute | solution.py:578
  38.5 26.6 %collective-permute-start.6 = (bf16[512,1024]{1,0:T(8,128)(2,1)}, bf16[512,1024]{1,0:T(8,128)(2,1)}, u32[]{:S(2)}, u32[]{:S(2)}) collective-permute-start(bf16[512,1024]{1,0:T(8,128)(2,1)} %refs_0_.1), channel_id=1, source_target_pairs={{0,2},{1,3},{2,0},{3,1},{4,6},{5,7},{6,4},{7,5},{8,10},{9,11},{10,... | collective-permute-start | bytes 3145736 | tf_op jit(solution)/shard_map/ppermute | solution.py:578
  40.1 25.1 %collective-permute-start.7 = (bf16[512,1024]{1,0:T(8,128)(2,1)}, bf16[512,1024]{1,0:T(8,128)(2,1)}, u32[]{:S(2)}, u32[]{:S(2)}) collective-permute-start(bf16[512,1024]{1,0:T(8,128)(2,1)} %refs_0_.1), channel_id=1, source_target_pairs={{0,1},{1,0},{2,3},{3,2},{4,5},{5,4},{6,7},{7,6},{8,9},{9,8},{10,11... | collective-permute-start | bytes 3145736 | tf_op jit(solution)/shard_map/ppermute | solution.py:578
  65.2 117.8 %all-gather.6.cloned.1.call-start = ((), (), s32[]{:S(2)}) async-start(), calls=%async_computation.1 | async-start | bytes 5242880 | tf_op jit(solution)/shard_map/all_gather | solution.py:893
  70.7 40.2 %collective-permute-start.11 = (bf16[512,1024]{1,0:T(8,128)(2,1)S(1)}, bf16[512,1024]{1,0:T(8,128)(2,1)}, u32[]{:S(2)}, u32[]{:S(2)}) collective-permute-start(bf16[512,1024]{1,0:T(8,128)(2,1)S(1)} %copy-done.40), channel_id=1, source_target_pairs={{0,1},{1,0},{2,3},{3,2},{4,5},{5,4},{6,7},{7,6},{8,9},{9,8},{10,11... | collective-permute-start | bytes 3145736 | tf_op jit(solution)/shard_map/ppermute | solution.py:578
  71.6 39.2 %collective-permute-start.10 = (bf16[256,1024]{1,0:T(8,128)(2,1)}, bf16[256,1024]{1,0:T(8,128)(2,1)}, u32[]{:S(2)}, u32[]{:S(2)}) collective-permute-start(bf16[256,1024]{1,0:T(8,128)(2,1)} %constant_dynamic-slice_fusion.2), channel_id=1, source_target_pairs={{0,2},{1,3},{2,0},{3,1},{4,6},{5,7},{6,4},{7,5},{8,10},{9,11},{10,... | collective-permute-start | bytes 1572872 | tf_op jit(solution)/shard_map/ppermute | solution.py:578
  125.7 328.0 %all-gather.8.cloned.1.call-start = ((), (), s32[]{:S(2)}) async-start(), calls=%async_computation.2 | async-start | bytes 5242880 | tf_op jit(solution)/shard_map/all_gather | solution.py:973
  126.0 41.6 %collective-permute-start.15 = (bf16[512,1024]{1,0:T(8,128)(2,1)}, bf16[512,1024]{1,0:T(8,128)(2,1)}, u32[]{:S(2)}, u32[]{:S(2)}) collective-permute-start(bf16[512,1024]{1,0:T(8,128)(2,1)} %refs_0_.4), channel_id=1, source_target_pairs={{0,2},{1,3},{2,0},{3,1},{4,6},{5,7},{6,4},{7,5},{8,10},{9,11},{10,... | collective-permute-start | bytes 3145736 | tf_op jit(solution)/shard_map/ppermute | solution.py:578
  126.6 40.9 %collective-permute-start.16 = (bf16[512,1024]{1,0:T(8,128)(2,1)}, bf16[512,1024]{1,0:T(8,128)(2,1)}, u32[]{:S(2)}, u32[]{:S(2)}) collective-permute-start(bf16[512,1024]{1,0:T(8,128)(2,1)} %refs_0_.4), channel_id=1, source_target_pairs={{0,1},{1,0},{2,3},{3,2},{4,5},{5,4},{6,7},{7,6},{8,9},{9,8},{10,11... | collective-permute-start | bytes 3145736 | tf_op jit(solution)/shard_map/ppermute | solution.py:578
  204.1 30.9 %collective-permute-start.22 = (bf16[512,1024]{1,0:T(8,128)(2,1)}, bf16[512,1024]{1,0:T(8,128)(2,1)}, u32[]{:S(2)}, u32[]{:S(2)}) collective-permute-start(bf16[512,1024]{1,0:T(8,128)(2,1)} %add_convert_fusion.3), channel_id=1, source_target_pairs={{0,2},{1,3},{2,0},{3,1},{4,6},{5,7},{6,4},{7,5},{8,10},{9,11},{10,... | collective-permute-start | bytes 3145736 | tf_op jit(solution)/shard_map/ppermute | solution.py:578
  228.2 28.5 %collective-permute-start.26 = (bf16[256,2048]{1,0:T(8,128)(2,1)}, bf16[256,2048]{1,0:T(8,128)(2,1)}, u32[]{:S(2)}, u32[]{:S(2)}) collective-permute-start(bf16[256,2048]{1,0:T(8,128)(2,1)} %fusion.13), channel_id=1, source_target_pairs={{0,2},{1,3},{2,0},{3,1},{4,6},{5,7},{6,4},{7,5},{8,10},{9,11},{10,... | collective-permute-start | bytes 3145736 | tf_op jit(solution)/shard_map/ppermute | solution.py:578
  245.7 30.9 %collective-permute-start.31 = (bf16[256,2048]{1,0:T(8,128)(2,1)}, bf16[256,2048]{1,0:T(8,128)(2,1)}, u32[]{:S(2)}, u32[]{:S(2)}) collective-permute-start(bf16[256,2048]{1,0:T(8,128)(2,1)} %fusion.14), channel_id=1, source_target_pairs={{0,2},{1,3},{2,0},{3,1},{4,6},{5,7},{6,4},{7,5},{8,10},{9,11},{10,... | collective-permute-start | bytes 3145736 | tf_op jit(solution)/shard_map/ppermute | solution.py:578
  284.8 32.7 %collective-permute-start.35 = (bf16[256,2304]{1,0:T(8,128)(2,1)}, bf16[256,2304]{1,0:T(8,128)(2,1)}, u32[]{:S(2)}, u32[]{:S(2)}) collective-permute-start(bf16[256,2304]{1,0:T(8,128)(2,1)} %convolution_convert_fusion.1), channel_id=1, source_target_pairs={{0,1},{1,0},{2,3},{3,2},{4,5},{5,4},{6,7},{7,6},{8,9},{9,8},{10,11... | collective-permute-start | bytes 3538952 | tf_op jit(solution)/shard_map/ppermute | solution.py:578
  284.8 32.7 %collective-permute-start.36 = (bf16[256,2304]{1,0:T(8,128)(2,1)}, bf16[256,2304]{1,0:T(8,128)(2,1)}, u32[]{:S(2)}, u32[]{:S(2)}) collective-permute-start(bf16[256,2304]{1,0:T(8,128)(2,1)} %convolution_convert_fusion), channel_id=1, source_target_pairs={{0,1},{1,0},{2,3},{3,2},{4,5},{5,4},{6,7},{7,6},{8,9},{9,8},{10,11... | collective-permute-start | bytes 3538952 | tf_op jit(solution)/shard_map/ppermute | solution.py:578
  287.4 26.3 %collective-permute-start.32 = (bf16[256,1024]{1,0:T(8,128)(2,1)}, bf16[256,1024]{1,0:T(8,128)(2,1)}, u32[]{:S(2)}, u32[]{:S(2)}) collective-permute-start(bf16[256,1024]{1,0:T(8,128)(2,1)} %add_convert_fusion.13), channel_id=1, source_target_pairs={{0,16},{4,20},{8,24},{12,28},{16,0},{20,4},{24,8},{28,12},{1,17},{... | collective-permute-start | bytes 1572872 | tf_op jit(solution)/shard_map/ppermute | solution.py:578
  313.7 29.5 %collective-permute-start.40 = (bf16[512,1024]{1,0:T(8,128)(2,1)}, bf16[512,1024]{1,0:T(8,128)(2,1)}, u32[]{:S(2)}, u32[]{:S(2)}) collective-permute-start(bf16[512,1024]{1,0:T(8,128)(2,1)} %add_convert_fusion.1), channel_id=1, source_target_pairs={{0,2},{1,3},{2,0},{3,1},{4,6},{5,7},{6,4},{7,5},{8,10},{9,11},{10,... | collective-permute-start | bytes 3145736 | tf_op jit(solution)/shard_map/ppermute | solution.py:578
  363.1 34.0 %collective-permute-start.46 = (bf16[256,2304]{1,0:T(8,128)(2,1)}, bf16[256,2304]{1,0:T(8,128)(2,1)}, u32[]{:S(2)}, u32[]{:S(2)}) collective-permute-start(bf16[256,2304]{1,0:T(8,128)(2,1)} %fusion.3), channel_id=1, source_target_pairs={{0,2},{1,3},{2,0},{3,1},{4,6},{5,7},{6,4},{7,5},{8,10},{9,11},{10,... | collective-permute-start | bytes 3538952 | tf_op jit(solution)/shard_map/ppermute | solution.py:578
  455.1 27.2 %collective-permute-start.55 = (bf16[128,2304]{1,0:T(8,128)(2,1)S(1)}, bf16[128,2304]{1,0:T(8,128)(2,1)}, u32[]{:S(2)}, u32[]{:S(2)}) collective-permute-start(bf16[128,2304]{1,0:T(8,128)(2,1)S(1)} %add_convert_fusion.5), channel_id=1, source_target_pairs={{0,16},{4,20},{8,24},{12,28},{16,0},{20,4},{24,8},{28,12},{1,17},{... | collective-permute-start | bytes 1769480 | tf_op jit(solution)/shard_map/ppermute | solution.py:578
  462.1 42.9 %collective-permute-start.64 = (bf16[512,1024]{1,0:T(8,128)(2,1)}, bf16[512,1024]{1,0:T(8,128)(2,1)}, u32[]{:S(2)}, u32[]{:S(2)}) collective-permute-start(bf16[512,1024]{1,0:T(8,128)(2,1)} %fusion.37.refs_0_), channel_id=1, source_target_pairs={{0,2},{1,3},{2,0},{3,1},{4,6},{5,7},{6,4},{7,5},{8,10},{9,11},{10,... | collective-permute-start | bytes 3145736 | tf_op jit(solution)/shard_map/ppermute | solution.py:578
  463.3 41.7 %collective-permute-start.65 = (bf16[512,1024]{1,0:T(8,128)(2,1)}, bf16[512,1024]{1,0:T(8,128)(2,1)}, u32[]{:S(2)}, u32[]{:S(2)}) collective-permute-start(bf16[512,1024]{1,0:T(8,128)(2,1)} %fusion.37.refs_0_), channel_id=1, source_target_pairs={{0,1},{1,0},{2,3},{3,2},{4,5},{5,4},{6,7},{7,6},{8,9},{9,8},{10,11... | collective-permute-start | bytes 3145736 | tf_op jit(solution)/shard_map/ppermute | solution.py:578
  (163 other events, 1606.1 us)
Sparse Core Ops, SparseCore 0:
  65.3 69.1 all-gather.3
  136.0 41.5 all-gather.5
  384.7 33.1 all-gather.7

commit v6 on v5

--- a/solution.py
+++ b/solution.py
@@ -845,9 +845,9 @@
 PLAN = (0, 2, 2)
 WAITS = {
     "down": (1, 2, 1, 1, 1),
-    "gate": (1, 2, 1, 1, 1),
-    "up": (1, 2, 1, 1, 1),
-    "output": (1, 3, 1, 1, 1),
+    "gate": (1, 2, 1, 1, 2),
+    "up": (1, 2, 1, 1, 3),
+    "output": (1, 3, 1, 1, 2),
     "qkvz": (1, 3, 1, 1, 1),
     "u": (1, 1, 1, 1, 1),
 }

time: 557 us -> 543 us (0.975)
  waiting for transfers between devices: 111 us -> 93 us
  starting transfers between devices: 58.1 us -> 66.6 us
    ppermute x77, waiting for transfers between devices: 111 us -> 93 us  [swap(): return lax.ppermute(values, axis, [(i, i ^ mask) for i in range(count)])]
    ppermute x77, starting transfers between devices: 57.6 us -> 66.1 us  [swap(): return lax.ppermute(values, axis, [(i, i ^ mask) for i in range(count)])]
    unnamed x224 -> x220, local copies, waits for them, and re-layouts: 14.1 us -> 14.9 us
  transfers between devices with their start and end apart: 80 -> 80, of which waited for: 23 -> 21; matrix products, arithmetic and copies ran while one was open for 37% -> 38% of each run, Pallas kernels for 25% -> 26%
where the time goes in v6:
time: 543 us; the launch traced here: 539 us
  Pallas kernels  140 us (26%)
  matrix products  129 us (24%)
  waiting for transfers between devices  93 us (17%)
  starting transfers between devices  66.6 us (12%)
  other arithmetic  56.2 us (10%)
  local copies, waits for them, and re-layouts  38.5 us (7%)
  between operations  15.7 us (3%)
    ppermute x77, waiting for transfers between devices, swap(): return lax.ppermute(values, axis, [(i, i ^ mask) for i in range(count)])  93 us
    dot_general x31, matrix products, transposed_dot(): lax.dot_general(left, right, (((0,), (0,)), ((), ())), preferred_element_...  70.4 us
    ppermute x77, starting transfers between devices, swap(): return lax.ppermute(values, axis, [(i, i ^ mask) for i in range(count)])  66.1 us
    dot_general x5, matrix products, back(): lax.dot_general(left, weight, (((1,), (1,)), ((), ())), preferred_element...  29.1 us
    dot_general x5, matrix products, dot(): return jnp.dot(left, right, preferred_element_type=jnp.float32)  27.7 us
    pallas_call x4, Pallas kernels, pick_rows(): pl.pallas_call(pick_kernel, out_shape=jax.ShapeDtypeStruct((wanted.shape[...  23.2 us
    pallas_call x2, Pallas kernels, conv_backward(): pl.pallas_call(partial(conv_backward_kernel, begin), grid=(blocks,), out_...  22.7 us
    convert_element_type x11, other arithmetic, add(): return total.astype(jnp.bfloat16)  20.2 us
  transfers between devices with their start and end apart: 80, of which 21 were waited for; matrix products, arithmetic and copies ran while one was open for 38% of the time, Pallas kernels for 26%

profile of v6, /device:TPU:0, one launch (start us, length us, event | category | flops | bytes accessed | tf_op | source)
XLA Modules:
  0.0 539.2 jit_solution(865045376354545361)
XLA Ops:
  20.4 16.4 %collective-permute-done.refs_2_ = bf16[128,4096]{1,0:T(8,128)(2,1)} collective-permute-done((bf16[128,4096]{1,0:T(8,128)(2,1)}, bf16[128,4096]{1,0:T(8,128)(2,1)}, u32[]{:S(2)}, u32[]{:S(2)}) %collective-permute-start) | collective-permute-done | bytes 1048608 | tf_op jit(solution)/shard_map/ppermute | solution.py:578
  41.0 24.1 %collective-permute-done.5 = bf16[2,9298]{1,0:T(2,128)(2,1)S(1)} collective-permute-done((bf16[2,9298]{1,0:T(2,128)(2,1)S(1)}, bf16[2,9298]{1,0:T(2,128)(2,1)S(1)}, u32[]{:S(2)}, u32[]{:S(2)}) %collective-permute-start.5) | collective-permute-done | bytes 37224 | tf_op jit(solution)/shard_map/ppermute | solution.py:578
  74.1 6.3 %pick_rows.4 = bf16[512,1024]{1,0:T(8,128)(2,1)} custom-call(s32[4]{0:T(128)} %add_multiply_fusion.shift_ref, s32[512,1]{1,0:T(8,128)} %copy.82.wanted_ref, bf16[512,1024]{1,0:T(8,128)(2,1)} %refs_0_.1, bf16[512,1024]{1,0:T(8,128)(2,1)} %collective-permute-done.6.refs_1_, bf16[512,1024]{1,0:T(8,128)(2,1)} %collective-permute-done.7.refs_2_, ...), custom_call_target="tpu_custom_call" | custom-call | tf_op jit(solution)/shard_map/pick_rows/pallas_call | solution.py:507
  80.3 7.6 %lay_rows.2 = bf16[1024,4096]{1,0:T(8,128)(2,1)} custom-call(s32[6]{0:T(128)} %and_select_fusion.1.place_ref, bf16[256,4096]{1,0:T(8,128)(2,1)} %refs_0_.2, bf16[256,4096]{1,0:T(8,128)(2,1)} %copy-done.42, bf16[128,4096]{1,0:T(8,128)(2,1)} %collective-permute-done.refs_2_, bf16[128,4096]{1,0:T(8,128)(2,1)} %collective-permute-done.4.refs_3_, ...), custom_call_target="tpu_custom_call" | custom-call | tf_op jit(solution)/shard_map/lay_rows/pallas_call | solution.py:534
  88.6 10.4 %fusion.173.u_ref.q_ref.k_ref.v_ref = f32[512,4096]{1,0:T(8,128)} fusion(bf16[512,1024]{1,0:T(8,128)(2,1)S(1)} %fusion.33, bf16[1024,4096]{1,0:T(8,128)(2,1)} %lay_rows.2), kind=kOutput, calls=%fused_computation.342 | convolution fusion | flops 4294967296 | bytes 17825792 | tf_op jit(solution)/shard_map/dot_general | solution.py:828
  101.2 9.7 %conv_forward.1 = (f32[512,1792]{1,0:T(8,128)}, bf16[512,1792]{1,0:T(8,128)(2,1)}) custom-call(f32[512,4096]{1,0:T(8,128)} %fusion.173.u_ref.q_ref.k_ref.v_ref, s32[512,1]{1,0:T(8,128)} %copy.80.place_ref, f32[4,1792]{1,0:T(4,128)} %reshape.304.weight_ref, f32[1,1792]{1,0:T(1,128)} %reshape.305.bias_ref, f32[512,128]{1,0:T(8,128)} %concatenate.40.step_ref), custom_call_target="tpu_custom_call" | custom-call | tf_op jit(solution)/shard_map/conv_forward/pallas_call | solution.py:380
  112.3 11.9 %attention_forward.1 = (bf16[512,512]{1,0:T(8,128)(2,1)}, f32[2,512,4]{2,1,0:T(8,128)}) custom-call(s32[1]{0:T(128)} %bitcast.20.limit_ref, f32[512,4096]{1,0:T(8,128)} %fusion.173.u_ref.q_ref.k_ref.v_ref, f32[512,4096]{1,0:T(8,128)} %fusion.173.u_ref.q_ref.k_ref.v_ref, f32[512,4096]{1,0:T(8,128)} %fusion.173.u_ref.q_ref.k_ref.v_ref, ...), custom_call_target="tpu_custom_call" | custom-call | tf_op jit(solution)/shard_map/attention_forward/pallas_call | solution.py:250
  129.2 9.2 %ssd_forward.1.y_ref = f32[512,1536]{1,0:T(8,128)} custom-call(s32[1]{0:T(128)} %bitcast.20.limit_ref, bf16[512,1792]{1,0:T(8,128)(2,1)} %get-tuple-element.233.c_ref.b_ref.x_ref.low_ref, bf16[512,1792]{1,0:T(8,128)(2,1)} %get-tuple-element.233.c_ref.b_ref.x_ref.low_ref, bf16[512,1792]{1,0:T(8,128)(2,1)} %get-tuple-element.233.c_ref.b_ref.x_ref.low_ref, ...), custom_call_target="tpu_custom_call" | custom-call | tf_op jit(solution)/shard_map/ssd_forward/pallas_call | solution.py:87
  156.1 7.6 %fusion.174 = f32[512,4096]{1,0:T(8,128)S(1)} fusion(bf16[512,1024]{1,0:T(8,128)(2,1)} %multiply_convert_fusion.1, bf16[1024,4096]{1,0:T(8,128)(2,1)} %all-gather.4.cloned.1.call-done), kind=kOutput, calls=%fused_computation.343 | convolution fusion | flops 4294967296 | bytes 17825792 | tf_op jit(solution)/shard_map/dot_general | solution.py:828
  170.8 5.7 %pick_rows.5 = bf16[512,1024]{1,0:T(8,128)(2,1)} custom-call(s32[4]{0:T(128)} %add_multiply_fusion.shift_ref, s32[512,1]{1,0:T(8,128)} %copy.82.wanted_ref, bf16[512,1024]{1,0:T(8,128)(2,1)} %refs_0_.4, bf16[512,1024]{1,0:T(8,128)(2,1)} %collective-permute-done.15.refs_1_, bf16[512,1024]{1,0:T(8,128)(2,1)} %collective-permute-done.16.refs_2_, ...), custom_call_target="tpu_custom_call" | custom-call | tf_op jit(solution)/shard_map/pick_rows/pallas_call | solution.py:507
  183.0 10.4 %multiply_multiply_fusion = (f32[512,2048]{1,0:T(8,128)S(1)}, f32[512,2048]{1,0:T(8,128)}) fusion(f32[512,4096]{1,0:T(8,128)} %copy-done.26, bf16[512,1024]{1,0:T(8,128)(2,1)} %pick_rows.5, bf16[2048,1024]{1,0:T(8,128)(2,1)} %all-gather.6.cloned.1.call-done), kind=kOutput, calls=%fused_computation.15 | convolution fusion | flops 2160066560 | bytes 22020096 | tf_op jit(solution)/shard_map/dot_general | solution.py:937
  204.1 8.0 %multiply_reduce_fusion.3 = (f32[1024]{0:T(1024)}, f32[512]{0:T(512)S(1)}, f32[512,1024]{1,0:T(8,128)S(1)}) fusion(f32[512,1024]{1,0:T(8,128)S(1)} %copy-done.28, f32[512]{0:T(512)S(1)} %fusion.147, f32[1024]{0:T(1024)S(1)} %bitcast.113, bf16[512,4096]{1,0:T(8,128)(2,1)S(1)} %add_convert_fusion, bf16[1024,4096]{1,0:T(8,128)(2,1)} %all-gather.4.cloned.1.call-done), kind=kOutput, calls=%fused_computation.93 | convolution fusion | flops 4298111488 | bytes 16789504 | tf_op jit(solution)/shard_map/dot_general | solution.py:937
  224.6 5.9 %fusion.169 = (bf16[512,1536]{1,0:T(8,128)(2,1)}, f32[512,1536]{1,0:T(8,128)}, bf16[512,1536]{1,0:T(8,128)(2,1)}) fusion(f32[512,4096]{1,0:T(8,128)} %fusion.173.u_ref.q_ref.k_ref.v_ref, f32[512,1536]{1,0:T(8,128)S(1)} %copy-done.7, f32[512]{0:T(512)S(1)} %multiply_multiply_fusion.2, f32[512]{0:T(512)S(1)} %fusion.146, f32[1536]{0:T(1024)S(1)} %reshape.308, ...), kind=kLoop, calls=%fused_computation.340 | loop fusion | flops 16515072 | bytes 22036480 | tf_op jit(solution)/shard_map/convert_element_type | solution.py:957
  242.9 9.6 %attention_backward.2 = (bf16[512,256]{1,0:T(8,128)(2,1)}, bf16[512,256]{1,0:T(8,128)(2,1)}) custom-call(s32[1]{0:T(128)} %bitcast.20.limit_ref, f32[512,4096]{1,0:T(8,128)} %fusion.173.u_ref.q_ref.k_ref.v_ref, f32[512,4096]{1,0:T(8,128)} %fusion.173.u_ref.q_ref.k_ref.v_ref, f32[512,4096]{1,0:T(8,128)} %fusion.173.u_ref.q_ref.k_ref.v_ref, ...), custom_call_target="tpu_custom_call" | custom-call | tf_op jit(solution)/shard_map/attention_backward/pallas_call | solution.py:313
  261.6 9.9 %attention_backward.3 = (bf16[512,256]{1,0:T(8,128)(2,1)}, bf16[512,256]{1,0:T(8,128)(2,1)}) custom-call(s32[1]{0:T(128)} %bitcast.20.limit_ref, f32[512,4096]{1,0:T(8,128)} %fusion.173.u_ref.q_ref.k_ref.v_ref, f32[512,4096]{1,0:T(8,128)} %fusion.173.u_ref.q_ref.k_ref.v_ref, f32[512,4096]{1,0:T(8,128)} %fusion.173.u_ref.q_ref.k_ref.v_ref, ...), custom_call_target="tpu_custom_call" | custom-call | tf_op jit(solution)/shard_map/attention_backward/pallas_call | solution.py:313
  296.1 8.5 %ssd_backward.2 = (f32[512,768]{1,0:T(8,128)}, f32[512,512]{1,0:T(8,128)}) custom-call(s32[1]{0:T(128)} %bitcast.20.limit_ref, bf16[512,1792]{1,0:T(8,128)(2,1)} %get-tuple-element.233.c_ref.b_ref.x_ref.low_ref, bf16[512,1792]{1,0:T(8,128)(2,1)} %get-tuple-element.233.c_ref.b_ref.x_ref.low_ref, ...), custom_call_target="tpu_custom_call" | custom-call | tf_op jit(solution)/shard_map/ssd_backward/pallas_call | solution.py:172
  323.4 9.7 %ssd_backward.3 = (f32[512,768]{1,0:T(8,128)}, f32[512,512]{1,0:T(8,128)}, f32[512,256]{1,0:T(8,128)}) custom-call(s32[1]{0:T(128)} %bitcast.20.limit_ref, bf16[512,1792]{1,0:T(8,128)(2,1)} %get-tuple-element.233.c_ref.b_ref.x_ref.low_ref, bf16[512,1792]{1,0:T(8,128)(2,1)} %get-tuple-element.233.c_ref.b_ref.x_ref.low_ref, ...), custom_call_target="tpu_custom_call" | custom-call | tf_op jit(solution)/shard_map/ssd_backward/pallas_call | solution.py:172
  333.2 6.8 %add_convert_fusion.2 = bf16[512,1024]{1,0:T(8,128)(2,1)} fusion(f32[512,1024]{1,0:T(8,128)} %copy-done.27, bf16[512,2048]{1,0:T(8,128)(2,1)} %fusion.2, bf16[2048,1024]{1,0:T(8,128)(2,1)} %all-gather.6.cloned.1.call-done), kind=kOutput, calls=%fused_computation.95 | convolution fusion | flops 2148532224 | bytes 9437184 | tf_op jit(solution)/shard_map/dot_general | solution.py:828
  349.6 9.9 %conv_backward.2 = (bf16[512,768]{1,0:T(8,128)(2,1)}, f32[8,768]{1,0:T(8,128)}, f32[512,128]{1,0:T(8,128)}) custom-call(f32[512,4096]{1,0:T(8,128)} %fusion.173.u_ref.q_ref.k_ref.v_ref, s32[512,1]{1,0:T(8,128)} %copy.80.place_ref, f32[4,1792]{1,0:T(4,128)} %reshape.304.weight_ref, f32[1,1792]{1,0:T(1,128)} %reshape.305.bias_ref, ...), custom_call_target="tpu_custom_call" | custom-call | tf_op jit(solution)/shard_map/conv_backward/pallas_call | solution.py:470
  370.0 12.8 %conv_backward.3 = (bf16[512,1024]{1,0:T(8,128)(2,1)}, f32[8,1024]{1,0:T(8,128)}, f32[512,128]{1,0:T(8,128)}) custom-call(f32[512,4096]{1,0:T(8,128)} %fusion.173.u_ref.q_ref.k_ref.v_ref, s32[512,1]{1,0:T(8,128)} %copy.80.place_ref, f32[4,1792]{1,0:T(4,128)} %reshape.304.weight_ref, f32[1,1792]{1,0:T(1,128)} %reshape.305.bias_ref, ...), custom_call_target="tpu_custom_call" | custom-call | tf_op jit(solution)/shard_map/conv_backward/pallas_call | solution.py:470
  416.3 7.8 %fusion.34 = (f32[1024]{0:T(1024)S(1)}, f32[512]{0:T(512)S(1)}, f32[512,1024]{1,0:T(8,128)S(1)}) fusion(bf16[512,1024]{1,0:T(8,128)(2,1)S(1)} %copy-done.20, f32[512]{0:T(512)S(1)} %copy-done.82, f32[1024]{0:T(1024)S(1)} %bitcast.110, f32[512,1024]{1,0:T(8,128)S(1)} %fusion.176, bf16[512,4096]{1,0:T(8,128)(2,1)S(1)} %copy-done.86, ...), kind=kOutput, calls=%fused_computation.86 | convolution fusion | flops 4299160064 | bytes 17838080 | tf_op jit(solution)/shard_map/dot_general | solution.py:937
  425.8 9.5 %collective-permute-done.51 = bf16[128,2304]{1,0:T(8,128)(2,1)S(1)} collective-permute-done((bf16[128,2304]{1,0:T(8,128)(2,1)S(1)}, bf16[128,2304]{1,0:T(8,128)(2,1)S(1)}, u32[]{:S(2)}, u32[]{:S(2)}) %collective-permute-start.51) | collective-permute-done | bytes 589856 | tf_op jit(solution)/shard_map/ppermute | solution.py:578
  452.3 10.2 %collective-permute-done.56 = bf16[128,1792]{1,0:T(8,128)(2,1)} collective-permute-done((bf16[128,1792]{1,0:T(8,128)(2,1)}, bf16[128,1792]{1,0:T(8,128)(2,1)}, u32[]{:S(2)}, u32[]{:S(2)}) %collective-permute-start.56) | collective-permute-done | bytes 458784 | tf_op jit(solution)/shard_map/ppermute | solution.py:578
  462.5 7.0 %collective-permute-done.55 = bf16[128,2304]{1,0:T(8,128)(2,1)} collective-permute-done((bf16[128,2304]{1,0:T(8,128)(2,1)S(1)}, bf16[128,2304]{1,0:T(8,128)(2,1)}, u32[]{:S(2)}, u32[]{:S(2)}) %collective-permute-start.55) | collective-permute-done | bytes 589856 | tf_op jit(solution)/shard_map/ppermute | solution.py:578
  (547 shorter events, 288.6 us)
Async XLA Ops:
  7.3 148.8 %all-gather.4.cloned.1.call-start = ((), (), s32[]{:S(2)}) async-start(), calls=%async_computation | async-start | bytes 10485760 | tf_op jit(solution)/shard_map/all_gather | solution.py:892
  7.3 29.5 %collective-permute-start.1 = (bf16[256,4096]{1,0:T(8,128)(2,1)}, bf16[256,4096]{1,0:T(8,128)(2,1)S(1)}, u32[]{:S(2)}, u32[]{:S(2)}) collective-permute-start(bf16[256,4096]{1,0:T(8,128)(2,1)} %refs_0_.2), channel_id=1, source_target_pairs={{0,1},{1,0},{2,3},{3,2},{4,5},{5,4},{6,7},{7,6},{8,9},{9,8},{10,11... | collective-permute-start | bytes 6291464 | tf_op jit(solution)/shard_map/ppermute | solution.py:578
  10.1 26.7 %collective-permute-start = (bf16[128,4096]{1,0:T(8,128)(2,1)}, bf16[128,4096]{1,0:T(8,128)(2,1)}, u32[]{:S(2)}, u32[]{:S(2)}) collective-permute-start(bf16[128,4096]{1,0:T(8,128)(2,1)} %constant_dynamic-slice_fusion.3), channel_id=1, source_target_pairs={{0,2},{1,3},{2,0},{3,1},{4,6},{5,7},{6,4},{7,5},{8,10},{9,11},{10,... | collective-permute-start | bytes 3145736 | tf_op jit(solution)/shard_map/ppermute | solution.py:578
  36.8 28.3 %collective-permute-start.3 = (bf16[128,4096]{1,0:T(8,128)(2,1)}, bf16[128,4096]{1,0:T(8,128)(2,1)}, u32[]{:S(2)}, u32[]{:S(2)}) collective-permute-start(bf16[128,4096]{1,0:T(8,128)(2,1)} %collective-permute-done.refs_2_), channel_id=1, source_target_pairs={{0,4},{4,0},{8,12},{12,8},{16,20},{20,16},{24,28},{28,24},{1,5},{5... | collective-permute-start | bytes 3145736 | tf_op jit(solution)/shard_map/ppermute | solution.py:578
  38.5 26.6 %collective-permute-start.6 = (bf16[512,1024]{1,0:T(8,128)(2,1)}, bf16[512,1024]{1,0:T(8,128)(2,1)}, u32[]{:S(2)}, u32[]{:S(2)}) collective-permute-start(bf16[512,1024]{1,0:T(8,128)(2,1)} %refs_0_.1), channel_id=1, source_target_pairs={{0,2},{1,3},{2,0},{3,1},{4,6},{5,7},{6,4},{7,5},{8,10},{9,11},{10,... | collective-permute-start | bytes 3145736 | tf_op jit(solution)/shard_map/ppermute | solution.py:578
  65.2 117.8 %all-gather.6.cloned.1.call-start = ((), (), s32[]{:S(2)}) async-start(), calls=%async_computation.1 | async-start | bytes 5242880 | tf_op jit(solution)/shard_map/all_gather | solution.py:893
  70.7 40.2 %collective-permute-start.11 = (bf16[512,1024]{1,0:T(8,128)(2,1)S(1)}, bf16[512,1024]{1,0:T(8,128)(2,1)}, u32[]{:S(2)}, u32[]{:S(2)}) collective-permute-start(bf16[512,1024]{1,0:T(8,128)(2,1)S(1)} %copy-done.37), channel_id=1, source_target_pairs={{0,1},{1,0},{2,3},{3,2},{4,5},{5,4},{6,7},{7,6},{8,9},{9,8},{10,11... | collective-permute-start | bytes 3145736 | tf_op jit(solution)/shard_map/ppermute | solution.py:578
  71.7 39.3 %collective-permute-start.10 = (bf16[256,1024]{1,0:T(8,128)(2,1)}, bf16[256,1024]{1,0:T(8,128)(2,1)}, u32[]{:S(2)}, u32[]{:S(2)}) collective-permute-start(bf16[256,1024]{1,0:T(8,128)(2,1)} %constant_dynamic-slice_fusion.2), channel_id=1, source_target_pairs={{0,2},{1,3},{2,0},{3,1},{4,6},{5,7},{6,4},{7,5},{8,10},{9,11},{10,... | collective-permute-start | bytes 1572872 | tf_op jit(solution)/shard_map/ppermute | solution.py:578
  125.8 311.1 %all-gather.8.cloned.1.call-start = ((), (), s32[]{:S(2)}) async-start(), calls=%async_computation.2 | async-start | bytes 5242880 | tf_op jit(solution)/shard_map/all_gather | solution.py:973
  126.1 41.6 %collective-permute-start.15 = (bf16[512,1024]{1,0:T(8,128)(2,1)}, bf16[512,1024]{1,0:T(8,128)(2,1)}, u32[]{:S(2)}, u32[]{:S(2)}) collective-permute-start(bf16[512,1024]{1,0:T(8,128)(2,1)} %refs_0_.4), channel_id=1, source_target_pairs={{0,2},{1,3},{2,0},{3,1},{4,6},{5,7},{6,4},{7,5},{8,10},{9,11},{10,... | collective-permute-start | bytes 3145736 | tf_op jit(solution)/shard_map/ppermute | solution.py:578
  126.8 41.0 %collective-permute-start.16 = (bf16[512,1024]{1,0:T(8,128)(2,1)}, bf16[512,1024]{1,0:T(8,128)(2,1)}, u32[]{:S(2)}, u32[]{:S(2)}) collective-permute-start(bf16[512,1024]{1,0:T(8,128)(2,1)} %refs_0_.4), channel_id=1, source_target_pairs={{0,1},{1,0},{2,3},{3,2},{4,5},{5,4},{6,7},{7,6},{8,9},{9,8},{10,11... | collective-permute-start | bytes 3145736 | tf_op jit(solution)/shard_map/ppermute | solution.py:578
  202.7 27.9 %collective-permute-start.22 = (bf16[512,1024]{1,0:T(8,128)(2,1)}, bf16[512,1024]{1,0:T(8,128)(2,1)S(1)}, u32[]{:S(2)}, u32[]{:S(2)}) collective-permute-start(bf16[512,1024]{1,0:T(8,128)(2,1)} %add_convert_fusion.3), channel_id=1, source_target_pairs={{0,2},{1,3},{2,0},{3,1},{4,6},{5,7},{6,4},{7,5},{8,10},{9,11},{10,... | collective-permute-start | bytes 3145736 | tf_op jit(solution)/shard_map/ppermute | solution.py:578
  224.0 28.4 %collective-permute-start.26 = (bf16[256,2048]{1,0:T(8,128)(2,1)}, bf16[256,2048]{1,0:T(8,128)(2,1)}, u32[]{:S(2)}, u32[]{:S(2)}) collective-permute-start(bf16[256,2048]{1,0:T(8,128)(2,1)} %fusion.13), channel_id=1, source_target_pairs={{0,2},{1,3},{2,0},{3,1},{4,6},{5,7},{6,4},{7,5},{8,10},{9,11},{10,... | collective-permute-start | bytes 3145736 | tf_op jit(solution)/shard_map/ppermute | solution.py:578
  241.5 31.8 %collective-permute-start.31 = (bf16[256,2048]{1,0:T(8,128)(2,1)}, bf16[256,2048]{1,0:T(8,128)(2,1)}, u32[]{:S(2)}, u32[]{:S(2)}) collective-permute-start(bf16[256,2048]{1,0:T(8,128)(2,1)} %fusion.14), channel_id=1, source_target_pairs={{0,2},{1,3},{2,0},{3,1},{4,6},{5,7},{6,4},{7,5},{8,10},{9,11},{10,... | collective-permute-start | bytes 3145736 | tf_op jit(solution)/shard_map/ppermute | solution.py:578
  280.6 31.8 %collective-permute-start.35 = (bf16[256,2304]{1,0:T(8,128)(2,1)}, bf16[256,2304]{1,0:T(8,128)(2,1)}, u32[]{:S(2)}, u32[]{:S(2)}) collective-permute-start(bf16[256,2304]{1,0:T(8,128)(2,1)} %convolution_convert_fusion.1), channel_id=1, source_target_pairs={{0,1},{1,0},{2,3},{3,2},{4,5},{5,4},{6,7},{7,6},{8,9},{9,8},{10,11... | collective-permute-start | bytes 3538952 | tf_op jit(solution)/shard_map/ppermute | solution.py:578
  280.6 31.8 %collective-permute-start.36 = (bf16[256,2304]{1,0:T(8,128)(2,1)}, bf16[256,2304]{1,0:T(8,128)(2,1)}, u32[]{:S(2)}, u32[]{:S(2)}) collective-permute-start(bf16[256,2304]{1,0:T(8,128)(2,1)} %convolution_convert_fusion), channel_id=1, source_target_pairs={{0,1},{1,0},{2,3},{3,2},{4,5},{5,4},{6,7},{7,6},{8,9},{9,8},{10,11... | collective-permute-start | bytes 3538952 | tf_op jit(solution)/shard_map/ppermute | solution.py:578
  309.5 30.4 %collective-permute-start.39 = (bf16[512,1024]{1,0:T(8,128)(2,1)}, bf16[512,1024]{1,0:T(8,128)(2,1)}, u32[]{:S(2)}, u32[]{:S(2)}) collective-permute-start(bf16[512,1024]{1,0:T(8,128)(2,1)} %add_convert_fusion.1), channel_id=1, source_target_pairs={{0,2},{1,3},{2,0},{3,1},{4,6},{5,7},{6,4},{7,5},{8,10},{9,11},{10,... | collective-permute-start | bytes 3145736 | tf_op jit(solution)/shard_map/ppermute | solution.py:578
  322.3 37.2 %collective-permute-start.40 = (bf16[128,2048]{1,0:T(8,128)(2,1)}, bf16[128,2048]{1,0:T(8,128)(2,1)}, u32[]{:S(2)}, u32[]{:S(2)}) collective-permute-start(bf16[128,2048]{1,0:T(8,128)(2,1)} %add_convert_fusion.11), channel_id=1, source_target_pairs={{0,16},{4,20},{8,24},{12,28},{16,0},{20,4},{24,8},{28,12},{1,17},{... | collective-permute-start | bytes 1572872 | tf_op jit(solution)/shard_map/ppermute | solution.py:578
  348.6 34.2 %collective-permute-start.44 = (bf16[256,2304]{1,0:T(8,128)(2,1)}, bf16[256,2304]{1,0:T(8,128)(2,1)}, u32[]{:S(2)}, u32[]{:S(2)}) collective-permute-start(bf16[256,2304]{1,0:T(8,128)(2,1)} %fusion.3), channel_id=1, source_target_pairs={{0,2},{1,3},{2,0},{3,1},{4,6},{5,7},{6,4},{7,5},{8,10},{9,11},{10,... | collective-permute-start | bytes 3538952 | tf_op jit(solution)/shard_map/ppermute | solution.py:578
  367.8 37.5 %collective-permute-start.45 = (bf16[128,2048]{1,0:T(8,128)(2,1)}, bf16[128,2048]{1,0:T(8,128)(2,1)}, u32[]{:S(2)}, u32[]{:S(2)}) collective-permute-start(bf16[128,2048]{1,0:T(8,128)(2,1)} %add_convert_fusion.9), channel_id=1, source_target_pairs={{0,16},{4,20},{8,24},{12,28},{16,0},{20,4},{24,8},{28,12},{1,17},{... | collective-permute-start | bytes 1572872 | tf_op jit(solution)/shard_map/ppermute | solution.py:578
  397.1 28.7 %collective-permute-start.50 = (bf16[256,1024]{1,0:T(8,128)(2,1)}, bf16[256,1024]{1,0:T(8,128)(2,1)}, u32[]{:S(2)}, u32[]{:S(2)}) collective-permute-start(bf16[256,1024]{1,0:T(8,128)(2,1)} %add_convert_fusion.7), channel_id=1, source_target_pairs={{0,16},{4,20},{8,24},{12,28},{16,0},{20,4},{24,8},{28,12},{1,17},{... | collective-permute-start | bytes 1572872 | tf_op jit(solution)/shard_map/ppermute | solution.py:578
  441.6 27.9 %collective-permute-start.55 = (bf16[128,2304]{1,0:T(8,128)(2,1)S(1)}, bf16[128,2304]{1,0:T(8,128)(2,1)}, u32[]{:S(2)}, u32[]{:S(2)}) collective-permute-start(bf16[128,2304]{1,0:T(8,128)(2,1)S(1)} %add_convert_fusion.5), channel_id=1, source_target_pairs={{0,16},{4,20},{8,24},{12,28},{16,0},{20,4},{24,8},{28,12},{1,17},{... | collective-permute-start | bytes 1769480 | tf_op jit(solution)/shard_map/ppermute | solution.py:578
  449.3 42.5 %collective-permute-start.64 = (bf16[512,1024]{1,0:T(8,128)(2,1)}, bf16[512,1024]{1,0:T(8,128)(2,1)}, u32[]{:S(2)}, u32[]{:S(2)}) collective-permute-start(bf16[512,1024]{1,0:T(8,128)(2,1)} %fusion.37.refs_0_), channel_id=1, source_target_pairs={{0,2},{1,3},{2,0},{3,1},{4,6},{5,7},{6,4},{7,5},{8,10},{9,11},{10,... | collective-permute-start | bytes 3145736 | tf_op jit(solution)/shard_map/ppermute | solution.py:578
  452.3 39.5 %collective-permute-start.65 = (bf16[512,1024]{1,0:T(8,128)(2,1)}, bf16[512,1024]{1,0:T(8,128)(2,1)}, u32[]{:S(2)}, u32[]{:S(2)}) collective-permute-start(bf16[512,1024]{1,0:T(8,128)(2,1)} %fusion.37.refs_0_), channel_id=1, source_target_pairs={{0,1},{1,0},{2,3},{3,2},{4,5},{5,4},{6,7},{7,6},{8,9},{9,8},{10,11... | collective-permute-start | bytes 3145736 | tf_op jit(solution)/shard_map/ppermute | solution.py:578
  (161 other events, 1602.6 us)
Sparse Core Ops, SparseCore 0:
  65.3 69.1 all-gather.3
  136.0 41.6 all-gather.5
  365.8 33.7 all-gather.7

commit v7 on v6

--- a/solution.py
+++ b/solution.py
@@ -846,7 +846,7 @@
 WAITS = {
     "down": (1, 2, 1, 1, 1),
     "gate": (1, 2, 1, 1, 2),
-    "up": (1, 2, 1, 1, 3),
+    "up": (1, 2, 1, 2, 2),
     "output": (1, 3, 1, 1, 2),
     "qkvz": (1, 3, 1, 1, 1),
     "u": (1, 1, 1, 1, 1),

time: 543 us -> 544 us (level)
    unnamed x220 -> x222, local copies, waits for them, and re-layouts: 14.9 us -> 14.9 us
  transfers between devices with their start and end apart: 80 -> 80, of which waited for: 21 -> 20; matrix products, arithmetic and copies ran while one was open for 38% -> 38% of each run, Pallas kernels for 26% -> 26%
where the time goes in v7:
time: 544 us; the launch traced here: 539 us
  Pallas kernels  140 us (26%)
  matrix products  129 us (24%)
  waiting for transfers between devices  91.9 us (17%)
  starting transfers between devices  67.6 us (12%)
  other arithmetic  56.3 us (10%)
  local copies, waits for them, and re-layouts  38.6 us (7%)
  between operations  15.7 us (3%)
    ppermute x77, waiting for transfers between devices, swap(): return lax.ppermute(values, axis, [(i, i ^ mask) for i in range(count)])  91.8 us
    dot_general x31, matrix products, transposed_dot(): lax.dot_general(left, right, (((0,), (0,)), ((), ())), preferred_element_...  70.4 us
    ppermute x77, starting transfers between devices, swap(): return lax.ppermute(values, axis, [(i, i ^ mask) for i in range(count)])  67.1 us
    dot_general x5, matrix products, back(): lax.dot_general(left, weight, (((1,), (1,)), ((), ())), preferred_element...  29 us
    dot_general x5, matrix products, dot(): return jnp.dot(left, right, preferred_element_type=jnp.float32)  27.7 us
    pallas_call x4, Pallas kernels, pick_rows(): pl.pallas_call(pick_kernel, out_shape=jax.ShapeDtypeStruct((wanted.shape[...  23.2 us
    pallas_call x2, Pallas kernels, conv_backward(): pl.pallas_call(partial(conv_backward_kernel, begin), grid=(blocks,), out_...  22.7 us
    convert_element_type x11, other arithmetic, add(): return total.astype(jnp.bfloat16)  20.3 us
  transfers between devices with their start and end apart: 80, of which 20 were waited for; matrix products, arithmetic and copies ran while one was open for 38% of the time, Pallas kernels for 26%

profile of v7, /device:TPU:0, one launch (start us, length us, event | category | flops | bytes accessed | tf_op | source)
XLA Modules:
  0.0 539.2 jit_solution(12477471619477911159)
XLA Ops:
  20.4 16.4 %collective-permute-done.refs_2_ = bf16[128,4096]{1,0:T(8,128)(2,1)} collective-permute-done((bf16[128,4096]{1,0:T(8,128)(2,1)}, bf16[128,4096]{1,0:T(8,128)(2,1)}, u32[]{:S(2)}, u32[]{:S(2)}) %collective-permute-start) | collective-permute-done | bytes 1048608 | tf_op jit(solution)/shard_map/ppermute | solution.py:578
  41.0 24.1 %collective-permute-done.5 = bf16[2,9298]{1,0:T(2,128)(2,1)S(1)} collective-permute-done((bf16[2,9298]{1,0:T(2,128)(2,1)S(1)}, bf16[2,9298]{1,0:T(2,128)(2,1)S(1)}, u32[]{:S(2)}, u32[]{:S(2)}) %collective-permute-start.5) | collective-permute-done | bytes 37224 | tf_op jit(solution)/shard_map/ppermute | solution.py:578
  74.1 6.3 %pick_rows.4 = bf16[512,1024]{1,0:T(8,128)(2,1)} custom-call(s32[4]{0:T(128)} %add_multiply_fusion.shift_ref, s32[512,1]{1,0:T(8,128)} %copy.82.wanted_ref, bf16[512,1024]{1,0:T(8,128)(2,1)} %refs_0_.1, bf16[512,1024]{1,0:T(8,128)(2,1)} %collective-permute-done.6.refs_1_, bf16[512,1024]{1,0:T(8,128)(2,1)} %collective-permute-done.7.refs_2_, ...), custom_call_target="tpu_custom_call" | custom-call | tf_op jit(solution)/shard_map/pick_rows/pallas_call | solution.py:507
  80.3 7.6 %lay_rows.2 = bf16[1024,4096]{1,0:T(8,128)(2,1)} custom-call(s32[6]{0:T(128)} %and_select_fusion.1.place_ref, bf16[256,4096]{1,0:T(8,128)(2,1)} %refs_0_.2, bf16[256,4096]{1,0:T(8,128)(2,1)} %copy-done.42, bf16[128,4096]{1,0:T(8,128)(2,1)} %collective-permute-done.refs_2_, bf16[128,4096]{1,0:T(8,128)(2,1)} %collective-permute-done.4.refs_3_, ...), custom_call_target="tpu_custom_call" | custom-call | tf_op jit(solution)/shard_map/lay_rows/pallas_call | solution.py:534
  88.6 10.5 %fusion.173.u_ref.q_ref.k_ref.v_ref = f32[512,4096]{1,0:T(8,128)} fusion(bf16[512,1024]{1,0:T(8,128)(2,1)S(1)} %fusion.33, bf16[1024,4096]{1,0:T(8,128)(2,1)} %lay_rows.2), kind=kOutput, calls=%fused_computation.342 | convolution fusion | flops 4294967296 | bytes 17825792 | tf_op jit(solution)/shard_map/dot_general | solution.py:828
  101.2 9.7 %conv_forward.1 = (f32[512,1792]{1,0:T(8,128)}, bf16[512,1792]{1,0:T(8,128)(2,1)}) custom-call(f32[512,4096]{1,0:T(8,128)} %fusion.173.u_ref.q_ref.k_ref.v_ref, s32[512,1]{1,0:T(8,128)} %copy.80.place_ref, f32[4,1792]{1,0:T(4,128)} %reshape.304.weight_ref, f32[1,1792]{1,0:T(1,128)} %reshape.305.bias_ref, f32[512,128]{1,0:T(8,128)} %concatenate.40.step_ref), custom_call_target="tpu_custom_call" | custom-call | tf_op jit(solution)/shard_map/conv_forward/pallas_call | solution.py:380
  112.3 11.9 %attention_forward.1 = (bf16[512,512]{1,0:T(8,128)(2,1)}, f32[2,512,4]{2,1,0:T(8,128)}) custom-call(s32[1]{0:T(128)} %bitcast.20.limit_ref, f32[512,4096]{1,0:T(8,128)} %fusion.173.u_ref.q_ref.k_ref.v_ref, f32[512,4096]{1,0:T(8,128)} %fusion.173.u_ref.q_ref.k_ref.v_ref, f32[512,4096]{1,0:T(8,128)} %fusion.173.u_ref.q_ref.k_ref.v_ref, ...), custom_call_target="tpu_custom_call" | custom-call | tf_op jit(solution)/shard_map/attention_forward/pallas_call | solution.py:250
  129.2 9.2 %ssd_forward.1.y_ref = f32[512,1536]{1,0:T(8,128)} custom-call(s32[1]{0:T(128)} %bitcast.20.limit_ref, bf16[512,1792]{1,0:T(8,128)(2,1)} %get-tuple-element.233.c_ref.b_ref.x_ref.low_ref, bf16[512,1792]{1,0:T(8,128)(2,1)} %get-tuple-element.233.c_ref.b_ref.x_ref.low_ref, bf16[512,1792]{1,0:T(8,128)(2,1)} %get-tuple-element.233.c_ref.b_ref.x_ref.low_ref, ...), custom_call_target="tpu_custom_call" | custom-call | tf_op jit(solution)/shard_map/ssd_forward/pallas_call | solution.py:87
  156.1 7.6 %fusion.174 = f32[512,4096]{1,0:T(8,128)S(1)} fusion(bf16[512,1024]{1,0:T(8,128)(2,1)} %multiply_convert_fusion.1, bf16[1024,4096]{1,0:T(8,128)(2,1)} %all-gather.4.cloned.1.call-done), kind=kOutput, calls=%fused_computation.343 | convolution fusion | flops 4294967296 | bytes 17825792 | tf_op jit(solution)/shard_map/dot_general | solution.py:828
  170.8 5.7 %pick_rows.5 = bf16[512,1024]{1,0:T(8,128)(2,1)} custom-call(s32[4]{0:T(128)} %add_multiply_fusion.shift_ref, s32[512,1]{1,0:T(8,128)} %copy.82.wanted_ref, bf16[512,1024]{1,0:T(8,128)(2,1)} %refs_0_.4, bf16[512,1024]{1,0:T(8,128)(2,1)} %collective-permute-done.15.refs_1_, bf16[512,1024]{1,0:T(8,128)(2,1)} %collective-permute-done.16.refs_2_, ...), custom_call_target="tpu_custom_call" | custom-call | tf_op jit(solution)/shard_map/pick_rows/pallas_call | solution.py:507
  183.0 10.4 %multiply_multiply_fusion = (f32[512,2048]{1,0:T(8,128)S(1)}, f32[512,2048]{1,0:T(8,128)}) fusion(f32[512,4096]{1,0:T(8,128)} %copy-done.26, bf16[512,1024]{1,0:T(8,128)(2,1)} %pick_rows.5, bf16[2048,1024]{1,0:T(8,128)(2,1)} %all-gather.6.cloned.1.call-done), kind=kOutput, calls=%fused_computation.15 | convolution fusion | flops 2160066560 | bytes 22020096 | tf_op jit(solution)/shard_map/dot_general | solution.py:937
  204.2 8.0 %multiply_reduce_fusion.3 = (f32[1024]{0:T(1024)}, f32[512]{0:T(512)S(1)}, f32[512,1024]{1,0:T(8,128)S(1)}) fusion(f32[512,1024]{1,0:T(8,128)S(1)} %copy-done.28, f32[512]{0:T(512)S(1)} %fusion.147, f32[1024]{0:T(1024)S(1)} %bitcast.113, bf16[512,4096]{1,0:T(8,128)(2,1)S(1)} %add_convert_fusion, bf16[1024,4096]{1,0:T(8,128)(2,1)} %all-gather.4.cloned.1.call-done), kind=kOutput, calls=%fused_computation.93 | convolution fusion | flops 4298111488 | bytes 16789504 | tf_op jit(solution)/shard_map/dot_general | solution.py:937
  224.6 6.0 %fusion.169 = (bf16[512,1536]{1,0:T(8,128)(2,1)}, f32[512,1536]{1,0:T(8,128)}, bf16[512,1536]{1,0:T(8,128)(2,1)}) fusion(f32[512,4096]{1,0:T(8,128)} %fusion.173.u_ref.q_ref.k_ref.v_ref, f32[512,1536]{1,0:T(8,128)S(1)} %copy-done.7, f32[512]{0:T(512)S(1)} %multiply_multiply_fusion.2, f32[512]{0:T(512)S(1)} %fusion.146, f32[1536]{0:T(1024)S(1)} %reshape.308, ...), kind=kLoop, calls=%fused_computation.340 | loop fusion | flops 16515072 | bytes 22036480 | tf_op jit(solution)/shard_map/convert_element_type | solution.py:957
  243.0 9.5 %attention_backward.2 = (bf16[512,256]{1,0:T(8,128)(2,1)}, bf16[512,256]{1,0:T(8,128)(2,1)}) custom-call(s32[1]{0:T(128)} %bitcast.20.limit_ref, f32[512,4096]{1,0:T(8,128)} %fusion.173.u_ref.q_ref.k_ref.v_ref, f32[512,4096]{1,0:T(8,128)} %fusion.173.u_ref.q_ref.k_ref.v_ref, f32[512,4096]{1,0:T(8,128)} %fusion.173.u_ref.q_ref.k_ref.v_ref, ...), custom_call_target="tpu_custom_call" | custom-call | tf_op jit(solution)/shard_map/attention_backward/pallas_call | solution.py:313
  261.7 9.9 %attention_backward.3 = (bf16[512,256]{1,0:T(8,128)(2,1)}, bf16[512,256]{1,0:T(8,128)(2,1)}) custom-call(s32[1]{0:T(128)} %bitcast.20.limit_ref, f32[512,4096]{1,0:T(8,128)} %fusion.173.u_ref.q_ref.k_ref.v_ref, f32[512,4096]{1,0:T(8,128)} %fusion.173.u_ref.q_ref.k_ref.v_ref, f32[512,4096]{1,0:T(8,128)} %fusion.173.u_ref.q_ref.k_ref.v_ref, ...), custom_call_target="tpu_custom_call" | custom-call | tf_op jit(solution)/shard_map/attention_backward/pallas_call | solution.py:313
  296.2 8.5 %ssd_backward.2 = (f32[512,768]{1,0:T(8,128)}, f32[512,512]{1,0:T(8,128)}) custom-call(s32[1]{0:T(128)} %bitcast.20.limit_ref, bf16[512,1792]{1,0:T(8,128)(2,1)} %get-tuple-element.233.c_ref.b_ref.x_ref.low_ref, bf16[512,1792]{1,0:T(8,128)(2,1)} %get-tuple-element.233.c_ref.b_ref.x_ref.low_ref, ...), custom_call_target="tpu_custom_call" | custom-call | tf_op jit(solution)/shard_map/ssd_backward/pallas_call | solution.py:172
  323.5 9.8 %ssd_backward.3 = (f32[512,768]{1,0:T(8,128)}, f32[512,512]{1,0:T(8,128)}, f32[512,256]{1,0:T(8,128)}) custom-call(s32[1]{0:T(128)} %bitcast.20.limit_ref, bf16[512,1792]{1,0:T(8,128)(2,1)} %get-tuple-element.233.c_ref.b_ref.x_ref.low_ref, bf16[512,1792]{1,0:T(8,128)(2,1)} %get-tuple-element.233.c_ref.b_ref.x_ref.low_ref, ...), custom_call_target="tpu_custom_call" | custom-call | tf_op jit(solution)/shard_map/ssd_backward/pallas_call | solution.py:172
  333.2 6.8 %add_convert_fusion.2 = bf16[512,1024]{1,0:T(8,128)(2,1)} fusion(f32[512,1024]{1,0:T(8,128)} %copy-done.27, bf16[512,2048]{1,0:T(8,128)(2,1)} %fusion.2, bf16[2048,1024]{1,0:T(8,128)(2,1)} %all-gather.6.cloned.1.call-done), kind=kOutput, calls=%fused_computation.95 | convolution fusion | flops 2148532224 | bytes 9437184 | tf_op jit(solution)/shard_map/dot_general | solution.py:828
  349.5 9.8 %conv_backward.2 = (bf16[512,768]{1,0:T(8,128)(2,1)}, f32[8,768]{1,0:T(8,128)}, f32[512,128]{1,0:T(8,128)}) custom-call(f32[512,4096]{1,0:T(8,128)} %fusion.173.u_ref.q_ref.k_ref.v_ref, s32[512,1]{1,0:T(8,128)} %copy.80.place_ref, f32[4,1792]{1,0:T(4,128)} %reshape.304.weight_ref, f32[1,1792]{1,0:T(1,128)} %reshape.305.bias_ref, ...), custom_call_target="tpu_custom_call" | custom-call | tf_op jit(solution)/shard_map/conv_backward/pallas_call | solution.py:470
  370.1 12.8 %conv_backward.3 = (bf16[512,1024]{1,0:T(8,128)(2,1)}, f32[8,1024]{1,0:T(8,128)}, f32[512,128]{1,0:T(8,128)}) custom-call(f32[512,4096]{1,0:T(8,128)} %fusion.173.u_ref.q_ref.k_ref.v_ref, s32[512,1]{1,0:T(8,128)} %copy.80.place_ref, f32[4,1792]{1,0:T(4,128)} %reshape.304.weight_ref, f32[1,1792]{1,0:T(1,128)} %reshape.305.bias_ref, ...), custom_call_target="tpu_custom_call" | custom-call | tf_op jit(solution)/shard_map/conv_backward/pallas_call | solution.py:470
  416.5 7.8 %fusion.34 = (f32[1024]{0:T(1024)S(1)}, f32[512]{0:T(512)S(1)}, f32[512,1024]{1,0:T(8,128)S(1)}) fusion(bf16[512,1024]{1,0:T(8,128)(2,1)S(1)} %copy-done.20, f32[512]{0:T(512)S(1)} %copy-done.83, f32[1024]{0:T(1024)S(1)} %bitcast.110, f32[512,1024]{1,0:T(8,128)S(1)} %fusion.176, bf16[512,4096]{1,0:T(8,128)(2,1)S(1)} %copy-done.87, ...), kind=kOutput, calls=%fused_computation.86 | convolution fusion | flops 4299160064 | bytes 17838080 | tf_op jit(solution)/shard_map/dot_general | solution.py:937
  425.9 9.3 %collective-permute-done.51 = bf16[128,2304]{1,0:T(8,128)(2,1)S(1)} collective-permute-done((bf16[128,2304]{1,0:T(8,128)(2,1)S(1)}, bf16[128,2304]{1,0:T(8,128)(2,1)S(1)}, u32[]{:S(2)}, u32[]{:S(2)}) %collective-permute-start.51) | collective-permute-done | bytes 589856 | tf_op jit(solution)/shard_map/ppermute | solution.py:578
  452.0 10.4 %collective-permute-done.56 = bf16[128,1792]{1,0:T(8,128)(2,1)} collective-permute-done((bf16[128,1792]{1,0:T(8,128)(2,1)}, bf16[128,1792]{1,0:T(8,128)(2,1)}, u32[]{:S(2)}, u32[]{:S(2)}) %collective-permute-start.56) | collective-permute-done | bytes 458784 | tf_op jit(solution)/shard_map/ppermute | solution.py:578
  462.4 7.1 %collective-permute-done.55 = bf16[128,2304]{1,0:T(8,128)(2,1)} collective-permute-done((bf16[128,2304]{1,0:T(8,128)(2,1)S(1)}, bf16[128,2304]{1,0:T(8,128)(2,1)}, u32[]{:S(2)}, u32[]{:S(2)}) %collective-permute-start.55) | collective-permute-done | bytes 589856 | tf_op jit(solution)/shard_map/ppermute | solution.py:578
  (549 shorter events, 288.5 us)
Async XLA Ops:
  7.3 148.8 %all-gather.4.cloned.1.call-start = ((), (), s32[]{:S(2)}) async-start(), calls=%async_computation | async-start | bytes 10485760 | tf_op jit(solution)/shard_map/all_gather | solution.py:892
  7.3 29.5 %collective-permute-start.1 = (bf16[256,4096]{1,0:T(8,128)(2,1)}, bf16[256,4096]{1,0:T(8,128)(2,1)S(1)}, u32[]{:S(2)}, u32[]{:S(2)}) collective-permute-start(bf16[256,4096]{1,0:T(8,128)(2,1)} %refs_0_.2), channel_id=1, source_target_pairs={{0,1},{1,0},{2,3},{3,2},{4,5},{5,4},{6,7},{7,6},{8,9},{9,8},{10,11... | collective-permute-start | bytes 6291464 | tf_op jit(solution)/shard_map/ppermute | solution.py:578
  10.1 26.7 %collective-permute-start = (bf16[128,4096]{1,0:T(8,128)(2,1)}, bf16[128,4096]{1,0:T(8,128)(2,1)}, u32[]{:S(2)}, u32[]{:S(2)}) collective-permute-start(bf16[128,4096]{1,0:T(8,128)(2,1)} %constant_dynamic-slice_fusion.3), channel_id=1, source_target_pairs={{0,2},{1,3},{2,0},{3,1},{4,6},{5,7},{6,4},{7,5},{8,10},{9,11},{10,... | collective-permute-start | bytes 3145736 | tf_op jit(solution)/shard_map/ppermute | solution.py:578
  36.8 28.3 %collective-permute-start.3 = (bf16[128,4096]{1,0:T(8,128)(2,1)}, bf16[128,4096]{1,0:T(8,128)(2,1)}, u32[]{:S(2)}, u32[]{:S(2)}) collective-permute-start(bf16[128,4096]{1,0:T(8,128)(2,1)} %collective-permute-done.refs_2_), channel_id=1, source_target_pairs={{0,4},{4,0},{8,12},{12,8},{16,20},{20,16},{24,28},{28,24},{1,5},{5... | collective-permute-start | bytes 3145736 | tf_op jit(solution)/shard_map/ppermute | solution.py:578
  65.2 117.8 %all-gather.6.cloned.1.call-start = ((), (), s32[]{:S(2)}) async-start(), calls=%async_computation.1 | async-start | bytes 5242880 | tf_op jit(solution)/shard_map/all_gather | solution.py:893
  70.8 40.2 %collective-permute-start.11 = (bf16[512,1024]{1,0:T(8,128)(2,1)S(1)}, bf16[512,1024]{1,0:T(8,128)(2,1)}, u32[]{:S(2)}, u32[]{:S(2)}) collective-permute-start(bf16[512,1024]{1,0:T(8,128)(2,1)S(1)} %copy-done.37), channel_id=1, source_target_pairs={{0,1},{1,0},{2,3},{3,2},{4,5},{5,4},{6,7},{7,6},{8,9},{9,8},{10,11... | collective-permute-start | bytes 3145736 | tf_op jit(solution)/shard_map/ppermute | solution.py:578
  71.7 39.3 %collective-permute-start.10 = (bf16[256,1024]{1,0:T(8,128)(2,1)}, bf16[256,1024]{1,0:T(8,128)(2,1)}, u32[]{:S(2)}, u32[]{:S(2)}) collective-permute-start(bf16[256,1024]{1,0:T(8,128)(2,1)} %constant_dynamic-slice_fusion.2), channel_id=1, source_target_pairs={{0,2},{1,3},{2,0},{3,1},{4,6},{5,7},{6,4},{7,5},{8,10},{9,11},{10,... | collective-permute-start | bytes 1572872 | tf_op jit(solution)/shard_map/ppermute | solution.py:578
  125.8 311.1 %all-gather.8.cloned.1.call-start = ((), (), s32[]{:S(2)}) async-start(), calls=%async_computation.2 | async-start | bytes 5242880 | tf_op jit(solution)/shard_map/all_gather | solution.py:973
  126.1 41.6 %collective-permute-start.15 = (bf16[512,1024]{1,0:T(8,128)(2,1)}, bf16[512,1024]{1,0:T(8,128)(2,1)}, u32[]{:S(2)}, u32[]{:S(2)}) collective-permute-start(bf16[512,1024]{1,0:T(8,128)(2,1)} %refs_0_.4), channel_id=1, source_target_pairs={{0,2},{1,3},{2,0},{3,1},{4,6},{5,7},{6,4},{7,5},{8,10},{9,11},{10,... | collective-permute-start | bytes 3145736 | tf_op jit(solution)/shard_map/ppermute | solution.py:578
  126.7 41.0 %collective-permute-start.16 = (bf16[512,1024]{1,0:T(8,128)(2,1)}, bf16[512,1024]{1,0:T(8,128)(2,1)}, u32[]{:S(2)}, u32[]{:S(2)}) collective-permute-start(bf16[512,1024]{1,0:T(8,128)(2,1)} %refs_0_.4), channel_id=1, source_target_pairs={{0,1},{1,0},{2,3},{3,2},{4,5},{5,4},{6,7},{7,6},{8,9},{9,8},{10,11... | collective-permute-start | bytes 3145736 | tf_op jit(solution)/shard_map/ppermute | solution.py:578
  202.7 27.9 %collective-permute-start.22 = (bf16[512,1024]{1,0:T(8,128)(2,1)}, bf16[512,1024]{1,0:T(8,128)(2,1)S(1)}, u32[]{:S(2)}, u32[]{:S(2)}) collective-permute-start(bf16[512,1024]{1,0:T(8,128)(2,1)} %add_convert_fusion.3), channel_id=1, source_target_pairs={{0,2},{1,3},{2,0},{3,1},{4,6},{5,7},{6,4},{7,5},{8,10},{9,11},{10,... | collective-permute-start | bytes 3145736 | tf_op jit(solution)/shard_map/ppermute | solution.py:578
  224.1 28.4 %collective-permute-start.26 = (bf16[256,2048]{1,0:T(8,128)(2,1)}, bf16[256,2048]{1,0:T(8,128)(2,1)}, u32[]{:S(2)}, u32[]{:S(2)}) collective-permute-start(bf16[256,2048]{1,0:T(8,128)(2,1)} %fusion.13), channel_id=1, source_target_pairs={{0,2},{1,3},{2,0},{3,1},{4,6},{5,7},{6,4},{7,5},{8,10},{9,11},{10,... | collective-permute-start | bytes 3145736 | tf_op jit(solution)/shard_map/ppermute | solution.py:578
  241.5 31.9 %collective-permute-start.31 = (bf16[256,2048]{1,0:T(8,128)(2,1)}, bf16[256,2048]{1,0:T(8,128)(2,1)}, u32[]{:S(2)}, u32[]{:S(2)}) collective-permute-start(bf16[256,2048]{1,0:T(8,128)(2,1)} %fusion.14), channel_id=1, source_target_pairs={{0,2},{1,3},{2,0},{3,1},{4,6},{5,7},{6,4},{7,5},{8,10},{9,11},{10,... | collective-permute-start | bytes 3145736 | tf_op jit(solution)/shard_map/ppermute | solution.py:578
  280.6 31.8 %collective-permute-start.35 = (bf16[256,2304]{1,0:T(8,128)(2,1)}, bf16[256,2304]{1,0:T(8,128)(2,1)}, u32[]{:S(2)}, u32[]{:S(2)}) collective-permute-start(bf16[256,2304]{1,0:T(8,128)(2,1)} %convolution_convert_fusion.1), channel_id=1, source_target_pairs={{0,1},{1,0},{2,3},{3,2},{4,5},{5,4},{6,7},{7,6},{8,9},{9,8},{10,11... | collective-permute-start | bytes 3538952 | tf_op jit(solution)/shard_map/ppermute | solution.py:578
  280.6 31.8 %collective-permute-start.36 = (bf16[256,2304]{1,0:T(8,128)(2,1)}, bf16[256,2304]{1,0:T(8,128)(2,1)}, u32[]{:S(2)}, u32[]{:S(2)}) collective-permute-start(bf16[256,2304]{1,0:T(8,128)(2,1)} %convolution_convert_fusion), channel_id=1, source_target_pairs={{0,1},{1,0},{2,3},{3,2},{4,5},{5,4},{6,7},{7,6},{8,9},{9,8},{10,11... | collective-permute-start | bytes 3538952 | tf_op jit(solution)/shard_map/ppermute | solution.py:578
  309.5 30.4 %collective-permute-start.38 = (bf16[512,1024]{1,0:T(8,128)(2,1)}, bf16[512,1024]{1,0:T(8,128)(2,1)}, u32[]{:S(2)}, u32[]{:S(2)}) collective-permute-start(bf16[512,1024]{1,0:T(8,128)(2,1)} %add_convert_fusion.1), channel_id=1, source_target_pairs={{0,2},{1,3},{2,0},{3,1},{4,6},{5,7},{6,4},{7,5},{8,10},{9,11},{10,... | collective-permute-start | bytes 3145736 | tf_op jit(solution)/shard_map/ppermute | solution.py:578
  319.1 40.2 %collective-permute-start.39 = (bf16[128,2048]{1,0:T(8,128)(2,1)}, bf16[128,2048]{1,0:T(8,128)(2,1)}, u32[]{:S(2)}, u32[]{:S(2)}) collective-permute-start(bf16[128,2048]{1,0:T(8,128)(2,1)} %add_convert_fusion.11), channel_id=1, source_target_pairs={{0,16},{4,20},{8,24},{12,28},{16,0},{20,4},{24,8},{28,12},{1,17},{... | collective-permute-start | bytes 1572872 | tf_op jit(solution)/shard_map/ppermute | solution.py:578
  322.4 36.9 %collective-permute-start.40 = (bf16[128,2048]{1,0:T(8,128)(2,1)}, bf16[128,2048]{1,0:T(8,128)(2,1)}, u32[]{:S(2)}, u32[]{:S(2)}) collective-permute-start(bf16[128,2048]{1,0:T(8,128)(2,1)} %fusion.31), channel_id=1, source_target_pairs={{0,8},{4,12},{8,0},{12,4},{16,24},{20,28},{24,16},{28,20},{1,9},{5... | collective-permute-start | bytes 1572872 | tf_op jit(solution)/shard_map/ppermute | solution.py:578
  348.2 34.7 %collective-permute-start.44 = (bf16[256,2304]{1,0:T(8,128)(2,1)}, bf16[256,2304]{1,0:T(8,128)(2,1)}, u32[]{:S(2)}, u32[]{:S(2)}) collective-permute-start(bf16[256,2304]{1,0:T(8,128)(2,1)} %fusion.3), channel_id=1, source_target_pairs={{0,2},{1,3},{2,0},{3,1},{4,6},{5,7},{6,4},{7,5},{8,10},{9,11},{10,... | collective-permute-start | bytes 3538952 | tf_op jit(solution)/shard_map/ppermute | solution.py:578
  367.8 37.5 %collective-permute-start.45 = (bf16[128,2048]{1,0:T(8,128)(2,1)}, bf16[128,2048]{1,0:T(8,128)(2,1)}, u32[]{:S(2)}, u32[]{:S(2)}) collective-permute-start(bf16[128,2048]{1,0:T(8,128)(2,1)} %add_convert_fusion.9), channel_id=1, source_target_pairs={{0,16},{4,20},{8,24},{12,28},{16,0},{20,4},{24,8},{28,12},{1,17},{... | collective-permute-start | bytes 1572872 | tf_op jit(solution)/shard_map/ppermute | solution.py:578
  396.9 29.0 %collective-permute-start.50 = (bf16[256,1024]{1,0:T(8,128)(2,1)}, bf16[256,1024]{1,0:T(8,128)(2,1)}, u32[]{:S(2)}, u32[]{:S(2)}) collective-permute-start(bf16[256,1024]{1,0:T(8,128)(2,1)} %add_convert_fusion.7), channel_id=1, source_target_pairs={{0,16},{4,20},{8,24},{12,28},{16,0},{20,4},{24,8},{28,12},{1,17},{... | collective-permute-start | bytes 1572872 | tf_op jit(solution)/shard_map/ppermute | solution.py:578
  441.5 27.9 %collective-permute-start.55 = (bf16[128,2304]{1,0:T(8,128)(2,1)S(1)}, bf16[128,2304]{1,0:T(8,128)(2,1)}, u32[]{:S(2)}, u32[]{:S(2)}) collective-permute-start(bf16[128,2304]{1,0:T(8,128)(2,1)S(1)} %add_convert_fusion.5), channel_id=1, source_target_pairs={{0,16},{4,20},{8,24},{12,28},{16,0},{20,4},{24,8},{28,12},{1,17},{... | collective-permute-start | bytes 1769480 | tf_op jit(solution)/shard_map/ppermute | solution.py:578
  449.3 42.3 %collective-permute-start.64 = (bf16[512,1024]{1,0:T(8,128)(2,1)}, bf16[512,1024]{1,0:T(8,128)(2,1)}, u32[]{:S(2)}, u32[]{:S(2)}) collective-permute-start(bf16[512,1024]{1,0:T(8,128)(2,1)} %fusion.37.refs_0_), channel_id=1, source_target_pairs={{0,2},{1,3},{2,0},{3,1},{4,6},{5,7},{6,4},{7,5},{8,10},{9,11},{10,... | collective-permute-start | bytes 3145736 | tf_op jit(solution)/shard_map/ppermute | solution.py:578
  452.0 39.6 %collective-permute-start.65 = (bf16[512,1024]{1,0:T(8,128)(2,1)}, bf16[512,1024]{1,0:T(8,128)(2,1)}, u32[]{:S(2)}, u32[]{:S(2)}) collective-permute-start(bf16[512,1024]{1,0:T(8,128)(2,1)} %fusion.37.refs_0_), channel_id=1, source_target_pairs={{0,1},{1,0},{2,3},{3,2},{4,5},{5,4},{6,7},{7,6},{8,9},{9,8},{10,11... | collective-permute-start | bytes 3145736 | tf_op jit(solution)/shard_map/ppermute | solution.py:578
  (162 other events, 1625.6 us)
Sparse Core Ops, SparseCore 0:
  65.3 69.1 all-gather.3
  136.1 41.5 all-gather.5
  365.8 33.8 all-gather.7
